TPU v7x, 32 devices: a whole 2x2x4 slice. The times are simulated.
32 devices in a mesh: dp: 16 (over z, y, x), tensor: 2 (over core).
Axes of the slice: x: 2, y: 2, z: 4, core: 2. Of those that a mesh axis runs over, the one named last changes fastest.
Arguments:
- tokens: bfloat16 [32768, 768], P(('dp', 'tensor')), may hold values from -6 to 6
- cotangent: bfloat16 [32768, 768], P(('dp', 'tensor')), may hold values from -6 to 6
- lengths: int32 [64], P('dp'), may hold values from 128 to 512, as said below
- query_weight: bfloat16 [768, 768], P('dp', 'tensor'), may hold values from -0.21875 to 0.21875
- key_weight: bfloat16 [768, 768], P('dp', 'tensor'), may hold values from -0.21875 to 0.21875
- value_weight: bfloat16 [768, 768], P('dp', 'tensor'), may hold values from -0.21875 to 0.21875
- out_weight: bfloat16 [768, 768], P('tensor', 'dp'), may hold values from -2.5 to 2.5
- query_bias: bfloat16 [768], P('dp'), may hold values from -3 to 3
- value_bias: bfloat16 [768], P('dp'), may hold values from -0.29882812 to 0.29882812
- out_bias: bfloat16 [768], P('dp'), may hold values from -3 to 3
- first_gain: bfloat16 [768], P('dp'), may hold values from 0.5 to 1.5
- first_shift: bfloat16 [768], P('dp'), may hold values from -2 to 2
- inner_weight: bfloat16 [768, 3072], P('dp', 'tensor'), may hold values from -0.21875 to 0.21875
- inner_bias: bfloat16 [3072], P('dp'), may hold values from -3 to 3
- outer_weight: bfloat16 [3072, 768], P('tensor', 'dp'), may hold values from -0.109375 to 0.109375
- outer_bias: bfloat16 [768], P('dp'), may hold values from -2 to 2
- second_gain: bfloat16 [768], P('dp'), may hold values from 0.5 to 1.5
- second_shift: bfloat16 [768], P('dp'), may hold values from -2 to 2
Outputs:
- layer_out: float32 [32768, 768], P(('dp', 'tensor'))
- token_grad: float32 [32768, 768], P(('dp', 'tensor'))
- query_weight_grad: float32 [768, 768], P('dp', 'tensor')
- key_weight_grad: float32 [768, 768], P('dp', 'tensor')
- value_weight_grad: float32 [768, 768], P('dp', 'tensor')
- out_weight_grad: float32 [768, 768], P('tensor', 'dp')
- query_bias_grad: float32 [768], P('dp')
- value_bias_grad: float32 [768], P('dp')
- out_bias_grad: float32 [768], P('dp')
- first_gain_grad: float32 [768], P('dp')
- first_shift_grad: float32 [768], P('dp')
- inner_weight_grad: float32 [768, 3072], P('dp', 'tensor')
- inner_bias_grad: float32 [3072], P('dp')
- outer_weight_grad: float32 [3072, 768], P('tensor', 'dp')
- outer_bias_grad: float32 [768], P('dp')
- second_gain_grad: float32 [768], P('dp')
- second_shift_grad: float32 [768], P('dp')
Inputs may be any that keep to these rules, and one draw needn't show every extreme that they name: `lengths`: at least one sequence has all 512 positions valid.
All inputs are finite; a program needn't handle non-finite values.
Results may differ from a plain program's by a relative error of at most 0.014.
Values may be sent and summed in bfloat16 or wider, within the bound.
No kernel may reach another device: no remote copies, remote signals or barrier semaphores. Data moves between devices by JAX's collectives and lax.ppermute only.
A program may use at most 192 MiB of HBM per device.

v0:
```python
import jax
import jax.numpy as jnp
from jax import lax
from jax.experimental import pallas as pl
from jax.experimental.pallas import tpu as pltpu
from jax.sharding import PartitionSpec as P

HD = 64
norm_eps = 1e-12
masked_score = -1000000000.0
score_scale = HD ** (-0.5)
f32 = jnp.float32
bf16 = jnp.bfloat16
NT = (((1,), (1,)), ((), ()))
TN = (((0,), (0,)), ((), ()))
NN = (((1,), (0,)), ((), ()))
ROWS = 256


def dot(left, right, dims):
    return lax.dot_general(left, right, dims, preferred_element_type=f32)


def stage_orders(size):
    up = [1 << k for k in range(size.bit_length() - 1)]
    down = up[::-1]
    return (down, down[:-2] + [down[-1], down[-2]], [down[0]] + up[:-1])


def swap_dp(value, mask, size):
    return lax.ppermute(value, "dp", [(i, i ^ mask) for i in range(size)])


def swap_core(value):
    return lax.ppermute(value, "tensor", [(0, 1), (1, 0)])


def after(value, *others):
    return lax.optimization_barrier((value, *others))[0]


def gather_rows(shard, order, size, index):
    rows, cols = shard.shape
    have = []
    buf = shard
    for mask in order:
        received = swap_dp(buf, mask, size)
        have = sorted(have + [mask], reverse=True)
        axis = have.index(mask)
        buf = jnp.where(
            (index & mask) != 0,
            jnp.stack([received, buf], axis),
            jnp.stack([buf, received], axis),
        )
    return buf.reshape(size * rows, cols)


def scatter_rows(own, order, size, index):
    total, cols = own.shape
    have = sorted(order, reverse=True)
    buf = own.reshape([2] * len(have) + [total // size, cols])
    for mask in order[::-1]:
        axis = have.index(mask)
        bit = ((index & mask) != 0).astype(jnp.int32)
        keep = lax.dynamic_index_in_dim(buf, bit, axis, keepdims=False)
        give = lax.dynamic_index_in_dim(buf, 1 - bit, axis, keepdims=False)
        received = swap_dp(give, mask, size)
        buf = keep.astype(f32) + received.astype(f32)
        have.remove(mask)
        if have:
            buf = buf.astype(own.dtype)
    return buf


HINT = pl.CostEstimate(flops=1, transcendentals=0, bytes_accessed=1)


def distance_of(piece, k):
    return (4 * (piece % 2) + 8 * k) ^ piece // 2


def vmem(shape):
    return pl.BlockSpec(shape, lambda *_: (0,) * len(shape))


def pack_first(weights, vectors):
    rows, cols = weights[0].shape
    count = len(weights)

    def kernel(*refs):
        ins, out_ref, table = refs[: count + len(vectors)], refs[-2], refs[-1]
        for g in range(count):
            out_ref[g * rows : (g + 1) * rows, :] = ins[g][...]
        table[...] = jnp.zeros(table.shape, f32)
        for i, ref in enumerate(ins[count:]):
            table[i : i + 1, : ref.shape[1]] = ref[...].astype(f32)
        out_ref[count * rows :, :] = table[...].astype(bf16)

    return pl.pallas_call(
        kernel,
        out_shape=jax.ShapeDtypeStruct((count * rows + 16, cols), bf16),
        scratch_shapes=[pltpu.VMEM((16, cols), f32)],
        cost_estimate=HINT,
    )(*weights, *[item.reshape(1, -1) for item in vectors])


def place_first(pieces, index, count, size, lengths):
    total_rows, cols = pieces[0].shape[1:]
    rows = (total_rows - 16) // count

    def kernel(index_ref, *refs):
        ins = refs[: len(pieces)]
        w_ref, v_ref, last_ref, table = refs[len(pieces) :]
        for n, ref in enumerate(ins):
            for k in range(ref.shape[0]):
                block = index_ref[0] ^ distance_of(n, k)
                at = pl.ds(pl.multiple_of(block * rows, 16), rows)
                for g in range(count):
                    w_ref[g, at, :] = ref[k, g * rows : (g + 1) * rows, :]
                table[block] = ref[k, count * rows :, :].astype(f32)
        one, last = lengths
        for c in range(size):
            v_ref[:, c * one : (c + 1) * one] = table[c][:, :one]
            last_ref[:, c * last : (c + 1) * last] = table[c][8:9, :last]

    out = [(count, size * rows, cols), (16, size * lengths[0]), (1, size * lengths[1])]
    return pl.pallas_call(
        kernel,
        out_shape=[jax.ShapeDtypeStruct(o, d) for o, d in zip(out, (bf16, f32, f32))],
        grid_spec=pltpu.PrefetchScalarGridSpec(
            num_scalar_prefetch=1,
            grid=(1,),
            in_specs=[vmem(p.shape) for p in pieces],
            out_specs=[vmem(o) for o in out],
            scratch_shapes=[pltpu.VMEM((size, 16, cols), f32)],
        ),
        cost_estimate=HINT,
    )(index[None], *pieces)


def place_cols(pieces, index, widths, size):
    rows = pieces[0].shape[1]

    def kernel(index_ref, *refs):
        ins, outs = refs[: len(pieces)], refs[len(pieces) :]
        for n, ref in enumerate(ins):
            for k in range(ref.shape[0]):
                block = index_ref[0] ^ distance_of(n, k)
                at = 0
                for out_ref, width in zip(outs, widths):
                    here = pl.ds(pl.multiple_of(block * rows, 16), rows)
                    out_ref[here, :] = ref[k, :, at : at + width]
                    at += width

    out = [(size * rows, w) for w in widths]
    return pl.pallas_call(
        kernel,
        out_shape=[jax.ShapeDtypeStruct(o, bf16) for o in out],
        grid_spec=pltpu.PrefetchScalarGridSpec(
            num_scalar_prefetch=1,
            grid=(1,),
            in_specs=[vmem(p.shape) for p in pieces],
            out_specs=[vmem(o) for o in out],
        ),
        cost_estimate=HINT,
    )(index[None], *pieces)


PARTS = (
    ((3, (0, 1)), (1, (0, 1))),
    ((3, (2, 3)), (2, (2, 3))),
    ((1, (2, 3)),),
    ((2, (0, 1)),),
    ((0, (0, 1, 2, 3)),),
)


def split_out_specs(rows, step):
    return [
        pl.BlockSpec((sum(len(ks) for _, ks in part), rows, step), lambda i, *_: (0, 0, i))
        for part in PARTS
    ]


def split_shapes(rows, cols):
    return [
        jax.ShapeDtypeStruct(
            (sum(len(ks) for _, ks in part), rows, cols), bf16
        )
        for part in PARTS
    ]


def split_cols(pairs, index, size, step):
    total = pairs[0][0].shape[0]
    rows = total // size
    counts = [a.shape[1] // step for a, _ in pairs]
    starts = [sum(counts[:i]) for i in range(len(counts))]

    def kernel(index_ref, *refs):
        ins, outs = refs[: 2 * len(pairs)], refs[2 * len(pairs) :]
        for n, (first, count) in enumerate(zip(starts, counts)):

            @pl.when((pl.program_id(0) >= first) & (pl.program_id(0) < first + count))
            def _(n=n):
                for part, out_ref in zip(PARTS, outs):
                    at = 0
                    for offset, ks in part:
                        for k in ks:
                            block = index_ref[0] ^ (4 * k ^ offset)
                            here = pl.ds(pl.multiple_of(block * rows, 16), rows)
                            out_ref[at] = ins[2 * n][here, :] + ins[2 * n + 1][here, :]
                            at += 1

    specs = []
    for a, n in zip(starts, counts):
        spec = pl.BlockSpec((total, step), lambda i, *_, a=a, n=n: (0, jnp.clip(i - a, 0, n - 1)))
        specs += [spec, spec]
    return pl.pallas_call(
        kernel,
        out_shape=split_shapes(rows, sum(counts) * step),
        grid_spec=pltpu.PrefetchScalarGridSpec(
            num_scalar_prefetch=1,
            grid=(sum(counts),),
            in_specs=specs,
            out_specs=split_out_specs(rows, step),
        ),
        cost_estimate=HINT,
    )(index[None], *[item for pair in pairs for item in pair])


def gradients_other(tokens_t, deltas):
    width, rows = tokens_t.shape
    count, _, cols = deltas.shape

    def kernel(t_ref, d_ref, o_ref, s_ref):
        o_ref[0] = dot(t_ref[...], d_ref[0], NN).astype(bf16)
        s_ref[0] = dot(jnp.ones((8, rows), bf16), d_ref[0], NN)

    return pl.pallas_call(
        kernel,
        out_shape=[
            jax.ShapeDtypeStruct((count, width, cols), bf16),
            jax.ShapeDtypeStruct((count, 8, cols), f32),
        ],
        grid=(count,),
        in_specs=[vmem(tokens_t.shape), pl.BlockSpec((1, rows, cols), lambda g: (g, 0, 0))],
        out_specs=[
            pl.BlockSpec((1, width, cols), lambda g: (g, 0, 0)),
            pl.BlockSpec((1, 8, cols), lambda g: (g, 0, 0)),
        ],
        cost_estimate=HINT,
    )(tokens_t, deltas)


def gradients_own(tokens_t, deltas, others, other_sums, table, index, core, size, one):
    width, rows = tokens_t.shape
    count, _, cols = deltas.shape
    part_rows = width // size
    height = count * part_rows + 16

    def kernel(at_ref, t_ref, d_ref, other_ref, sums_ref, table_ref, *refs):
        outs, total, own_sums, vec = refs[: len(PARTS)], refs[-3], refs[-2], refs[-1]
        g = pl.program_id(0)
        total[...] = dot(t_ref[...], d_ref[0], NN) + other_ref[0].astype(f32)
        own_sums[g] = dot(jnp.ones((8, rows), bf16), d_ref[0], NN)

        def blocks():
            for part, out_ref in zip(PARTS, outs):
                at = 0
                for offset, ks in part:
                    for k in ks:
                        yield at_ref[0] ^ (4 * k ^ offset), out_ref, at
                        at += 1

        for block, out_ref, at in blocks():
            value = total[pl.ds(pl.multiple_of(block * part_rows, 16), part_rows), :]
            out_ref[at, pl.ds(pl.multiple_of(g * part_rows, 16), part_rows), :] = value.astype(bf16)

        @pl.when(g == count - 1)
        def _():
            vec[...] = table_ref[...]
            for row, which in ((0, 0), (1, 2)):
                for ref, side in ((own_sums, 0), (sums_ref, 1)):
                    first = (at_ref[1] ^ side) * (size // 2)
                    for j in range(size // 2):
                        vec[first + j, row : row + 1, :one] = ref[which, 0:1, j * one : (j + 1) * one]
            for block, out_ref, at in blocks():
                out_ref[at, count * part_rows :, :] = vec[block].astype(bf16)

    return pl.pallas_call(
        kernel,
        out_shape=split_shapes(height, cols),
        grid_spec=pltpu.PrefetchScalarGridSpec(
            num_scalar_prefetch=1,
            grid=(count,),
            in_specs=[
                vmem(tokens_t.shape),
                pl.BlockSpec((1, rows, cols), lambda g, *_: (g, 0, 0)),
                pl.BlockSpec((1, width, cols), lambda g, *_: (g, 0, 0)),
                vmem(other_sums.shape),
                vmem(table.shape),
            ],
            out_specs=[vmem(shape.shape) for shape in split_shapes(height, cols)],
            scratch_shapes=[
                pltpu.VMEM((width, cols), f32),
                pltpu.VMEM((count, 8, cols), f32),
                pltpu.VMEM(table.shape, f32),
            ],
        ),
        cost_estimate=HINT,
    )(jnp.stack([index, core]), tokens_t, deltas, others, other_sums, table)


def pack_table(first_sums, second_sums, last, size, cols):
    one = first_sums.shape[1] // size
    end = last.shape[1] // size

    def kernel(a_ref, b_ref, last_ref, out_ref, table):
        table[...] = jnp.zeros(table.shape, f32)
        out_ref[...] = jnp.zeros(out_ref.shape, f32)
        table[2:5, :] = a_ref[0:3, :]
        table[5:8, :] = b_ref[0:3, :]
        for c in range(size):
            out_ref[c, :, :one] = table[:, c * one : (c + 1) * one]
            out_ref[c, 8:9, :end] = last_ref[:, c * end : (c + 1) * end]

    return pl.pallas_call(
        kernel,
        out_shape=jax.ShapeDtypeStruct((size, 16, cols), f32),
        scratch_shapes=[pltpu.VMEM((16, first_sums.shape[1]), f32)],
        cost_estimate=HINT,
    )(first_sums, second_sums, last)


def whole_call(kernel, outs, ins, blocks):
    return pl.pallas_call(
        kernel,
        out_shape=[jax.ShapeDtypeStruct(o, d) for o, d in outs],
        grid=(1,),
        in_specs=[vmem((n, *a.shape[1:])) for a, n in zip(ins, blocks)],
        out_specs=[vmem(o) for o, _ in outs],
        cost_estimate=HINT,
    )(*ins)


def corner_back(parts, size):
    return swap_dp(parts[0], 1, size), swap_dp(parts[1], 2, size)


def corner_add(parts, got):
    keep = parts[2:4]

    def kernel(one_ref, two_ref, r1_ref, r2_ref, o1_ref, o2_ref):
        o1_ref[...] = one_ref[...] + r2_ref[...]
        o2_ref[...] = two_ref[...] + r1_ref[...]

    return whole_call(
        kernel, [(item.shape, bf16) for item in keep], [*keep, *got], (2, 2, 2, 2)
    )


def near_back(sums, size):
    return swap_dp(sums[0], 1, size), swap_dp(sums[1], 2, size)


def near_add(own, first, got):
    def kernel(own_ref, f1_ref, f2_ref, r1_ref, r2_ref, keep_ref, *outs):
        def total(k):
            early = f1_ref[2 + k] if k < 2 else f2_ref[k]
            late = r2_ref[k] if k < 2 else r1_ref[k - 2]
            return own_ref[k].astype(f32) + early.astype(f32) + late.astype(f32)

        keep_ref[...] = total(0)
        for k in (1, 2, 3):
            outs[k - 1][...] = total(k).astype(bf16)

    shape = own.shape[1:]
    return whole_call(
        kernel, [(shape, f32)] + [(shape, bf16)] * 3, [own, *first, *got], (4, 4, 4, 2, 2)
    )


def far_back(sums, size):
    return [swap_dp(item, 4 * (k + 1), size) for k, item in enumerate(sums[1:])]


def project(tokens, weights, vectors, core, side):
    rows, width = tokens.shape
    cols = weights.shape[2]

    def kernel(core_ref, x_ref, w_ref, v_ref, q_out, k_out, v_out):
        half = core_ref[0] ^ side
        bias = jnp.where(half == 0, v_ref[0:8, :cols], v_ref[0:8, cols:])
        x = x_ref[...]
        q_out[...] = (dot(x, w_ref[0], NN) + bias[0:1]).astype(bf16)
        k_out[...] = dot(x, w_ref[1], NN).astype(bf16)
        v_out[...] = (dot(x, w_ref[2], NN) + bias[1:2]).astype(bf16)

    tile = pl.BlockSpec((ROWS, cols), lambda i, *_: (i, 0))
    return pl.pallas_call(
        kernel,
        out_shape=[jax.ShapeDtypeStruct((rows, cols), bf16)] * 3,
        grid_spec=pltpu.PrefetchScalarGridSpec(
            num_scalar_prefetch=1,
            grid=(rows // ROWS,),
            in_specs=[
                pl.BlockSpec((ROWS, width), lambda i, *_: (i, 0)),
                vmem(weights.shape),
                vmem(vectors.shape),
            ],
            out_specs=[tile] * 3,
        ),
        cost_estimate=HINT,
    )(core[None], tokens, weights, vectors)


def token_gradient(first_delta, deltas, weights, part, parts):
    count, rows, cols = deltas[0].shape
    width = weights[0].shape[1]
    steps = rows // ROWS // parts

    def kernel(f_ref, d0_ref, d1_ref, w0_ref, w1_ref, *refs):
        o_ref = refs[-1]
        total = f_ref[...]
        for d_ref, w_ref in ((d0_ref, w0_ref), (d1_ref, w1_ref)):
            for g in range(count):
                total = total + dot(d_ref[g], w_ref[g], NT)
        o_ref[...] = total

    tile = pl.BlockSpec((ROWS, width), lambda i: (i + part * steps, 0))
    delta_part = pl.BlockSpec((count, ROWS, cols), lambda i: (0, i + part * steps, 0))
    return pl.pallas_call(
        kernel,
        out_shape=jax.ShapeDtypeStruct((rows, width), f32),
        grid=(steps,),
        in_specs=[tile, delta_part, delta_part] + [vmem(weights[0].shape)] * 2,
        out_specs=tile,
        input_output_aliases={0: 0},
        cost_estimate=HINT,
    )(first_delta, *deltas, *weights)


def center(values):
    mean = jnp.mean(values, axis=-1, keepdims=True)
    centred = values - mean
    var = jnp.mean(centred * centred, axis=-1, keepdims=True)
    rinv = lax.rsqrt(var + norm_eps)
    return centred * rinv, rinv


def norm_back(grad, normed, rinv, gain):
    scaled = grad * gain
    return rinv * (
        scaled
        - jnp.mean(scaled, axis=-1, keepdims=True)
        - normed * jnp.mean(scaled * normed, axis=-1, keepdims=True)
    )


def add_rows(ref, items):
    @pl.when(pl.program_id(0) == 0)
    def _():
        ref[...] = jnp.zeros(ref.shape, f32)

    for i, item in enumerate(items):
        ref[i : i + 1, :] += jnp.sum(item, axis=0, keepdims=True)


def row_call(kernel, tiles, wholes, outs, sums=True):
    rows = tiles[0].shape[0]
    width = outs[0][0]

    def tile(cols):
        return pl.BlockSpec((ROWS, cols), lambda i: (i, 0))

    return pl.pallas_call(
        kernel,
        out_shape=[jax.ShapeDtypeStruct((rows, n), d) for n, d in outs]
        + [jax.ShapeDtypeStruct((8, width), f32)] * sums,
        grid=(rows // ROWS,),
        in_specs=[tile(a.shape[1]) for a in tiles] + [vmem(a.shape) for a in wholes],
        out_specs=[tile(n) for n, _ in outs] + [vmem((8, width))] * sums,
        cost_estimate=HINT,
    )(*tiles, *wholes)


def first_block(tokens, context, weights, vectors):
    def kernel(x_ref, c0_ref, c1_ref, w0_ref, w1_ref, v_ref, out, low):
        total = dot(c0_ref[...], w0_ref[...], NT) + dot(c1_ref[...], w1_ref[...], NT)
        total = x_ref[...].astype(f32) + total + v_ref[2:3]
        out[...] = total
        low[...] = (center(total)[0] * v_ref[3:4] + v_ref[4:5]).astype(bf16)

    width = tokens.shape[1]
    return row_call(
        kernel,
        [tokens, *context],
        [*weights, vectors],
        [(width, f32), (width, bf16)],
        sums=False,
    )


def outer_block(hidden, cotangent, act, weights, vectors):
    def kernel(h_ref, c_ref, a0_ref, a1_ref, w0_ref, w1_ref, v_ref, out, delta, low, sums):
        feed = v_ref[5:6] + dot(a0_ref[...], w0_ref[...], NT) + dot(a1_ref[...], w1_ref[...], NT)
        normed, rinv = center(h_ref[...].astype(f32) + feed)
        out[...] = normed * v_ref[6:7] + v_ref[7:8]
        cot = c_ref[...].astype(f32)
        found = norm_back(cot, normed, rinv, v_ref[6:7])
        delta[...] = found
        low[...] = found.astype(bf16)
        add_rows(sums, (found, cot * normed, cot))

    width = hidden.shape[1]
    return row_call(
        kernel,
        [hidden, cotangent, *act],
        [*weights, vectors],
        [(width, f32), (width, f32), (width, bf16)],
    )


def inner_back(second_delta, inner_delta, first_in, weights, vectors):
    def kernel(s_ref, d0_ref, d1_ref, f_ref, w0_ref, w1_ref, v_ref, delta, low, sums):
        grad = s_ref[...] + dot(d0_ref[...], w0_ref[...], NT) + dot(d1_ref[...], w1_ref[...], NT)
        normed, rinv = center(f_ref[...])
        found = norm_back(grad, normed, rinv, v_ref[3:4])
        delta[...] = found
        low[...] = found.astype(bf16)
        add_rows(sums, (found, grad * normed, grad))

    width = first_in.shape[1]
    return row_call(
        kernel,
        [second_delta, *inner_delta, first_in],
        [*weights, vectors],
        [(width, f32), (width, bf16)],
    )


def three_parts(row):
    high = row.astype(bf16).astype(f32)
    middle = (row - high).astype(bf16).astype(f32)
    return [high, middle, row - high - middle]


def extra_lanes(shape, keys_valid):
    lane = lax.broadcasted_iota(jnp.int32, shape, 1) % HD
    row = lax.broadcasted_iota(jnp.int32, shape, 0)
    bias = jnp.where(row < keys_valid, 0.0, masked_score)
    return jnp.where(lane == 0, bias, jnp.where(lane < 4, 1.0, 0.0)).astype(bf16)


def extra_rows(first, row, length):
    rows = [jnp.full((1, length), first, f32)]
    rows += three_parts(row) if row is not None else []
    rows.append(jnp.zeros((16 - len(rows), length), f32))
    return jnp.concatenate(rows, 0).astype(bf16)


def with_rows(own_t, h, first, row):
    length = own_t.shape[1]
    own = own_t[h * HD : (h + 1) * HD]
    rest = [extra_rows(first, row, length), jnp.zeros((HD - 16, length), bf16)]
    return jnp.concatenate([own] + rest if h == 0 else rest + [own], 0)


def attend_forward_kernel(lens, q_ref, k_ref, v_ref, ctx_ref, lse_ref):
    seq_len, lanes = q_ref.shape
    lane = lax.broadcasted_iota(jnp.int32, (seq_len, lanes), 1)
    extra = extra_lanes((seq_len, lanes), lens[pl.program_id(0)])
    ones = jnp.ones((16, seq_len), bf16)
    loaded = {}

    def scores(h):
        if h == 0:
            query_t = (q_ref[...] * jnp.bfloat16(score_scale)).T
            loaded[0] = (query_t, k_ref[...], v_ref[...].T)
        query_t, keys, _ = loaded[0]
        return dot(jnp.where(lane // HD == h, keys, extra), with_rows(query_t, h, 1.0, None), NN)

    pieces = []
    ahead = scores(0)
    for h in range(2):
        now = ahead
        if h == 0:
            ahead = scores(1)
        top = jnp.max(now, axis=0, keepdims=True)
        expo = jnp.exp(now - top).astype(bf16)
        value_t = loaded[0][2][h * HD : (h + 1) * HD]
        found = dot(jnp.concatenate([value_t, ones], 0), expo, NN)
        total = found[HD : HD + 1]
        pieces.append(found[:HD] / total)
        lse_ref[0, 0, h : h + 1, :] = top + jnp.log(total)
        if h == 1:
            ctx_ref[...] = jnp.concatenate(pieces, 0).T.astype(bf16)
            pieces = []


def attend_backward_kernel(lens, q_ref, k_ref, v_ref, d_ref, c_ref, lse_ref, out_ref):
    seq_len, lanes = q_ref.shape
    lane = lax.broadcasted_iota(jnp.int32, (seq_len, lanes), 1)
    extra = extra_lanes((seq_len, lanes), lens[pl.program_id(0)])
    loaded = {}

    def products(h):
        if h == 0:
            query = q_ref[...] * jnp.bfloat16(score_scale)
            delta = d_ref[...]
            delta_t = delta.T
            inner = delta_t.astype(f32) * c_ref[...].T.astype(f32)
            keys = k_ref[...]
            loaded[0] = (query, query.T, delta, delta_t, inner, keys, keys.T, v_ref[...])
        _, query_t, _, delta_t, inner, keys, _, values = loaded[0]
        own = lane // HD == h
        inner = jnp.sum(inner[h * HD : (h + 1) * HD], axis=0, keepdims=True)
        lse = lse_ref[0, 0, h : h + 1, :]
        logs = dot(jnp.where(own, keys, extra), with_rows(query_t, h, 1.0, -lse), NN)
        centred = dot(jnp.where(own, values, extra), with_rows(delta_t, h, 0.0, -inner), NN)
        return logs, centred

    ahead = products(0)
    for h in range(2):
        logs, centred = ahead
        if h == 0:
            ahead = products(1)
        query, _, delta, _, _, _, keys_t, _ = loaded[0]
        probs = jnp.exp(logs)
        score_delta = (probs * centred).astype(bf16)
        own = lane // HD == h
        part_v = dot(probs.astype(bf16), jnp.where(own, delta, jnp.bfloat16(0)), NN)
        part_k = dot(score_delta, jnp.where(own, query, jnp.bfloat16(0)), NN)
        part_q = dot(keys_t[h * HD : (h + 1) * HD], score_delta, NN)
        if h == 0:
            dv, dk, dq = part_v, part_k, part_q
        else:
            out_ref[0] = (jnp.concatenate([dq, part_q], 0).T * score_scale).astype(bf16)
            out_ref[1] = (dk + part_k).astype(bf16)
            out_ref[2] = (dv + part_v).astype(bf16)


def attend_call(kernel, lens, operands, lse_in, seq_count):
    rows, cols = operands[0].shape
    seq_len = rows // seq_count
    pairs = cols // (2 * HD)
    tile = pl.BlockSpec((seq_len, 2 * HD), lambda s, p, *_: (s, p))
    stat = pl.BlockSpec((1, 1, 2, seq_len), lambda s, p, *_: (s, p, 0, 0))
    if lse_in:
        out_shape = jax.ShapeDtypeStruct((3, rows, cols), bf16)
        out_specs = pl.BlockSpec((3, seq_len, 2 * HD), lambda s, p, *_: (0, s, p))
    else:
        out_shape = [
            jax.ShapeDtypeStruct((rows, cols), bf16),
            jax.ShapeDtypeStruct((seq_count, pairs, 2, seq_len), f32),
        ]
        out_specs = [tile, stat]
    return pl.pallas_call(
        kernel,
        out_shape=out_shape,
        grid_spec=pltpu.PrefetchScalarGridSpec(
            num_scalar_prefetch=1,
            grid=(seq_count, pairs),
            in_specs=[tile] * len(operands) + [stat] * len(lse_in),
            out_specs=out_specs,
        ),
        cost_estimate=HINT,
    )(lens, *operands, *lse_in)


def on_device(
    tokens,
    cotangent,
    lengths,
    query_weight,
    key_weight,
    value_weight,
    out_weight,
    query_bias,
    value_bias,
    out_bias,
    first_gain,
    first_shift,
    inner_weight,
    inner_bias,
    outer_weight,
    outer_bias,
    second_gain,
    second_shift,
):
    size = lax.axis_size("dp")
    index = lax.axis_index("dp")
    core = lax.axis_index("tensor")
    orders = stage_orders(size)
    seq_count = lengths.shape[0] // 2
    lens = lax.dynamic_slice_in_dim(lengths, core * seq_count, seq_count, 0)
    fast = size == 16 and query_weight.shape[0] % 16 == 0
    half = query_weight.shape[1]
    step = half

    vectors = (
        query_bias,
        value_bias,
        out_bias,
        first_gain,
        first_shift,
        outer_bias,
        second_gain,
        second_shift,
        inner_bias,
    )
    bounds = [0]
    for item in vectors:
        bounds.append(bounds[-1] + item.shape[0])
    projections = (query_weight, key_weight, value_weight)
    out_t = out_weight.T
    outer_t = outer_weight.T

    if fast:
        shard = pack_first(projections, vectors)
        far = [swap_dp(shard, d, size) for d in (8, 4, 12)]
        low, high = jnp.stack([shard, far[0]]), jnp.stack(far[1:])
        two_low, one_high = swap_dp(low, 2, size), swap_dp(high, 1, size)
        one_low, two_high = swap_dp(low, 1, size), swap_dp(high, 2, size)
        shard_a = jnp.concatenate([out_t, inner_weight], 1)
        far_a = swap_dp(after(shard_a, low, high), 8, size)
        tokens_t = tokens.T
        pieces = [low, high, one_low, one_high, two_low, two_high]
        pieces += [swap_dp(two_low, 1, size), swap_dp(one_high, 2, size)]
        far_a, *pieces, tokens_t = lax.optimization_barrier((far_a, *pieces, tokens_t))
        low_a = jnp.stack([shard_a, far_a])
        high_a = swap_dp(low_a, 4, size)
        two_low_a, one_low_a = swap_dp(low_a, 2, size), swap_dp(low_a, 1, size)
        wqkv0, vecs, ib = place_first(
            pieces, index, 3, size, (query_bias.shape[0], inner_bias.shape[0])
        )
    else:
        own_vec = jnp.concatenate(vectors)[None, :]
        all_vec = gather_rows(own_vec, orders[0], size, index).astype(f32)
        found = [all_vec[:, a:b].reshape(1, -1) for a, b in zip(bounds[:-1], bounds[1:])]
        vecs = jnp.concatenate(found[:-1] + [jnp.zeros_like(found[0])] * 8, 0)
        ib = found[-1]
        wqkv0 = jnp.stack(
            [gather_rows(w, o, size, index) for w, o in zip(projections, orders)]
        )
        wo0 = gather_rows(out_t, orders[2], size, index)
        wi0 = gather_rows(inner_weight, orders[0], size, index)
        wu0 = gather_rows(outer_t, orders[1], size, index)

    wqkv = (wqkv0, swap_core(wqkv0))
    hidden_half = inner_weight.shape[1]
    ib = (
        jnp.where(core == 0, ib[:, :hidden_half], ib[:, hidden_half:]),
        jnp.where(core == 0, ib[:, hidden_half:], ib[:, :hidden_half]),
    )

    q, k, v, ctx, lse = [], [], [], [], []
    for t in range(2):
        found = project(tokens, wqkv[t], vecs, core, t)
        if fast and t == 0:
            high_a, other, *found = lax.optimization_barrier((high_a, wqkv[1], *found))
            wqkv = (wqkv[0], other)
            one_high_a, two_high_a = swap_dp(high_a, 1, size), swap_dp(high_a, 2, size)
            far_b = swap_dp(after(outer_t, other), 8, size)
        q.append(found[0])
        k.append(found[1])
        v.append(found[2])
    if fast:
        far_b, one_low_a, two_low_a, *q = lax.optimization_barrier(
            (far_b, one_low_a, two_low_a, *q)
        )
        low_b = jnp.stack([outer_t, far_b])
        two_low_b, one_low_b = swap_dp(low_b, 2, size), swap_dp(low_b, 1, size)
        high_b = swap_dp(low_b, 4, size)
    for t in range(2):
        if fast and t == 1:
            q[1] = after(q[1], ctx[0])
        c, s = attend_call(attend_forward_kernel, lens, (q[t], k[t], v[t]), (), seq_count)
        lse.append(s)
        if fast and t == 0:
            pieces_a = [low_a, high_a, one_low_a, one_high_a, two_low_a, two_high_a]
            *pieces_a, high_b, two_low_b, one_low_b, c = lax.optimization_barrier(
                (*pieces_a, high_b, two_low_b, one_low_b, c)
            )
            pieces_a += [swap_dp(pieces_a[4], 1, size), swap_dp(pieces_a[3], 2, size)]
        if fast and t == 1:
            *pieces_a, c = lax.optimization_barrier((*pieces_a, c))
            one_high_b, two_high_b = swap_dp(high_b, 1, size), swap_dp(high_b, 2, size)
            pieces_b = [low_b, high_b, one_low_b, one_high_b, two_low_b, two_high_b]
            pieces_b.append(swap_dp(two_low_b, 1, size))
            wo0, wi0 = place_cols(pieces_a, index, (half, inner_weight.shape[1]), size)
        ctx.append(c)

    wo = (wo0, swap_core(wo0))
    wi = (wi0, swap_core(wi0))
    first_in, hidden = first_block(tokens, ctx, wo, vecs)
    if fast:
        *pieces_b, hidden = lax.optimization_barrier((*pieces_b, hidden))
        pieces_b.append(swap_dp(pieces_b[3], 2, size))
    act, slope = [], []
    for t in range(2):
        u = dot(hidden, wi[t], NN) + ib[t]
        cdf = 0.5 * (1.0 + lax.erf(u * (0.5**0.5)))
        act.append((u * cdf).astype(bf16))
        pdf = jnp.exp(-0.5 * u * u) * 0.3989422804014327
        slope.append((cdf + u * pdf).astype(bf16))
        if fast and t == 0:
            *pieces_b, act[0] = lax.optimization_barrier((*pieces_b, act[0]))
            (wu0,) = place_cols(pieces_b, index, (inner_weight.shape[1],), size)
            hidden = after(hidden, wu0)
    wu = (wu0, swap_core(wu0))
    layer_out, second_delta, feed_delta, second_sums = outer_block(
        hidden, cotangent, act, wu, vecs
    )

    def product(left, right):
        other = dot(left, right[1], TN).astype(bf16)
        other = swap_core(other)
        return dot(left, right[0], TN).astype(bf16), other

    gu = product(feed_delta, act)
    feed_delta, *gu = lax.optimization_barrier((feed_delta, *gu))
    inner_delta = [None, None]
    for t in (1, 0):
        inner_delta[t] = (dot(feed_delta, wu[t], NN) * slope[t].astype(f32)).astype(bf16)
    gi = product(hidden, inner_delta)
    inner_delta[0], inner_delta[1], *gi = lax.optimization_barrier((*inner_delta, *gi))
    grad_ib = [jnp.sum(inner_delta[t].astype(f32), axis=0, keepdims=True) for t in range(2)]
    if fast:
        parts_u = split_cols([gu, gi], index, size, 2 * step)
        first_u = corner_back(parts_u, size)
        inner_delta[0], inner_delta[1] = [after(d, parts_u[4]) for d in inner_delta]
    first_delta, branch_delta, first_sums = inner_back(
        second_delta, inner_delta, first_in, wi, vecs
    )
    go = product(branch_delta, ctx)
    ctx_delta = [dot(branch_delta, wo[t], NN).astype(bf16) for t in range(2)]

    def joined(pair):
        return jnp.where(
            core == 0, jnp.concatenate(pair, 1), jnp.concatenate(pair[::-1], 1)
        )

    grad_ib = joined(grad_ib)
    if fast:
        table = pack_table(first_sums, second_sums, grad_ib, size, half)
        parts_i = split_cols([go], index, size, step)
        first_i = corner_back(parts_i, size)
        *first_u, ctx_delta[1], _ = lax.optimization_barrier(
            (*first_u, ctx_delta[1], parts_i[4])
        )
        sums_u = corner_add(parts_u, first_u)
        got_u = near_back(sums_u, size)
        ctx_delta[1] = after(ctx_delta[1], table, sums_u[0])

    def attend_back(t):
        return attend_call(
            attend_backward_kernel,
            lens,
            (q[t], k[t], v[t], ctx_delta[t], ctx[t]),
            (lse[t],),
            seq_count,
        )

    deltas = [None, None]
    deltas[1] = attend_back(1)
    if fast:
        arrived = lax.optimization_barrier((*first_i, *got_u, deltas[1]))
        first_i, got_u, deltas[1] = arrived[:2], arrived[2:4], arrived[4]
        last_u = near_add(parts_u[4], first_u, got_u)
        got_u = far_back(last_u, size)
        sums_i = corner_add(parts_i, first_i)
        got_i = near_back(sums_i, size)
        deltas[1] = after(deltas[1], last_u[0], sums_i[0])
        others, other_sums = gradients_other(tokens_t, deltas[1])
        *got_i, others = lax.optimization_barrier((*got_i, others))
        last_i = near_add(parts_i[4], first_i, got_i)
        others = swap_core(others)
        got_i = far_back(last_i, size)
        ctx_delta[0] = after(ctx_delta[0], last_i[0])
        deltas[0] = attend_back(0)
        *got_u, deltas[0] = lax.optimization_barrier((*got_u, deltas[0]))
        parts_q = gradients_own(
            tokens_t,
            deltas[0],
            others,
            other_sums,
            table,
            index,
            core,
            size,
            query_bias.shape[0],
        )
        first_q = corner_back(parts_q, size)
        *got_i, _ = lax.optimization_barrier((*got_i, parts_q[4]))
        token_grad = token_gradient(
            after(first_delta, parts_q[4]), [after(d, parts_q[4]) for d in deltas], wqkv, 0, 2
        )
        *first_q, token_grad = lax.optimization_barrier((*first_q, token_grad))

        def total(last, got):
            return last[0] + got[0].astype(f32) + got[1].astype(f32) + got[2].astype(f32)

        out_ui = total(last_u, got_u)
        hidden_half = out_ui.shape[1] // 2
        out_gu = out_ui[:, :hidden_half].T
        out_gi = out_ui[:, hidden_half:]
        out_go = total(last_i, got_i).T
        sums_q = corner_add(parts_q, first_q)
        got_q = near_back(sums_q, size)
        last_q = near_add(parts_q[4], first_q, got_q)
        got_q = far_back(last_q, size)
        token_grad = token_gradient(token_grad, [after(d, last_q[0]) for d in deltas], wqkv, 1, 2)
        out_q = total(last_q, got_q)
        n = query_weight.shape[0]
        out_qkv = [out_q[g * n : (g + 1) * n] for g in range(3)]
        vec = out_q[3 * n :]
        vec = vec + swap_core(vec)
        vec_out = [vec[i, : item.shape[0]] for i, item in enumerate(vectors)]
    else:
        deltas[0] = attend_back(0)
        token_grad = token_gradient(first_delta, deltas, wqkv, 0, 1)

        def reduce(pair, order):
            summed = (pair[0].astype(f32) + pair[1].astype(f32)).astype(bf16)
            return scatter_rows(summed, order, size, index)

        out_gu = reduce(gu, orders[1]).T
        out_gi = reduce(gi, orders[0])
        out_go = reduce(go, orders[2]).T
        out_qkv = [
            reduce(product(tokens, [d[g] for d in deltas]), order) for g, order in enumerate(orders)
        ]
        bias_grads = [
            joined([jnp.sum(d[g].astype(f32), axis=0, keepdims=True) for d in deltas]) for g in (0, 2)
        ]
        bias_grads += [s[i : i + 1] for s in (first_sums, second_sums) for i in range(3)]
        bias_grads.append(grad_ib)
        packed = jnp.concatenate([item.reshape(size, -1) for item in bias_grads], axis=1)
        packed = packed + swap_core(packed)
        own = scatter_rows(packed, orders[0], size, index).reshape(-1)
        vec_out = [own[a:b] for a, b in zip(bounds[:-1], bounds[1:])]
    return (
        layer_out,
        token_grad,
        out_qkv[0],
        out_qkv[1],
        out_qkv[2],
        out_go,
        vec_out[0],
        vec_out[1],
        vec_out[2],
        vec_out[3],
        vec_out[4],
        out_gi,
        vec_out[8],
        out_gu,
        vec_out[5],
        vec_out[6],
        vec_out[7],
    )


def solution(mesh):
    both = P(("dp", "tensor"), None)
    cols = P("dp", "tensor")
    rows = P("tensor", "dp")
    vec = P("dp")
    in_specs = (
        both, both, vec, cols, cols, cols, rows, vec, vec, vec, vec, vec, cols, vec, rows, vec, vec, vec,
    )
    out_specs = (
        both, both, cols, cols, cols, rows, vec, vec, vec, vec, vec, cols, vec, rows, vec, vec, vec,
    )
    return jax.shard_map(
        on_device, mesh=mesh, in_specs=in_specs, out_specs=out_specs, check_vma=False
    )
```

profile of v0, /device:TPU:0, one launch (start us, length us, event | category | flops | bytes accessed | tf_op | source)
XLA Modules:
  0.0 327.9 jit_solution(2092869601897956898)
XLA Ops:
  1.9 1.5 shard_map.305
  3.4 4.1 %collective-permute-start = (bf16[160,384]{1,0:T(8,128)(2,1)}, bf16[160,384]{1,0:T(8,128)(2,1)S(1)}, u32[]{:S(2)}, u32[]{:S(2)}) collective-permute-start(bf16[160,384]{1,0:T(8,128)(2,1)} %shard_map.305), channel_id=1, source_target_pairs={{0,16},{2,18},{4,20},{6,22},{8,24},{10,26},{12,28},{14,30},{16,0},... | collective-permute-start | bytes 368648 | tf_op jit(solution)/shard_map/ppermute | solution.py:31
  9.1 8.1 %collective-permute-done = bf16[160,384]{1,0:T(8,128)(2,1)S(1)} collective-permute-done((bf16[160,384]{1,0:T(8,128)(2,1)}, bf16[160,384]{1,0:T(8,128)(2,1)S(1)}, u32[]{:S(2)}, u32[]{:S(2)}) %collective-permute-start) | collective-permute-done | bytes 122912 | tf_op jit(solution)/shard_map/ppermute | solution.py:31
  18.1 1.9 collective-permute-start.6
  20.1 1.6 collective-permute-start.5
  22.4 4.7 %collective-permute-done.6.refs_4_ = bf16[2,160,384]{2,1,0:T(8,128)(2,1)S(1)} collective-permute-done((bf16[2,160,384]{2,1,0:T(8,128)(2,1)S(1)}, bf16[2,160,384]{2,1,0:T(8,128)(2,1)S(1)}, u32[]{:S(2)}, u32[]{:S(2)}) %collective-permute-start.6) | collective-permute-done | bytes 245792 | tf_op jit(solution)/shard_map/ppermute | solution.py:31
  27.0 1.8 collective-permute-start.8
  31.3 1.8 collective-permute-start.3
  33.1 2.6 copy.37
  35.7 4.1 %collective-permute-done.3 = bf16[48,1920]{1,0:T(8,128)(2,1)S(1)} collective-permute-done((bf16[48,1920]{1,0:T(8,128)(2,1)S(1)}, bf16[48,1920]{1,0:T(8,128)(2,1)S(1)}, u32[]{:S(2)}, u32[]{:S(2)}) %collective-permute-start.3) | collective-permute-done | bytes 184352 | tf_op jit(solution)/shard_map/ppermute | solution.py:31
  40.7 3.0 shard_map.306
  45.9 5.8 %shard_map.307 = (bf16[1024,384]{1,0:T(8,128)(2,1)}, bf16[1024,384]{1,0:T(8,128)(2,1)}, bf16[1024,384]{1,0:T(8,128)(2,1)}) custom-call(s32[1]{0:T(128)} %bitcast.19.core_ref, bf16[1024,768]{1,0:T(8,128)(2,1)} %x_ref.5, bf16[3,768,384]{2,1,0:T(8,128)(2,1)} %get-tuple-element.184.w_ref.w0_ref, f32[16,768]{1,0:T(8,128)} %get-tuple-element.185.v_ref), custom_call_target="tpu_custom_call" | custom-call | flops 1 | bytes 1 | tf_op jit(solution)/shard_map/pallas_call | solution.py:401
  51.7 3.1 collective-permute-done.10.refs_1_
  54.9 1.8 collective-permute-start.12
  58.6 5.8 %shard_map.308 = (bf16[1024,384]{1,0:T(8,128)(2,1)}, bf16[1024,384]{1,0:T(8,128)(2,1)}, bf16[1024,384]{1,0:T(8,128)(2,1)}) custom-call(s32[1]{0:T(128)} %bitcast.19.core_ref, bf16[1024,768]{1,0:T(8,128)(2,1)} %x_ref.5, bf16[3,768,384]{2,1,0:T(8,128)(2,1)} %copy-done, f32[16,768]{1,0:T(8,128)} %get-tuple-element.185.v_ref), custom_call_target="tpu_custom_call" | custom-call | flops 1 | bytes 1 | tf_op jit(solution)/shard_map/pallas_call | solution.py:401
  64.5 1.6 collective-permute-start.19
  66.7 1.7 collective-permute-start.17
  69.0 9.0 %shard_map.309 = (bf16[1024,384]{1,0:T(8,128)(2,1)}, f32[2,3,2,512]{3,2,1,0:T(2,128)}) custom-call(s32[2]{0:T(128)} %dynamic_slice.3.lens, bf16[1024,384]{1,0:T(8,128)(2,1)} %get-tuple-element.197.q_ref, bf16[1024,384]{1,0:T(8,128)(2,1)} %get-tuple-element.198.k_ref, bf16[1024,384]{1,0:T(8,128)(2,1)} %get-tuple-element.199.v_ref), custom_call_target="tpu_custom_call" | custom-call | flops 1 | bytes 1 | tf_op jit(solution)/shard_map/pallas_call | solution.py:659
  81.4 9.0 %shard_map.310 = (bf16[1024,384]{1,0:T(8,128)(2,1)}, f32[2,3,2,512]{3,2,1,0:T(2,128)}) custom-call(s32[2]{0:T(128)} %dynamic_slice.3.lens, bf16[1024,384]{1,0:T(8,128)(2,1)} %get-tuple-element.212.q_ref, bf16[1024,384]{1,0:T(8,128)(2,1)} %get-tuple-element.213.k_ref, bf16[1024,384]{1,0:T(8,128)(2,1)} %get-tuple-element.214.v_ref), custom_call_target="tpu_custom_call" | custom-call | flops 1 | bytes 1 | tf_op jit(solution)/shard_map/pallas_call | solution.py:659
  91.3 3.6 %shard_map.311 = (bf16[768,384]{1,0:T(8,128)(2,1)}, bf16[768,1536]{1,0:T(8,128)(2,1)}) custom-call(s32[1]{0:T(128)} %bitcast.18.index_ref, bf16[2,48,1920]{2,1,0:T(8,128)(2,1)} %copy-done.19, bf16[2,48,1920]{2,1,0:T(8,128)(2,1)} %copy-done.29, bf16[2,48,1920]{2,1,0:T(8,128)(2,1)} %copy-done.31, bf16[2,48,1920]{2,1,0:T(8,128)(2,1)} %collective-permute-done.15.refs_3_, ...), custom_call_target="tpu_custom_call" | custom-call | flops 1 | bytes 1 | tf_op jit(solution)/shard_map/pallas_call | solution.py:156
  95.8 1.5 collective-permute-start.21
  99.3 6.3 %shard_map.312 = (f32[1024,768]{1,0:T(8,128)}, bf16[1024,768]{1,0:T(8,128)(2,1)}) custom-call(bf16[1024,768]{1,0:T(8,128)(2,1)} %x_ref.5, bf16[1024,384]{1,0:T(8,128)(2,1)} %get-tuple-element.204.c0_ref.c_ref, bf16[1024,384]{1,0:T(8,128)(2,1)} %get-tuple-element.216.c1_ref.c_ref, bf16[768,384]{1,0:T(8,128)(2,1)} %get-tuple-element.225.w0_ref, ...), custom_call_target="tpu_custom_call" | custom-call | flops 1 | bytes 1 | tf_op jit(solution)/shard_map/pallas_call | solution.py:477
  105.6 5.5 %collective-permute-done.20.refs_3_ = bf16[2,48,1536]{2,1,0:T(8,128)(2,1)} collective-permute-done((bf16[2,48,1536]{2,1,0:T(8,128)(2,1)}, bf16[2,48,1536]{2,1,0:T(8,128)(2,1)}, u32[]{:S(2)}, u32[]{:S(2)}) %collective-permute-start.20) | collective-permute-done | bytes 294944 | tf_op jit(solution)/shard_map/ppermute | solution.py:31
  111.8 6.9 %multiply_convert_fusion.3 = (bf16[1024,1536]{1,0:T(8,128)(2,1)}, f32[1024,1536]{1,0:T(8,128)}) fusion(f32[1536]{0:T(1024)S(1)} %copy-done.53, bf16[1024,768]{1,0:T(8,128)(2,1)} %get-tuple-element.245.h_ref, bf16[768,1536]{1,0:T(8,128)(2,1)S(1)} %copy-done.9), kind=kOutput, calls=%fused_computation.18 | convolution fusion | flops 2425356288 | bytes 13375488 | tf_op jit(solution)/shard_map/dot_general | solution.py:21
  120.5 3.2 shard_map.313.w0_ref
  123.7 7.2 %multiply_convert_fusion.2 = (bf16[1024,1536]{1,0:T(8,128)(2,1)}, f32[1024,1536]{1,0:T(8,128)}) fusion(f32[1536]{0:T(1024)S(1)} %copy-done.54, bf16[1024,768]{1,0:T(8,128)(2,1)S(1)} %copy-done.17, bf16[768,1536]{1,0:T(8,128)(2,1)} %collective-permute-done.27.w1_ref), kind=kOutput, calls=%fused_computation.16 | convolution fusion | flops 2425356288 | bytes 13375488 | tf_op jit(solution)/shard_map/dot_general | solution.py:21
  132.3 13.0 %shard_map.314 = (f32[1024,768]{1,0:T(8,128)}, f32[1024,768]{1,0:T(8,128)}, bf16[1024,768]{1,0:T(8,128)(2,1)}, f32[8,768]{1,0:T(8,128)}) custom-call(bf16[1024,768]{1,0:T(8,128)(2,1)} %get-tuple-element.245.h_ref, bf16[1024,768]{1,0:T(8,128)(2,1)} %c_ref.1, bf16[1024,1536]{1,0:T(8,128)(2,1)} %get-tuple-element.246.a0_ref, ...), custom_call_target="tpu_custom_call" | custom-call | flops 1 | bytes 1 | tf_op jit(solution)/shard_map/pallas_call | solution.py:477
  145.3 4.5 %convolution_convert_fusion.2 = bf16[768,1536]{1,0:T(8,128)(2,1)S(1)} fusion(bf16[1024,768]{1,0:T(8,128)(2,1)} %get-tuple-element.252, bf16[1024,1536]{1,0:T(8,128)(2,1)S(1)} %copy-done.6), kind=kOutput, calls=%fused_computation.22 | convolution fusion | flops 2417098752 | bytes 7077888 | tf_op jit(solution)/shard_map/dot_general | solution.py:21
  150.4 4.1 %convolution_convert_fusion.3.refs_0_ = bf16[768,1536]{1,0:T(8,128)(2,1)} fusion(bf16[1024,768]{1,0:T(8,128)(2,1)S(1)} %copy-done.56, bf16[1024,1536]{1,0:T(8,128)(2,1)S(1)} %copy-done.5), kind=kOutput, calls=%fused_computation.23 | convolution fusion | flops 2417098752 | bytes 7077888 | tf_op jit(solution)/shard_map/dot_general | solution.py:21
  154.6 5.4 %multiply_convert_fusion.d1_ref = bf16[1024,1536]{1,0:T(8,128)(2,1)S(1)} fusion(bf16[1024,768]{1,0:T(8,128)(2,1)S(1)} %copy-done.56, bf16[768,1536]{1,0:T(8,128)(2,1)S(1)} %copy-done.12, f32[1024,1536]{1,0:T(8,128)S(1)} %copy-done.62, f32[1536]{0:T(1024)S(1)} %copy-done.54), kind=kOutput, calls=%fused_computation.14 | convolution fusion | flops 2436366336 | bytes 13375488 | tf_op jit(solution)/shard_map/dot_general | solution.py:21
  160.0 2.9 convolution_convert_fusion
  163.4 5.4 %multiply_convert_fusion.1.d0_ref = bf16[1024,1536]{1,0:T(8,128)(2,1)S(1)} fusion(bf16[1024,768]{1,0:T(8,128)(2,1)S(1)} %copy-done.56, bf16[768,1536]{1,0:T(8,128)(2,1)S(1)} %copy-done.4, f32[1024,1536]{1,0:T(8,128)S(1)} %bitcast.89, f32[1536]{0:T(1024)S(1)} %copy-done.53), kind=kOutput, calls=%fused_computation.15 | convolution fusion | flops 2436366336 | bytes 13375488 | tf_op jit(solution)/shard_map/dot_general | solution.py:21
  168.8 4.0 %convolution_convert_fusion.1.refs_2_ = bf16[768,1536]{1,0:T(8,128)(2,1)} fusion(bf16[1024,768]{1,0:T(8,128)(2,1)S(1)} %copy-done.18, bf16[1024,1536]{1,0:T(8,128)(2,1)S(1)} %multiply_convert_fusion.1.d0_ref), kind=kOutput, calls=%fused_computation.21 | convolution fusion | flops 2417098752 | bytes 7077888 | tf_op jit(solution)/shard_map/dot_general | solution.py:21
  174.3 6.9 %shard_map.315 = (bf16[4,48,3072]{2,1,0:T(8,128)(2,1)}, bf16[4,48,3072]{2,1,0:T(8,128)(2,1)}, bf16[2,48,3072]{2,1,0:T(8,128)(2,1)}, bf16[2,48,3072]{2,1,0:T(8,128)(2,1)}, bf16[4,48,3072]{2,1,0:T(8,128)(2,1)}) custom-call(s32[1]{0:T(128)} %bitcast.18.index_ref, bf16[768,1536]{1,0:T(8,128)(2,1)} %convolution_convert_fusion.3.refs_0_, ...), custom_call_target="tpu_custom_call" | custom-call | flops 1 | bytes 1 | tf_op jit(solution)/shard_map/pallas_call | solution.py:219
  183.3 12.2 %shard_map.316 = (f32[1024,768]{1,0:T(8,128)}, bf16[1024,768]{1,0:T(8,128)(2,1)}, f32[8,768]{1,0:T(8,128)}) custom-call(f32[1024,768]{1,0:T(8,128)} %get-tuple-element.258.s_ref, bf16[1024,1536]{1,0:T(8,128)(2,1)} %copy-done.3, bf16[1024,1536]{1,0:T(8,128)(2,1)} %copy-done.1, f32[1024,768]{1,0:T(8,128)} %get-tuple-element.263.f_ref, ...), custom_call_target="tpu_custom_call" | custom-call | flops 1 | bytes 1 | tf_op jit(solution)/shard_map/pallas_call | solution.py:477
  195.6 2.6 convolution_convert_fusion.6
  198.2 1.9 convolution_convert_fusion.7.refs_0_
  200.1 1.9 convolution_convert_fusion.5.d_ref
  202.0 2.3 shard_map.317
  204.2 5.2 %collective-permute-done.31.r1_ref.f1_ref = bf16[4,48,3072]{2,1,0:T(8,128)(2,1)} collective-permute-done((bf16[4,48,3072]{2,1,0:T(8,128)(2,1)}, bf16[4,48,3072]{2,1,0:T(8,128)(2,1)}, u32[]{:S(2)}, u32[]{:S(2)}) %collective-permute-start.31) | collective-permute-done | bytes 1179680 | tf_op jit(solution)/shard_map/ppermute | solution.py:31
  209.9 2.7 shard_map.318
  214.6 2.9 convert_reduce_fusion
  217.5 1.6 collective-permute-start.34
  220.2 1.6 shard_map.319.table_ref
  221.8 12.0 %shard_map.320.d_ref.d1_ref = bf16[3,1024,384]{2,1,0:T(8,128)(2,1)} custom-call(s32[2]{0:T(128)} %dynamic_slice.3.lens, bf16[1024,384]{1,0:T(8,128)(2,1)} %get-tuple-element.212.q_ref, bf16[1024,384]{1,0:T(8,128)(2,1)} %get-tuple-element.213.k_ref, bf16[1024,384]{1,0:T(8,128)(2,1)} %get-tuple-element.214.v_ref, ...), custom_call_target="tpu_custom_call" | custom-call | flops 1 | bytes 1 | tf_op jit(solution)/shard_map/pallas_call | solution.py:659
  234.5 1.7 shard_map.322
  238.2 3.5 %shard_map.321 = (f32[48,3072]{1,0:T(8,128)}, bf16[48,3072]{1,0:T(8,128)(2,1)}, bf16[48,3072]{1,0:T(8,128)(2,1)}, bf16[48,3072]{1,0:T(8,128)(2,1)}) custom-call(bf16[4,48,3072]{2,1,0:T(8,128)(2,1)} %get-tuple-element.255.own_ref, bf16[4,48,3072]{2,1,0:T(8,128)(2,1)} %collective-permute-done.31.r1_ref.f1_ref, ...), custom_call_target="tpu_custom_call" | custom-call | flops 1 | bytes 1 | tf_op jit(solution)/shard_map/pallas_call | solution.py:337
  241.7 5.9 %shard_map.323 = (bf16[3,768,384]{2,1,0:T(8,128)(2,1)}, f32[3,8,384]{2,1,0:T(8,128)}) custom-call(bf16[768,1024]{1,0:T(8,128)(2,1)} %bitcast.68, bf16[3,1024,384]{2,1,0:T(8,128)(2,1)} %shard_map.320.d_ref.d1_ref), custom_call_target="tpu_custom_call" | custom-call | flops 1 | bytes 1 | tf_op jit(solution)/shard_map/pallas_call | solution.py:240
  248.6 2.1 collective-permute-start.39
  250.8 2.0 collective-permute-start.40
  252.7 3.3 convolution_convert_fusion.4.d_ref
  256.0 1.8 shard_map.324
  257.8 12.1 %shard_map.325.d_ref.d0_ref = bf16[3,1024,384]{2,1,0:T(8,128)(2,1)} custom-call(s32[2]{0:T(128)} %dynamic_slice.3.lens, bf16[1024,384]{1,0:T(8,128)(2,1)} %get-tuple-element.197.q_ref, bf16[1024,384]{1,0:T(8,128)(2,1)} %get-tuple-element.198.k_ref, bf16[1024,384]{1,0:T(8,128)(2,1)} %get-tuple-element.199.v_ref, ...), custom_call_target="tpu_custom_call" | custom-call | flops 1 | bytes 1 | tf_op jit(solution)/shard_map/pallas_call | solution.py:659
  270.0 2.5 collective-permute-start.52
  272.5 2.6 collective-permute-start.53
  276.3 7.5 %shard_map.326 = (bf16[4,160,384]{2,1,0:T(8,128)(2,1)}, bf16[4,160,384]{2,1,0:T(8,128)(2,1)}, bf16[2,160,384]{2,1,0:T(8,128)(2,1)}, bf16[2,160,384]{2,1,0:T(8,128)(2,1)}, bf16[4,160,384]{2,1,0:T(8,128)(2,1)}) custom-call(s32[2]{0:T(128)} %pad_add_fusion.at_ref, bf16[768,1024]{1,0:T(8,128)(2,1)} %bitcast.69, bf16[3,1024,384]{2,1,0:T(8,128)(2,1)} %shard_map.325.d_ref.d0_ref, ...), custom_call_target="tpu_custom_call" | custom-call | flops 1 | bytes 1 | tf_op jit(solution)/shard_map/pallas_call | solution.py:291
  286.0 6.3 %shard_map.327.f_ref = f32[1024,768]{1,0:T(8,128)} custom-call(f32[1024,768]{1,0:T(8,128)} %get-tuple-element.306.f_ref, bf16[3,1024,384]{2,1,0:T(8,128)(2,1)} %shard_map.325.d_ref.d0_ref, bf16[3,1024,384]{2,1,0:T(8,128)(2,1)} %shard_map.320.d_ref.d1_ref, bf16[3,768,384]{2,1,0:T(8,128)(2,1)} %get-tuple-element.184.w_ref.w0_ref, ...), custom_call_target="tpu_custom_call", output_to_operand_aliasing={{}: (0, {})} | custom-call | flops 1 | bytes 1 | tf_op jit(solution)/shard_map/pallas_call | solution.py:433
  292.3 3.2 collective-permute-done.44.r1_ref.f1_ref
  297.4 2.1 shard_map.328
  300.2 1.5 collective-permute-start.47
  302.6 3.3 %collective-permute-done.46.r1_ref = bf16[2,160,384]{2,1,0:T(8,128)(2,1)S(1)} collective-permute-done((bf16[2,160,384]{2,1,0:T(8,128)(2,1)}, bf16[2,160,384]{2,1,0:T(8,128)(2,1)S(1)}, u32[]{:S(2)}, u32[]{:S(2)}) %collective-permute-start.46) | collective-permute-done | bytes 245792 | tf_op jit(solution)/shard_map/ppermute | solution.py:31
  307.3 2.4 shard_map.329
  309.7 6.1 %collective-permute-start.48 = (bf16[160,384]{1,0:T(8,128)(2,1)}, bf16[160,384]{1,0:T(8,128)(2,1)S(1)}, u32[]{:S(2)}, u32[]{:S(2)}) collective-permute-start(bf16[160,384]{1,0:T(8,128)(2,1)} %get-tuple-element.319), channel_id=1, source_target_pairs={{0,8},{2,10},{4,12},{6,14},{8,0},{10,2},{12,4},{14,6},{16,24},{18,... | collective-permute-start | bytes 368648 | tf_op jit(solution)/shard_map/ppermute | solution.py:31
  319.1 6.3 %shard_map.330 = f32[1024,768]{1,0:T(8,128)} custom-call(f32[1024,768]{1,0:T(8,128)} %shard_map.327.f_ref, bf16[3,1024,384]{2,1,0:T(8,128)(2,1)} %shard_map.325.d_ref.d0_ref, bf16[3,1024,384]{2,1,0:T(8,128)(2,1)} %shard_map.320.d_ref.d1_ref, bf16[3,768,384]{2,1,0:T(8,128)(2,1)} %get-tuple-element.184.w_ref.w0_ref, ...), custom_call_target="tpu_custom_call", output_to_operand_aliasing={{}: (0, {})} | custom-call | flops 1 | bytes 1 | tf_op jit(solution)/shard_map/pallas_call | solution.py:433
  (238 shorter events, 50.3 us)
Async XLA Ops:
  3.4 13.8 %collective-permute-start = (bf16[160,384]{1,0:T(8,128)(2,1)}, bf16[160,384]{1,0:T(8,128)(2,1)S(1)}, u32[]{:S(2)}, u32[]{:S(2)}) collective-permute-start(bf16[160,384]{1,0:T(8,128)(2,1)} %shard_map.305), channel_id=1, source_target_pairs={{0,16},{2,18},{4,20},{6,22},{8,24},{10,26},{12,28},{14,30},{16,0},... | collective-permute-start | bytes 368648 | tf_op jit(solution)/shard_map/ppermute | solution.py:31
  7.5 12.5 %collective-permute-start.2 = (bf16[160,384]{1,0:T(8,128)(2,1)}, bf16[160,384]{1,0:T(8,128)(2,1)S(1)}, u32[]{:S(2)}, u32[]{:S(2)}) collective-permute-start(bf16[160,384]{1,0:T(8,128)(2,1)} %shard_map.305), channel_id=1, source_target_pairs={{0,24},{2,26},{4,28},{6,30},{8,16},{10,18},{12,20},{14,22},{16,8},... | collective-permute-start | bytes 368648 | tf_op jit(solution)/shard_map/ppermute | solution.py:31
  8.8 11.2 %collective-permute-start.1 = (bf16[160,384]{1,0:T(8,128)(2,1)}, bf16[160,384]{1,0:T(8,128)(2,1)S(1)}, u32[]{:S(2)}, u32[]{:S(2)}) collective-permute-start(bf16[160,384]{1,0:T(8,128)(2,1)} %shard_map.305), channel_id=1, source_target_pairs={{0,8},{2,10},{4,12},{6,14},{8,0},{10,2},{12,4},{14,6},{16,24},{18,... | collective-permute-start | bytes 368648 | tf_op jit(solution)/shard_map/ppermute | solution.py:31
  18.1 21.7 %copy-start.21 = (bf16[2,160,384]{2,1,0:T(8,128)(2,1)}, bf16[2,160,384]{2,1,0:T(8,128)(2,1)S(1)}, u32[]{:S(2)}) copy-start(bf16[2,160,384]{2,1,0:T(8,128)(2,1)S(1)} %pad_maximum_fusion.2.refs_0_) | copy-start | bytes 737284
  18.1 8.9 %collective-permute-start.6 = (bf16[2,160,384]{2,1,0:T(8,128)(2,1)S(1)}, bf16[2,160,384]{2,1,0:T(8,128)(2,1)S(1)}, u32[]{:S(2)}, u32[]{:S(2)}) collective-permute-start(bf16[2,160,384]{2,1,0:T(8,128)(2,1)S(1)} %pad_maximum_fusion.2.refs_0_), channel_id=1, source_target_pairs={{0,4},{2,6},{4,0},{6,2},{8,12},{10,14},{12,8},{14,10},{16,20},{18,... | collective-permute-start | bytes 737288 | tf_op jit(solution)/shard_map/ppermute | solution.py:31
  20.1 8.9 %collective-permute-start.5 = (bf16[2,160,384]{2,1,0:T(8,128)(2,1)S(1)}, bf16[2,160,384]{2,1,0:T(8,128)(2,1)S(1)}, u32[]{:S(2)}, u32[]{:S(2)}) collective-permute-start(bf16[2,160,384]{2,1,0:T(8,128)(2,1)S(1)} %pad_maximum_fusion.3.refs_1_), channel_id=1, source_target_pairs={{0,2},{2,0},{4,6},{6,4},{8,10},{10,8},{12,14},{14,12},{16,18},{18,... | collective-permute-start | bytes 737288 | tf_op jit(solution)/shard_map/ppermute | solution.py:31
  21.6 18.1 %collective-permute-start.4 = (bf16[2,160,384]{2,1,0:T(8,128)(2,1)S(1)}, bf16[2,160,384]{2,1,0:T(8,128)(2,1)S(1)}, u32[]{:S(2)}, u32[]{:S(2)}) collective-permute-start(bf16[2,160,384]{2,1,0:T(8,128)(2,1)S(1)} %pad_maximum_fusion.2.refs_0_), channel_id=1, source_target_pairs={{0,2},{2,0},{4,6},{6,4},{8,10},{10,8},{12,14},{14,12},{16,18},{18,... | collective-permute-start | bytes 737288 | tf_op jit(solution)/shard_map/ppermute | solution.py:31
  22.2 17.6 %collective-permute-start.7 = (bf16[2,160,384]{2,1,0:T(8,128)(2,1)S(1)}, bf16[2,160,384]{2,1,0:T(8,128)(2,1)S(1)}, u32[]{:S(2)}, u32[]{:S(2)}) collective-permute-start(bf16[2,160,384]{2,1,0:T(8,128)(2,1)S(1)} %pad_maximum_fusion.3.refs_1_), channel_id=1, source_target_pairs={{0,4},{2,6},{4,0},{6,2},{8,12},{10,14},{12,8},{14,10},{16,20},{18,... | collective-permute-start | bytes 737288 | tf_op jit(solution)/shard_map/ppermute | solution.py:31
  27.0 12.8 %collective-permute-start.8 = (bf16[2,160,384]{2,1,0:T(8,128)(2,1)S(1)}, bf16[2,160,384]{2,1,0:T(8,128)(2,1)S(1)}, u32[]{:S(2)}, u32[]{:S(2)}) collective-permute-start(bf16[2,160,384]{2,1,0:T(8,128)(2,1)S(1)} %collective-permute-done.6.refs_4_), channel_id=1, source_target_pairs={{0,2},{2,0},{4,6},{6,4},{8,10},{10,8},{12,14},{14,12},{16,18},{18,... | collective-permute-start | bytes 737288 | tf_op jit(solution)/shard_map/ppermute | solution.py:31
  29.0 10.8 %collective-permute-start.9 = (bf16[2,160,384]{2,1,0:T(8,128)(2,1)S(1)}, bf16[2,160,384]{2,1,0:T(8,128)(2,1)S(1)}, u32[]{:S(2)}, u32[]{:S(2)}) collective-permute-start(bf16[2,160,384]{2,1,0:T(8,128)(2,1)S(1)} %collective-permute-done.5.refs_3_), channel_id=1, source_target_pairs={{0,4},{2,6},{4,0},{6,2},{8,12},{10,14},{12,8},{14,10},{16,20},{18,... | collective-permute-start | bytes 737288 | tf_op jit(solution)/shard_map/ppermute | solution.py:31
  31.3 8.5 %collective-permute-start.3 = (bf16[48,1920]{1,0:T(8,128)(2,1)S(1)}, bf16[48,1920]{1,0:T(8,128)(2,1)S(1)}, u32[]{:S(2)}, u32[]{:S(2)}) collective-permute-start(bf16[48,1920]{1,0:T(8,128)(2,1)S(1)} %get-tuple-element.174), channel_id=1, source_target_pairs={{0,16},{2,18},{4,20},{6,22},{8,24},{10,26},{12,28},{14,30},{16,0},... | collective-permute-start | bytes 552968 | tf_op jit(solution)/shard_map/ppermute | solution.py:31
  43.7 11.1 %collective-permute-start.11 = (bf16[3,768,384]{2,1,0:T(8,128)(2,1)}, bf16[3,768,384]{2,1,0:T(8,128)(2,1)S(1)}, u32[]{:S(2)}, u32[]{:S(2)}) collective-permute-start(bf16[3,768,384]{2,1,0:T(8,128)(2,1)} %get-tuple-element.184.w_ref.w0_ref), channel_id=1, source_target_pairs={{0,1},{1,0},{2,3},{3,2},{4,5},{5,4},{6,7},{7,6},{8,9},{9,8},{10,11... | collective-permute-start | bytes 5308424 | tf_op jit(solution)/shard_map/ppermute | solution.py:35
  43.8 20.5 %copy-start.19 = (bf16[2,48,1920]{2,1,0:T(8,128)(2,1)}, bf16[2,48,1920]{2,1,0:T(8,128)(2,1)S(1)}, u32[]{:S(2)}) copy-start(bf16[2,48,1920]{2,1,0:T(8,128)(2,1)S(1)} %pad_maximum_fusion.refs_0_) | copy-start | bytes 1105924
  43.8 11.1 %collective-permute-start.10 = (bf16[2,48,1920]{2,1,0:T(8,128)(2,1)S(1)}, bf16[2,48,1920]{2,1,0:T(8,128)(2,1)S(1)}, u32[]{:S(2)}, u32[]{:S(2)}) collective-permute-start(bf16[2,48,1920]{2,1,0:T(8,128)(2,1)S(1)} %pad_maximum_fusion.refs_0_), channel_id=1, source_target_pairs={{0,8},{2,10},{4,12},{6,14},{8,0},{10,2},{12,4},{14,6},{16,24},{18,... | collective-permute-start | bytes 1105928 | tf_op jit(solution)/shard_map/ppermute | solution.py:31
  44.0 20.4 %collective-permute-start.14 = (bf16[2,48,1920]{2,1,0:T(8,128)(2,1)S(1)}, bf16[2,48,1920]{2,1,0:T(8,128)(2,1)S(1)}, u32[]{:S(2)}, u32[]{:S(2)}) collective-permute-start(bf16[2,48,1920]{2,1,0:T(8,128)(2,1)S(1)} %pad_maximum_fusion.refs_0_), channel_id=1, source_target_pairs={{0,4},{2,6},{4,0},{6,2},{8,12},{10,14},{12,8},{14,10},{16,20},{18,... | collective-permute-start | bytes 1105928 | tf_op jit(solution)/shard_map/ppermute | solution.py:31
  44.5 19.9 %collective-permute-start.13 = (bf16[2,48,1920]{2,1,0:T(8,128)(2,1)S(1)}, bf16[2,48,1920]{2,1,0:T(8,128)(2,1)S(1)}, u32[]{:S(2)}, u32[]{:S(2)}) collective-permute-start(bf16[2,48,1920]{2,1,0:T(8,128)(2,1)S(1)} %pad_maximum_fusion.refs_0_), channel_id=1, source_target_pairs={{0,2},{2,0},{4,6},{6,4},{8,10},{10,8},{12,14},{14,12},{16,18},{18,... | collective-permute-start | bytes 1105928 | tf_op jit(solution)/shard_map/ppermute | solution.py:31
  45.9 22.5 %copy-start.61 = (s32[4]{0:T(128)S(1)}, s32[4]{0:T(128)}, u32[]{:S(2)}) copy-start(s32[4]{0:T(128)} %param.20) | copy-start | bytes 52
  54.9 35.6 %copy-start.29 = (bf16[2,48,1920]{2,1,0:T(8,128)(2,1)}, bf16[2,48,1920]{2,1,0:T(8,128)(2,1)S(1)}, u32[]{:S(2)}) copy-start(bf16[2,48,1920]{2,1,0:T(8,128)(2,1)S(1)} %collective-permute-done.10.refs_1_) | copy-start | bytes 1105924
  54.9 9.5 %collective-permute-start.12 = (bf16[48,1536]{1,0:T(8,128)(2,1)S(1)}, bf16[48,1536]{1,0:T(8,128)(2,1)S(1)}, u32[]{:S(2)}, u32[]{:S(2)}) collective-permute-start(bf16[48,1536]{1,0:T(8,128)(2,1)S(1)} %bitcast.72), channel_id=1, source_target_pairs={{0,16},{2,18},{4,20},{6,22},{8,24},{10,26},{12,28},{14,30},{16,0},... | collective-permute-start | bytes 442376 | tf_op jit(solution)/shard_map/ppermute | solution.py:31
  56.7 21.3 %collective-permute-start.16 = (bf16[2,48,1920]{2,1,0:T(8,128)(2,1)S(1)}, bf16[2,48,1920]{2,1,0:T(8,128)(2,1)}, u32[]{:S(2)}, u32[]{:S(2)}) collective-permute-start(bf16[2,48,1920]{2,1,0:T(8,128)(2,1)S(1)} %collective-permute-done.10.refs_1_), channel_id=1, source_target_pairs={{0,4},{2,6},{4,0},{6,2},{8,12},{10,14},{12,8},{14,10},{16,20},{18,... | collective-permute-start | bytes 1105928 | tf_op jit(solution)/shard_map/ppermute | solution.py:31
  57.2 20.8 %collective-permute-start.15 = (bf16[2,48,1920]{2,1,0:T(8,128)(2,1)S(1)}, bf16[2,48,1920]{2,1,0:T(8,128)(2,1)}, u32[]{:S(2)}, u32[]{:S(2)}) collective-permute-start(bf16[2,48,1920]{2,1,0:T(8,128)(2,1)S(1)} %collective-permute-done.10.refs_1_), channel_id=1, source_target_pairs={{0,2},{2,0},{4,6},{6,4},{8,10},{10,8},{12,14},{14,12},{16,18},{18,... | collective-permute-start | bytes 1105928 | tf_op jit(solution)/shard_map/ppermute | solution.py:31
  64.3 26.2 %copy-start.30 = (bf16[2,48,1920]{2,1,0:T(8,128)(2,1)}, bf16[2,48,1920]{2,1,0:T(8,128)(2,1)S(1)}, u32[]{:S(2)}) copy-start(bf16[2,48,1920]{2,1,0:T(8,128)(2,1)S(1)} %collective-permute-done.14.refs_4_) | copy-start | bytes 1105924
  64.3 26.1 %copy-start.31 = (bf16[2,48,1920]{2,1,0:T(8,128)(2,1)}, bf16[2,48,1920]{2,1,0:T(8,128)(2,1)S(1)}, u32[]{:S(2)}) copy-start(bf16[2,48,1920]{2,1,0:T(8,128)(2,1)S(1)} %collective-permute-done.13.refs_2_) | copy-start | bytes 1105924
  64.4 30.5 %copy-start.20 = (bf16[2,48,1536]{2,1,0:T(8,128)(2,1)}, bf16[2,48,1536]{2,1,0:T(8,128)(2,1)S(1)}, u32[]{:S(2)}) copy-start(bf16[2,48,1536]{2,1,0:T(8,128)(2,1)S(1)} %pad_maximum_fusion.1.refs_0_) | copy-start | bytes 884740
  64.5 13.6 %collective-permute-start.19 = (bf16[2,48,1536]{2,1,0:T(8,128)(2,1)S(1)}, bf16[2,48,1536]{2,1,0:T(8,128)(2,1)S(1)}, u32[]{:S(2)}, u32[]{:S(2)}) collective-permute-start(bf16[2,48,1536]{2,1,0:T(8,128)(2,1)S(1)} %pad_maximum_fusion.1.refs_0_), channel_id=1, source_target_pairs={{0,2},{2,0},{4,6},{6,4},{8,10},{10,8},{12,14},{14,12},{16,18},{18,... | collective-permute-start | bytes 884744 | tf_op jit(solution)/shard_map/ppermute | solution.py:31
  66.0 12.1 %collective-permute-start.18 = (bf16[2,48,1536]{2,1,0:T(8,128)(2,1)S(1)}, bf16[2,48,1536]{2,1,0:T(8,128)(2,1)S(1)}, u32[]{:S(2)}, u32[]{:S(2)}) collective-permute-start(bf16[2,48,1536]{2,1,0:T(8,128)(2,1)S(1)} %pad_maximum_fusion.1.refs_0_), channel_id=1, source_target_pairs={{0,4},{2,6},{4,0},{6,2},{8,12},{10,14},{12,8},{14,10},{16,20},{18,... | collective-permute-start | bytes 884744 | tf_op jit(solution)/shard_map/ppermute | solution.py:31
  66.7 11.4 %collective-permute-start.17 = (bf16[2,48,1536]{2,1,0:T(8,128)(2,1)S(1)}, bf16[2,48,1536]{2,1,0:T(8,128)(2,1)S(1)}, u32[]{:S(2)}, u32[]{:S(2)}) collective-permute-start(bf16[2,48,1536]{2,1,0:T(8,128)(2,1)S(1)} %pad_maximum_fusion.1.refs_0_), channel_id=1, source_target_pairs={{0,8},{2,10},{4,12},{6,14},{8,0},{10,2},{12,4},{14,6},{16,24},{18,... | collective-permute-start | bytes 884744 | tf_op jit(solution)/shard_map/ppermute | solution.py:31
  78.1 27.5 %copy-start.34 = (bf16[2,48,1536]{2,1,0:T(8,128)(2,1)}, bf16[2,48,1536]{2,1,0:T(8,128)(2,1)S(1)}, u32[]{:S(2)}) copy-start(bf16[2,48,1536]{2,1,0:T(8,128)(2,1)S(1)} %collective-permute-done.19.refs_2_) | copy-start | bytes 884740
  79.5 10.9 %collective-permute-start.24 = (bf16[2,48,1920]{2,1,0:T(8,128)(2,1)}, bf16[2,48,1920]{2,1,0:T(8,128)(2,1)S(1)}, u32[]{:S(2)}, u32[]{:S(2)}) collective-permute-start(bf16[2,48,1920]{2,1,0:T(8,128)(2,1)} %collective-permute-done.15.refs_3_), channel_id=1, source_target_pairs={{0,4},{2,6},{4,0},{6,2},{8,12},{10,14},{12,8},{14,10},{16,20},{18,... | collective-permute-start | bytes 1105928 | tf_op jit(solution)/shard_map/ppermute | solution.py:31
  80.0 10.4 %collective-permute-start.23 = (bf16[2,48,1920]{2,1,0:T(8,128)(2,1)S(1)}, bf16[2,48,1920]{2,1,0:T(8,128)(2,1)S(1)}, u32[]{:S(2)}, u32[]{:S(2)}) collective-permute-start(bf16[2,48,1920]{2,1,0:T(8,128)(2,1)S(1)} %collective-permute-done.14.refs_4_), channel_id=1, source_target_pairs={{0,2},{2,0},{4,6},{6,4},{8,10},{10,8},{12,14},{14,12},{16,18},{18,... | collective-permute-start | bytes 1105928 | tf_op jit(solution)/shard_map/ppermute | solution.py:31
  95.0 3.5 %collective-permute-start.25 = (bf16[768,384]{1,0:T(8,128)(2,1)}, bf16[768,384]{1,0:T(8,128)(2,1)S(1)}, u32[]{:S(2)}, u32[]{:S(2)}) collective-permute-start(bf16[768,384]{1,0:T(8,128)(2,1)} %get-tuple-element.225.w0_ref), channel_id=1, source_target_pairs={{0,1},{1,0},{2,3},{3,2},{4,5},{5,4},{6,7},{7,6},{8,9},{9,8},{10,11... | collective-permute-start | bytes 1769480 | tf_op jit(solution)/shard_map/ppermute | solution.py:35
  95.0 10.5 %collective-permute-start.22 = (bf16[2,48,1536]{2,1,0:T(8,128)(2,1)}, bf16[2,48,1536]{2,1,0:T(8,128)(2,1)S(1)}, u32[]{:S(2)}, u32[]{:S(2)}) collective-permute-start(bf16[2,48,1536]{2,1,0:T(8,128)(2,1)} %copy-done.35), channel_id=1, source_target_pairs={{0,2},{2,0},{4,6},{6,4},{8,10},{10,8},{12,14},{14,12},{16,18},{18,... | collective-permute-start | bytes 884744 | tf_op jit(solution)/shard_map/ppermute | solution.py:31
  95.8 9.8 %collective-permute-start.21 = (bf16[2,48,1536]{2,1,0:T(8,128)(2,1)}, bf16[2,48,1536]{2,1,0:T(8,128)(2,1)}, u32[]{:S(2)}, u32[]{:S(2)}) collective-permute-start(bf16[2,48,1536]{2,1,0:T(8,128)(2,1)} %copy-done.36), channel_id=1, source_target_pairs={{0,4},{2,6},{4,0},{6,2},{8,12},{10,14},{12,8},{14,10},{16,20},{18,... | collective-permute-start | bytes 884744 | tf_op jit(solution)/shard_map/ppermute | solution.py:31
  97.3 13.8 %collective-permute-start.20 = (bf16[2,48,1536]{2,1,0:T(8,128)(2,1)}, bf16[2,48,1536]{2,1,0:T(8,128)(2,1)}, u32[]{:S(2)}, u32[]{:S(2)}) collective-permute-start(bf16[2,48,1536]{2,1,0:T(8,128)(2,1)} %copy-done.36), channel_id=1, source_target_pairs={{0,2},{2,0},{4,6},{6,4},{8,10},{10,8},{12,14},{14,12},{16,18},{18,... | collective-permute-start | bytes 884744 | tf_op jit(solution)/shard_map/ppermute | solution.py:31
  98.5 25.2 %collective-permute-start.27 = (bf16[768,1536]{1,0:T(8,128)(2,1)}, bf16[768,1536]{1,0:T(8,128)(2,1)}, u32[]{:S(2)}, u32[]{:S(2)}) collective-permute-start(bf16[768,1536]{1,0:T(8,128)(2,1)} %get-tuple-element.235.w0_ref), channel_id=1, source_target_pairs={{0,1},{1,0},{2,3},{3,2},{4,5},{5,4},{6,7},{7,6},{8,9},{9,8},{10,11... | collective-permute-start | bytes 7077896 | tf_op jit(solution)/shard_map/ppermute | solution.py:35
  111.1 8.7 %collective-permute-start.26 = (bf16[2,48,1536]{2,1,0:T(8,128)(2,1)}, bf16[2,48,1536]{2,1,0:T(8,128)(2,1)S(1)}, u32[]{:S(2)}, u32[]{:S(2)}) collective-permute-start(bf16[2,48,1536]{2,1,0:T(8,128)(2,1)} %collective-permute-done.20.refs_3_), channel_id=1, source_target_pairs={{0,4},{2,6},{4,0},{6,2},{8,12},{10,14},{12,8},{14,10},{16,20},{18,... | collective-permute-start | bytes 884744 | tf_op jit(solution)/shard_map/ppermute | solution.py:31
  123.7 7.2 %collective-permute-start.28 = (bf16[768,1536]{1,0:T(8,128)(2,1)}, bf16[768,1536]{1,0:T(8,128)(2,1)S(1)}, u32[]{:S(2)}, u32[]{:S(2)}) collective-permute-start(bf16[768,1536]{1,0:T(8,128)(2,1)} %shard_map.313.w0_ref), channel_id=1, source_target_pairs={{0,1},{1,0},{2,3},{3,2},{4,5},{5,4},{6,7},{7,6},{8,9},{9,8},{10,11... | collective-permute-start | bytes 7077896 | tf_op jit(solution)/shard_map/ppermute | solution.py:35
  149.8 4.7 %collective-permute-start.29 = (bf16[768,1536]{1,0:T(8,128)(2,1)S(1)}, bf16[768,1536]{1,0:T(8,128)(2,1)S(1)}, u32[]{:S(2)}, u32[]{:S(2)}) collective-permute-start(bf16[768,1536]{1,0:T(8,128)(2,1)S(1)} %convolution_convert_fusion.2), channel_id=1, source_target_pairs={{0,1},{1,0},{2,3},{3,2},{4,5},{5,4},{6,7},{7,6},{8,9},{9,8},{10,11... | collective-permute-start | bytes 7077896 | tf_op jit(solution)/shard_map/ppermute | solution.py:35
  163.0 9.8 %collective-permute-start.30 = (bf16[768,1536]{1,0:T(8,128)(2,1)S(1)}, bf16[768,1536]{1,0:T(8,128)(2,1)S(1)}, u32[]{:S(2)}, u32[]{:S(2)}) collective-permute-start(bf16[768,1536]{1,0:T(8,128)(2,1)S(1)} %convolution_convert_fusion), channel_id=1, source_target_pairs={{0,1},{1,0},{2,3},{3,2},{4,5},{5,4},{6,7},{7,6},{8,9},{9,8},{10,11... | collective-permute-start | bytes 7077896 | tf_op jit(solution)/shard_map/ppermute | solution.py:35
  181.1 28.3 %collective-permute-start.31 = (bf16[4,48,3072]{2,1,0:T(8,128)(2,1)}, bf16[4,48,3072]{2,1,0:T(8,128)(2,1)}, u32[]{:S(2)}, u32[]{:S(2)}) collective-permute-start(bf16[4,48,3072]{2,1,0:T(8,128)(2,1)} %get-tuple-element.256), channel_id=1, source_target_pairs={{0,2},{2,0},{4,6},{6,4},{8,10},{10,8},{12,14},{14,12},{16,18},{18,... | collective-permute-start | bytes 3538952 | tf_op jit(solution)/shard_map/ppermute | solution.py:31
  181.8 28.1 %collective-permute-start.32 = (bf16[4,48,3072]{2,1,0:T(8,128)(2,1)}, bf16[4,48,3072]{2,1,0:T(8,128)(2,1)}, u32[]{:S(2)}, u32[]{:S(2)}) collective-permute-start(bf16[4,48,3072]{2,1,0:T(8,128)(2,1)} %get-tuple-element.257), channel_id=1, source_target_pairs={{0,4},{2,6},{4,0},{6,2},{8,12},{10,14},{12,8},{14,10},{16,20},{18,... | collective-permute-start | bytes 3538952 | tf_op jit(solution)/shard_map/ppermute | solution.py:31
  198.1 3.8 %collective-permute-start.33 = (bf16[768,384]{1,0:T(8,128)(2,1)S(1)}, bf16[768,384]{1,0:T(8,128)(2,1)}, u32[]{:S(2)}, u32[]{:S(2)}) collective-permute-start(bf16[768,384]{1,0:T(8,128)(2,1)S(1)} %convolution_convert_fusion.6), channel_id=1, source_target_pairs={{0,1},{1,0},{2,3},{3,2},{4,5},{5,4},{6,7},{7,6},{8,9},{9,8},{10,11... | collective-permute-start | bytes 1769480 | tf_op jit(solution)/shard_map/ppermute | solution.py:35
  212.5 21.3 %collective-permute-start.37 = (bf16[2,48,3072]{2,1,0:T(8,128)(2,1)}, bf16[2,48,3072]{2,1,0:T(8,128)(2,1)}, u32[]{:S(2)}, u32[]{:S(2)}) collective-permute-start(bf16[2,48,3072]{2,1,0:T(8,128)(2,1)} %get-tuple-element.273), channel_id=1, source_target_pairs={{0,4},{2,6},{4,0},{6,2},{8,12},{10,14},{12,8},{14,10},{16,20},{18,... | collective-permute-start | bytes 1769480 | tf_op jit(solution)/shard_map/ppermute | solution.py:31
  214.0 19.8 %collective-permute-start.36 = (bf16[2,48,3072]{2,1,0:T(8,128)(2,1)}, bf16[2,48,3072]{2,1,0:T(8,128)(2,1)}, u32[]{:S(2)}, u32[]{:S(2)}) collective-permute-start(bf16[2,48,3072]{2,1,0:T(8,128)(2,1)} %get-tuple-element.272), channel_id=1, source_target_pairs={{0,2},{2,0},{4,6},{6,4},{8,10},{10,8},{12,14},{14,12},{16,18},{18,... | collective-permute-start | bytes 1769480 | tf_op jit(solution)/shard_map/ppermute | solution.py:31
  217.5 16.3 %collective-permute-start.34 = (bf16[4,48,384]{2,1,0:T(8,128)(2,1)S(1)}, bf16[4,48,384]{2,1,0:T(8,128)(2,1)S(1)}, u32[]{:S(2)}, u32[]{:S(2)}) collective-permute-start(bf16[4,48,384]{2,1,0:T(8,128)(2,1)S(1)} %copy-done.58), channel_id=1, source_target_pairs={{0,2},{2,0},{4,6},{6,4},{8,10},{10,8},{12,14},{14,12},{16,18},{18,... | collective-permute-start | bytes 442376 | tf_op jit(solution)/shard_map/ppermute | solution.py:31
  219.0 14.8 %collective-permute-start.35 = (bf16[4,48,384]{2,1,0:T(8,128)(2,1)S(1)}, bf16[4,48,384]{2,1,0:T(8,128)(2,1)S(1)}, u32[]{:S(2)}, u32[]{:S(2)}) collective-permute-start(bf16[4,48,384]{2,1,0:T(8,128)(2,1)S(1)} %copy-done.57), channel_id=1, source_target_pairs={{0,4},{2,6},{4,0},{6,2},{8,12},{10,14},{12,8},{14,10},{16,20},{18,... | collective-permute-start | bytes 442376 | tf_op jit(solution)/shard_map/ppermute | solution.py:31
  236.2 11.5 %collective-permute-start.42 = (bf16[2,48,384]{2,1,0:T(8,128)(2,1)}, bf16[2,48,384]{2,1,0:T(8,128)(2,1)S(1)}, u32[]{:S(2)}, u32[]{:S(2)}) collective-permute-start(bf16[2,48,384]{2,1,0:T(8,128)(2,1)} %get-tuple-element.289), channel_id=1, source_target_pairs={{0,4},{2,6},{4,0},{6,2},{8,12},{10,14},{12,8},{14,10},{16,20},{18,... | collective-permute-start | bytes 221192 | tf_op jit(solution)/shard_map/ppermute | solution.py:31
  237.7 10.0 %collective-permute-start.41 = (bf16[2,48,384]{2,1,0:T(8,128)(2,1)}, bf16[2,48,384]{2,1,0:T(8,128)(2,1)S(1)}, u32[]{:S(2)}, u32[]{:S(2)}) collective-permute-start(bf16[2,48,384]{2,1,0:T(8,128)(2,1)} %get-tuple-element.288), channel_id=1, source_target_pairs={{0,2},{2,0},{4,6},{6,4},{8,10},{10,8},{12,14},{14,12},{16,18},{18,... | collective-permute-start | bytes 221192 | tf_op jit(solution)/shard_map/ppermute | solution.py:31
  247.7 27.4 %collective-permute-start.43 = (bf16[3,768,384]{2,1,0:T(8,128)(2,1)}, bf16[3,768,384]{2,1,0:T(8,128)(2,1)S(1)}, u32[]{:S(2)}, u32[]{:S(2)}) collective-permute-start(bf16[3,768,384]{2,1,0:T(8,128)(2,1)} %get-tuple-element.300), channel_id=1, source_target_pairs={{0,1},{1,0},{2,3},{3,2},{4,5},{5,4},{6,7},{7,6},{8,9},{9,8},{10,11... | collective-permute-start | bytes 5308424 | tf_op jit(solution)/shard_map/ppermute | solution.py:35
  248.3 21.6 %collective-permute-start.38 = (bf16[48,3072]{1,0:T(8,128)(2,1)}, bf16[48,3072]{1,0:T(8,128)(2,1)S(1)}, u32[]{:S(2)}, u32[]{:S(2)}) collective-permute-start(bf16[48,3072]{1,0:T(8,128)(2,1)} %get-tuple-element.281), channel_id=1, source_target_pairs={{0,8},{2,10},{4,12},{6,14},{8,0},{10,2},{12,4},{14,6},{16,24},{18,... | collective-permute-start | bytes 884744 | tf_op jit(solution)/shard_map/ppermute | solution.py:31
  248.6 23.8 %collective-permute-start.39 = (bf16[48,3072]{1,0:T(8,128)(2,1)}, bf16[48,3072]{1,0:T(8,128)(2,1)S(1)}, u32[]{:S(2)}, u32[]{:S(2)}) collective-permute-start(bf16[48,3072]{1,0:T(8,128)(2,1)} %get-tuple-element.282), channel_id=1, source_target_pairs={{0,16},{2,18},{4,20},{6,22},{8,24},{10,26},{12,28},{14,30},{16,0},... | collective-permute-start | bytes 884744 | tf_op jit(solution)/shard_map/ppermute | solution.py:31
  250.8 24.3 %collective-permute-start.40 = (bf16[48,3072]{1,0:T(8,128)(2,1)}, bf16[48,3072]{1,0:T(8,128)(2,1)S(1)}, u32[]{:S(2)}, u32[]{:S(2)}) collective-permute-start(bf16[48,3072]{1,0:T(8,128)(2,1)} %get-tuple-element.283), channel_id=1, source_target_pairs={{0,24},{2,26},{4,28},{6,30},{8,16},{10,18},{12,20},{14,22},{16,8},... | collective-permute-start | bytes 884744 | tf_op jit(solution)/shard_map/ppermute | solution.py:31
  257.8 44.7 %collective-permute-start.51 = (bf16[48,384]{1,0:T(8,128)(2,1)}, bf16[48,384]{1,0:T(8,128)(2,1)S(1)}, u32[]{:S(2)}, u32[]{:S(2)}) collective-permute-start(bf16[48,384]{1,0:T(8,128)(2,1)} %get-tuple-element.322), channel_id=1, source_target_pairs={{0,8},{2,10},{4,12},{6,14},{8,0},{10,2},{12,4},{14,6},{16,24},{18,... | collective-permute-start | bytes 110600 | tf_op jit(solution)/shard_map/ppermute | solution.py:31
  270.0 32.6 %collective-permute-start.52 = (bf16[48,384]{1,0:T(8,128)(2,1)S(1)}, bf16[48,384]{1,0:T(8,128)(2,1)S(1)}, u32[]{:S(2)}, u32[]{:S(2)}) collective-permute-start(bf16[48,384]{1,0:T(8,128)(2,1)S(1)} %copy-done.60), channel_id=1, source_target_pairs={{0,16},{2,18},{4,20},{6,22},{8,24},{10,26},{12,28},{14,30},{16,0},... | collective-permute-start | bytes 110600 | tf_op jit(solution)/shard_map/ppermute | solution.py:31
  272.5 30.1 %collective-permute-start.53 = (bf16[48,384]{1,0:T(8,128)(2,1)S(1)}, bf16[48,384]{1,0:T(8,128)(2,1)S(1)}, u32[]{:S(2)}, u32[]{:S(2)}) collective-permute-start(bf16[48,384]{1,0:T(8,128)(2,1)S(1)} %copy-done.59), channel_id=1, source_target_pairs={{0,24},{2,26},{4,28},{6,30},{8,16},{10,18},{12,20},{14,22},{16,8},... | collective-permute-start | bytes 110600 | tf_op jit(solution)/shard_map/ppermute | solution.py:31
  283.8 11.7 %collective-permute-start.44 = (bf16[4,160,384]{2,1,0:T(8,128)(2,1)}, bf16[4,160,384]{2,1,0:T(8,128)(2,1)S(1)}, u32[]{:S(2)}, u32[]{:S(2)}) collective-permute-start(bf16[4,160,384]{2,1,0:T(8,128)(2,1)} %get-tuple-element.302), channel_id=1, source_target_pairs={{0,2},{2,0},{4,6},{6,4},{8,10},{10,8},{12,14},{14,12},{16,18},{18,... | collective-permute-start | bytes 1474568 | tf_op jit(solution)/shard_map/ppermute | solution.py:31
  285.2 11.4 %collective-permute-start.45 = (bf16[4,160,384]{2,1,0:T(8,128)(2,1)}, bf16[4,160,384]{2,1,0:T(8,128)(2,1)S(1)}, u32[]{:S(2)}, u32[]{:S(2)}) collective-permute-start(bf16[4,160,384]{2,1,0:T(8,128)(2,1)} %get-tuple-element.303), channel_id=1, source_target_pairs={{0,4},{2,6},{4,0},{6,2},{8,12},{10,14},{12,8},{14,10},{16,20},{18,... | collective-permute-start | bytes 1474568 | tf_op jit(solution)/shard_map/ppermute | solution.py:31
  292.3 26.1 %copy-start.51 = (f32[48,384]{1,0:T(8,128)S(1)}, f32[48,384]{1,0:T(8,128)}, u32[]{:S(2)}) copy-start(f32[48,384]{1,0:T(8,128)} %get-tuple-element.296) | copy-start | bytes 221188
  299.5 6.4 %collective-permute-start.46 = (bf16[2,160,384]{2,1,0:T(8,128)(2,1)}, bf16[2,160,384]{2,1,0:T(8,128)(2,1)S(1)}, u32[]{:S(2)}, u32[]{:S(2)}) collective-permute-start(bf16[2,160,384]{2,1,0:T(8,128)(2,1)} %get-tuple-element.314), channel_id=1, source_target_pairs={{0,2},{2,0},{4,6},{6,4},{8,10},{10,8},{12,14},{14,12},{16,18},{18,... | collective-permute-start | bytes 737288 | tf_op jit(solution)/shard_map/ppermute | solution.py:31
  300.2 6.4 %collective-permute-start.47 = (bf16[2,160,384]{2,1,0:T(8,128)(2,1)}, bf16[2,160,384]{2,1,0:T(8,128)(2,1)S(1)}, u32[]{:S(2)}, u32[]{:S(2)}) collective-permute-start(bf16[2,160,384]{2,1,0:T(8,128)(2,1)} %get-tuple-element.315), channel_id=1, source_target_pairs={{0,4},{2,6},{4,0},{6,2},{8,12},{10,14},{12,8},{14,10},{16,20},{18,... | collective-permute-start | bytes 737288 | tf_op jit(solution)/shard_map/ppermute | solution.py:31
  309.7 15.7 %collective-permute-start.48 = (bf16[160,384]{1,0:T(8,128)(2,1)}, bf16[160,384]{1,0:T(8,128)(2,1)S(1)}, u32[]{:S(2)}, u32[]{:S(2)}) collective-permute-start(bf16[160,384]{1,0:T(8,128)(2,1)} %get-tuple-element.319), channel_id=1, source_target_pairs={{0,8},{2,10},{4,12},{6,14},{8,0},{10,2},{12,4},{14,6},{16,24},{18,... | collective-permute-start | bytes 368648 | tf_op jit(solution)/shard_map/ppermute | solution.py:31
  315.8 9.6 %collective-permute-start.49 = (bf16[160,384]{1,0:T(8,128)(2,1)}, bf16[160,384]{1,0:T(8,128)(2,1)S(1)}, u32[]{:S(2)}, u32[]{:S(2)}) collective-permute-start(bf16[160,384]{1,0:T(8,128)(2,1)} %get-tuple-element.320), channel_id=1, source_target_pairs={{0,16},{2,18},{4,20},{6,22},{8,24},{10,26},{12,28},{14,30},{16,0},... | collective-permute-start | bytes 368648 | tf_op jit(solution)/shard_map/ppermute | solution.py:31
  317.0 8.5 %collective-permute-start.50 = (bf16[160,384]{1,0:T(8,128)(2,1)}, bf16[160,384]{1,0:T(8,128)(2,1)S(1)}, u32[]{:S(2)}, u32[]{:S(2)}) collective-permute-start(bf16[160,384]{1,0:T(8,128)(2,1)} %get-tuple-element.321), channel_id=1, source_target_pairs={{0,24},{2,26},{4,28},{6,30},{8,16},{10,18},{12,20},{14,22},{16,8},... | collective-permute-start | bytes 368648 | tf_op jit(solution)/shard_map/ppermute | solution.py:31
  325.6 1.3 collective-permute-start.54
  (56 other events, 342.4 us)
where the time goes:
time: 329 us; the launch traced here: 328 us
  Pallas kernels  148 us (45%)
  starting transfers between devices  62 us (19%)
  matrix products  49.9 us (15%)
  waiting for transfers between devices  41.3 us (13%)
  local copies, waits for them, and re-layouts  18.2 us (6%)
  other arithmetic  7.51 us (2%)
    ppermute x46, starting transfers between devices, swap_dp(): return lax.ppermute(value, 'dp', [(i, i ^ mask) for i in range(size)])  60.7 us
    dot_general x12, matrix products, dot(): return lax.dot_general(left, right, dims, preferred_element_type=f32)  49.9 us
    pallas_call x4, Pallas kernels, attend_call(): pl.pallas_call(kernel, out_shape=out_shape, grid_spec=pltpu.PrefetchScala...  42.2 us
    ppermute x46, waiting for transfers between devices, swap_dp(): return lax.ppermute(value, 'dp', [(i, i ^ mask) for i in range(size)])  40.7 us
    pallas_call x3, Pallas kernels, row_call(): pl.pallas_call(kernel, out_shape=[jax.ShapeDtypeStruct((rows, n), d) for...  31.5 us
    pallas_call x6, Pallas kernels, whole_call(): pl.pallas_call(kernel, out_shape=[jax.ShapeDtypeStruct(o, d) for o, d in...  14.2 us
    unnamed x131, local copies, waits for them, and re-layouts  13.8 us
    pallas_call x2, Pallas kernels, token_gradient(): pl.pallas_call(kernel, out_shape=jax.ShapeDtypeStruct((rows, width), f32)...  12.7 us
  transfers between devices with their start and end apart: 55, of which 14 were waited for; matrix products, arithmetic and copies ran while one was open for 15% of the time, Pallas kernels for 34%

commit v1 on v0

--- a/solution.py
+++ b/solution.py
@@ -72,6 +72,8 @@
     return buf
 
 
+BLOCK = 256
+PART = 128
 HINT = pl.CostEstimate(flops=1, transcendentals=0, bytes_accessed=1)
 
 
@@ -312,25 +314,35 @@
     )(jnp.stack([index, core]), tokens_t, deltas, others, other_sums, table)
 
 
-def pack_table(first_sums, second_sums, last, size, cols):
+def pack_table(first_sums, second_sums, inner_sums, core, size, cols):
     one = first_sums.shape[1] // size
-    end = last.shape[1] // size
-
-    def kernel(a_ref, b_ref, last_ref, out_ref, table):
+    end = inner_sums.shape[1] // size
+
+    def kernel(core_ref, a_ref, b_ref, inner_ref, out_ref, table):
         table[...] = jnp.zeros(table.shape, f32)
         out_ref[...] = jnp.zeros(out_ref.shape, f32)
         table[2:5, :] = a_ref[0:3, :]
         table[5:8, :] = b_ref[0:3, :]
         for c in range(size):
             out_ref[c, :, :one] = table[:, c * one : (c + 1) * one]
-            out_ref[c, 8:9, :end] = last_ref[:, c * end : (c + 1) * end]
-
+            d = (c + size // 2) % size
+            here = inner_ref[0:1, c * end : (c + 1) * end]
+            there = inner_ref[0:1, d * end : (d + 1) * end]
+            out_ref[c, 8:9, :end] = jnp.where(core_ref[0] == 0, here, there)
+
+    ins = (first_sums, second_sums, inner_sums)
     return pl.pallas_call(
         kernel,
         out_shape=jax.ShapeDtypeStruct((size, 16, cols), f32),
-        scratch_shapes=[pltpu.VMEM((16, first_sums.shape[1]), f32)],
-        cost_estimate=HINT,
-    )(first_sums, second_sums, last)
+        grid_spec=pltpu.PrefetchScalarGridSpec(
+            num_scalar_prefetch=1,
+            grid=(1,),
+            in_specs=[vmem(a.shape) for a in ins],
+            out_specs=vmem((size, 16, cols)),
+            scratch_shapes=[pltpu.VMEM((16, first_sums.shape[1]), f32)],
+        ),
+        cost_estimate=HINT,
+    )(core[None], *ins)
 
 
 def whole_call(kernel, outs, ins, blocks):
@@ -459,59 +471,79 @@
 
 
 def add_rows(ref, items):
+    for i, item in enumerate(items):
+        ref[i : i + 1, : item.shape[1]] += jnp.sum(item, axis=0, keepdims=True)
+
+
+def clear(*refs):
     @pl.when(pl.program_id(0) == 0)
     def _():
-        ref[...] = jnp.zeros(ref.shape, f32)
-
-    for i, item in enumerate(items):
-        ref[i : i + 1, :] += jnp.sum(item, axis=0, keepdims=True)
-
-
-def row_call(kernel, tiles, wholes, outs, sums=True):
+        for ref in refs:
+            ref[...] = jnp.zeros(ref.shape, f32)
+
+
+def in_turns(product, finish):
+    parts = [slice(i, i + PART) for i in range(0, BLOCK, PART)]
+    ahead = product(parts[0])
+    for n, part in enumerate(parts):
+        now = ahead
+        if n + 1 < len(parts):
+            ahead = product(parts[n + 1])
+        finish(part, now)
+
+
+def row_call(kernel, tiles, wholes, outs, sums):
     rows = tiles[0].shape[0]
-    width = outs[0][0]
 
     def tile(cols):
-        return pl.BlockSpec((ROWS, cols), lambda i: (i, 0))
+        return pl.BlockSpec((BLOCK, cols), lambda i: (i, 0))
 
     return pl.pallas_call(
         kernel,
         out_shape=[jax.ShapeDtypeStruct((rows, n), d) for n, d in outs]
-        + [jax.ShapeDtypeStruct((8, width), f32)] * sums,
-        grid=(rows // ROWS,),
+        + [jax.ShapeDtypeStruct((8, n), f32) for n in sums],
+        grid=(rows // BLOCK,),
         in_specs=[tile(a.shape[1]) for a in tiles] + [vmem(a.shape) for a in wholes],
-        out_specs=[tile(n) for n, _ in outs] + [vmem((8, width))] * sums,
+        out_specs=[tile(n) for n, _ in outs] + [vmem((8, n)) for n in sums],
         cost_estimate=HINT,
     )(*tiles, *wholes)
 
 
 def first_block(tokens, context, weights, vectors):
     def kernel(x_ref, c0_ref, c1_ref, w0_ref, w1_ref, v_ref, out, low):
-        total = dot(c0_ref[...], w0_ref[...], NT) + dot(c1_ref[...], w1_ref[...], NT)
-        total = x_ref[...].astype(f32) + total + v_ref[2:3]
-        out[...] = total
-        low[...] = (center(total)[0] * v_ref[3:4] + v_ref[4:5]).astype(bf16)
+        def product(at):
+            return dot(c0_ref[at], w0_ref[...], NT) + dot(c1_ref[at], w1_ref[...], NT)
+
+        def finish(at, total):
+            total = x_ref[at].astype(f32) + total + v_ref[2:3]
+            out[at] = total
+            low[at] = (center(total)[0] * v_ref[3:4] + v_ref[4:5]).astype(bf16)
+
+        in_turns(product, finish)
 
     width = tokens.shape[1]
     return row_call(
-        kernel,
-        [tokens, *context],
-        [*weights, vectors],
-        [(width, f32), (width, bf16)],
-        sums=False,
+        kernel, [tokens, *context], [*weights, vectors], [(width, f32), (width, bf16)], ()
     )
 
 
 def outer_block(hidden, cotangent, act, weights, vectors):
     def kernel(h_ref, c_ref, a0_ref, a1_ref, w0_ref, w1_ref, v_ref, out, delta, low, sums):
-        feed = v_ref[5:6] + dot(a0_ref[...], w0_ref[...], NT) + dot(a1_ref[...], w1_ref[...], NT)
-        normed, rinv = center(h_ref[...].astype(f32) + feed)
-        out[...] = normed * v_ref[6:7] + v_ref[7:8]
-        cot = c_ref[...].astype(f32)
-        found = norm_back(cot, normed, rinv, v_ref[6:7])
-        delta[...] = found
-        low[...] = found.astype(bf16)
-        add_rows(sums, (found, cot * normed, cot))
+        clear(sums)
+
+        def product(at):
+            return dot(a0_ref[at], w0_ref[...], NT) + dot(a1_ref[at], w1_ref[...], NT)
+
+        def finish(at, feed):
+            normed, rinv = center(h_ref[at].astype(f32) + (v_ref[5:6] + feed))
+            out[at] = normed * v_ref[6:7] + v_ref[7:8]
+            cot = c_ref[at].astype(f32)
+            found = norm_back(cot, normed, rinv, v_ref[6:7])
+            delta[at] = found
+            low[at] = found.astype(bf16)
+            add_rows(sums, (found, cot * normed, cot))
+
+        in_turns(product, finish)
 
     width = hidden.shape[1]
     return row_call(
@@ -519,17 +551,30 @@
         [hidden, cotangent, *act],
         [*weights, vectors],
         [(width, f32), (width, f32), (width, bf16)],
+        (width,),
     )
 
 
 def inner_back(second_delta, inner_delta, first_in, weights, vectors):
-    def kernel(s_ref, d0_ref, d1_ref, f_ref, w0_ref, w1_ref, v_ref, delta, low, sums):
-        grad = s_ref[...] + dot(d0_ref[...], w0_ref[...], NT) + dot(d1_ref[...], w1_ref[...], NT)
-        normed, rinv = center(f_ref[...])
-        found = norm_back(grad, normed, rinv, v_ref[3:4])
-        delta[...] = found
-        low[...] = found.astype(bf16)
-        add_rows(sums, (found, grad * normed, grad))
+    def kernel(s_ref, d0_ref, d1_ref, f_ref, w0_ref, w1_ref, v_ref, delta, low, sums, inner):
+        clear(sums, inner)
+        ones = jnp.ones((8, BLOCK), bf16)
+        half = d0_ref.shape[1]
+        inner[:, :half] += dot(ones, d0_ref[...], NN)
+        inner[:, half:] += dot(ones, d1_ref[...], NN)
+
+        def product(at):
+            return dot(d0_ref[at], w0_ref[...], NT) + dot(d1_ref[at], w1_ref[...], NT)
+
+        def finish(at, grad):
+            grad = s_ref[at] + grad
+            normed, rinv = center(f_ref[at])
+            found = norm_back(grad, normed, rinv, v_ref[3:4])
+            delta[at] = found
+            low[at] = found.astype(bf16)
+            add_rows(sums, (found, grad * normed, grad))
+
+        in_turns(product, finish)
 
     width = first_in.shape[1]
     return row_call(
@@ -537,6 +582,7 @@
         [second_delta, *inner_delta, first_in],
         [*weights, vectors],
         [(width, f32), (width, bf16)],
+        (width, 2 * inner_delta[0].shape[1]),
     )
 
 
@@ -826,12 +872,11 @@
         inner_delta[t] = (dot(feed_delta, wu[t], NN) * slope[t].astype(f32)).astype(bf16)
     gi = product(hidden, inner_delta)
     inner_delta[0], inner_delta[1], *gi = lax.optimization_barrier((*inner_delta, *gi))
-    grad_ib = [jnp.sum(inner_delta[t].astype(f32), axis=0, keepdims=True) for t in range(2)]
     if fast:
         parts_u = split_cols([gu, gi], index, size, 2 * step)
         first_u = corner_back(parts_u, size)
         inner_delta[0], inner_delta[1] = [after(d, parts_u[4]) for d in inner_delta]
-    first_delta, branch_delta, first_sums = inner_back(
+    first_delta, branch_delta, first_sums, inner_sums = inner_back(
         second_delta, inner_delta, first_in, wi, vecs
     )
     go = product(branch_delta, ctx)
@@ -842,9 +887,8 @@
             core == 0, jnp.concatenate(pair, 1), jnp.concatenate(pair[::-1], 1)
         )
 
-    grad_ib = joined(grad_ib)
     if fast:
-        table = pack_table(first_sums, second_sums, grad_ib, size, half)
+        table = pack_table(first_sums, second_sums, inner_sums, core, size, half)
         parts_i = split_cols([go], index, size, step)
         first_i = corner_back(parts_i, size)
         *first_u, ctx_delta[1], _ = lax.optimization_barrier(
@@ -877,10 +921,8 @@
         *got_i, others = lax.optimization_barrier((*got_i, others))
         last_i = near_add(parts_i[4], first_i, got_i)
         others = swap_core(others)
-        got_i = far_back(last_i, size)
         ctx_delta[0] = after(ctx_delta[0], last_i[0])
         deltas[0] = attend_back(0)
-        *got_u, deltas[0] = lax.optimization_barrier((*got_u, deltas[0]))
         parts_q = gradients_own(
             tokens_t,
             deltas[0],
@@ -892,12 +934,15 @@
             size,
             query_bias.shape[0],
         )
+        *got_u, own = lax.optimization_barrier((*got_u, parts_q[4]))
+        parts_q = [*parts_q[:4], own]
         first_q = corner_back(parts_q, size)
-        *got_i, _ = lax.optimization_barrier((*got_i, parts_q[4]))
         token_grad = token_gradient(
             after(first_delta, parts_q[4]), [after(d, parts_q[4]) for d in deltas], wqkv, 0, 2
         )
-        *first_q, token_grad = lax.optimization_barrier((*first_q, token_grad))
+        got_i = far_back([after(item, parts_q[4]) for item in last_i], size)
+        arrived = lax.optimization_barrier((*first_q, *got_i, token_grad))
+        first_q, got_i, token_grad = arrived[:2], arrived[2:5], arrived[5]
 
         def total(last, got):
             return last[0] + got[0].astype(f32) + got[1].astype(f32) + got[2].astype(f32)
@@ -936,7 +981,7 @@
             joined([jnp.sum(d[g].astype(f32), axis=0, keepdims=True) for d in deltas]) for g in (0, 2)
         ]
         bias_grads += [s[i : i + 1] for s in (first_sums, second_sums) for i in range(3)]
-        bias_grads.append(grad_ib)
+        bias_grads.append(joined(jnp.split(inner_sums[:1], 2, 1)))
         packed = jnp.concatenate([item.reshape(size, -1) for item in bias_grads], axis=1)
         packed = packed + swap_core(packed)
         own = scatter_rows(packed, orders[0], size, index).reshape(-1)

time: 329 us -> 336 us (1.021)
  Pallas kernels: 148 us -> 162 us
  starting transfers between devices: 62 us -> 54.7 us
    pallas_call x3, Pallas kernels: 31.5 us -> 45.7 us  [row_call(): pl.pallas_call(kernel, out_shape=[jax.ShapeDtypeStruct((rows, n), d) for...]
    ppermute x46, starting transfers between devices: 60.7 us -> 53.3 us  [swap_dp(): return lax.ppermute(value, 'dp', [(i, i ^ mask) for i in range(size)])]
    unnamed x131 -> x139, local copies, waits for them, and re-layouts: 13.8 us -> 16.1 us
  transfers between devices with their start and end apart: 55 -> 55, of which waited for: 14 -> 18; matrix products, arithmetic and copies ran while one was open for 15% -> 14% of each run, Pallas kernels for 34% -> 35%
where the time goes in v1:
time: 336 us; the launch traced here: 334 us
  Pallas kernels  162 us (48%)
  starting transfers between devices  54.7 us (16%)
  matrix products  49.9 us (15%)
  waiting for transfers between devices  40.6 us (12%)
  local copies, waits for them, and re-layouts  20.6 us (6%)
  other arithmetic  5.2 us (2%)
    ppermute x46, starting transfers between devices, swap_dp(): return lax.ppermute(value, 'dp', [(i, i ^ mask) for i in range(size)])  53.3 us
    dot_general x12, matrix products, dot(): return lax.dot_general(left, right, dims, preferred_element_type=f32)  49.9 us
    pallas_call x3, Pallas kernels, row_call(): pl.pallas_call(kernel, out_shape=[jax.ShapeDtypeStruct((rows, n), d) for...  45.7 us
    pallas_call x4, Pallas kernels, attend_call(): pl.pallas_call(kernel, out_shape=out_shape, grid_spec=pltpu.PrefetchScala...  42 us
    ppermute x46, waiting for transfers between devices, swap_dp(): return lax.ppermute(value, 'dp', [(i, i ^ mask) for i in range(size)])  39.9 us
    unnamed x139, local copies, waits for them, and re-layouts  16.1 us
    pallas_call x6, Pallas kernels, whole_call(): pl.pallas_call(kernel, out_shape=[jax.ShapeDtypeStruct(o, d) for o, d in...  14.3 us
    pallas_call x2, Pallas kernels, token_gradient(): pl.pallas_call(kernel, out_shape=jax.ShapeDtypeStruct((rows, width), f32)...  12.7 us
  transfers between devices with their start and end apart: 55, of which 18 were waited for; matrix products, arithmetic and copies ran while one was open for 14% of the time, Pallas kernels for 35%

profile of v1, /device:TPU:0, one launch (start us, length us, event | category | flops | bytes accessed | tf_op | source)
XLA Modules:
  0.0 334.2 jit_solution(16330003257219158769)
XLA Ops:
  1.9 1.5 shard_map.305
  3.4 3.1 collective-permute-start.1
  6.5 2.5 collective-permute-start.2
  10.0 6.1 %collective-permute-done.2 = bf16[160,384]{1,0:T(8,128)(2,1)S(1)} collective-permute-done((bf16[160,384]{1,0:T(8,128)(2,1)}, bf16[160,384]{1,0:T(8,128)(2,1)S(1)}, u32[]{:S(2)}, u32[]{:S(2)}) %collective-permute-start.2) | collective-permute-done | bytes 122912 | tf_op jit(solution)/shard_map/ppermute | solution.py:31
  16.1 1.6 collective-permute-start.5
  17.7 2.6 collective-permute-done
  21.2 1.6 collective-permute-start.6
  23.3 1.5 collective-permute-start.4
  24.8 1.5 collective-permute-start.9
  26.3 3.8 %collective-permute-done.6.refs_4_ = bf16[2,160,384]{2,1,0:T(8,128)(2,1)S(1)} collective-permute-done((bf16[2,160,384]{2,1,0:T(8,128)(2,1)S(1)}, bf16[2,160,384]{2,1,0:T(8,128)(2,1)S(1)}, u32[]{:S(2)}, u32[]{:S(2)}) %collective-permute-start.6) | collective-permute-done | bytes 245792 | tf_op jit(solution)/shard_map/ppermute | solution.py:31
  30.1 1.5 collective-permute-start.8
  33.4 2.6 copy.37
  36.0 4.7 %collective-permute-done.3 = bf16[48,1920]{1,0:T(8,128)(2,1)S(1)} collective-permute-done((bf16[48,1920]{1,0:T(8,128)(2,1)S(1)}, bf16[48,1920]{1,0:T(8,128)(2,1)S(1)}, u32[]{:S(2)}, u32[]{:S(2)}) %collective-permute-start.3) | collective-permute-done | bytes 184352 | tf_op jit(solution)/shard_map/ppermute | solution.py:31
  41.6 3.0 shard_map.306
  45.5 1.5 collective-permute-start.14
  47.1 5.8 %shard_map.307 = (bf16[1024,384]{1,0:T(8,128)(2,1)}, bf16[1024,384]{1,0:T(8,128)(2,1)}, bf16[1024,384]{1,0:T(8,128)(2,1)}) custom-call(s32[1]{0:T(128)} %bitcast.19.core_ref, bf16[1024,768]{1,0:T(8,128)(2,1)} %x_ref.5, bf16[3,768,384]{2,1,0:T(8,128)(2,1)} %get-tuple-element.188.w_ref.w0_ref, f32[16,768]{1,0:T(8,128)} %get-tuple-element.189.v_ref), custom_call_target="tpu_custom_call" | custom-call | flops 1 | bytes 1 | tf_op jit(solution)/shard_map/pallas_call | solution.py:413
  52.8 3.0 collective-permute-done.10.refs_1_
  57.1 5.8 %shard_map.308 = (bf16[1024,384]{1,0:T(8,128)(2,1)}, bf16[1024,384]{1,0:T(8,128)(2,1)}, bf16[1024,384]{1,0:T(8,128)(2,1)}) custom-call(s32[1]{0:T(128)} %bitcast.19.core_ref, bf16[1024,768]{1,0:T(8,128)(2,1)} %x_ref.5, bf16[3,768,384]{2,1,0:T(8,128)(2,1)} %copy-done, f32[16,768]{1,0:T(8,128)} %get-tuple-element.189.v_ref), custom_call_target="tpu_custom_call" | custom-call | flops 1 | bytes 1 | tf_op jit(solution)/shard_map/pallas_call | solution.py:413
  63.9 1.5 collective-permute-start.16
  66.7 1.8 collective-permute-start.17
  70.3 9.0 %shard_map.309 = (bf16[1024,384]{1,0:T(8,128)(2,1)}, f32[2,3,2,512]{3,2,1,0:T(2,128)}) custom-call(s32[2]{0:T(128)} %dynamic_slice.3.lens, bf16[1024,384]{1,0:T(8,128)(2,1)} %get-tuple-element.201.q_ref, bf16[1024,384]{1,0:T(8,128)(2,1)} %get-tuple-element.202.k_ref, bf16[1024,384]{1,0:T(8,128)(2,1)} %get-tuple-element.203.v_ref), custom_call_target="tpu_custom_call" | custom-call | flops 1 | bytes 1 | tf_op jit(solution)/shard_map/pallas_call | solution.py:705
  82.5 1.6 collective-permute-start.24
  84.1 9.0 %shard_map.310 = (bf16[1024,384]{1,0:T(8,128)(2,1)}, f32[2,3,2,512]{3,2,1,0:T(2,128)}) custom-call(s32[2]{0:T(128)} %dynamic_slice.3.lens, bf16[1024,384]{1,0:T(8,128)(2,1)} %get-tuple-element.216.q_ref, bf16[1024,384]{1,0:T(8,128)(2,1)} %get-tuple-element.217.k_ref, bf16[1024,384]{1,0:T(8,128)(2,1)} %get-tuple-element.218.v_ref), custom_call_target="tpu_custom_call" | custom-call | flops 1 | bytes 1 | tf_op jit(solution)/shard_map/pallas_call | solution.py:705
  93.9 3.6 %shard_map.311 = (bf16[768,384]{1,0:T(8,128)(2,1)}, bf16[768,1536]{1,0:T(8,128)(2,1)}) custom-call(s32[1]{0:T(128)} %bitcast.18.index_ref, bf16[2,48,1920]{2,1,0:T(8,128)(2,1)} %copy-done.20, bf16[2,48,1920]{2,1,0:T(8,128)(2,1)} %copy-done.33, bf16[2,48,1920]{2,1,0:T(8,128)(2,1)} %copy-done.34, bf16[2,48,1920]{2,1,0:T(8,128)(2,1)} %copy-done.36, ...), custom_call_target="tpu_custom_call" | custom-call | flops 1 | bytes 1 | tf_op jit(solution)/shard_map/pallas_call | solution.py:158
  101.8 7.1 %shard_map.312 = (f32[1024,768]{1,0:T(8,128)}, bf16[1024,768]{1,0:T(8,128)(2,1)}) custom-call(bf16[1024,768]{1,0:T(8,128)(2,1)} %x_ref.5, bf16[1024,384]{1,0:T(8,128)(2,1)} %get-tuple-element.208.c0_ref.c_ref, bf16[1024,384]{1,0:T(8,128)(2,1)} %get-tuple-element.220.c1_ref.c_ref, bf16[768,384]{1,0:T(8,128)(2,1)} %get-tuple-element.229.w0_ref, ...), custom_call_target="tpu_custom_call" | custom-call | flops 1 | bytes 1 | tf_op jit(solution)/shard_map/pallas_call | solution.py:501
  108.9 4.8 %collective-permute-done.22.refs_6_ = bf16[2,48,1536]{2,1,0:T(8,128)(2,1)} collective-permute-done((bf16[2,48,1536]{2,1,0:T(8,128)(2,1)}, bf16[2,48,1536]{2,1,0:T(8,128)(2,1)}, u32[]{:S(2)}, u32[]{:S(2)}) %collective-permute-start.22) | collective-permute-done | bytes 294944 | tf_op jit(solution)/shard_map/ppermute | solution.py:31
  114.1 6.8 %multiply_convert_fusion.3 = (bf16[1024,1536]{1,0:T(8,128)(2,1)}, f32[1024,1536]{1,0:T(8,128)}) fusion(f32[1536]{0:T(1024)S(1)} %get-tuple-element.340, bf16[1024,768]{1,0:T(8,128)(2,1)} %get-tuple-element.249.h_ref, bf16[768,1536]{1,0:T(8,128)(2,1)S(1)} %copy-done.10), kind=kOutput, calls=%fused_computation.16 | convolution fusion | flops 2425356288 | bytes 13375488 | tf_op jit(solution)/shard_map/dot_general | solution.py:21
  122.9 3.2 shard_map.313.w0_ref
  126.1 7.3 %multiply_convert_fusion.2 = (bf16[1024,1536]{1,0:T(8,128)(2,1)}, f32[1024,1536]{1,0:T(8,128)}) fusion(f32[1536]{0:T(1024)S(1)} %get-tuple-element.339, bf16[1024,768]{1,0:T(8,128)(2,1)S(1)} %copy-done.18, bf16[768,1536]{1,0:T(8,128)(2,1)} %collective-permute-done.27.w1_ref), kind=kOutput, calls=%fused_computation.14 | convolution fusion | flops 2425356288 | bytes 13375488 | tf_op jit(solution)/shard_map/dot_general | solution.py:21
  134.7 19.7 %shard_map.314 = (f32[1024,768]{1,0:T(8,128)}, f32[1024,768]{1,0:T(8,128)}, bf16[1024,768]{1,0:T(8,128)(2,1)}, f32[8,768]{1,0:T(8,128)}) custom-call(bf16[1024,768]{1,0:T(8,128)(2,1)} %get-tuple-element.249.h_ref, bf16[1024,768]{1,0:T(8,128)(2,1)} %c_ref.1, bf16[1024,1536]{1,0:T(8,128)(2,1)} %get-tuple-element.250.a0_ref, ...), custom_call_target="tpu_custom_call" | custom-call | flops 1 | bytes 1 | tf_op jit(solution)/shard_map/pallas_call | solution.py:501
  154.4 4.7 %convolution_convert_fusion.2 = bf16[768,1536]{1,0:T(8,128)(2,1)S(1)} fusion(bf16[1024,768]{1,0:T(8,128)(2,1)} %get-tuple-element.255, bf16[1024,1536]{1,0:T(8,128)(2,1)S(1)} %copy-done.7), kind=kOutput, calls=%fused_computation.20 | convolution fusion | flops 2417098752 | bytes 7077888 | tf_op jit(solution)/shard_map/dot_general | solution.py:21
  159.7 3.9 %convolution_convert_fusion.3.refs_0_ = bf16[768,1536]{1,0:T(8,128)(2,1)} fusion(bf16[1024,768]{1,0:T(8,128)(2,1)S(1)} %copy-done.59, bf16[1024,1536]{1,0:T(8,128)(2,1)S(1)} %copy-done.6), kind=kOutput, calls=%fused_computation.21 | convolution fusion | flops 2417098752 | bytes 7077888 | tf_op jit(solution)/shard_map/dot_general | solution.py:21
  163.9 5.4 %multiply_convert_fusion.d1_ref = bf16[1024,1536]{1,0:T(8,128)(2,1)S(1)} fusion(bf16[1024,768]{1,0:T(8,128)(2,1)S(1)} %copy-done.59, bf16[768,1536]{1,0:T(8,128)(2,1)S(1)} %copy-done.13, f32[1024,1536]{1,0:T(8,128)S(1)} %copy-done.66, f32[1536]{0:T(1024)S(1)} %get-tuple-element.339), kind=kOutput, calls=%fused_computation.12 | convolution fusion | flops 2436366336 | bytes 13375488 | tf_op jit(solution)/shard_map/dot_general | solution.py:21
  169.3 2.9 convolution_convert_fusion
  172.7 5.4 %multiply_convert_fusion.1.d0_ref = bf16[1024,1536]{1,0:T(8,128)(2,1)S(1)} fusion(bf16[1024,768]{1,0:T(8,128)(2,1)S(1)} %copy-done.59, bf16[768,1536]{1,0:T(8,128)(2,1)S(1)} %copy-done.1, f32[1024,1536]{1,0:T(8,128)S(1)} %bitcast.88, f32[1536]{0:T(1024)S(1)} %get-tuple-element.340), kind=kOutput, calls=%fused_computation.13 | convolution fusion | flops 2436366336 | bytes 13375488 | tf_op jit(solution)/shard_map/dot_general | solution.py:21
  178.1 4.0 %convolution_convert_fusion.1.refs_2_ = bf16[768,1536]{1,0:T(8,128)(2,1)} fusion(bf16[1024,768]{1,0:T(8,128)(2,1)S(1)} %copy-done.19, bf16[1024,1536]{1,0:T(8,128)(2,1)S(1)} %multiply_convert_fusion.1.d0_ref), kind=kOutput, calls=%fused_computation.19 | convolution fusion | flops 2417098752 | bytes 7077888 | tf_op jit(solution)/shard_map/dot_general | solution.py:21
  183.6 6.8 %shard_map.315 = (bf16[4,48,3072]{2,1,0:T(8,128)(2,1)}, bf16[4,48,3072]{2,1,0:T(8,128)(2,1)}, bf16[2,48,3072]{2,1,0:T(8,128)(2,1)}, bf16[2,48,3072]{2,1,0:T(8,128)(2,1)}, bf16[4,48,3072]{2,1,0:T(8,128)(2,1)}) custom-call(s32[1]{0:T(128)} %bitcast.18.index_ref, bf16[768,1536]{1,0:T(8,128)(2,1)} %convolution_convert_fusion.3.refs_0_, ...), custom_call_target="tpu_custom_call" | custom-call | flops 1 | bytes 1 | tf_op jit(solution)/shard_map/pallas_call | solution.py:221
  191.9 18.9 %shard_map.316 = (f32[1024,768]{1,0:T(8,128)}, bf16[1024,768]{1,0:T(8,128)(2,1)}, f32[8,768]{1,0:T(8,128)}, f32[8,3072]{1,0:T(8,128)}) custom-call(f32[1024,768]{1,0:T(8,128)} %get-tuple-element.253.s_ref, bf16[1024,1536]{1,0:T(8,128)(2,1)} %copy-done.5, bf16[1024,1536]{1,0:T(8,128)(2,1)} %copy-done.4, f32[1024,768]{1,0:T(8,128)} %get-tuple-element.265.f_ref, ...), custom_call_target="tpu_custom_call" | custom-call | flops 1 | bytes 1 | tf_op jit(solution)/shard_map/pallas_call | solution.py:501
  210.9 2.6 convolution_convert_fusion.6
  213.6 1.9 convolution_convert_fusion.7.refs_0_
  215.4 1.9 convolution_convert_fusion.4.d_ref
  218.1 2.1 shard_map.317
  221.6 2.7 shard_map.318
  225.3 1.6 collective-permute-start.37
  228.4 1.8 shard_map.319.table_ref
  230.2 12.0 %shard_map.320.d_ref.d1_ref = bf16[3,1024,384]{2,1,0:T(8,128)(2,1)} custom-call(s32[2]{0:T(128)} %dynamic_slice.3.lens, bf16[1024,384]{1,0:T(8,128)(2,1)} %get-tuple-element.216.q_ref, bf16[1024,384]{1,0:T(8,128)(2,1)} %get-tuple-element.217.k_ref, bf16[1024,384]{1,0:T(8,128)(2,1)} %get-tuple-element.218.v_ref, ...), custom_call_target="tpu_custom_call" | custom-call | flops 1 | bytes 1 | tf_op jit(solution)/shard_map/pallas_call | solution.py:705
  244.7 1.7 shard_map.321
  247.5 1.5 collective-permute-start.39
  249.0 3.6 %shard_map.322 = (f32[48,3072]{1,0:T(8,128)}, bf16[48,3072]{1,0:T(8,128)(2,1)}, bf16[48,3072]{1,0:T(8,128)(2,1)}, bf16[48,3072]{1,0:T(8,128)(2,1)}) custom-call(bf16[4,48,3072]{2,1,0:T(8,128)(2,1)} %get-tuple-element.261.own_ref, bf16[4,48,3072]{2,1,0:T(8,128)(2,1)} %copy-done.2, bf16[4,48,3072]{2,1,0:T(8,128)(2,1)} %copy-done.3, ...), custom_call_target="tpu_custom_call" | custom-call | flops 1 | bytes 1 | tf_op jit(solution)/shard_map/pallas_call | solution.py:349
  252.6 5.9 %shard_map.323 = (bf16[3,768,384]{2,1,0:T(8,128)(2,1)}, f32[3,8,384]{2,1,0:T(8,128)}) custom-call(bf16[768,1024]{1,0:T(8,128)(2,1)} %bitcast.68, bf16[3,1024,384]{2,1,0:T(8,128)(2,1)} %shard_map.320.d_ref.d1_ref), custom_call_target="tpu_custom_call" | custom-call | flops 1 | bytes 1 | tf_op jit(solution)/shard_map/pallas_call | solution.py:242
  263.6 3.3 convolution_convert_fusion.5.d_ref
  266.9 1.8 shard_map.324
  268.7 12.0 %shard_map.325.d_ref.d0_ref = bf16[3,1024,384]{2,1,0:T(8,128)(2,1)} custom-call(s32[2]{0:T(128)} %dynamic_slice.3.lens, bf16[1024,384]{1,0:T(8,128)(2,1)} %get-tuple-element.201.q_ref, bf16[1024,384]{1,0:T(8,128)(2,1)} %get-tuple-element.202.k_ref, bf16[1024,384]{1,0:T(8,128)(2,1)} %get-tuple-element.203.v_ref, ...), custom_call_target="tpu_custom_call" | custom-call | flops 1 | bytes 1 | tf_op jit(solution)/shard_map/pallas_call | solution.py:705
  282.0 7.5 %shard_map.326 = (bf16[4,160,384]{2,1,0:T(8,128)(2,1)}, bf16[4,160,384]{2,1,0:T(8,128)(2,1)}, bf16[2,160,384]{2,1,0:T(8,128)(2,1)}, bf16[2,160,384]{2,1,0:T(8,128)(2,1)}, bf16[4,160,384]{2,1,0:T(8,128)(2,1)}) custom-call(s32[2]{0:T(128)} %pad_add_fusion.at_ref, bf16[768,1024]{1,0:T(8,128)(2,1)} %bitcast.69, bf16[3,1024,384]{2,1,0:T(8,128)(2,1)} %shard_map.325.d_ref.d0_ref, ...), custom_call_target="tpu_custom_call" | custom-call | flops 1 | bytes 1 | tf_op jit(solution)/shard_map/pallas_call | solution.py:293
  289.6 2.4 collective-permute-start.48
  292.0 2.0 collective-permute-start.46
  295.6 6.3 %shard_map.327.f_ref = f32[1024,768]{1,0:T(8,128)} custom-call(f32[1024,768]{1,0:T(8,128)} %get-tuple-element.317.f_ref, bf16[3,1024,384]{2,1,0:T(8,128)(2,1)} %shard_map.325.d_ref.d0_ref, bf16[3,1024,384]{2,1,0:T(8,128)(2,1)} %shard_map.320.d_ref.d1_ref, bf16[3,768,384]{2,1,0:T(8,128)(2,1)} %get-tuple-element.188.w_ref.w0_ref, ...), custom_call_target="tpu_custom_call", output_to_operand_aliasing={{}: (0, {})} | custom-call | flops 1 | bytes 1 | tf_op jit(solution)/shard_map/pallas_call | solution.py:445
  301.9 4.2 %collective-permute-done.41.r1_ref.f1_ref = bf16[4,160,384]{2,1,0:T(8,128)(2,1)S(1)} collective-permute-done((bf16[4,160,384]{2,1,0:T(8,128)(2,1)}, bf16[4,160,384]{2,1,0:T(8,128)(2,1)S(1)}, u32[]{:S(2)}, u32[]{:S(2)}) %collective-permute-start.41) | collective-permute-done | bytes 491552 | tf_op jit(solution)/shard_map/ppermute | solution.py:31
  307.7 2.1 shard_map.328
  312.2 4.0 %collective-permute-done.49.r1_ref = bf16[2,160,384]{2,1,0:T(8,128)(2,1)S(1)} collective-permute-done((bf16[2,160,384]{2,1,0:T(8,128)(2,1)}, bf16[2,160,384]{2,1,0:T(8,128)(2,1)S(1)}, u32[]{:S(2)}, u32[]{:S(2)}) %collective-permute-start.49) | collective-permute-done | bytes 245792 | tf_op jit(solution)/shard_map/ppermute | solution.py:31
  318.0 2.4 shard_map.329
  320.7 2.6 collective-permute-start.52
  323.3 1.5 collective-permute-start.53
  325.4 6.3 %shard_map.330 = f32[1024,768]{1,0:T(8,128)} custom-call(f32[1024,768]{1,0:T(8,128)} %shard_map.327.f_ref, bf16[3,1024,384]{2,1,0:T(8,128)(2,1)} %shard_map.325.d_ref.d0_ref, bf16[3,1024,384]{2,1,0:T(8,128)(2,1)} %shard_map.320.d_ref.d1_ref, bf16[3,768,384]{2,1,0:T(8,128)(2,1)} %get-tuple-element.188.w_ref.w0_ref, ...), custom_call_target="tpu_custom_call", output_to_operand_aliasing={{}: (0, {})} | custom-call | flops 1 | bytes 1 | tf_op jit(solution)/shard_map/pallas_call | solution.py:445
  (242 shorter events, 54.2 us)
Async XLA Ops:
  3.4 6.6 %collective-permute-start.1 = (bf16[160,384]{1,0:T(8,128)(2,1)}, bf16[160,384]{1,0:T(8,128)(2,1)S(1)}, u32[]{:S(2)}, u32[]{:S(2)}) collective-permute-start(bf16[160,384]{1,0:T(8,128)(2,1)} %shard_map.305), channel_id=1, source_target_pairs={{0,8},{2,10},{4,12},{6,14},{8,0},{10,2},{12,4},{14,6},{16,24},{18,... | collective-permute-start | bytes 368648 | tf_op jit(solution)/shard_map/ppermute | solution.py:31
  6.5 9.6 %collective-permute-start.2 = (bf16[160,384]{1,0:T(8,128)(2,1)}, bf16[160,384]{1,0:T(8,128)(2,1)S(1)}, u32[]{:S(2)}, u32[]{:S(2)}) collective-permute-start(bf16[160,384]{1,0:T(8,128)(2,1)} %shard_map.305), channel_id=1, source_target_pairs={{0,24},{2,26},{4,28},{6,30},{8,16},{10,18},{12,20},{14,22},{16,8},... | collective-permute-start | bytes 368648 | tf_op jit(solution)/shard_map/ppermute | solution.py:31
  9.0 11.3 %collective-permute-start = (bf16[160,384]{1,0:T(8,128)(2,1)}, bf16[160,384]{1,0:T(8,128)(2,1)S(1)}, u32[]{:S(2)}, u32[]{:S(2)}) collective-permute-start(bf16[160,384]{1,0:T(8,128)(2,1)} %shard_map.305), channel_id=1, source_target_pairs={{0,16},{2,18},{4,20},{6,22},{8,24},{10,26},{12,28},{14,30},{16,0},... | collective-permute-start | bytes 368648 | tf_op jit(solution)/shard_map/ppermute | solution.py:31
  16.1 24.7 %copy-start.22 = (bf16[2,160,384]{2,1,0:T(8,128)(2,1)}, bf16[2,160,384]{2,1,0:T(8,128)(2,1)S(1)}, u32[]{:S(2)}) copy-start(bf16[2,160,384]{2,1,0:T(8,128)(2,1)S(1)} %pad_maximum_fusion.3.refs_1_) | copy-start | bytes 737284
  16.1 8.7 %collective-permute-start.5 = (bf16[2,160,384]{2,1,0:T(8,128)(2,1)S(1)}, bf16[2,160,384]{2,1,0:T(8,128)(2,1)S(1)}, u32[]{:S(2)}, u32[]{:S(2)}) collective-permute-start(bf16[2,160,384]{2,1,0:T(8,128)(2,1)S(1)} %pad_maximum_fusion.3.refs_1_), channel_id=1, source_target_pairs={{0,2},{2,0},{4,6},{6,4},{8,10},{10,8},{12,14},{14,12},{16,18},{18,... | collective-permute-start | bytes 737288 | tf_op jit(solution)/shard_map/ppermute | solution.py:31
  21.2 19.6 %copy-start.23 = (bf16[2,160,384]{2,1,0:T(8,128)(2,1)}, bf16[2,160,384]{2,1,0:T(8,128)(2,1)S(1)}, u32[]{:S(2)}) copy-start(bf16[2,160,384]{2,1,0:T(8,128)(2,1)S(1)} %pad_maximum_fusion.2.refs_0_) | copy-start | bytes 737284
  21.2 8.9 %collective-permute-start.6 = (bf16[2,160,384]{2,1,0:T(8,128)(2,1)S(1)}, bf16[2,160,384]{2,1,0:T(8,128)(2,1)S(1)}, u32[]{:S(2)}, u32[]{:S(2)}) collective-permute-start(bf16[2,160,384]{2,1,0:T(8,128)(2,1)S(1)} %pad_maximum_fusion.2.refs_0_), channel_id=1, source_target_pairs={{0,4},{2,6},{4,0},{6,2},{8,12},{10,14},{12,8},{14,10},{16,20},{18,... | collective-permute-start | bytes 737288 | tf_op jit(solution)/shard_map/ppermute | solution.py:31
  22.8 17.9 %collective-permute-start.7 = (bf16[2,160,384]{2,1,0:T(8,128)(2,1)S(1)}, bf16[2,160,384]{2,1,0:T(8,128)(2,1)S(1)}, u32[]{:S(2)}, u32[]{:S(2)}) collective-permute-start(bf16[2,160,384]{2,1,0:T(8,128)(2,1)S(1)} %pad_maximum_fusion.3.refs_1_), channel_id=1, source_target_pairs={{0,4},{2,6},{4,0},{6,2},{8,12},{10,14},{12,8},{14,10},{16,20},{18,... | collective-permute-start | bytes 737288 | tf_op jit(solution)/shard_map/ppermute | solution.py:31
  23.3 17.4 %collective-permute-start.4 = (bf16[2,160,384]{2,1,0:T(8,128)(2,1)S(1)}, bf16[2,160,384]{2,1,0:T(8,128)(2,1)S(1)}, u32[]{:S(2)}, u32[]{:S(2)}) collective-permute-start(bf16[2,160,384]{2,1,0:T(8,128)(2,1)S(1)} %pad_maximum_fusion.2.refs_0_), channel_id=1, source_target_pairs={{0,2},{2,0},{4,6},{6,4},{8,10},{10,8},{12,14},{14,12},{16,18},{18,... | collective-permute-start | bytes 737288 | tf_op jit(solution)/shard_map/ppermute | solution.py:31
  24.8 15.9 %collective-permute-start.9 = (bf16[2,160,384]{2,1,0:T(8,128)(2,1)S(1)}, bf16[2,160,384]{2,1,0:T(8,128)(2,1)S(1)}, u32[]{:S(2)}, u32[]{:S(2)}) collective-permute-start(bf16[2,160,384]{2,1,0:T(8,128)(2,1)S(1)} %collective-permute-done.5.refs_3_), channel_id=1, source_target_pairs={{0,4},{2,6},{4,0},{6,2},{8,12},{10,14},{12,8},{14,10},{16,20},{18,... | collective-permute-start | bytes 737288 | tf_op jit(solution)/shard_map/ppermute | solution.py:31
  30.1 10.6 %collective-permute-start.8 = (bf16[2,160,384]{2,1,0:T(8,128)(2,1)S(1)}, bf16[2,160,384]{2,1,0:T(8,128)(2,1)S(1)}, u32[]{:S(2)}, u32[]{:S(2)}) collective-permute-start(bf16[2,160,384]{2,1,0:T(8,128)(2,1)S(1)} %collective-permute-done.6.refs_4_), channel_id=1, source_target_pairs={{0,2},{2,0},{4,6},{6,4},{8,10},{10,8},{12,14},{14,12},{16,18},{18,... | collective-permute-start | bytes 737288 | tf_op jit(solution)/shard_map/ppermute | solution.py:31
  32.5 8.2 %collective-permute-start.3 = (bf16[48,1920]{1,0:T(8,128)(2,1)S(1)}, bf16[48,1920]{1,0:T(8,128)(2,1)S(1)}, u32[]{:S(2)}, u32[]{:S(2)}) collective-permute-start(bf16[48,1920]{1,0:T(8,128)(2,1)S(1)} %get-tuple-element.178), channel_id=1, source_target_pairs={{0,16},{2,18},{4,20},{6,22},{8,24},{10,26},{12,28},{14,30},{16,0},... | collective-permute-start | bytes 552968 | tf_op jit(solution)/shard_map/ppermute | solution.py:31
  44.7 11.1 %collective-permute-start.11 = (bf16[3,768,384]{2,1,0:T(8,128)(2,1)}, bf16[3,768,384]{2,1,0:T(8,128)(2,1)S(1)}, u32[]{:S(2)}, u32[]{:S(2)}) collective-permute-start(bf16[3,768,384]{2,1,0:T(8,128)(2,1)} %get-tuple-element.188.w_ref.w0_ref), channel_id=1, source_target_pairs={{0,1},{1,0},{2,3},{3,2},{4,5},{5,4},{6,7},{7,6},{8,9},{9,8},{10,11... | collective-permute-start | bytes 5308424 | tf_op jit(solution)/shard_map/ppermute | solution.py:35
  44.7 11.1 %collective-permute-start.10 = (bf16[2,48,1920]{2,1,0:T(8,128)(2,1)S(1)}, bf16[2,48,1920]{2,1,0:T(8,128)(2,1)S(1)}, u32[]{:S(2)}, u32[]{:S(2)}) collective-permute-start(bf16[2,48,1920]{2,1,0:T(8,128)(2,1)S(1)} %pad_maximum_fusion.refs_0_), channel_id=1, source_target_pairs={{0,8},{2,10},{4,12},{6,14},{8,0},{10,2},{12,4},{14,6},{16,24},{18,... | collective-permute-start | bytes 1105928 | tf_op jit(solution)/shard_map/ppermute | solution.py:31
  44.8 20.6 %collective-permute-start.13 = (bf16[2,48,1920]{2,1,0:T(8,128)(2,1)S(1)}, bf16[2,48,1920]{2,1,0:T(8,128)(2,1)S(1)}, u32[]{:S(2)}, u32[]{:S(2)}) collective-permute-start(bf16[2,48,1920]{2,1,0:T(8,128)(2,1)S(1)} %pad_maximum_fusion.refs_0_), channel_id=1, source_target_pairs={{0,2},{2,0},{4,6},{6,4},{8,10},{10,8},{12,14},{14,12},{16,18},{18,... | collective-permute-start | bytes 1105928 | tf_op jit(solution)/shard_map/ppermute | solution.py:31
  45.5 19.9 %collective-permute-start.14 = (bf16[2,48,1920]{2,1,0:T(8,128)(2,1)S(1)}, bf16[2,48,1920]{2,1,0:T(8,128)(2,1)S(1)}, u32[]{:S(2)}, u32[]{:S(2)}) collective-permute-start(bf16[2,48,1920]{2,1,0:T(8,128)(2,1)S(1)} %pad_maximum_fusion.refs_0_), channel_id=1, source_target_pairs={{0,4},{2,6},{4,0},{6,2},{8,12},{10,14},{12,8},{14,10},{16,20},{18,... | collective-permute-start | bytes 1105928 | tf_op jit(solution)/shard_map/ppermute | solution.py:31
  47.1 22.6 %copy-start.65 = (s32[4]{0:T(128)S(1)}, s32[4]{0:T(128)}, u32[]{:S(2)}) copy-start(s32[4]{0:T(128)} %param.20) | copy-start | bytes 52
  55.8 37.3 %copy-start.33 = (bf16[2,48,1920]{2,1,0:T(8,128)(2,1)}, bf16[2,48,1920]{2,1,0:T(8,128)(2,1)S(1)}, u32[]{:S(2)}) copy-start(bf16[2,48,1920]{2,1,0:T(8,128)(2,1)S(1)} %collective-permute-done.10.refs_1_) | copy-start | bytes 1105924
  55.8 9.8 %collective-permute-start.12 = (bf16[48,1536]{1,0:T(8,128)(2,1)}, bf16[48,1536]{1,0:T(8,128)(2,1)}, u32[]{:S(2)}, u32[]{:S(2)}) collective-permute-start(bf16[48,1536]{1,0:T(8,128)(2,1)} %bitcast.72), channel_id=1, source_target_pairs={{0,16},{2,18},{4,20},{6,22},{8,24},{10,26},{12,28},{14,30},{16,0},... | collective-permute-start | bytes 442376 | tf_op jit(solution)/shard_map/ppermute | solution.py:31
  62.8 16.4 %collective-permute-start.15 = (bf16[2,48,1920]{2,1,0:T(8,128)(2,1)S(1)}, bf16[2,48,1920]{2,1,0:T(8,128)(2,1)S(1)}, u32[]{:S(2)}, u32[]{:S(2)}) collective-permute-start(bf16[2,48,1920]{2,1,0:T(8,128)(2,1)S(1)} %collective-permute-done.10.refs_1_), channel_id=1, source_target_pairs={{0,2},{2,0},{4,6},{6,4},{8,10},{10,8},{12,14},{14,12},{16,18},{18,... | collective-permute-start | bytes 1105928 | tf_op jit(solution)/shard_map/ppermute | solution.py:31
  63.9 15.4 %collective-permute-start.16 = (bf16[2,48,1920]{2,1,0:T(8,128)(2,1)S(1)}, bf16[2,48,1920]{2,1,0:T(8,128)(2,1)S(1)}, u32[]{:S(2)}, u32[]{:S(2)}) collective-permute-start(bf16[2,48,1920]{2,1,0:T(8,128)(2,1)S(1)} %collective-permute-done.10.refs_1_), channel_id=1, source_target_pairs={{0,4},{2,6},{4,0},{6,2},{8,12},{10,14},{12,8},{14,10},{16,20},{18,... | collective-permute-start | bytes 1105928 | tf_op jit(solution)/shard_map/ppermute | solution.py:31
  65.5 27.7 %copy-start.34 = (bf16[2,48,1920]{2,1,0:T(8,128)(2,1)}, bf16[2,48,1920]{2,1,0:T(8,128)(2,1)S(1)}, u32[]{:S(2)}) copy-start(bf16[2,48,1920]{2,1,0:T(8,128)(2,1)S(1)} %collective-permute-done.13.refs_2_) | copy-start | bytes 1105924
  65.5 27.7 %copy-start.35 = (bf16[2,48,1920]{2,1,0:T(8,128)(2,1)}, bf16[2,48,1920]{2,1,0:T(8,128)(2,1)S(1)}, u32[]{:S(2)}) copy-start(bf16[2,48,1920]{2,1,0:T(8,128)(2,1)S(1)} %collective-permute-done.14.refs_4_) | copy-start | bytes 1105924
  66.7 30.8 %copy-start.21 = (bf16[2,48,1536]{2,1,0:T(8,128)(2,1)}, bf16[2,48,1536]{2,1,0:T(8,128)(2,1)S(1)}, u32[]{:S(2)}) copy-start(bf16[2,48,1536]{2,1,0:T(8,128)(2,1)S(1)} %pad_maximum_fusion.1.refs_0_) | copy-start | bytes 884740
  66.7 12.6 %collective-permute-start.17 = (bf16[2,48,1536]{2,1,0:T(8,128)(2,1)S(1)}, bf16[2,48,1536]{2,1,0:T(8,128)(2,1)S(1)}, u32[]{:S(2)}, u32[]{:S(2)}) collective-permute-start(bf16[2,48,1536]{2,1,0:T(8,128)(2,1)S(1)} %pad_maximum_fusion.1.refs_0_), channel_id=1, source_target_pairs={{0,8},{2,10},{4,12},{6,14},{8,0},{10,2},{12,4},{14,6},{16,24},{18,... | collective-permute-start | bytes 884744 | tf_op jit(solution)/shard_map/ppermute | solution.py:31
  68.6 11.5 %collective-permute-start.18 = (bf16[2,48,1536]{2,1,0:T(8,128)(2,1)S(1)}, bf16[2,48,1536]{2,1,0:T(8,128)(2,1)S(1)}, u32[]{:S(2)}, u32[]{:S(2)}) collective-permute-start(bf16[2,48,1536]{2,1,0:T(8,128)(2,1)S(1)} %pad_maximum_fusion.1.refs_0_), channel_id=1, source_target_pairs={{0,4},{2,6},{4,0},{6,2},{8,12},{10,14},{12,8},{14,10},{16,20},{18,... | collective-permute-start | bytes 884744 | tf_op jit(solution)/shard_map/ppermute | solution.py:31
  69.1 11.0 %collective-permute-start.19 = (bf16[2,48,1536]{2,1,0:T(8,128)(2,1)S(1)}, bf16[2,48,1536]{2,1,0:T(8,128)(2,1)S(1)}, u32[]{:S(2)}, u32[]{:S(2)}) collective-permute-start(bf16[2,48,1536]{2,1,0:T(8,128)(2,1)S(1)} %pad_maximum_fusion.1.refs_0_), channel_id=1, source_target_pairs={{0,2},{2,0},{4,6},{6,4},{8,10},{10,8},{12,14},{14,12},{16,18},{18,... | collective-permute-start | bytes 884744 | tf_op jit(solution)/shard_map/ppermute | solution.py:31
  81.5 11.5 %collective-permute-start.23 = (bf16[2,48,1920]{2,1,0:T(8,128)(2,1)S(1)}, bf16[2,48,1920]{2,1,0:T(8,128)(2,1)S(1)}, u32[]{:S(2)}, u32[]{:S(2)}) collective-permute-start(bf16[2,48,1920]{2,1,0:T(8,128)(2,1)S(1)} %collective-permute-done.14.refs_4_), channel_id=1, source_target_pairs={{0,2},{2,0},{4,6},{6,4},{8,10},{10,8},{12,14},{14,12},{16,18},{18,... | collective-permute-start | bytes 1105928 | tf_op jit(solution)/shard_map/ppermute | solution.py:31
  82.5 10.6 %collective-permute-start.24 = (bf16[2,48,1920]{2,1,0:T(8,128)(2,1)S(1)}, bf16[2,48,1920]{2,1,0:T(8,128)(2,1)S(1)}, u32[]{:S(2)}, u32[]{:S(2)}) collective-permute-start(bf16[2,48,1920]{2,1,0:T(8,128)(2,1)S(1)} %collective-permute-done.15.refs_3_), channel_id=1, source_target_pairs={{0,4},{2,6},{4,0},{6,2},{8,12},{10,14},{12,8},{14,10},{16,20},{18,... | collective-permute-start | bytes 1105928 | tf_op jit(solution)/shard_map/ppermute | solution.py:31
  97.6 3.4 %collective-permute-start.25 = (bf16[768,384]{1,0:T(8,128)(2,1)}, bf16[768,384]{1,0:T(8,128)(2,1)S(1)}, u32[]{:S(2)}, u32[]{:S(2)}) collective-permute-start(bf16[768,384]{1,0:T(8,128)(2,1)} %get-tuple-element.229.w0_ref), channel_id=1, source_target_pairs={{0,1},{1,0},{2,3},{3,2},{4,5},{5,4},{6,7},{7,6},{8,9},{9,8},{10,11... | collective-permute-start | bytes 1769480 | tf_op jit(solution)/shard_map/ppermute | solution.py:35
  97.6 11.3 %collective-permute-start.20 = (bf16[2,48,1536]{2,1,0:T(8,128)(2,1)}, bf16[2,48,1536]{2,1,0:T(8,128)(2,1)S(1)}, u32[]{:S(2)}, u32[]{:S(2)}) collective-permute-start(bf16[2,48,1536]{2,1,0:T(8,128)(2,1)} %copy-done.40), channel_id=1, source_target_pairs={{0,2},{2,0},{4,6},{6,4},{8,10},{10,8},{12,14},{14,12},{16,18},{18,... | collective-permute-start | bytes 884744 | tf_op jit(solution)/shard_map/ppermute | solution.py:31
  98.7 10.2 %collective-permute-start.21 = (bf16[2,48,1536]{2,1,0:T(8,128)(2,1)}, bf16[2,48,1536]{2,1,0:T(8,128)(2,1)S(1)}, u32[]{:S(2)}, u32[]{:S(2)}) collective-permute-start(bf16[2,48,1536]{2,1,0:T(8,128)(2,1)} %copy-done.40), channel_id=1, source_target_pairs={{0,4},{2,6},{4,0},{6,2},{8,12},{10,14},{12,8},{14,10},{16,20},{18,... | collective-permute-start | bytes 884744 | tf_op jit(solution)/shard_map/ppermute | solution.py:31
  99.2 14.4 %collective-permute-start.22 = (bf16[2,48,1536]{2,1,0:T(8,128)(2,1)}, bf16[2,48,1536]{2,1,0:T(8,128)(2,1)}, u32[]{:S(2)}, u32[]{:S(2)}) collective-permute-start(bf16[2,48,1536]{2,1,0:T(8,128)(2,1)} %copy-done.41), channel_id=1, source_target_pairs={{0,2},{2,0},{4,6},{6,4},{8,10},{10,8},{12,14},{14,12},{16,18},{18,... | collective-permute-start | bytes 884744 | tf_op jit(solution)/shard_map/ppermute | solution.py:31
  100.9 25.2 %collective-permute-start.27 = (bf16[768,1536]{1,0:T(8,128)(2,1)}, bf16[768,1536]{1,0:T(8,128)(2,1)}, u32[]{:S(2)}, u32[]{:S(2)}) collective-permute-start(bf16[768,1536]{1,0:T(8,128)(2,1)} %get-tuple-element.239.w0_ref), channel_id=1, source_target_pairs={{0,1},{1,0},{2,3},{3,2},{4,5},{5,4},{6,7},{7,6},{8,9},{9,8},{10,11... | collective-permute-start | bytes 7077896 | tf_op jit(solution)/shard_map/ppermute | solution.py:35
  113.7 8.5 %collective-permute-start.26 = (bf16[2,48,1536]{2,1,0:T(8,128)(2,1)S(1)}, bf16[2,48,1536]{2,1,0:T(8,128)(2,1)S(1)}, u32[]{:S(2)}, u32[]{:S(2)}) collective-permute-start(bf16[2,48,1536]{2,1,0:T(8,128)(2,1)S(1)} %collective-permute-done.20.refs_3_), channel_id=1, source_target_pairs={{0,4},{2,6},{4,0},{6,2},{8,12},{10,14},{12,8},{14,10},{16,20},{18,... | collective-permute-start | bytes 884744 | tf_op jit(solution)/shard_map/ppermute | solution.py:31
  126.1 7.3 %collective-permute-start.28 = (bf16[768,1536]{1,0:T(8,128)(2,1)}, bf16[768,1536]{1,0:T(8,128)(2,1)S(1)}, u32[]{:S(2)}, u32[]{:S(2)}) collective-permute-start(bf16[768,1536]{1,0:T(8,128)(2,1)} %shard_map.313.w0_ref), channel_id=1, source_target_pairs={{0,1},{1,0},{2,3},{3,2},{4,5},{5,4},{6,7},{7,6},{8,9},{9,8},{10,11... | collective-permute-start | bytes 7077896 | tf_op jit(solution)/shard_map/ppermute | solution.py:35
  134.7 19.7 %copy-start.7 = (bf16[1024,1536]{1,0:T(8,128)(2,1)S(1)}, bf16[1024,1536]{1,0:T(8,128)(2,1)}, u32[]{:S(2)}) copy-start(bf16[1024,1536]{1,0:T(8,128)(2,1)} %get-tuple-element.358.a1_ref) | copy-start | bytes 9437188
  159.1 4.7 %collective-permute-start.29 = (bf16[768,1536]{1,0:T(8,128)(2,1)S(1)}, bf16[768,1536]{1,0:T(8,128)(2,1)S(1)}, u32[]{:S(2)}, u32[]{:S(2)}) collective-permute-start(bf16[768,1536]{1,0:T(8,128)(2,1)S(1)} %convolution_convert_fusion.2), channel_id=1, source_target_pairs={{0,1},{1,0},{2,3},{3,2},{4,5},{5,4},{6,7},{7,6},{8,9},{9,8},{10,11... | collective-permute-start | bytes 7077896 | tf_op jit(solution)/shard_map/ppermute | solution.py:35
  172.3 9.8 %collective-permute-start.30 = (bf16[768,1536]{1,0:T(8,128)(2,1)S(1)}, bf16[768,1536]{1,0:T(8,128)(2,1)S(1)}, u32[]{:S(2)}, u32[]{:S(2)}) collective-permute-start(bf16[768,1536]{1,0:T(8,128)(2,1)S(1)} %convolution_convert_fusion), channel_id=1, source_target_pairs={{0,1},{1,0},{2,3},{3,2},{4,5},{5,4},{6,7},{7,6},{8,9},{9,8},{10,11... | collective-permute-start | bytes 7077896 | tf_op jit(solution)/shard_map/ppermute | solution.py:35
  190.4 29.9 %collective-permute-start.34 = (bf16[4,48,3072]{2,1,0:T(8,128)(2,1)}, bf16[4,48,3072]{2,1,0:T(8,128)(2,1)S(1)}, u32[]{:S(2)}, u32[]{:S(2)}) collective-permute-start(bf16[4,48,3072]{2,1,0:T(8,128)(2,1)} %get-tuple-element.272), channel_id=1, source_target_pairs={{0,2},{2,0},{4,6},{6,4},{8,10},{10,8},{12,14},{14,12},{16,18},{18,... | collective-permute-start | bytes 3538952 | tf_op jit(solution)/shard_map/ppermute | solution.py:31
  191.4 28.9 %collective-permute-start.35 = (bf16[4,48,3072]{2,1,0:T(8,128)(2,1)}, bf16[4,48,3072]{2,1,0:T(8,128)(2,1)S(1)}, u32[]{:S(2)}, u32[]{:S(2)}) collective-permute-start(bf16[4,48,3072]{2,1,0:T(8,128)(2,1)} %get-tuple-element.273), channel_id=1, source_target_pairs={{0,4},{2,6},{4,0},{6,2},{8,12},{10,14},{12,8},{14,10},{16,20},{18,... | collective-permute-start | bytes 3538952 | tf_op jit(solution)/shard_map/ppermute | solution.py:31
  213.5 3.8 %collective-permute-start.31 = (bf16[768,384]{1,0:T(8,128)(2,1)S(1)}, bf16[768,384]{1,0:T(8,128)(2,1)S(1)}, u32[]{:S(2)}, u32[]{:S(2)}) collective-permute-start(bf16[768,384]{1,0:T(8,128)(2,1)S(1)} %convolution_convert_fusion.6), channel_id=1, source_target_pairs={{0,1},{1,0},{2,3},{3,2},{4,5},{5,4},{6,7},{7,6},{8,9},{9,8},{10,11... | collective-permute-start | bytes 1769480 | tf_op jit(solution)/shard_map/ppermute | solution.py:35
  224.3 19.7 %collective-permute-start.36 = (bf16[2,48,3072]{2,1,0:T(8,128)(2,1)}, bf16[2,48,3072]{2,1,0:T(8,128)(2,1)S(1)}, u32[]{:S(2)}, u32[]{:S(2)}) collective-permute-start(bf16[2,48,3072]{2,1,0:T(8,128)(2,1)} %get-tuple-element.276), channel_id=1, source_target_pairs={{0,2},{2,0},{4,6},{6,4},{8,10},{10,8},{12,14},{14,12},{16,18},{18,... | collective-permute-start | bytes 1769480 | tf_op jit(solution)/shard_map/ppermute | solution.py:31
  225.3 18.8 %collective-permute-start.37 = (bf16[2,48,3072]{2,1,0:T(8,128)(2,1)}, bf16[2,48,3072]{2,1,0:T(8,128)(2,1)S(1)}, u32[]{:S(2)}, u32[]{:S(2)}) collective-permute-start(bf16[2,48,3072]{2,1,0:T(8,128)(2,1)} %get-tuple-element.277), channel_id=1, source_target_pairs={{0,4},{2,6},{4,0},{6,2},{8,12},{10,14},{12,8},{14,10},{16,20},{18,... | collective-permute-start | bytes 1769480 | tf_op jit(solution)/shard_map/ppermute | solution.py:31
  226.9 16.6 %collective-permute-start.32 = (bf16[4,48,384]{2,1,0:T(8,128)(2,1)S(1)}, bf16[4,48,384]{2,1,0:T(8,128)(2,1)S(1)}, u32[]{:S(2)}, u32[]{:S(2)}) collective-permute-start(bf16[4,48,384]{2,1,0:T(8,128)(2,1)S(1)} %copy-done.61), channel_id=1, source_target_pairs={{0,2},{2,0},{4,6},{6,4},{8,10},{10,8},{12,14},{14,12},{16,18},{18,... | collective-permute-start | bytes 442376 | tf_op jit(solution)/shard_map/ppermute | solution.py:31
  227.9 16.2 %collective-permute-start.33 = (bf16[4,48,384]{2,1,0:T(8,128)(2,1)S(1)}, bf16[4,48,384]{2,1,0:T(8,128)(2,1)S(1)}, u32[]{:S(2)}, u32[]{:S(2)}) collective-permute-start(bf16[4,48,384]{2,1,0:T(8,128)(2,1)S(1)} %copy-done.60), channel_id=1, source_target_pairs={{0,4},{2,6},{4,0},{6,2},{8,12},{10,14},{12,8},{14,10},{16,20},{18,... | collective-permute-start | bytes 442376 | tf_op jit(solution)/shard_map/ppermute | solution.py:31
  246.4 12.1 %collective-permute-start.38 = (bf16[2,48,384]{2,1,0:T(8,128)(2,1)}, bf16[2,48,384]{2,1,0:T(8,128)(2,1)S(1)}, u32[]{:S(2)}, u32[]{:S(2)}) collective-permute-start(bf16[2,48,384]{2,1,0:T(8,128)(2,1)} %get-tuple-element.288), channel_id=1, source_target_pairs={{0,2},{2,0},{4,6},{6,4},{8,10},{10,8},{12,14},{14,12},{16,18},{18,... | collective-permute-start | bytes 221192 | tf_op jit(solution)/shard_map/ppermute | solution.py:31
  247.5 11.0 %collective-permute-start.39 = (bf16[2,48,384]{2,1,0:T(8,128)(2,1)}, bf16[2,48,384]{2,1,0:T(8,128)(2,1)S(1)}, u32[]{:S(2)}, u32[]{:S(2)}) collective-permute-start(bf16[2,48,384]{2,1,0:T(8,128)(2,1)} %get-tuple-element.289), channel_id=1, source_target_pairs={{0,4},{2,6},{4,0},{6,2},{8,12},{10,14},{12,8},{14,10},{16,20},{18,... | collective-permute-start | bytes 221192 | tf_op jit(solution)/shard_map/ppermute | solution.py:31
  258.5 22.2 %collective-permute-start.40 = (bf16[3,768,384]{2,1,0:T(8,128)(2,1)}, bf16[3,768,384]{2,1,0:T(8,128)(2,1)S(1)}, u32[]{:S(2)}, u32[]{:S(2)}) collective-permute-start(bf16[3,768,384]{2,1,0:T(8,128)(2,1)} %get-tuple-element.301), channel_id=1, source_target_pairs={{0,1},{1,0},{2,3},{3,2},{4,5},{5,4},{6,7},{7,6},{8,9},{9,8},{10,11... | collective-permute-start | bytes 5308424 | tf_op jit(solution)/shard_map/ppermute | solution.py:35
  259.2 30.3 %collective-permute-start.43 = (bf16[48,3072]{1,0:T(8,128)(2,1)}, bf16[48,3072]{1,0:T(8,128)(2,1)S(1)}, u32[]{:S(2)}, u32[]{:S(2)}) collective-permute-start(bf16[48,3072]{1,0:T(8,128)(2,1)} %get-tuple-element.306), channel_id=1, source_target_pairs={{0,8},{2,10},{4,12},{6,14},{8,0},{10,2},{12,4},{14,6},{16,24},{18,... | collective-permute-start | bytes 884744 | tf_op jit(solution)/shard_map/ppermute | solution.py:31
  260.7 28.9 %collective-permute-start.44 = (bf16[48,3072]{1,0:T(8,128)(2,1)}, bf16[48,3072]{1,0:T(8,128)(2,1)S(1)}, u32[]{:S(2)}, u32[]{:S(2)}) collective-permute-start(bf16[48,3072]{1,0:T(8,128)(2,1)} %get-tuple-element.307), channel_id=1, source_target_pairs={{0,16},{2,18},{4,20},{6,22},{8,24},{10,26},{12,28},{14,30},{16,0},... | collective-permute-start | bytes 884744 | tf_op jit(solution)/shard_map/ppermute | solution.py:31
  262.1 27.4 %collective-permute-start.45 = (bf16[48,3072]{1,0:T(8,128)(2,1)}, bf16[48,3072]{1,0:T(8,128)(2,1)S(1)}, u32[]{:S(2)}, u32[]{:S(2)}) collective-permute-start(bf16[48,3072]{1,0:T(8,128)(2,1)} %get-tuple-element.308), channel_id=1, source_target_pairs={{0,24},{2,26},{4,28},{6,30},{8,16},{10,18},{12,20},{14,22},{16,8},... | collective-permute-start | bytes 884744 | tf_op jit(solution)/shard_map/ppermute | solution.py:31
  289.6 12.4 %collective-permute-start.48 = (bf16[48,384]{1,0:T(8,128)(2,1)S(1)}, bf16[48,384]{1,0:T(8,128)(2,1)S(1)}, u32[]{:S(2)}, u32[]{:S(2)}) collective-permute-start(bf16[48,384]{1,0:T(8,128)(2,1)S(1)} %copy-done.64), channel_id=1, source_target_pairs={{0,24},{2,26},{4,28},{6,30},{8,16},{10,18},{12,20},{14,22},{16,8},... | collective-permute-start | bytes 110600 | tf_op jit(solution)/shard_map/ppermute | solution.py:31
  292.0 9.9 %collective-permute-start.47 = (bf16[48,384]{1,0:T(8,128)(2,1)S(1)}, bf16[48,384]{1,0:T(8,128)(2,1)S(1)}, u32[]{:S(2)}, u32[]{:S(2)}) collective-permute-start(bf16[48,384]{1,0:T(8,128)(2,1)S(1)} %copy-done.63), channel_id=1, source_target_pairs={{0,16},{2,18},{4,20},{6,22},{8,24},{10,26},{12,28},{14,30},{16,0},... | collective-permute-start | bytes 110600 | tf_op jit(solution)/shard_map/ppermute | solution.py:31
  292.0 9.9 %collective-permute-start.46 = (bf16[48,384]{1,0:T(8,128)(2,1)S(1)}, bf16[48,384]{1,0:T(8,128)(2,1)S(1)}, u32[]{:S(2)}, u32[]{:S(2)}) collective-permute-start(bf16[48,384]{1,0:T(8,128)(2,1)S(1)} %copy-done.62), channel_id=1, source_target_pairs={{0,8},{2,10},{4,12},{6,14},{8,0},{10,2},{12,4},{14,6},{16,24},{18,... | collective-permute-start | bytes 110600 | tf_op jit(solution)/shard_map/ppermute | solution.py:31
  294.0 12.2 %collective-permute-start.41 = (bf16[4,160,384]{2,1,0:T(8,128)(2,1)}, bf16[4,160,384]{2,1,0:T(8,128)(2,1)S(1)}, u32[]{:S(2)}, u32[]{:S(2)}) collective-permute-start(bf16[4,160,384]{2,1,0:T(8,128)(2,1)} %get-tuple-element.303), channel_id=1, source_target_pairs={{0,2},{2,0},{4,6},{6,4},{8,10},{10,8},{12,14},{14,12},{16,18},{18,... | collective-permute-start | bytes 1474568 | tf_op jit(solution)/shard_map/ppermute | solution.py:31
  295.0 11.9 %collective-permute-start.42 = (bf16[4,160,384]{2,1,0:T(8,128)(2,1)}, bf16[4,160,384]{2,1,0:T(8,128)(2,1)S(1)}, u32[]{:S(2)}, u32[]{:S(2)}) collective-permute-start(bf16[4,160,384]{2,1,0:T(8,128)(2,1)} %get-tuple-element.304), channel_id=1, source_target_pairs={{0,4},{2,6},{4,0},{6,2},{8,12},{10,14},{12,8},{14,10},{16,20},{18,... | collective-permute-start | bytes 1474568 | tf_op jit(solution)/shard_map/ppermute | solution.py:31
  301.9 22.8 %copy-start.57 = (f32[48,384]{1,0:T(8,128)S(1)}, f32[48,384]{1,0:T(8,128)}, u32[]{:S(2)}) copy-start(f32[48,384]{1,0:T(8,128)} %get-tuple-element.298) | copy-start | bytes 221188
  309.8 6.4 %collective-permute-start.49 = (bf16[2,160,384]{2,1,0:T(8,128)(2,1)}, bf16[2,160,384]{2,1,0:T(8,128)(2,1)S(1)}, u32[]{:S(2)}, u32[]{:S(2)}) collective-permute-start(bf16[2,160,384]{2,1,0:T(8,128)(2,1)} %get-tuple-element.325), channel_id=1, source_target_pairs={{0,2},{2,0},{4,6},{6,4},{8,10},{10,8},{12,14},{14,12},{16,18},{18,... | collective-permute-start | bytes 737288 | tf_op jit(solution)/shard_map/ppermute | solution.py:31
  310.8 6.4 %collective-permute-start.50 = (bf16[2,160,384]{2,1,0:T(8,128)(2,1)}, bf16[2,160,384]{2,1,0:T(8,128)(2,1)S(1)}, u32[]{:S(2)}, u32[]{:S(2)}) collective-permute-start(bf16[2,160,384]{2,1,0:T(8,128)(2,1)} %get-tuple-element.326), channel_id=1, source_target_pairs={{0,4},{2,6},{4,0},{6,2},{8,12},{10,14},{12,8},{14,10},{16,20},{18,... | collective-permute-start | bytes 737288 | tf_op jit(solution)/shard_map/ppermute | solution.py:31
  320.4 11.4 %collective-permute-start.51 = (bf16[160,384]{1,0:T(8,128)(2,1)}, bf16[160,384]{1,0:T(8,128)(2,1)S(1)}, u32[]{:S(2)}, u32[]{:S(2)}) collective-permute-start(bf16[160,384]{1,0:T(8,128)(2,1)} %get-tuple-element.330), channel_id=1, source_target_pairs={{0,8},{2,10},{4,12},{6,14},{8,0},{10,2},{12,4},{14,6},{16,24},{18,... | collective-permute-start | bytes 368648 | tf_op jit(solution)/shard_map/ppermute | solution.py:31
  320.7 11.0 %collective-permute-start.52 = (bf16[160,384]{1,0:T(8,128)(2,1)}, bf16[160,384]{1,0:T(8,128)(2,1)S(1)}, u32[]{:S(2)}, u32[]{:S(2)}) collective-permute-start(bf16[160,384]{1,0:T(8,128)(2,1)} %get-tuple-element.331), channel_id=1, source_target_pairs={{0,16},{2,18},{4,20},{6,22},{8,24},{10,26},{12,28},{14,30},{16,0},... | collective-permute-start | bytes 368648 | tf_op jit(solution)/shard_map/ppermute | solution.py:31
  323.3 8.5 %collective-permute-start.53 = (bf16[160,384]{1,0:T(8,128)(2,1)}, bf16[160,384]{1,0:T(8,128)(2,1)S(1)}, u32[]{:S(2)}, u32[]{:S(2)}) collective-permute-start(bf16[160,384]{1,0:T(8,128)(2,1)} %get-tuple-element.332), channel_id=1, source_target_pairs={{0,24},{2,26},{4,28},{6,30},{8,16},{10,18},{12,20},{14,22},{16,8},... | collective-permute-start | bytes 368648 | tf_op jit(solution)/shard_map/ppermute | solution.py:31
  331.9 1.3 collective-permute-start.54
  (60 other events, 327.2 us)

commit v2 on v1

--- a/solution.py
+++ b/solution.py
@@ -72,7 +72,7 @@
     return buf
 
 
-BLOCK = 256
+BLOCK = 512
 PART = 128
 HINT = pl.CostEstimate(flops=1, transcendentals=0, bytes_accessed=1)
 
@@ -255,13 +255,15 @@
     )(tokens_t, deltas)
 
 
-def gradients_own(tokens_t, deltas, others, other_sums, table, index, core, size, one):
+def gradients_own(
+    tokens_t, deltas, others, other_sums, ready, table, index, core, size, one
+):
     width, rows = tokens_t.shape
     count, _, cols = deltas.shape
     part_rows = width // size
-    height = count * part_rows + 16
-
-    def kernel(at_ref, t_ref, d_ref, other_ref, sums_ref, table_ref, *refs):
+    height = (count + 1) * part_rows + 16
+
+    def kernel(at_ref, t_ref, d_ref, other_ref, sums_ref, r0_ref, r1_ref, table_ref, *refs):
         outs, total, own_sums, vec = refs[: len(PARTS)], refs[-3], refs[-2], refs[-1]
         g = pl.program_id(0)
         total[...] = dot(t_ref[...], d_ref[0], NN) + other_ref[0].astype(f32)
@@ -288,7 +290,10 @@
                     for j in range(size // 2):
                         vec[first + j, row : row + 1, :one] = ref[which, 0:1, j * one : (j + 1) * one]
             for block, out_ref, at in blocks():
-                out_ref[at, count * part_rows :, :] = vec[block].astype(bf16)
+                here = pl.ds(pl.multiple_of(block * part_rows, 16), part_rows)
+                value = r0_ref[here, :] + r1_ref[here, :]
+                out_ref[at, count * part_rows : (count + 1) * part_rows, :] = value
+                out_ref[at, (count + 1) * part_rows :, :] = vec[block].astype(bf16)
 
     return pl.pallas_call(
         kernel,
@@ -301,6 +306,7 @@
                 pl.BlockSpec((1, rows, cols), lambda g, *_: (g, 0, 0)),
                 pl.BlockSpec((1, width, cols), lambda g, *_: (g, 0, 0)),
                 vmem(other_sums.shape),
+                *[vmem(a.shape) for a in ready],
                 vmem(table.shape),
             ],
             out_specs=[vmem(shape.shape) for shape in split_shapes(height, cols)],
@@ -311,7 +317,7 @@
             ],
         ),
         cost_estimate=HINT,
-    )(jnp.stack([index, core]), tokens_t, deltas, others, other_sums, table)
+    )(jnp.stack([index, core]), tokens_t, deltas, others, other_sums, *ready, table)
 
 
 def pack_table(first_sums, second_sums, inner_sums, core, size, cols):
@@ -430,7 +436,7 @@
 def token_gradient(first_delta, deltas, weights, part, parts):
     count, rows, cols = deltas[0].shape
     width = weights[0].shape[1]
-    steps = rows // ROWS // parts
+    steps = rows // BLOCK // parts
 
     def kernel(f_ref, d0_ref, d1_ref, w0_ref, w1_ref, *refs):
         o_ref = refs[-1]
@@ -440,8 +446,8 @@
                 total = total + dot(d_ref[g], w_ref[g], NT)
         o_ref[...] = total
 
-    tile = pl.BlockSpec((ROWS, width), lambda i: (i + part * steps, 0))
-    delta_part = pl.BlockSpec((count, ROWS, cols), lambda i: (0, i + part * steps, 0))
+    tile = pl.BlockSpec((BLOCK, width), lambda i: (i + part * steps, 0))
+    delta_part = pl.BlockSpec((count, BLOCK, cols), lambda i: (0, i + part * steps, 0))
     return pl.pallas_call(
         kernel,
         out_shape=jax.ShapeDtypeStruct((rows, width), f32),
@@ -449,7 +455,11 @@
         in_specs=[tile, delta_part, delta_part] + [vmem(weights[0].shape)] * 2,
         out_specs=tile,
         input_output_aliases={0: 0},
-        cost_estimate=HINT,
+        cost_estimate=pl.CostEstimate(
+            flops=4 * count * rows * width * cols // parts,
+            transcendentals=0,
+            bytes_accessed=16 * rows * cols // parts,
+        ),
     )(first_delta, *deltas, *weights)
 
 
@@ -482,14 +492,13 @@
             ref[...] = jnp.zeros(ref.shape, f32)
 
 
-def in_turns(product, finish):
-    parts = [slice(i, i + PART) for i in range(0, BLOCK, PART)]
-    ahead = product(parts[0])
-    for n, part in enumerate(parts):
-        now = ahead
-        if n + 1 < len(parts):
-            ahead = product(parts[n + 1])
-        finish(part, now)
+def in_parts(total, finish):
+    def body(i, carry):
+        at = pl.ds(pl.multiple_of(i * PART, PART), PART)
+        finish(at, total[at, :])
+        return carry
+
+    lax.fori_loop(0, BLOCK // PART, body, 0)
 
 
 def row_call(kernel, tiles, wholes, outs, sums):
@@ -505,21 +514,21 @@
         grid=(rows // BLOCK,),
         in_specs=[tile(a.shape[1]) for a in tiles] + [vmem(a.shape) for a in wholes],
         out_specs=[tile(n) for n, _ in outs] + [vmem((8, n)) for n in sums],
+        scratch_shapes=[pltpu.VMEM((BLOCK, outs[0][0]), f32)],
         cost_estimate=HINT,
     )(*tiles, *wholes)
 
 
 def first_block(tokens, context, weights, vectors):
-    def kernel(x_ref, c0_ref, c1_ref, w0_ref, w1_ref, v_ref, out, low):
-        def product(at):
-            return dot(c0_ref[at], w0_ref[...], NT) + dot(c1_ref[at], w1_ref[...], NT)
+    def kernel(x_ref, c0_ref, c1_ref, w0_ref, w1_ref, v_ref, out, low, products):
+        products[...] = dot(c0_ref[...], w0_ref[...], NT) + dot(c1_ref[...], w1_ref[...], NT)
 
         def finish(at, total):
-            total = x_ref[at].astype(f32) + total + v_ref[2:3]
-            out[at] = total
-            low[at] = (center(total)[0] * v_ref[3:4] + v_ref[4:5]).astype(bf16)
-
-        in_turns(product, finish)
+            total = x_ref[at, :].astype(f32) + total + v_ref[2:3]
+            out[at, :] = total
+            low[at, :] = (center(total)[0] * v_ref[3:4] + v_ref[4:5]).astype(bf16)
+
+        in_parts(products, finish)
 
     width = tokens.shape[1]
     return row_call(
@@ -528,22 +537,23 @@
 
 
 def outer_block(hidden, cotangent, act, weights, vectors):
-    def kernel(h_ref, c_ref, a0_ref, a1_ref, w0_ref, w1_ref, v_ref, out, delta, low, sums):
+    def kernel(
+        h_ref, c_ref, a0_ref, a1_ref, w0_ref, w1_ref, v_ref, out, delta, low, sums, products
+    ):
         clear(sums)
 
-        def product(at):
-            return dot(a0_ref[at], w0_ref[...], NT) + dot(a1_ref[at], w1_ref[...], NT)
+        products[...] = dot(a0_ref[...], w0_ref[...], NT) + dot(a1_ref[...], w1_ref[...], NT)
 
         def finish(at, feed):
-            normed, rinv = center(h_ref[at].astype(f32) + (v_ref[5:6] + feed))
-            out[at] = normed * v_ref[6:7] + v_ref[7:8]
-            cot = c_ref[at].astype(f32)
+            normed, rinv = center(h_ref[at, :].astype(f32) + (v_ref[5:6] + feed))
+            out[at, :] = normed * v_ref[6:7] + v_ref[7:8]
+            cot = c_ref[at, :].astype(f32)
             found = norm_back(cot, normed, rinv, v_ref[6:7])
-            delta[at] = found
-            low[at] = found.astype(bf16)
+            delta[at, :] = found
+            low[at, :] = found.astype(bf16)
             add_rows(sums, (found, cot * normed, cot))
 
-        in_turns(product, finish)
+        in_parts(products, finish)
 
     width = hidden.shape[1]
     return row_call(
@@ -556,25 +566,26 @@
 
 
 def inner_back(second_delta, inner_delta, first_in, weights, vectors):
-    def kernel(s_ref, d0_ref, d1_ref, f_ref, w0_ref, w1_ref, v_ref, delta, low, sums, inner):
+    def kernel(
+        s_ref, d0_ref, d1_ref, f_ref, w0_ref, w1_ref, v_ref, delta, low, sums, inner, products
+    ):
         clear(sums, inner)
         ones = jnp.ones((8, BLOCK), bf16)
         half = d0_ref.shape[1]
         inner[:, :half] += dot(ones, d0_ref[...], NN)
         inner[:, half:] += dot(ones, d1_ref[...], NN)
 
-        def product(at):
-            return dot(d0_ref[at], w0_ref[...], NT) + dot(d1_ref[at], w1_ref[...], NT)
+        products[...] = dot(d0_ref[...], w0_ref[...], NT) + dot(d1_ref[...], w1_ref[...], NT)
 
         def finish(at, grad):
-            grad = s_ref[at] + grad
-            normed, rinv = center(f_ref[at])
+            grad = s_ref[at, :] + grad
+            normed, rinv = center(f_ref[at, :])
             found = norm_back(grad, normed, rinv, v_ref[3:4])
-            delta[at] = found
-            low[at] = found.astype(bf16)
+            delta[at, :] = found
+            low[at, :] = found.astype(bf16)
             add_rows(sums, (found, grad * normed, grad))
 
-        in_turns(product, finish)
+        in_parts(products, finish)
 
     width = first_in.shape[1]
     return row_call(
@@ -879,7 +890,7 @@
     first_delta, branch_delta, first_sums, inner_sums = inner_back(
         second_delta, inner_delta, first_in, wi, vecs
     )
-    go = product(branch_delta, ctx)
+    go = list(product(branch_delta, ctx))
     ctx_delta = [dot(branch_delta, wo[t], NN).astype(bf16) for t in range(2)]
 
     def joined(pair):
@@ -889,10 +900,8 @@
 
     if fast:
         table = pack_table(first_sums, second_sums, inner_sums, core, size, half)
-        parts_i = split_cols([go], index, size, step)
-        first_i = corner_back(parts_i, size)
-        *first_u, ctx_delta[1], _ = lax.optimization_barrier(
-            (*first_u, ctx_delta[1], parts_i[4])
+        *first_u, ctx_delta[1], go[0], go[1] = lax.optimization_barrier(
+            (*first_u, ctx_delta[1], *go)
         )
         sums_u = corner_add(parts_u, first_u)
         got_u = near_back(sums_u, size)
@@ -910,24 +919,20 @@
     deltas = [None, None]
     deltas[1] = attend_back(1)
     if fast:
-        arrived = lax.optimization_barrier((*first_i, *got_u, deltas[1]))
-        first_i, got_u, deltas[1] = arrived[:2], arrived[2:4], arrived[4]
+        *got_u, deltas[1] = lax.optimization_barrier((*got_u, deltas[1]))
         last_u = near_add(parts_u[4], first_u, got_u)
         got_u = far_back(last_u, size)
-        sums_i = corner_add(parts_i, first_i)
-        got_i = near_back(sums_i, size)
-        deltas[1] = after(deltas[1], last_u[0], sums_i[0])
+        deltas[1] = after(deltas[1], last_u[0])
         others, other_sums = gradients_other(tokens_t, deltas[1])
-        *got_i, others = lax.optimization_barrier((*got_i, others))
-        last_i = near_add(parts_i[4], first_i, got_i)
+        ctx_delta[0] = after(ctx_delta[0], others)
         others = swap_core(others)
-        ctx_delta[0] = after(ctx_delta[0], last_i[0])
         deltas[0] = attend_back(0)
         parts_q = gradients_own(
             tokens_t,
             deltas[0],
             others,
             other_sums,
+            go,
             table,
             index,
             core,
@@ -940,9 +945,7 @@
         token_grad = token_gradient(
             after(first_delta, parts_q[4]), [after(d, parts_q[4]) for d in deltas], wqkv, 0, 2
         )
-        got_i = far_back([after(item, parts_q[4]) for item in last_i], size)
-        arrived = lax.optimization_barrier((*first_q, *got_i, token_grad))
-        first_q, got_i, token_grad = arrived[:2], arrived[2:5], arrived[5]
+        *first_q, token_grad = lax.optimization_barrier((*first_q, token_grad))
 
         def total(last, got):
             return last[0] + got[0].astype(f32) + got[1].astype(f32) + got[2].astype(f32)
@@ -951,7 +954,6 @@
         hidden_half = out_ui.shape[1] // 2
         out_gu = out_ui[:, :hidden_half].T
         out_gi = out_ui[:, hidden_half:]
-        out_go = total(last_i, got_i).T
         sums_q = corner_add(parts_q, first_q)
         got_q = near_back(sums_q, size)
         last_q = near_add(parts_q[4], first_q, got_q)
@@ -960,7 +962,8 @@
         out_q = total(last_q, got_q)
         n = query_weight.shape[0]
         out_qkv = [out_q[g * n : (g + 1) * n] for g in range(3)]
-        vec = out_q[3 * n :]
+        out_go = out_q[3 * n : 4 * n].T
+        vec = out_q[4 * n :]
         vec = vec + swap_core(vec)
         vec_out = [vec[i, : item.shape[0]] for i, item in enumerate(vectors)]
     else:

time: 336 us -> 324 us (0.964)
  Pallas kernels: 162 us -> 150 us
  waiting for transfers between devices: 40.6 us -> 49.3 us
  starting transfers between devices: 54.7 us -> 47.5 us
    ppermute x46 -> x39, waiting for transfers between devices: 39.9 us -> 48.6 us  [swap_dp(): return lax.ppermute(value, 'dp', [(i, i ^ mask) for i in range(size)])]
    pallas_call x3, Pallas kernels: 45.7 us -> 37.2 us  [row_call(): pl.pallas_call(kernel, out_shape=[jax.ShapeDtypeStruct((rows, n), d) for...]
    ppermute x46 -> x39, starting transfers between devices: 53.3 us -> 46.3 us  [swap_dp(): return lax.ppermute(value, 'dp', [(i, i ^ mask) for i in range(size)])]
    pallas_call x6 -> x4, Pallas kernels: 14.3 us -> 11 us  [whole_call(): pl.pallas_call(kernel, out_shape=[jax.ShapeDtypeStruct(o, d) for o, d in...]
    pallas_call x2 -> x1, Pallas kernels: 8.96 us -> 6.83 us  [split_cols(): pl.pallas_call(kernel, out_shape=split_shapes(rows, sum(counts) * step),...]
    unnamed x139 -> x129, local copies, waits for them, and re-layouts: 16.1 us -> 16.8 us
  transfers between devices with their start and end apart: 55 -> 48, of which waited for: 18 -> 18; matrix products, arithmetic and copies ran while one was open for 14% -> 14% of each run, Pallas kernels for 35% -> 32%
where the time goes in v2:
time: 324 us; the launch traced here: 323 us
  Pallas kernels  150 us (46%)
  matrix products  49.9 us (15%)
  waiting for transfers between devices  49.3 us (15%)
  starting transfers between devices  47.5 us (15%)
  local copies, waits for them, and re-layouts  21.3 us (7%)
  other arithmetic  4.31 us (1%)
    dot_general x12, matrix products, dot(): return lax.dot_general(left, right, dims, preferred_element_type=f32)  49.9 us
    ppermute x39, waiting for transfers between devices, swap_dp(): return lax.ppermute(value, 'dp', [(i, i ^ mask) for i in range(size)])  48.6 us
    ppermute x39, starting transfers between devices, swap_dp(): return lax.ppermute(value, 'dp', [(i, i ^ mask) for i in range(size)])  46.3 us
    pallas_call x4, Pallas kernels, attend_call(): pl.pallas_call(kernel, out_shape=out_shape, grid_spec=pltpu.PrefetchScala...  42.1 us
    pallas_call x3, Pallas kernels, row_call(): pl.pallas_call(kernel, out_shape=[jax.ShapeDtypeStruct((rows, n), d) for...  37.2 us
    unnamed x129, local copies, waits for them, and re-layouts  16.8 us
    pallas_call x2, Pallas kernels, token_gradient(): pl.pallas_call(kernel, out_shape=jax.ShapeDtypeStruct((rows, width), f32)...  13.9 us
    pallas_call x2, Pallas kernels, project(): pl.pallas_call(kernel, out_shape=[jax.ShapeDtypeStruct((rows, cols), bf16...  11.5 us
  transfers between devices with their start and end apart: 48, of which 18 were waited for; matrix products, arithmetic and copies ran while one was open for 14% of the time, Pallas kernels for 32%

profile of v2, /device:TPU:0, one launch (start us, length us, event | category | flops | bytes accessed | tf_op | source)
XLA Modules:
  0.0 323.3 jit_solution(8204251833559236722)
XLA Ops:
  1.9 1.5 shard_map.305
  3.4 3.1 collective-permute-start.1
  6.5 2.5 collective-permute-start.2
  10.0 6.1 %collective-permute-done.2 = bf16[160,384]{1,0:T(8,128)(2,1)S(1)} collective-permute-done((bf16[160,384]{1,0:T(8,128)(2,1)}, bf16[160,384]{1,0:T(8,128)(2,1)S(1)}, u32[]{:S(2)}, u32[]{:S(2)}) %collective-permute-start.2) | collective-permute-done | bytes 122912 | tf_op jit(solution)/shard_map/ppermute | solution.py:31
  16.1 1.6 collective-permute-start.5
  17.7 2.6 collective-permute-done
  21.2 1.6 collective-permute-start.6
  23.3 1.5 collective-permute-start.4
  24.8 1.5 collective-permute-start.9
  26.3 3.8 %collective-permute-done.6.refs_4_ = bf16[2,160,384]{2,1,0:T(8,128)(2,1)S(1)} collective-permute-done((bf16[2,160,384]{2,1,0:T(8,128)(2,1)S(1)}, bf16[2,160,384]{2,1,0:T(8,128)(2,1)S(1)}, u32[]{:S(2)}, u32[]{:S(2)}) %collective-permute-start.6) | collective-permute-done | bytes 245792 | tf_op jit(solution)/shard_map/ppermute | solution.py:31
  30.1 1.5 collective-permute-start.8
  33.4 2.6 copy.37
  36.0 4.7 %collective-permute-done.3 = bf16[48,1920]{1,0:T(8,128)(2,1)S(1)} collective-permute-done((bf16[48,1920]{1,0:T(8,128)(2,1)S(1)}, bf16[48,1920]{1,0:T(8,128)(2,1)S(1)}, u32[]{:S(2)}, u32[]{:S(2)}) %collective-permute-start.3) | collective-permute-done | bytes 184352 | tf_op jit(solution)/shard_map/ppermute | solution.py:31
  41.6 3.0 shard_map.306
  45.5 1.5 collective-permute-start.14
  47.1 5.8 %shard_map.307 = (bf16[1024,384]{1,0:T(8,128)(2,1)}, bf16[1024,384]{1,0:T(8,128)(2,1)}, bf16[1024,384]{1,0:T(8,128)(2,1)}) custom-call(s32[1]{0:T(128)} %bitcast.19.core_ref, bf16[1024,768]{1,0:T(8,128)(2,1)} %x_ref.5, bf16[3,768,384]{2,1,0:T(8,128)(2,1)} %get-tuple-element.168.w_ref.w0_ref, f32[16,768]{1,0:T(8,128)} %get-tuple-element.169.v_ref), custom_call_target="tpu_custom_call" | custom-call | flops 1 | bytes 1 | tf_op jit(solution)/shard_map/pallas_call | solution.py:419
  52.8 3.0 collective-permute-done.10.refs_1_
  57.0 5.8 %shard_map.308 = (bf16[1024,384]{1,0:T(8,128)(2,1)}, bf16[1024,384]{1,0:T(8,128)(2,1)}, bf16[1024,384]{1,0:T(8,128)(2,1)}) custom-call(s32[1]{0:T(128)} %bitcast.19.core_ref, bf16[1024,768]{1,0:T(8,128)(2,1)} %x_ref.5, bf16[3,768,384]{2,1,0:T(8,128)(2,1)} %copy-done, f32[16,768]{1,0:T(8,128)} %get-tuple-element.169.v_ref), custom_call_target="tpu_custom_call" | custom-call | flops 1 | bytes 1 | tf_op jit(solution)/shard_map/pallas_call | solution.py:419
  63.9 1.5 collective-permute-start.16
  67.2 1.8 collective-permute-start.17
  70.7 9.0 %shard_map.309 = (bf16[1024,384]{1,0:T(8,128)(2,1)}, f32[2,3,2,512]{3,2,1,0:T(2,128)}) custom-call(s32[2]{0:T(128)} %dynamic_slice.3.lens, bf16[1024,384]{1,0:T(8,128)(2,1)} %get-tuple-element.181.q_ref, bf16[1024,384]{1,0:T(8,128)(2,1)} %get-tuple-element.182.k_ref, bf16[1024,384]{1,0:T(8,128)(2,1)} %get-tuple-element.183.v_ref), custom_call_target="tpu_custom_call" | custom-call | flops 1 | bytes 1 | tf_op jit(solution)/shard_map/pallas_call | solution.py:716
  82.7 1.5 collective-permute-start.24
  84.3 9.0 %shard_map.310 = (bf16[1024,384]{1,0:T(8,128)(2,1)}, f32[2,3,2,512]{3,2,1,0:T(2,128)}) custom-call(s32[2]{0:T(128)} %dynamic_slice.3.lens, bf16[1024,384]{1,0:T(8,128)(2,1)} %get-tuple-element.196.q_ref, bf16[1024,384]{1,0:T(8,128)(2,1)} %get-tuple-element.197.k_ref, bf16[1024,384]{1,0:T(8,128)(2,1)} %get-tuple-element.198.v_ref), custom_call_target="tpu_custom_call" | custom-call | flops 1 | bytes 1 | tf_op jit(solution)/shard_map/pallas_call | solution.py:716
  94.2 3.6 %shard_map.311 = (bf16[768,384]{1,0:T(8,128)(2,1)}, bf16[768,1536]{1,0:T(8,128)(2,1)}) custom-call(s32[1]{0:T(128)} %bitcast.18.index_ref, bf16[2,48,1920]{2,1,0:T(8,128)(2,1)} %copy-done.20, bf16[2,48,1920]{2,1,0:T(8,128)(2,1)} %copy-done.31, bf16[2,48,1920]{2,1,0:T(8,128)(2,1)} %copy-done.32, bf16[2,48,1920]{2,1,0:T(8,128)(2,1)} %copy-done.34, ...), custom_call_target="tpu_custom_call" | custom-call | flops 1 | bytes 1 | tf_op jit(solution)/shard_map/pallas_call | solution.py:158
  102.0 7.1 %shard_map.312 = (f32[1024,768]{1,0:T(8,128)}, bf16[1024,768]{1,0:T(8,128)(2,1)}) custom-call(bf16[1024,768]{1,0:T(8,128)(2,1)} %x_ref.5, bf16[1024,384]{1,0:T(8,128)(2,1)} %get-tuple-element.188.c0_ref.c_ref, bf16[1024,384]{1,0:T(8,128)(2,1)} %get-tuple-element.200.c1_ref.c_ref, bf16[768,384]{1,0:T(8,128)(2,1)} %get-tuple-element.209.w0_ref, ...), custom_call_target="tpu_custom_call" | custom-call | flops 1 | bytes 1 | tf_op jit(solution)/shard_map/pallas_call | solution.py:510
  109.1 4.8 %collective-permute-done.22.refs_6_ = bf16[2,48,1536]{2,1,0:T(8,128)(2,1)} collective-permute-done((bf16[2,48,1536]{2,1,0:T(8,128)(2,1)}, bf16[2,48,1536]{2,1,0:T(8,128)(2,1)}, u32[]{:S(2)}, u32[]{:S(2)}) %collective-permute-start.22) | collective-permute-done | bytes 294944 | tf_op jit(solution)/shard_map/ppermute | solution.py:31
  114.4 6.8 %multiply_convert_fusion.3 = (bf16[1024,1536]{1,0:T(8,128)(2,1)}, f32[1024,1536]{1,0:T(8,128)}) fusion(f32[1536]{0:T(1024)S(1)} %copy-done.56, bf16[1024,768]{1,0:T(8,128)(2,1)} %get-tuple-element.229.h_ref, bf16[768,1536]{1,0:T(8,128)(2,1)S(1)} %copy-done.12), kind=kOutput, calls=%fused_computation.16 | convolution fusion | flops 2425356288 | bytes 13375488 | tf_op jit(solution)/shard_map/dot_general | solution.py:21
  123.1 3.2 shard_map.313.w0_ref
  126.4 7.2 %multiply_convert_fusion.2 = (bf16[1024,1536]{1,0:T(8,128)(2,1)}, f32[1024,1536]{1,0:T(8,128)}) fusion(f32[1536]{0:T(1024)S(1)} %copy-done.57, bf16[1024,768]{1,0:T(8,128)(2,1)S(1)} %copy-done.18, bf16[768,1536]{1,0:T(8,128)(2,1)} %collective-permute-done.27.w1_ref), kind=kOutput, calls=%fused_computation.14 | convolution fusion | flops 2425356288 | bytes 13375488 | tf_op jit(solution)/shard_map/dot_general | solution.py:21
  133.6 1.4 copy-done.14
  135.0 14.8 %shard_map.314 = (f32[1024,768]{1,0:T(8,128)}, f32[1024,768]{1,0:T(8,128)}, bf16[1024,768]{1,0:T(8,128)(2,1)}, f32[8,768]{1,0:T(8,128)}) custom-call(bf16[1024,768]{1,0:T(8,128)(2,1)} %get-tuple-element.229.h_ref, bf16[1024,768]{1,0:T(8,128)(2,1)} %c_ref.1, bf16[1024,1536]{1,0:T(8,128)(2,1)} %get-tuple-element.230.a0_ref, ...), custom_call_target="tpu_custom_call" | custom-call | flops 1 | bytes 1 | tf_op jit(solution)/shard_map/pallas_call | solution.py:510
  149.8 4.7 %convolution_convert_fusion.2 = bf16[768,1536]{1,0:T(8,128)(2,1)S(1)} fusion(bf16[1024,768]{1,0:T(8,128)(2,1)} %get-tuple-element.235, bf16[1024,1536]{1,0:T(8,128)(2,1)S(1)} %copy-done.7), kind=kOutput, calls=%fused_computation.20 | convolution fusion | flops 2417098752 | bytes 7077888 | tf_op jit(solution)/shard_map/dot_general | solution.py:21
  155.1 3.9 %convolution_convert_fusion.3.refs_0_ = bf16[768,1536]{1,0:T(8,128)(2,1)} fusion(bf16[1024,768]{1,0:T(8,128)(2,1)S(1)} %copy-done.59, bf16[1024,1536]{1,0:T(8,128)(2,1)S(1)} %copy-done.6), kind=kOutput, calls=%fused_computation.21 | convolution fusion | flops 2417098752 | bytes 7077888 | tf_op jit(solution)/shard_map/dot_general | solution.py:21
  159.3 5.4 %multiply_convert_fusion.d1_ref = bf16[1024,1536]{1,0:T(8,128)(2,1)S(1)} fusion(bf16[1024,768]{1,0:T(8,128)(2,1)S(1)} %copy-done.59, bf16[768,1536]{1,0:T(8,128)(2,1)S(1)} %copy-done.15, f32[1024,1536]{1,0:T(8,128)S(1)} %copy-done.61, f32[1536]{0:T(1024)S(1)} %copy-done.57), kind=kOutput, calls=%fused_computation.12 | convolution fusion | flops 2436366336 | bytes 13375488 | tf_op jit(solution)/shard_map/dot_general | solution.py:21
  164.7 2.9 convolution_convert_fusion
  168.1 5.4 %multiply_convert_fusion.1.d0_ref = bf16[1024,1536]{1,0:T(8,128)(2,1)S(1)} fusion(bf16[1024,768]{1,0:T(8,128)(2,1)S(1)} %copy-done.59, bf16[768,1536]{1,0:T(8,128)(2,1)S(1)} %copy-done.1, f32[1024,1536]{1,0:T(8,128)S(1)} %bitcast.89, f32[1536]{0:T(1024)S(1)} %copy-done.56), kind=kOutput, calls=%fused_computation.13 | convolution fusion | flops 2436366336 | bytes 13375488 | tf_op jit(solution)/shard_map/dot_general | solution.py:21
  173.5 4.0 %convolution_convert_fusion.1.refs_2_ = bf16[768,1536]{1,0:T(8,128)(2,1)} fusion(bf16[1024,768]{1,0:T(8,128)(2,1)S(1)} %copy-done.19, bf16[1024,1536]{1,0:T(8,128)(2,1)S(1)} %multiply_convert_fusion.1.d0_ref), kind=kOutput, calls=%fused_computation.19 | convolution fusion | flops 2417098752 | bytes 7077888 | tf_op jit(solution)/shard_map/dot_general | solution.py:21
  177.5 1.4 copy-done.16
  179.0 6.8 %shard_map.315 = (bf16[4,48,3072]{2,1,0:T(8,128)(2,1)}, bf16[4,48,3072]{2,1,0:T(8,128)(2,1)}, bf16[2,48,3072]{2,1,0:T(8,128)(2,1)}, bf16[2,48,3072]{2,1,0:T(8,128)(2,1)}, bf16[4,48,3072]{2,1,0:T(8,128)(2,1)}) custom-call(s32[1]{0:T(128)} %bitcast.18.index_ref, bf16[768,1536]{1,0:T(8,128)(2,1)} %convolution_convert_fusion.3.refs_0_, ...), custom_call_target="tpu_custom_call" | custom-call | flops 1 | bytes 1 | tf_op jit(solution)/shard_map/pallas_call | solution.py:221
  187.1 15.3 %shard_map.316 = (f32[1024,768]{1,0:T(8,128)}, bf16[1024,768]{1,0:T(8,128)(2,1)}, f32[8,768]{1,0:T(8,128)}, f32[8,3072]{1,0:T(8,128)}) custom-call(f32[1024,768]{1,0:T(8,128)} %get-tuple-element.233.s_ref, bf16[1024,1536]{1,0:T(8,128)(2,1)} %copy-done.5, bf16[1024,1536]{1,0:T(8,128)(2,1)} %copy-done.4, f32[1024,768]{1,0:T(8,128)} %get-tuple-element.245.f_ref, ...), custom_call_target="tpu_custom_call" | custom-call | flops 1 | bytes 1 | tf_op jit(solution)/shard_map/pallas_call | solution.py:510
  202.4 2.6 convolution_convert_fusion.6
  205.1 1.8 convolution_convert_fusion.7.r0_ref
  206.9 1.9 convolution_convert_fusion.4.d_ref
  208.8 5.2 %collective-permute-done.31.r1_ref.f1_ref = bf16[4,48,3072]{2,1,0:T(8,128)(2,1)S(1)} collective-permute-done((bf16[4,48,3072]{2,1,0:T(8,128)(2,1)}, bf16[4,48,3072]{2,1,0:T(8,128)(2,1)S(1)}, u32[]{:S(2)}, u32[]{:S(2)}) %collective-permute-start.31) | collective-permute-done | bytes 1179680 | tf_op jit(solution)/shard_map/ppermute | solution.py:31
  215.5 2.7 shard_map.317
  220.0 1.8 shard_map.318.table_ref
  221.8 12.0 %shard_map.319.d_ref.d1_ref = bf16[3,1024,384]{2,1,0:T(8,128)(2,1)} custom-call(s32[2]{0:T(128)} %dynamic_slice.3.lens, bf16[1024,384]{1,0:T(8,128)(2,1)} %get-tuple-element.196.q_ref, bf16[1024,384]{1,0:T(8,128)(2,1)} %get-tuple-element.197.k_ref, bf16[1024,384]{1,0:T(8,128)(2,1)} %get-tuple-element.198.v_ref, ...), custom_call_target="tpu_custom_call" | custom-call | flops 1 | bytes 1 | tf_op jit(solution)/shard_map/pallas_call | solution.py:716
  235.4 3.5 %shard_map.320 = (f32[48,3072]{1,0:T(8,128)}, bf16[48,3072]{1,0:T(8,128)(2,1)}, bf16[48,3072]{1,0:T(8,128)(2,1)}, bf16[48,3072]{1,0:T(8,128)(2,1)}) custom-call(bf16[4,48,3072]{2,1,0:T(8,128)(2,1)} %get-tuple-element.241.own_ref, bf16[4,48,3072]{2,1,0:T(8,128)(2,1)} %copy-done.2, bf16[4,48,3072]{2,1,0:T(8,128)(2,1)} %copy-done.3, ...), custom_call_target="tpu_custom_call" | custom-call | flops 1 | bytes 1 | tf_op jit(solution)/shard_map/pallas_call | solution.py:355
  239.0 5.9 %shard_map.321 = (bf16[3,768,384]{2,1,0:T(8,128)(2,1)}, f32[3,8,384]{2,1,0:T(8,128)}) custom-call(bf16[768,1024]{1,0:T(8,128)(2,1)} %bitcast.68, bf16[3,1024,384]{2,1,0:T(8,128)(2,1)} %shard_map.319.d_ref.d1_ref), custom_call_target="tpu_custom_call" | custom-call | flops 1 | bytes 1 | tf_op jit(solution)/shard_map/pallas_call | solution.py:242
  247.9 2.0 collective-permute-start.41
  249.9 3.3 %convolution_convert_fusion.5.d_ref = bf16[1024,384]{1,0:T(8,128)(2,1)} fusion(bf16[1024,768]{1,0:T(8,128)(2,1)} %get-tuple-element.246, bf16[768,384]{1,0:T(8,128)(2,1)S(1)} %copy-done.24), kind=kOutput, calls=%fused_computation.23 | convolution fusion | flops 604372992 | bytes 2949120 | tf_op jit(solution)/shard_map/dot_general | solution.py:21
  253.1 12.0 %shard_map.322.d_ref.d0_ref = bf16[3,1024,384]{2,1,0:T(8,128)(2,1)} custom-call(s32[2]{0:T(128)} %dynamic_slice.3.lens, bf16[1024,384]{1,0:T(8,128)(2,1)} %get-tuple-element.181.q_ref, bf16[1024,384]{1,0:T(8,128)(2,1)} %get-tuple-element.182.k_ref, bf16[1024,384]{1,0:T(8,128)(2,1)} %get-tuple-element.183.v_ref, ...), custom_call_target="tpu_custom_call" | custom-call | flops 1 | bytes 1 | tf_op jit(solution)/shard_map/pallas_call | solution.py:716
  266.4 8.0 %shard_map.323 = (bf16[4,208,384]{2,1,0:T(8,128)(2,1)}, bf16[4,208,384]{2,1,0:T(8,128)(2,1)}, bf16[2,208,384]{2,1,0:T(8,128)(2,1)}, bf16[2,208,384]{2,1,0:T(8,128)(2,1)}, bf16[4,208,384]{2,1,0:T(8,128)(2,1)}) custom-call(s32[2]{0:T(128)} %pad_add_fusion.at_ref, bf16[768,1024]{1,0:T(8,128)(2,1)} %bitcast.69, bf16[3,1024,384]{2,1,0:T(8,128)(2,1)} %shard_map.322.d_ref.d0_ref, ...), custom_call_target="tpu_custom_call" | custom-call | flops 1 | bytes 1 | tf_op jit(solution)/shard_map/pallas_call | solution.py:298
  275.3 1.5 collective-permute-start.38
  276.9 6.9 %shard_map.324.f_ref = f32[1024,768]{1,0:T(8,128)} custom-call(f32[1024,768]{1,0:T(8,128)} %get-tuple-element.280.f_ref, bf16[3,1024,384]{2,1,0:T(8,128)(2,1)} %shard_map.322.d_ref.d0_ref, bf16[3,1024,384]{2,1,0:T(8,128)(2,1)} %shard_map.319.d_ref.d1_ref, bf16[3,768,384]{2,1,0:T(8,128)(2,1)} %get-tuple-element.168.w_ref.w0_ref, ...), custom_call_target="tpu_custom_call", output_to_operand_aliasing={{}: (0, {})} | custom-call | flops 1811939328 | bytes 3145728 | tf_op jit(solution)/shard_map/pallas_call | solution.py:451
  283.9 6.8 %collective-permute-done.37.r1_ref.f1_ref = bf16[4,208,384]{2,1,0:T(8,128)(2,1)S(1)} collective-permute-done((bf16[4,208,384]{2,1,0:T(8,128)(2,1)}, bf16[4,208,384]{2,1,0:T(8,128)(2,1)S(1)}, u32[]{:S(2)}, u32[]{:S(2)}) %collective-permute-start.37) | collective-permute-done | bytes 639008 | tf_op jit(solution)/shard_map/ppermute | solution.py:31
  292.1 2.2 shard_map.325
  295.4 1.5 collective-permute-start.43
  297.8 4.6 %collective-permute-done.42.r1_ref = bf16[2,208,384]{2,1,0:T(8,128)(2,1)S(1)} collective-permute-done((bf16[2,208,384]{2,1,0:T(8,128)(2,1)}, bf16[2,208,384]{2,1,0:T(8,128)(2,1)S(1)}, u32[]{:S(2)}, u32[]{:S(2)}) %collective-permute-start.42) | collective-permute-done | bytes 319520 | tf_op jit(solution)/shard_map/ppermute | solution.py:31
  304.1 2.6 shard_map.326
  306.7 1.4 collective-permute-start.44
  309.4 1.7 collective-permute-start.46
  311.1 6.9 %shard_map.327 = f32[1024,768]{1,0:T(8,128)} custom-call(f32[1024,768]{1,0:T(8,128)} %shard_map.324.f_ref, bf16[3,1024,384]{2,1,0:T(8,128)(2,1)} %shard_map.322.d_ref.d0_ref, bf16[3,1024,384]{2,1,0:T(8,128)(2,1)} %shard_map.319.d_ref.d1_ref, bf16[3,768,384]{2,1,0:T(8,128)(2,1)} %get-tuple-element.168.w_ref.w0_ref, ...), custom_call_target="tpu_custom_call", output_to_operand_aliasing={{}: (0, {})} | custom-call | flops 1811939328 | bytes 3145728 | tf_op jit(solution)/shard_map/pallas_call | solution.py:451
  318.0 2.8 collective-permute-done.45
  (214 shorter events, 45.0 us)
Async XLA Ops:
  3.4 6.6 %collective-permute-start.1 = (bf16[160,384]{1,0:T(8,128)(2,1)}, bf16[160,384]{1,0:T(8,128)(2,1)S(1)}, u32[]{:S(2)}, u32[]{:S(2)}) collective-permute-start(bf16[160,384]{1,0:T(8,128)(2,1)} %shard_map.305), channel_id=1, source_target_pairs={{0,8},{2,10},{4,12},{6,14},{8,0},{10,2},{12,4},{14,6},{16,24},{18,... | collective-permute-start | bytes 368648 | tf_op jit(solution)/shard_map/ppermute | solution.py:31
  6.5 9.6 %collective-permute-start.2 = (bf16[160,384]{1,0:T(8,128)(2,1)}, bf16[160,384]{1,0:T(8,128)(2,1)S(1)}, u32[]{:S(2)}, u32[]{:S(2)}) collective-permute-start(bf16[160,384]{1,0:T(8,128)(2,1)} %shard_map.305), channel_id=1, source_target_pairs={{0,24},{2,26},{4,28},{6,30},{8,16},{10,18},{12,20},{14,22},{16,8},... | collective-permute-start | bytes 368648 | tf_op jit(solution)/shard_map/ppermute | solution.py:31
  9.0 11.3 %collective-permute-start = (bf16[160,384]{1,0:T(8,128)(2,1)}, bf16[160,384]{1,0:T(8,128)(2,1)S(1)}, u32[]{:S(2)}, u32[]{:S(2)}) collective-permute-start(bf16[160,384]{1,0:T(8,128)(2,1)} %shard_map.305), channel_id=1, source_target_pairs={{0,16},{2,18},{4,20},{6,22},{8,24},{10,26},{12,28},{14,30},{16,0},... | collective-permute-start | bytes 368648 | tf_op jit(solution)/shard_map/ppermute | solution.py:31
  16.1 24.7 %copy-start.22 = (bf16[2,160,384]{2,1,0:T(8,128)(2,1)}, bf16[2,160,384]{2,1,0:T(8,128)(2,1)S(1)}, u32[]{:S(2)}) copy-start(bf16[2,160,384]{2,1,0:T(8,128)(2,1)S(1)} %pad_maximum_fusion.3.refs_1_) | copy-start | bytes 737284
  16.1 8.7 %collective-permute-start.5 = (bf16[2,160,384]{2,1,0:T(8,128)(2,1)S(1)}, bf16[2,160,384]{2,1,0:T(8,128)(2,1)S(1)}, u32[]{:S(2)}, u32[]{:S(2)}) collective-permute-start(bf16[2,160,384]{2,1,0:T(8,128)(2,1)S(1)} %pad_maximum_fusion.3.refs_1_), channel_id=1, source_target_pairs={{0,2},{2,0},{4,6},{6,4},{8,10},{10,8},{12,14},{14,12},{16,18},{18,... | collective-permute-start | bytes 737288 | tf_op jit(solution)/shard_map/ppermute | solution.py:31
  21.2 19.6 %copy-start.23 = (bf16[2,160,384]{2,1,0:T(8,128)(2,1)}, bf16[2,160,384]{2,1,0:T(8,128)(2,1)S(1)}, u32[]{:S(2)}) copy-start(bf16[2,160,384]{2,1,0:T(8,128)(2,1)S(1)} %pad_maximum_fusion.2.refs_0_) | copy-start | bytes 737284
  21.2 8.9 %collective-permute-start.6 = (bf16[2,160,384]{2,1,0:T(8,128)(2,1)S(1)}, bf16[2,160,384]{2,1,0:T(8,128)(2,1)S(1)}, u32[]{:S(2)}, u32[]{:S(2)}) collective-permute-start(bf16[2,160,384]{2,1,0:T(8,128)(2,1)S(1)} %pad_maximum_fusion.2.refs_0_), channel_id=1, source_target_pairs={{0,4},{2,6},{4,0},{6,2},{8,12},{10,14},{12,8},{14,10},{16,20},{18,... | collective-permute-start | bytes 737288 | tf_op jit(solution)/shard_map/ppermute | solution.py:31
  22.8 17.9 %collective-permute-start.7 = (bf16[2,160,384]{2,1,0:T(8,128)(2,1)S(1)}, bf16[2,160,384]{2,1,0:T(8,128)(2,1)S(1)}, u32[]{:S(2)}, u32[]{:S(2)}) collective-permute-start(bf16[2,160,384]{2,1,0:T(8,128)(2,1)S(1)} %pad_maximum_fusion.3.refs_1_), channel_id=1, source_target_pairs={{0,4},{2,6},{4,0},{6,2},{8,12},{10,14},{12,8},{14,10},{16,20},{18,... | collective-permute-start | bytes 737288 | tf_op jit(solution)/shard_map/ppermute | solution.py:31
  23.3 17.4 %collective-permute-start.4 = (bf16[2,160,384]{2,1,0:T(8,128)(2,1)S(1)}, bf16[2,160,384]{2,1,0:T(8,128)(2,1)S(1)}, u32[]{:S(2)}, u32[]{:S(2)}) collective-permute-start(bf16[2,160,384]{2,1,0:T(8,128)(2,1)S(1)} %pad_maximum_fusion.2.refs_0_), channel_id=1, source_target_pairs={{0,2},{2,0},{4,6},{6,4},{8,10},{10,8},{12,14},{14,12},{16,18},{18,... | collective-permute-start | bytes 737288 | tf_op jit(solution)/shard_map/ppermute | solution.py:31
  24.8 16.0 %copy-start.47 = (bf16[2,160,384]{2,1,0:T(8,128)(2,1)}, bf16[2,160,384]{2,1,0:T(8,128)(2,1)S(1)}, u32[]{:S(2)}) copy-start(bf16[2,160,384]{2,1,0:T(8,128)(2,1)S(1)} %collective-permute-done.5.refs_3_) | copy-start | bytes 737284
  24.8 15.9 %collective-permute-start.9 = (bf16[2,160,384]{2,1,0:T(8,128)(2,1)S(1)}, bf16[2,160,384]{2,1,0:T(8,128)(2,1)S(1)}, u32[]{:S(2)}, u32[]{:S(2)}) collective-permute-start(bf16[2,160,384]{2,1,0:T(8,128)(2,1)S(1)} %collective-permute-done.5.refs_3_), channel_id=1, source_target_pairs={{0,4},{2,6},{4,0},{6,2},{8,12},{10,14},{12,8},{14,10},{16,20},{18,... | collective-permute-start | bytes 737288 | tf_op jit(solution)/shard_map/ppermute | solution.py:31
  30.1 10.6 %collective-permute-start.8 = (bf16[2,160,384]{2,1,0:T(8,128)(2,1)S(1)}, bf16[2,160,384]{2,1,0:T(8,128)(2,1)S(1)}, u32[]{:S(2)}, u32[]{:S(2)}) collective-permute-start(bf16[2,160,384]{2,1,0:T(8,128)(2,1)S(1)} %collective-permute-done.6.refs_4_), channel_id=1, source_target_pairs={{0,2},{2,0},{4,6},{6,4},{8,10},{10,8},{12,14},{14,12},{16,18},{18,... | collective-permute-start | bytes 737288 | tf_op jit(solution)/shard_map/ppermute | solution.py:31
  32.5 8.2 %collective-permute-start.3 = (bf16[48,1920]{1,0:T(8,128)(2,1)S(1)}, bf16[48,1920]{1,0:T(8,128)(2,1)S(1)}, u32[]{:S(2)}, u32[]{:S(2)}) collective-permute-start(bf16[48,1920]{1,0:T(8,128)(2,1)S(1)} %get-tuple-element.158), channel_id=1, source_target_pairs={{0,16},{2,18},{4,20},{6,22},{8,24},{10,26},{12,28},{14,30},{16,0},... | collective-permute-start | bytes 552968 | tf_op jit(solution)/shard_map/ppermute | solution.py:31
  36.0 19.8 %copy-start.53 = (bf16[1536,48]{0,1:T(8,128)(2,1)S(1)}, bf16[1536,48]{0,1:T(8,128)(2,1)}, u32[]{:S(2)}) copy-start(bf16[1536,48]{0,1:T(8,128)(2,1)} %param.32) | copy-start | bytes 442372
  44.7 11.1 %collective-permute-start.11 = (bf16[3,768,384]{2,1,0:T(8,128)(2,1)}, bf16[3,768,384]{2,1,0:T(8,128)(2,1)S(1)}, u32[]{:S(2)}, u32[]{:S(2)}) collective-permute-start(bf16[3,768,384]{2,1,0:T(8,128)(2,1)} %get-tuple-element.168.w_ref.w0_ref), channel_id=1, source_target_pairs={{0,1},{1,0},{2,3},{3,2},{4,5},{5,4},{6,7},{7,6},{8,9},{9,8},{10,11... | collective-permute-start | bytes 5308424 | tf_op jit(solution)/shard_map/ppermute | solution.py:35
  44.7 18.1 %copy-start.20 = (bf16[2,48,1920]{2,1,0:T(8,128)(2,1)}, bf16[2,48,1920]{2,1,0:T(8,128)(2,1)S(1)}, u32[]{:S(2)}) copy-start(bf16[2,48,1920]{2,1,0:T(8,128)(2,1)S(1)} %pad_maximum_fusion.refs_0_) | copy-start | bytes 1105924
  44.7 11.1 %collective-permute-start.10 = (bf16[2,48,1920]{2,1,0:T(8,128)(2,1)S(1)}, bf16[2,48,1920]{2,1,0:T(8,128)(2,1)S(1)}, u32[]{:S(2)}, u32[]{:S(2)}) collective-permute-start(bf16[2,48,1920]{2,1,0:T(8,128)(2,1)S(1)} %pad_maximum_fusion.refs_0_), channel_id=1, source_target_pairs={{0,8},{2,10},{4,12},{6,14},{8,0},{10,2},{12,4},{14,6},{16,24},{18,... | collective-permute-start | bytes 1105928 | tf_op jit(solution)/shard_map/ppermute | solution.py:31
  44.8 20.6 %collective-permute-start.13 = (bf16[2,48,1920]{2,1,0:T(8,128)(2,1)S(1)}, bf16[2,48,1920]{2,1,0:T(8,128)(2,1)S(1)}, u32[]{:S(2)}, u32[]{:S(2)}) collective-permute-start(bf16[2,48,1920]{2,1,0:T(8,128)(2,1)S(1)} %pad_maximum_fusion.refs_0_), channel_id=1, source_target_pairs={{0,2},{2,0},{4,6},{6,4},{8,10},{10,8},{12,14},{14,12},{16,18},{18,... | collective-permute-start | bytes 1105928 | tf_op jit(solution)/shard_map/ppermute | solution.py:31
  45.5 19.9 %collective-permute-start.14 = (bf16[2,48,1920]{2,1,0:T(8,128)(2,1)S(1)}, bf16[2,48,1920]{2,1,0:T(8,128)(2,1)S(1)}, u32[]{:S(2)}, u32[]{:S(2)}) collective-permute-start(bf16[2,48,1920]{2,1,0:T(8,128)(2,1)S(1)} %pad_maximum_fusion.refs_0_), channel_id=1, source_target_pairs={{0,4},{2,6},{4,0},{6,2},{8,12},{10,14},{12,8},{14,10},{16,20},{18,... | collective-permute-start | bytes 1105928 | tf_op jit(solution)/shard_map/ppermute | solution.py:31
  47.1 23.1 %copy-start.60 = (s32[4]{0:T(128)S(1)}, s32[4]{0:T(128)}, u32[]{:S(2)}) copy-start(s32[4]{0:T(128)} %param.20) | copy-start | bytes 52
  55.8 37.5 %copy-start.31 = (bf16[2,48,1920]{2,1,0:T(8,128)(2,1)}, bf16[2,48,1920]{2,1,0:T(8,128)(2,1)S(1)}, u32[]{:S(2)}) copy-start(bf16[2,48,1920]{2,1,0:T(8,128)(2,1)S(1)} %collective-permute-done.10.refs_1_) | copy-start | bytes 1105924
  55.8 9.6 %collective-permute-start.12 = (bf16[48,1536]{1,0:T(8,128)(2,1)S(1)}, bf16[48,1536]{1,0:T(8,128)(2,1)S(1)}, u32[]{:S(2)}, u32[]{:S(2)}) collective-permute-start(bf16[48,1536]{1,0:T(8,128)(2,1)S(1)} %bitcast.72), channel_id=1, source_target_pairs={{0,16},{2,18},{4,20},{6,22},{8,24},{10,26},{12,28},{14,30},{16,0},... | collective-permute-start | bytes 442376 | tf_op jit(solution)/shard_map/ppermute | solution.py:31
  62.8 17.0 %collective-permute-start.15 = (bf16[2,48,1920]{2,1,0:T(8,128)(2,1)S(1)}, bf16[2,48,1920]{2,1,0:T(8,128)(2,1)S(1)}, u32[]{:S(2)}, u32[]{:S(2)}) collective-permute-start(bf16[2,48,1920]{2,1,0:T(8,128)(2,1)S(1)} %collective-permute-done.10.refs_1_), channel_id=1, source_target_pairs={{0,2},{2,0},{4,6},{6,4},{8,10},{10,8},{12,14},{14,12},{16,18},{18,... | collective-permute-start | bytes 1105928 | tf_op jit(solution)/shard_map/ppermute | solution.py:31
  63.9 15.9 %collective-permute-start.16 = (bf16[2,48,1920]{2,1,0:T(8,128)(2,1)S(1)}, bf16[2,48,1920]{2,1,0:T(8,128)(2,1)S(1)}, u32[]{:S(2)}, u32[]{:S(2)}) collective-permute-start(bf16[2,48,1920]{2,1,0:T(8,128)(2,1)S(1)} %collective-permute-done.10.refs_1_), channel_id=1, source_target_pairs={{0,4},{2,6},{4,0},{6,2},{8,12},{10,14},{12,8},{14,10},{16,20},{18,... | collective-permute-start | bytes 1105928 | tf_op jit(solution)/shard_map/ppermute | solution.py:31
  65.4 27.9 %copy-start.32 = (bf16[2,48,1920]{2,1,0:T(8,128)(2,1)}, bf16[2,48,1920]{2,1,0:T(8,128)(2,1)S(1)}, u32[]{:S(2)}) copy-start(bf16[2,48,1920]{2,1,0:T(8,128)(2,1)S(1)} %collective-permute-done.13.refs_2_) | copy-start | bytes 1105924
  67.2 30.6 %copy-start.21 = (bf16[2,48,1536]{2,1,0:T(8,128)(2,1)}, bf16[2,48,1536]{2,1,0:T(8,128)(2,1)S(1)}, u32[]{:S(2)}) copy-start(bf16[2,48,1536]{2,1,0:T(8,128)(2,1)S(1)} %pad_maximum_fusion.1.refs_0_) | copy-start | bytes 884740
  67.2 12.6 %collective-permute-start.17 = (bf16[2,48,1536]{2,1,0:T(8,128)(2,1)S(1)}, bf16[2,48,1536]{2,1,0:T(8,128)(2,1)S(1)}, u32[]{:S(2)}, u32[]{:S(2)}) collective-permute-start(bf16[2,48,1536]{2,1,0:T(8,128)(2,1)S(1)} %pad_maximum_fusion.1.refs_0_), channel_id=1, source_target_pairs={{0,8},{2,10},{4,12},{6,14},{8,0},{10,2},{12,4},{14,6},{16,24},{18,... | collective-permute-start | bytes 884744 | tf_op jit(solution)/shard_map/ppermute | solution.py:31
  69.0 11.1 %collective-permute-start.18 = (bf16[2,48,1536]{2,1,0:T(8,128)(2,1)S(1)}, bf16[2,48,1536]{2,1,0:T(8,128)(2,1)S(1)}, u32[]{:S(2)}, u32[]{:S(2)}) collective-permute-start(bf16[2,48,1536]{2,1,0:T(8,128)(2,1)S(1)} %pad_maximum_fusion.1.refs_0_), channel_id=1, source_target_pairs={{0,4},{2,6},{4,0},{6,2},{8,12},{10,14},{12,8},{14,10},{16,20},{18,... | collective-permute-start | bytes 884744 | tf_op jit(solution)/shard_map/ppermute | solution.py:31
  69.5 10.6 %collective-permute-start.19 = (bf16[2,48,1536]{2,1,0:T(8,128)(2,1)S(1)}, bf16[2,48,1536]{2,1,0:T(8,128)(2,1)S(1)}, u32[]{:S(2)}, u32[]{:S(2)}) collective-permute-start(bf16[2,48,1536]{2,1,0:T(8,128)(2,1)S(1)} %pad_maximum_fusion.1.refs_0_), channel_id=1, source_target_pairs={{0,2},{2,0},{4,6},{6,4},{8,10},{10,8},{12,14},{14,12},{16,18},{18,... | collective-permute-start | bytes 884744 | tf_op jit(solution)/shard_map/ppermute | solution.py:31
  79.7 20.7 %copy-start.55 = (f32[1,3072]{1,0:T(1,128)S(1)}, f32[1,3072]{1,0:T(1,128)}, u32[]{:S(2)}) copy-start(f32[1,3072]{1,0:T(1,128)} %get-tuple-element.220) | copy-start | bytes 36868
  79.8 13.6 %copy-start.34 = (bf16[2,48,1920]{2,1,0:T(8,128)(2,1)}, bf16[2,48,1920]{2,1,0:T(8,128)(2,1)S(1)}, u32[]{:S(2)}) copy-start(bf16[2,48,1920]{2,1,0:T(8,128)(2,1)S(1)} %collective-permute-done.15.refs_3_) | copy-start | bytes 1105924
  79.8 13.6 %copy-start.35 = (bf16[2,48,1920]{2,1,0:T(8,128)(2,1)}, bf16[2,48,1920]{2,1,0:T(8,128)(2,1)S(1)}, u32[]{:S(2)}) copy-start(bf16[2,48,1920]{2,1,0:T(8,128)(2,1)S(1)} %collective-permute-done.16.refs_5_) | copy-start | bytes 1105924
  81.5 11.8 %collective-permute-start.23 = (bf16[2,48,1920]{2,1,0:T(8,128)(2,1)}, bf16[2,48,1920]{2,1,0:T(8,128)(2,1)S(1)}, u32[]{:S(2)}, u32[]{:S(2)}) collective-permute-start(bf16[2,48,1920]{2,1,0:T(8,128)(2,1)} %copy-done.33), channel_id=1, source_target_pairs={{0,2},{2,0},{4,6},{6,4},{8,10},{10,8},{12,14},{14,12},{16,18},{18,... | collective-permute-start | bytes 1105928 | tf_op jit(solution)/shard_map/ppermute | solution.py:31
  82.7 10.6 %collective-permute-start.24 = (bf16[2,48,1920]{2,1,0:T(8,128)(2,1)S(1)}, bf16[2,48,1920]{2,1,0:T(8,128)(2,1)S(1)}, u32[]{:S(2)}, u32[]{:S(2)}) collective-permute-start(bf16[2,48,1920]{2,1,0:T(8,128)(2,1)S(1)} %collective-permute-done.15.refs_3_), channel_id=1, source_target_pairs={{0,4},{2,6},{4,0},{6,2},{8,12},{10,14},{12,8},{14,10},{16,20},{18,... | collective-permute-start | bytes 1105928 | tf_op jit(solution)/shard_map/ppermute | solution.py:31
  97.8 16.6 %copy-start.12 = (bf16[768,1536]{1,0:T(8,128)(2,1)S(1)}, bf16[768,1536]{1,0:T(8,128)(2,1)}, u32[]{:S(2)}) copy-start(bf16[768,1536]{1,0:T(8,128)(2,1)} %get-tuple-element.219.w0_ref) | copy-start | bytes 7077892
  97.8 3.3 %collective-permute-start.25 = (bf16[768,384]{1,0:T(8,128)(2,1)}, bf16[768,384]{1,0:T(8,128)(2,1)S(1)}, u32[]{:S(2)}, u32[]{:S(2)}) collective-permute-start(bf16[768,384]{1,0:T(8,128)(2,1)} %get-tuple-element.209.w0_ref), channel_id=1, source_target_pairs={{0,1},{1,0},{2,3},{3,2},{4,5},{5,4},{6,7},{7,6},{8,9},{9,8},{10,11... | collective-permute-start | bytes 1769480 | tf_op jit(solution)/shard_map/ppermute | solution.py:35
  97.9 11.2 %collective-permute-start.20 = (bf16[2,48,1536]{2,1,0:T(8,128)(2,1)}, bf16[2,48,1536]{2,1,0:T(8,128)(2,1)S(1)}, u32[]{:S(2)}, u32[]{:S(2)}) collective-permute-start(bf16[2,48,1536]{2,1,0:T(8,128)(2,1)} %copy-done.41), channel_id=1, source_target_pairs={{0,2},{2,0},{4,6},{6,4},{8,10},{10,8},{12,14},{14,12},{16,18},{18,... | collective-permute-start | bytes 884744 | tf_op jit(solution)/shard_map/ppermute | solution.py:31
  98.7 10.4 %collective-permute-start.21 = (bf16[2,48,1536]{2,1,0:T(8,128)(2,1)}, bf16[2,48,1536]{2,1,0:T(8,128)(2,1)S(1)}, u32[]{:S(2)}, u32[]{:S(2)}) collective-permute-start(bf16[2,48,1536]{2,1,0:T(8,128)(2,1)} %copy-done.41), channel_id=1, source_target_pairs={{0,4},{2,6},{4,0},{6,2},{8,12},{10,14},{12,8},{14,10},{16,20},{18,... | collective-permute-start | bytes 884744 | tf_op jit(solution)/shard_map/ppermute | solution.py:31
  99.2 14.7 %collective-permute-start.22 = (bf16[2,48,1536]{2,1,0:T(8,128)(2,1)}, bf16[2,48,1536]{2,1,0:T(8,128)(2,1)}, u32[]{:S(2)}, u32[]{:S(2)}) collective-permute-start(bf16[2,48,1536]{2,1,0:T(8,128)(2,1)} %copy-done.42), channel_id=1, source_target_pairs={{0,2},{2,0},{4,6},{6,4},{8,10},{10,8},{12,14},{14,12},{16,18},{18,... | collective-permute-start | bytes 884744 | tf_op jit(solution)/shard_map/ppermute | solution.py:31
  101.1 25.2 %collective-permute-start.27 = (bf16[768,1536]{1,0:T(8,128)(2,1)}, bf16[768,1536]{1,0:T(8,128)(2,1)}, u32[]{:S(2)}, u32[]{:S(2)}) collective-permute-start(bf16[768,1536]{1,0:T(8,128)(2,1)} %get-tuple-element.219.w0_ref), channel_id=1, source_target_pairs={{0,1},{1,0},{2,3},{3,2},{4,5},{5,4},{6,7},{7,6},{8,9},{9,8},{10,11... | collective-permute-start | bytes 7077896 | tf_op jit(solution)/shard_map/ppermute | solution.py:35
  113.9 8.5 %collective-permute-start.26 = (bf16[2,48,1536]{2,1,0:T(8,128)(2,1)S(1)}, bf16[2,48,1536]{2,1,0:T(8,128)(2,1)S(1)}, u32[]{:S(2)}, u32[]{:S(2)}) collective-permute-start(bf16[2,48,1536]{2,1,0:T(8,128)(2,1)S(1)} %collective-permute-done.20.refs_3_), channel_id=1, source_target_pairs={{0,4},{2,6},{4,0},{6,2},{8,12},{10,14},{12,8},{14,10},{16,20},{18,... | collective-permute-start | bytes 884744 | tf_op jit(solution)/shard_map/ppermute | solution.py:31
  126.3 7.2 %collective-permute-start.28 = (bf16[768,1536]{1,0:T(8,128)(2,1)}, bf16[768,1536]{1,0:T(8,128)(2,1)S(1)}, u32[]{:S(2)}, u32[]{:S(2)}) collective-permute-start(bf16[768,1536]{1,0:T(8,128)(2,1)} %shard_map.313.w0_ref), channel_id=1, source_target_pairs={{0,1},{1,0},{2,3},{3,2},{4,5},{5,4},{6,7},{7,6},{8,9},{9,8},{10,11... | collective-permute-start | bytes 7077896 | tf_op jit(solution)/shard_map/ppermute | solution.py:35
  135.0 14.8 %copy-start.7 = (bf16[1024,1536]{1,0:T(8,128)(2,1)S(1)}, bf16[1024,1536]{1,0:T(8,128)(2,1)}, u32[]{:S(2)}) copy-start(bf16[1024,1536]{1,0:T(8,128)(2,1)} %get-tuple-element.319.a1_ref) | copy-start | bytes 9437188
  154.5 4.7 %collective-permute-start.29 = (bf16[768,1536]{1,0:T(8,128)(2,1)S(1)}, bf16[768,1536]{1,0:T(8,128)(2,1)S(1)}, u32[]{:S(2)}, u32[]{:S(2)}) collective-permute-start(bf16[768,1536]{1,0:T(8,128)(2,1)S(1)} %convolution_convert_fusion.2), channel_id=1, source_target_pairs={{0,1},{1,0},{2,3},{3,2},{4,5},{5,4},{6,7},{7,6},{8,9},{9,8},{10,11... | collective-permute-start | bytes 7077896 | tf_op jit(solution)/shard_map/ppermute | solution.py:35
  167.7 9.8 %collective-permute-start.30 = (bf16[768,1536]{1,0:T(8,128)(2,1)S(1)}, bf16[768,1536]{1,0:T(8,128)(2,1)S(1)}, u32[]{:S(2)}, u32[]{:S(2)}) collective-permute-start(bf16[768,1536]{1,0:T(8,128)(2,1)S(1)} %convolution_convert_fusion), channel_id=1, source_target_pairs={{0,1},{1,0},{2,3},{3,2},{4,5},{5,4},{6,7},{7,6},{8,9},{9,8},{10,11... | collective-permute-start | bytes 7077896 | tf_op jit(solution)/shard_map/ppermute | solution.py:35
  185.8 28.2 %collective-permute-start.31 = (bf16[4,48,3072]{2,1,0:T(8,128)(2,1)}, bf16[4,48,3072]{2,1,0:T(8,128)(2,1)S(1)}, u32[]{:S(2)}, u32[]{:S(2)}) collective-permute-start(bf16[4,48,3072]{2,1,0:T(8,128)(2,1)} %get-tuple-element.249), channel_id=1, source_target_pairs={{0,2},{2,0},{4,6},{6,4},{8,10},{10,8},{12,14},{14,12},{16,18},{18,... | collective-permute-start | bytes 3538952 | tf_op jit(solution)/shard_map/ppermute | solution.py:31
  186.6 27.9 %collective-permute-start.32 = (bf16[4,48,3072]{2,1,0:T(8,128)(2,1)}, bf16[4,48,3072]{2,1,0:T(8,128)(2,1)S(1)}, u32[]{:S(2)}, u32[]{:S(2)}) collective-permute-start(bf16[4,48,3072]{2,1,0:T(8,128)(2,1)} %get-tuple-element.250), channel_id=1, source_target_pairs={{0,4},{2,6},{4,0},{6,2},{8,12},{10,14},{12,8},{14,10},{16,20},{18,... | collective-permute-start | bytes 3538952 | tf_op jit(solution)/shard_map/ppermute | solution.py:31
  187.1 15.3 %copy-start.9 = (bf16[1024,384]{1,0:T(8,128)(2,1)S(1)}, bf16[1024,384]{1,0:T(8,128)(2,1)}, u32[]{:S(2)}) copy-start(bf16[1024,384]{1,0:T(8,128)(2,1)} %get-tuple-element.200.c1_ref.c_ref) | copy-start | bytes 2359300
  205.0 3.8 %collective-permute-start.33 = (bf16[768,384]{1,0:T(8,128)(2,1)S(1)}, bf16[768,384]{1,0:T(8,128)(2,1)S(1)}, u32[]{:S(2)}, u32[]{:S(2)}) collective-permute-start(bf16[768,384]{1,0:T(8,128)(2,1)S(1)} %convolution_convert_fusion.6), channel_id=1, source_target_pairs={{0,1},{1,0},{2,3},{3,2},{4,5},{5,4},{6,7},{7,6},{8,9},{9,8},{10,11... | collective-permute-start | bytes 1769480 | tf_op jit(solution)/shard_map/ppermute | solution.py:35
  208.8 36.1 %copy-start.27 = (bf16[768,384]{1,0:T(8,128)(2,1)}, bf16[768,384]{1,0:T(8,128)(2,1)S(1)}, u32[]{:S(2)}) copy-start(bf16[768,384]{1,0:T(8,128)(2,1)S(1)} %collective-permute-done.33.r1_ref) | copy-start | bytes 1769476
  218.2 15.6 %collective-permute-start.34 = (bf16[2,48,3072]{2,1,0:T(8,128)(2,1)}, bf16[2,48,3072]{2,1,0:T(8,128)(2,1)S(1)}, u32[]{:S(2)}, u32[]{:S(2)}) collective-permute-start(bf16[2,48,3072]{2,1,0:T(8,128)(2,1)} %get-tuple-element.253), channel_id=1, source_target_pairs={{0,2},{2,0},{4,6},{6,4},{8,10},{10,8},{12,14},{14,12},{16,18},{18,... | collective-permute-start | bytes 1769480 | tf_op jit(solution)/shard_map/ppermute | solution.py:31
  219.4 14.3 %collective-permute-start.35 = (bf16[2,48,3072]{2,1,0:T(8,128)(2,1)}, bf16[2,48,3072]{2,1,0:T(8,128)(2,1)S(1)}, u32[]{:S(2)}, u32[]{:S(2)}) collective-permute-start(bf16[2,48,3072]{2,1,0:T(8,128)(2,1)} %get-tuple-element.254), channel_id=1, source_target_pairs={{0,4},{2,6},{4,0},{6,2},{8,12},{10,14},{12,8},{14,10},{16,20},{18,... | collective-permute-start | bytes 1769480 | tf_op jit(solution)/shard_map/ppermute | solution.py:31
  244.9 20.3 %collective-permute-start.36 = (bf16[3,768,384]{2,1,0:T(8,128)(2,1)}, bf16[3,768,384]{2,1,0:T(8,128)(2,1)S(1)}, u32[]{:S(2)}, u32[]{:S(2)}) collective-permute-start(bf16[3,768,384]{2,1,0:T(8,128)(2,1)} %get-tuple-element.266), channel_id=1, source_target_pairs={{0,1},{1,0},{2,3},{3,2},{4,5},{5,4},{6,7},{7,6},{8,9},{9,8},{10,11... | collective-permute-start | bytes 5308424 | tf_op jit(solution)/shard_map/ppermute | solution.py:35
  245.5 29.0 %collective-permute-start.39 = (bf16[48,3072]{1,0:T(8,128)(2,1)}, bf16[48,3072]{1,0:T(8,128)(2,1)S(1)}, u32[]{:S(2)}, u32[]{:S(2)}) collective-permute-start(bf16[48,3072]{1,0:T(8,128)(2,1)} %get-tuple-element.275), channel_id=1, source_target_pairs={{0,8},{2,10},{4,12},{6,14},{8,0},{10,2},{12,4},{14,6},{16,24},{18,... | collective-permute-start | bytes 884744 | tf_op jit(solution)/shard_map/ppermute | solution.py:31
  246.5 28.0 %collective-permute-start.40 = (bf16[48,3072]{1,0:T(8,128)(2,1)}, bf16[48,3072]{1,0:T(8,128)(2,1)S(1)}, u32[]{:S(2)}, u32[]{:S(2)}) collective-permute-start(bf16[48,3072]{1,0:T(8,128)(2,1)} %get-tuple-element.276), channel_id=1, source_target_pairs={{0,16},{2,18},{4,20},{6,22},{8,24},{10,26},{12,28},{14,30},{16,0},... | collective-permute-start | bytes 884744 | tf_op jit(solution)/shard_map/ppermute | solution.py:31
  247.9 26.6 %collective-permute-start.41 = (bf16[48,3072]{1,0:T(8,128)(2,1)}, bf16[48,3072]{1,0:T(8,128)(2,1)S(1)}, u32[]{:S(2)}, u32[]{:S(2)}) collective-permute-start(bf16[48,3072]{1,0:T(8,128)(2,1)} %get-tuple-element.277), channel_id=1, source_target_pairs={{0,24},{2,26},{4,28},{6,30},{8,16},{10,18},{12,20},{14,22},{16,8},... | collective-permute-start | bytes 884744 | tf_op jit(solution)/shard_map/ppermute | solution.py:31
  274.5 16.2 %collective-permute-start.37 = (bf16[4,208,384]{2,1,0:T(8,128)(2,1)}, bf16[4,208,384]{2,1,0:T(8,128)(2,1)S(1)}, u32[]{:S(2)}, u32[]{:S(2)}) collective-permute-start(bf16[4,208,384]{2,1,0:T(8,128)(2,1)} %get-tuple-element.272), channel_id=1, source_target_pairs={{0,2},{2,0},{4,6},{6,4},{8,10},{10,8},{12,14},{14,12},{16,18},{18,... | collective-permute-start | bytes 1916936 | tf_op jit(solution)/shard_map/ppermute | solution.py:31
  275.3 15.9 %collective-permute-start.38 = (bf16[4,208,384]{2,1,0:T(8,128)(2,1)}, bf16[4,208,384]{2,1,0:T(8,128)(2,1)S(1)}, u32[]{:S(2)}, u32[]{:S(2)}) collective-permute-start(bf16[4,208,384]{2,1,0:T(8,128)(2,1)} %get-tuple-element.273), channel_id=1, source_target_pairs={{0,4},{2,6},{4,0},{6,2},{8,12},{10,14},{12,8},{14,10},{16,20},{18,... | collective-permute-start | bytes 1916936 | tf_op jit(solution)/shard_map/ppermute | solution.py:31
  294.2 8.2 %collective-permute-start.42 = (bf16[2,208,384]{2,1,0:T(8,128)(2,1)}, bf16[2,208,384]{2,1,0:T(8,128)(2,1)S(1)}, u32[]{:S(2)}, u32[]{:S(2)}) collective-permute-start(bf16[2,208,384]{2,1,0:T(8,128)(2,1)} %get-tuple-element.288), channel_id=1, source_target_pairs={{0,2},{2,0},{4,6},{6,4},{8,10},{10,8},{12,14},{14,12},{16,18},{18,... | collective-permute-start | bytes 958472 | tf_op jit(solution)/shard_map/ppermute | solution.py:31
  295.4 7.9 %collective-permute-start.43 = (bf16[2,208,384]{2,1,0:T(8,128)(2,1)}, bf16[2,208,384]{2,1,0:T(8,128)(2,1)S(1)}, u32[]{:S(2)}, u32[]{:S(2)}) collective-permute-start(bf16[2,208,384]{2,1,0:T(8,128)(2,1)} %get-tuple-element.289), channel_id=1, source_target_pairs={{0,4},{2,6},{4,0},{6,2},{8,12},{10,14},{12,8},{14,10},{16,20},{18,... | collective-permute-start | bytes 958472 | tf_op jit(solution)/shard_map/ppermute | solution.py:31
  306.7 11.3 %collective-permute-start.44 = (bf16[208,384]{1,0:T(8,128)(2,1)}, bf16[208,384]{1,0:T(8,128)(2,1)S(1)}, u32[]{:S(2)}, u32[]{:S(2)}) collective-permute-start(bf16[208,384]{1,0:T(8,128)(2,1)} %get-tuple-element.293), channel_id=1, source_target_pairs={{0,8},{2,10},{4,12},{6,14},{8,0},{10,2},{12,4},{14,6},{16,24},{18,... | collective-permute-start | bytes 479240 | tf_op jit(solution)/shard_map/ppermute | solution.py:31
  308.1 12.8 %collective-permute-start.45 = (bf16[208,384]{1,0:T(8,128)(2,1)}, bf16[208,384]{1,0:T(8,128)(2,1)S(1)}, u32[]{:S(2)}, u32[]{:S(2)}) collective-permute-start(bf16[208,384]{1,0:T(8,128)(2,1)} %get-tuple-element.294), channel_id=1, source_target_pairs={{0,16},{2,18},{4,20},{6,22},{8,24},{10,26},{12,28},{14,30},{16,0},... | collective-permute-start | bytes 479240 | tf_op jit(solution)/shard_map/ppermute | solution.py:31
  309.4 11.5 %collective-permute-start.46 = (bf16[208,384]{1,0:T(8,128)(2,1)}, bf16[208,384]{1,0:T(8,128)(2,1)S(1)}, u32[]{:S(2)}, u32[]{:S(2)}) collective-permute-start(bf16[208,384]{1,0:T(8,128)(2,1)} %get-tuple-element.295), channel_id=1, source_target_pairs={{0,24},{2,26},{4,28},{6,30},{8,16},{10,18},{12,20},{14,22},{16,8},... | collective-permute-start | bytes 479240 | tf_op jit(solution)/shard_map/ppermute | solution.py:31
  321.0 1.3 collective-permute-start.47
  (48 other events, 182.3 us)

commit v3 on v2

--- a/solution.py
+++ b/solution.py
@@ -72,8 +72,6 @@
     return buf
 
 
-BLOCK = 512
-PART = 128
 HINT = pl.CostEstimate(flops=1, transcendentals=0, bytes_accessed=1)
 
 
@@ -436,7 +434,7 @@
 def token_gradient(first_delta, deltas, weights, part, parts):
     count, rows, cols = deltas[0].shape
     width = weights[0].shape[1]
-    steps = rows // BLOCK // parts
+    steps = rows // ROWS // parts
 
     def kernel(f_ref, d0_ref, d1_ref, w0_ref, w1_ref, *refs):
         o_ref = refs[-1]
@@ -446,8 +444,8 @@
                 total = total + dot(d_ref[g], w_ref[g], NT)
         o_ref[...] = total
 
-    tile = pl.BlockSpec((BLOCK, width), lambda i: (i + part * steps, 0))
-    delta_part = pl.BlockSpec((count, BLOCK, cols), lambda i: (0, i + part * steps, 0))
+    tile = pl.BlockSpec((ROWS, width), lambda i: (i + part * steps, 0))
+    delta_part = pl.BlockSpec((count, ROWS, cols), lambda i: (0, i + part * steps, 0))
     return pl.pallas_call(
         kernel,
         out_shape=jax.ShapeDtypeStruct((rows, width), f32),
@@ -492,43 +490,29 @@
             ref[...] = jnp.zeros(ref.shape, f32)
 
 
-def in_parts(total, finish):
-    def body(i, carry):
-        at = pl.ds(pl.multiple_of(i * PART, PART), PART)
-        finish(at, total[at, :])
-        return carry
-
-    lax.fori_loop(0, BLOCK // PART, body, 0)
-
-
 def row_call(kernel, tiles, wholes, outs, sums):
     rows = tiles[0].shape[0]
 
     def tile(cols):
-        return pl.BlockSpec((BLOCK, cols), lambda i: (i, 0))
+        return pl.BlockSpec((ROWS, cols), lambda i: (i, 0))
 
     return pl.pallas_call(
         kernel,
         out_shape=[jax.ShapeDtypeStruct((rows, n), d) for n, d in outs]
         + [jax.ShapeDtypeStruct((8, n), f32) for n in sums],
-        grid=(rows // BLOCK,),
+        grid=(rows // ROWS,),
         in_specs=[tile(a.shape[1]) for a in tiles] + [vmem(a.shape) for a in wholes],
         out_specs=[tile(n) for n, _ in outs] + [vmem((8, n)) for n in sums],
-        scratch_shapes=[pltpu.VMEM((BLOCK, outs[0][0]), f32)],
         cost_estimate=HINT,
     )(*tiles, *wholes)
 
 
 def first_block(tokens, context, weights, vectors):
-    def kernel(x_ref, c0_ref, c1_ref, w0_ref, w1_ref, v_ref, out, low, products):
-        products[...] = dot(c0_ref[...], w0_ref[...], NT) + dot(c1_ref[...], w1_ref[...], NT)
-
-        def finish(at, total):
-            total = x_ref[at, :].astype(f32) + total + v_ref[2:3]
-            out[at, :] = total
-            low[at, :] = (center(total)[0] * v_ref[3:4] + v_ref[4:5]).astype(bf16)
-
-        in_parts(products, finish)
+    def kernel(x_ref, c0_ref, c1_ref, w0_ref, w1_ref, v_ref, out, low):
+        total = dot(c0_ref[...], w0_ref[...], NT) + dot(c1_ref[...], w1_ref[...], NT)
+        total = x_ref[...].astype(f32) + total + v_ref[2:3]
+        out[...] = total
+        low[...] = (center(total)[0] * v_ref[3:4] + v_ref[4:5]).astype(bf16)
 
     width = tokens.shape[1]
     return row_call(
@@ -538,22 +522,18 @@
 
 def outer_block(hidden, cotangent, act, weights, vectors):
     def kernel(
-        h_ref, c_ref, a0_ref, a1_ref, w0_ref, w1_ref, v_ref, out, delta, low, sums, products
+        h_ref, c_ref, a0_ref, a1_ref, w0_ref, w1_ref, v_ref, out, delta, low, sums
     ):
         clear(sums)
 
-        products[...] = dot(a0_ref[...], w0_ref[...], NT) + dot(a1_ref[...], w1_ref[...], NT)
-
-        def finish(at, feed):
-            normed, rinv = center(h_ref[at, :].astype(f32) + (v_ref[5:6] + feed))
-            out[at, :] = normed * v_ref[6:7] + v_ref[7:8]
-            cot = c_ref[at, :].astype(f32)
-            found = norm_back(cot, normed, rinv, v_ref[6:7])
-            delta[at, :] = found
-            low[at, :] = found.astype(bf16)
-            add_rows(sums, (found, cot * normed, cot))
-
-        in_parts(products, finish)
+        feed = dot(a0_ref[...], w0_ref[...], NT) + dot(a1_ref[...], w1_ref[...], NT)
+        normed, rinv = center(h_ref[...].astype(f32) + (v_ref[5:6] + feed))
+        out[...] = normed * v_ref[6:7] + v_ref[7:8]
+        cot = c_ref[...].astype(f32)
+        found = norm_back(cot, normed, rinv, v_ref[6:7])
+        delta[...] = found
+        low[...] = found.astype(bf16)
+        add_rows(sums, (found, cot * normed, cot))
 
     width = hidden.shape[1]
     return row_call(
@@ -567,25 +547,21 @@
 
 def inner_back(second_delta, inner_delta, first_in, weights, vectors):
     def kernel(
-        s_ref, d0_ref, d1_ref, f_ref, w0_ref, w1_ref, v_ref, delta, low, sums, inner, products
+        s_ref, d0_ref, d1_ref, f_ref, w0_ref, w1_ref, v_ref, delta, low, sums, inner
     ):
         clear(sums, inner)
-        ones = jnp.ones((8, BLOCK), bf16)
+        ones = jnp.ones((8, ROWS), bf16)
         half = d0_ref.shape[1]
         inner[:, :half] += dot(ones, d0_ref[...], NN)
         inner[:, half:] += dot(ones, d1_ref[...], NN)
 
-        products[...] = dot(d0_ref[...], w0_ref[...], NT) + dot(d1_ref[...], w1_ref[...], NT)
-
-        def finish(at, grad):
-            grad = s_ref[at, :] + grad
-            normed, rinv = center(f_ref[at, :])
-            found = norm_back(grad, normed, rinv, v_ref[3:4])
-            delta[at, :] = found
-            low[at, :] = found.astype(bf16)
-            add_rows(sums, (found, grad * normed, grad))
-
-        in_parts(products, finish)
+        grad = dot(d0_ref[...], w0_ref[...], NT) + dot(d1_ref[...], w1_ref[...], NT)
+        grad = s_ref[...] + grad
+        normed, rinv = center(f_ref[...])
+        found = norm_back(grad, normed, rinv, v_ref[3:4])
+        delta[...] = found
+        low[...] = found.astype(bf16)
+        add_rows(sums, (found, grad * normed, grad))
 
     width = first_in.shape[1]
     return row_call(
@@ -844,8 +820,6 @@
         if fast and t == 1:
             *pieces_a, c = lax.optimization_barrier((*pieces_a, c))
             one_high_b, two_high_b = swap_dp(high_b, 1, size), swap_dp(high_b, 2, size)
-            pieces_b = [low_b, high_b, one_low_b, one_high_b, two_low_b, two_high_b]
-            pieces_b.append(swap_dp(two_low_b, 1, size))
             wo0, wi0 = place_cols(pieces_a, index, (half, inner_weight.shape[1]), size)
         ctx.append(c)
 
@@ -853,8 +827,9 @@
     wi = (wi0, swap_core(wi0))
     first_in, hidden = first_block(tokens, ctx, wo, vecs)
     if fast:
-        *pieces_b, hidden = lax.optimization_barrier((*pieces_b, hidden))
-        pieces_b.append(swap_dp(pieces_b[3], 2, size))
+        one_high_b, two_low_b, hidden = lax.optimization_barrier((one_high_b, two_low_b, hidden))
+        pieces_b = [low_b, high_b, one_low_b, one_high_b, two_low_b, two_high_b]
+        pieces_b += [swap_dp(two_low_b, 1, size), swap_dp(one_high_b, 2, size)]
     act, slope = [], []
     for t in range(2):
         u = dot(hidden, wi[t], NN) + ib[t]
@@ -900,8 +875,8 @@
 
     if fast:
         table = pack_table(first_sums, second_sums, inner_sums, core, size, half)
-        *first_u, ctx_delta[1], go[0], go[1] = lax.optimization_barrier(
-            (*first_u, ctx_delta[1], *go)
+        *first_u, table, ctx_delta[0], ctx_delta[1], go[0], go[1] = lax.optimization_barrier(
+            (*first_u, table, *ctx_delta, *go)
         )
         sums_u = corner_add(parts_u, first_u)
         got_u = near_back(sums_u, size)

time: 324 us -> 317 us (0.978)
  Pallas kernels: 150 us -> 143 us
  waiting for transfers between devices: 49.3 us -> 44.6 us
  starting transfers between devices: 47.5 us -> 50.8 us
    pallas_call x3, Pallas kernels: 37.2 us -> 31.7 us  [row_call(): pl.pallas_call(kernel, out_shape=[jax.ShapeDtypeStruct((rows, n), d) for...]
    ppermute x39, waiting for transfers between devices: 48.6 us -> 44.1 us  [swap_dp(): return lax.ppermute(value, 'dp', [(i, i ^ mask) for i in range(size)])]
    ppermute x39, starting transfers between devices: 46.3 us -> 49.7 us  [swap_dp(): return lax.ppermute(value, 'dp', [(i, i ^ mask) for i in range(size)])]
    unnamed x129 -> x119, local copies, waits for them, and re-layouts: 16.8 us -> 15.4 us
  transfers between devices with their start and end apart: 48 -> 48, of which waited for: 18 -> 21; matrix products, arithmetic and copies ran while one was open for 14% -> 15% of each run, Pallas kernels for 32% -> 31%
where the time goes in v3:
time: 317 us; the launch traced here: 315 us
  Pallas kernels  143 us (45%)
  matrix products  51.2 us (16%)
  starting transfers between devices  50.8 us (16%)
  waiting for transfers between devices  44.6 us (14%)
  local copies, waits for them, and re-layouts  19.8 us (6%)
  other arithmetic  4.54 us (1%)
    dot_general x12, matrix products, dot(): return lax.dot_general(left, right, dims, preferred_element_type=f32)  51.2 us
    ppermute x39, starting transfers between devices, swap_dp(): return lax.ppermute(value, 'dp', [(i, i ^ mask) for i in range(size)])  49.7 us
    ppermute x39, waiting for transfers between devices, swap_dp(): return lax.ppermute(value, 'dp', [(i, i ^ mask) for i in range(size)])  44.1 us
    pallas_call x4, Pallas kernels, attend_call(): pl.pallas_call(kernel, out_shape=out_shape, grid_spec=pltpu.PrefetchScala...  42.2 us
    pallas_call x3, Pallas kernels, row_call(): pl.pallas_call(kernel, out_shape=[jax.ShapeDtypeStruct((rows, n), d) for...  31.7 us
    unnamed x119, local copies, waits for them, and re-layouts  15.4 us
    pallas_call x2, Pallas kernels, token_gradient(): pl.pallas_call(kernel, out_shape=jax.ShapeDtypeStruct((rows, width), f32)...  12.6 us
    pallas_call x2, Pallas kernels, project(): pl.pallas_call(kernel, out_shape=[jax.ShapeDtypeStruct((rows, cols), bf16...  11.5 us
  transfers between devices with their start and end apart: 48, of which 21 were waited for; matrix products, arithmetic and copies ran while one was open for 15% of the time, Pallas kernels for 31%

profile of v3, /device:TPU:0, one launch (start us, length us, event | category | flops | bytes accessed | tf_op | source)
XLA Modules:
  0.0 315.2 jit_solution(9050036429028150877)
XLA Ops:
  1.9 1.5 shard_map.305
  3.4 3.1 collective-permute-start.1
  6.5 2.5 collective-permute-start.2
  10.0 6.1 %collective-permute-done.2 = bf16[160,384]{1,0:T(8,128)(2,1)S(1)} collective-permute-done((bf16[160,384]{1,0:T(8,128)(2,1)}, bf16[160,384]{1,0:T(8,128)(2,1)S(1)}, u32[]{:S(2)}, u32[]{:S(2)}) %collective-permute-start.2) | collective-permute-done | bytes 122912 | tf_op jit(solution)/shard_map/ppermute | solution.py:31
  16.1 1.6 collective-permute-start.5
  17.7 2.6 collective-permute-done
  21.2 1.6 collective-permute-start.6
  23.3 1.5 collective-permute-start.4
  24.8 1.5 collective-permute-start.9
  26.3 3.8 %collective-permute-done.6.refs_4_ = bf16[2,160,384]{2,1,0:T(8,128)(2,1)S(1)} collective-permute-done((bf16[2,160,384]{2,1,0:T(8,128)(2,1)S(1)}, bf16[2,160,384]{2,1,0:T(8,128)(2,1)S(1)}, u32[]{:S(2)}, u32[]{:S(2)}) %collective-permute-start.6) | collective-permute-done | bytes 245792 | tf_op jit(solution)/shard_map/ppermute | solution.py:31
  30.1 1.5 collective-permute-start.8
  33.4 2.6 copy.37
  36.0 4.7 %collective-permute-done.3 = bf16[48,1920]{1,0:T(8,128)(2,1)S(1)} collective-permute-done((bf16[48,1920]{1,0:T(8,128)(2,1)S(1)}, bf16[48,1920]{1,0:T(8,128)(2,1)S(1)}, u32[]{:S(2)}, u32[]{:S(2)}) %collective-permute-start.3) | collective-permute-done | bytes 184352 | tf_op jit(solution)/shard_map/ppermute | solution.py:31
  41.6 3.0 shard_map.306
  45.5 1.5 collective-permute-start.14
  47.1 5.8 %shard_map.307 = (bf16[1024,384]{1,0:T(8,128)(2,1)}, bf16[1024,384]{1,0:T(8,128)(2,1)}, bf16[1024,384]{1,0:T(8,128)(2,1)}) custom-call(s32[1]{0:T(128)} %bitcast.17.core_ref, bf16[1024,768]{1,0:T(8,128)(2,1)} %x_ref.5, bf16[3,768,384]{2,1,0:T(8,128)(2,1)} %get-tuple-element.165.w_ref.w0_ref, f32[16,768]{1,0:T(8,128)} %get-tuple-element.166.v_ref), custom_call_target="tpu_custom_call" | custom-call | flops 1 | bytes 1 | tf_op jit(solution)/shard_map/pallas_call | solution.py:417
  52.8 3.0 collective-permute-done.10.refs_1_
  57.0 5.7 %shard_map.308 = (bf16[1024,384]{1,0:T(8,128)(2,1)}, bf16[1024,384]{1,0:T(8,128)(2,1)}, bf16[1024,384]{1,0:T(8,128)(2,1)}) custom-call(s32[1]{0:T(128)} %bitcast.17.core_ref, bf16[1024,768]{1,0:T(8,128)(2,1)} %x_ref.5, bf16[3,768,384]{2,1,0:T(8,128)(2,1)} %copy-done, f32[16,768]{1,0:T(8,128)} %get-tuple-element.166.v_ref), custom_call_target="tpu_custom_call" | custom-call | flops 1 | bytes 1 | tf_op jit(solution)/shard_map/pallas_call | solution.py:417
  63.9 1.5 collective-permute-start.16
  66.7 1.8 collective-permute-start.17
  70.2 9.0 %shard_map.309 = (bf16[1024,384]{1,0:T(8,128)(2,1)}, f32[2,3,2,512]{3,2,1,0:T(2,128)}) custom-call(s32[2]{0:T(128)} %dynamic_slice.3.lens, bf16[1024,384]{1,0:T(8,128)(2,1)} %get-tuple-element.178.q_ref, bf16[1024,384]{1,0:T(8,128)(2,1)} %get-tuple-element.179.k_ref, bf16[1024,384]{1,0:T(8,128)(2,1)} %get-tuple-element.180.v_ref), custom_call_target="tpu_custom_call" | custom-call | flops 1 | bytes 1 | tf_op jit(solution)/shard_map/pallas_call | solution.py:692
  82.4 1.5 collective-permute-start.22
  84.0 9.0 %shard_map.310 = (bf16[1024,384]{1,0:T(8,128)(2,1)}, f32[2,3,2,512]{3,2,1,0:T(2,128)}) custom-call(s32[2]{0:T(128)} %dynamic_slice.3.lens, bf16[1024,384]{1,0:T(8,128)(2,1)} %get-tuple-element.192.q_ref, bf16[1024,384]{1,0:T(8,128)(2,1)} %get-tuple-element.193.k_ref, bf16[1024,384]{1,0:T(8,128)(2,1)} %get-tuple-element.194.v_ref), custom_call_target="tpu_custom_call" | custom-call | flops 1 | bytes 1 | tf_op jit(solution)/shard_map/pallas_call | solution.py:692
  93.9 3.6 %shard_map.311 = (bf16[768,384]{1,0:T(8,128)(2,1)}, bf16[768,1536]{1,0:T(8,128)(2,1)}) custom-call(s32[1]{0:T(128)} %bitcast.16.index_ref, bf16[2,48,1920]{2,1,0:T(8,128)(2,1)} %copy-done.19, bf16[2,48,1920]{2,1,0:T(8,128)(2,1)} %copy-done.29, bf16[2,48,1920]{2,1,0:T(8,128)(2,1)} %copy-done.30, bf16[2,48,1920]{2,1,0:T(8,128)(2,1)} %copy-done.32, ...), custom_call_target="tpu_custom_call" | custom-call | flops 1 | bytes 1 | tf_op jit(solution)/shard_map/pallas_call | solution.py:156
  100.9 6.2 %shard_map.312 = (f32[1024,768]{1,0:T(8,128)}, bf16[1024,768]{1,0:T(8,128)(2,1)}) custom-call(bf16[1024,768]{1,0:T(8,128)(2,1)} %x_ref.5, bf16[1024,384]{1,0:T(8,128)(2,1)} %get-tuple-element.184.c0_ref.c_ref, bf16[1024,384]{1,0:T(8,128)(2,1)} %get-tuple-element.196.c1_ref.c_ref, bf16[768,384]{1,0:T(8,128)(2,1)} %get-tuple-element.205.w0_ref, ...), custom_call_target="tpu_custom_call" | custom-call | flops 1 | bytes 1 | tf_op jit(solution)/shard_map/pallas_call | solution.py:499
  109.7 6.8 %multiply_convert_fusion.3 = (bf16[1024,1536]{1,0:T(8,128)(2,1)}, f32[1024,1536]{1,0:T(8,128)}) fusion(f32[1536]{0:T(1024)S(1)} %get-tuple-element.294, bf16[1024,768]{1,0:T(8,128)(2,1)} %get-tuple-element.221.h_ref, bf16[768,1536]{1,0:T(8,128)(2,1)S(1)} %copy-done.11), kind=kOutput, calls=%fused_computation.16 | convolution fusion | flops 2425356288 | bytes 13375488 | tf_op jit(solution)/shard_map/dot_general | solution.py:21
  118.2 3.2 %shard_map.313.w0_ref = bf16[768,1536]{1,0:T(8,128)(2,1)} custom-call(s32[1]{0:T(128)} %bitcast.16.index_ref, bf16[2,48,1536]{2,1,0:T(8,128)(2,1)} %copy-done.20, bf16[2,48,1536]{2,1,0:T(8,128)(2,1)} %copy-done.39, bf16[2,48,1536]{2,1,0:T(8,128)(2,1)} %copy-done.42, bf16[2,48,1536]{2,1,0:T(8,128)(2,1)} %collective-permute-done.20.refs_3_, ...), custom_call_target="tpu_custom_call" | custom-call | flops 1 | bytes 1 | tf_op jit(solution)/shard_map/pallas_call | solution.py:156
  121.4 7.4 %multiply_convert_fusion.2 = (bf16[1024,1536]{1,0:T(8,128)(2,1)}, f32[1024,1536]{1,0:T(8,128)}) fusion(f32[1536]{0:T(1024)S(1)} %get-tuple-element.293, bf16[1024,768]{1,0:T(8,128)(2,1)S(1)} %copy-done.17, bf16[768,1536]{1,0:T(8,128)(2,1)} %collective-permute-done.27.w1_ref), kind=kOutput, calls=%fused_computation.14 | convolution fusion | flops 2425356288 | bytes 13375488 | tf_op jit(solution)/shard_map/dot_general | solution.py:21
  128.8 1.4 copy-done.13
  130.2 12.7 %shard_map.314 = (f32[1024,768]{1,0:T(8,128)}, f32[1024,768]{1,0:T(8,128)}, bf16[1024,768]{1,0:T(8,128)(2,1)}, f32[8,768]{1,0:T(8,128)}) custom-call(bf16[1024,768]{1,0:T(8,128)(2,1)} %get-tuple-element.221.h_ref, bf16[1024,768]{1,0:T(8,128)(2,1)} %c_ref.1, bf16[1024,1536]{1,0:T(8,128)(2,1)} %get-tuple-element.222.a0_ref, ...), custom_call_target="tpu_custom_call" | custom-call | flops 1 | bytes 1 | tf_op jit(solution)/shard_map/pallas_call | solution.py:499
  143.0 4.5 %convolution_convert_fusion.2 = bf16[768,1536]{1,0:T(8,128)(2,1)S(1)} fusion(bf16[1024,768]{1,0:T(8,128)(2,1)} %get-tuple-element.228, bf16[1024,1536]{1,0:T(8,128)(2,1)S(1)} %copy-done.7), kind=kOutput, calls=%fused_computation.20 | convolution fusion | flops 2417098752 | bytes 7077888 | tf_op jit(solution)/shard_map/dot_general | solution.py:21
  148.0 4.1 %convolution_convert_fusion.3.refs_0_ = bf16[768,1536]{1,0:T(8,128)(2,1)} fusion(bf16[1024,768]{1,0:T(8,128)(2,1)S(1)} %copy-done.51, bf16[1024,1536]{1,0:T(8,128)(2,1)S(1)} %copy-done.6), kind=kOutput, calls=%fused_computation.21 | convolution fusion | flops 2417098752 | bytes 7077888 | tf_op jit(solution)/shard_map/dot_general | solution.py:21
  152.2 5.4 %multiply_convert_fusion.d1_ref = bf16[1024,1536]{1,0:T(8,128)(2,1)S(1)} fusion(bf16[1024,768]{1,0:T(8,128)(2,1)S(1)} %copy-done.51, bf16[768,1536]{1,0:T(8,128)(2,1)S(1)} %copy-done.14, f32[1024,1536]{1,0:T(8,128)S(1)} %copy-done.56, f32[1536]{0:T(1024)S(1)} %get-tuple-element.293), kind=kOutput, calls=%fused_computation.12 | convolution fusion | flops 2436366336 | bytes 13375488 | tf_op jit(solution)/shard_map/dot_general | solution.py:21
  157.7 2.9 convolution_convert_fusion
  161.1 5.4 %multiply_convert_fusion.1.d0_ref = bf16[1024,1536]{1,0:T(8,128)(2,1)S(1)} fusion(bf16[1024,768]{1,0:T(8,128)(2,1)S(1)} %copy-done.51, bf16[768,1536]{1,0:T(8,128)(2,1)S(1)} %copy-done.1, f32[1024,1536]{1,0:T(8,128)S(1)} %bitcast.88, f32[1536]{0:T(1024)S(1)} %get-tuple-element.294), kind=kOutput, calls=%fused_computation.13 | convolution fusion | flops 2436366336 | bytes 13375488 | tf_op jit(solution)/shard_map/dot_general | solution.py:21
  166.5 4.0 %convolution_convert_fusion.1.refs_2_ = bf16[768,1536]{1,0:T(8,128)(2,1)} fusion(bf16[1024,768]{1,0:T(8,128)(2,1)S(1)} %copy-done.18, bf16[1024,1536]{1,0:T(8,128)(2,1)S(1)} %multiply_convert_fusion.1.d0_ref), kind=kOutput, calls=%fused_computation.19 | convolution fusion | flops 2417098752 | bytes 7077888 | tf_op jit(solution)/shard_map/dot_general | solution.py:21
  170.5 1.4 copy-done.15
  171.9 6.8 %shard_map.315 = (bf16[4,48,3072]{2,1,0:T(8,128)(2,1)}, bf16[4,48,3072]{2,1,0:T(8,128)(2,1)}, bf16[2,48,3072]{2,1,0:T(8,128)(2,1)}, bf16[2,48,3072]{2,1,0:T(8,128)(2,1)}, bf16[4,48,3072]{2,1,0:T(8,128)(2,1)}) custom-call(s32[1]{0:T(128)} %bitcast.16.index_ref, bf16[768,1536]{1,0:T(8,128)(2,1)} %convolution_convert_fusion.3.refs_0_, ...), custom_call_target="tpu_custom_call" | custom-call | flops 1 | bytes 1 | tf_op jit(solution)/shard_map/pallas_call | solution.py:219
  179.8 1.5 collective-permute-start.32
  181.3 12.7 %shard_map.316 = (f32[1024,768]{1,0:T(8,128)}, bf16[1024,768]{1,0:T(8,128)(2,1)}, f32[8,768]{1,0:T(8,128)}, f32[8,3072]{1,0:T(8,128)}) custom-call(f32[1024,768]{1,0:T(8,128)} %get-tuple-element.233.s_ref, bf16[1024,1536]{1,0:T(8,128)(2,1)} %copy-done.5, bf16[1024,1536]{1,0:T(8,128)(2,1)} %copy-done.4, f32[1024,768]{1,0:T(8,128)} %get-tuple-element.239.f_ref, ...), custom_call_target="tpu_custom_call" | custom-call | flops 1 | bytes 1 | tf_op jit(solution)/shard_map/pallas_call | solution.py:499
  194.1 3.5 %convolution_convert_fusion.6 = bf16[768,384]{1,0:T(8,128)(2,1)} fusion(bf16[1024,768]{1,0:T(8,128)(2,1)} %get-tuple-element.243, bf16[1024,384]{1,0:T(8,128)(2,1)} %get-tuple-element.196.c1_ref.c_ref), kind=kOutput, calls=%fused_computation.24 | convolution fusion | flops 604274688 | bytes 2949120 | tf_op jit(solution)/shard_map/dot_general | solution.py:21
  197.6 1.8 shard_map.317.table_ref
  199.4 3.4 %convolution_convert_fusion.7.r0_ref = bf16[768,384]{1,0:T(8,128)(2,1)} fusion(bf16[1024,768]{1,0:T(8,128)(2,1)} %get-tuple-element.243, bf16[1024,384]{1,0:T(8,128)(2,1)S(1)} %copy-done.8), kind=kOutput, calls=%fused_computation.25 | convolution fusion | flops 604274688 | bytes 2949120 | tf_op jit(solution)/shard_map/dot_general | solution.py:21
  202.8 1.9 convolution_convert_fusion.5.d_ref
  204.7 1.9 convolution_convert_fusion.4.d_ref
  208.8 2.7 shard_map.318
  212.4 1.5 collective-permute-start.35
  213.9 12.2 %shard_map.319.d_ref.d1_ref = bf16[3,1024,384]{2,1,0:T(8,128)(2,1)} custom-call(s32[2]{0:T(128)} %dynamic_slice.3.lens, bf16[1024,384]{1,0:T(8,128)(2,1)} %get-tuple-element.192.q_ref, bf16[1024,384]{1,0:T(8,128)(2,1)} %get-tuple-element.193.k_ref, bf16[1024,384]{1,0:T(8,128)(2,1)} %get-tuple-element.194.v_ref, ...), custom_call_target="tpu_custom_call" | custom-call | flops 1 | bytes 1 | tf_op jit(solution)/shard_map/pallas_call | solution.py:692
  228.3 3.5 %shard_map.320 = (f32[48,3072]{1,0:T(8,128)}, bf16[48,3072]{1,0:T(8,128)(2,1)}, bf16[48,3072]{1,0:T(8,128)(2,1)}, bf16[48,3072]{1,0:T(8,128)(2,1)}) custom-call(bf16[4,48,3072]{2,1,0:T(8,128)(2,1)} %get-tuple-element.235.own_ref, bf16[4,48,3072]{2,1,0:T(8,128)(2,1)} %copy-done.2, bf16[4,48,3072]{2,1,0:T(8,128)(2,1)} %copy-done.3, ...), custom_call_target="tpu_custom_call" | custom-call | flops 1 | bytes 1 | tf_op jit(solution)/shard_map/pallas_call | solution.py:353
  231.9 5.9 %shard_map.321 = (bf16[3,768,384]{2,1,0:T(8,128)(2,1)}, f32[3,8,384]{2,1,0:T(8,128)}) custom-call(bf16[768,1024]{1,0:T(8,128)(2,1)} %bitcast.68, bf16[3,1024,384]{2,1,0:T(8,128)(2,1)} %shard_map.319.d_ref.d1_ref), custom_call_target="tpu_custom_call" | custom-call | flops 1 | bytes 1 | tf_op jit(solution)/shard_map/pallas_call | solution.py:240
  237.8 1.5 collective-permute-start.39
  239.2 1.4 collective-permute-start.40
  240.7 1.5 collective-permute-start.41
  242.8 12.0 %shard_map.322.d_ref.d0_ref = bf16[3,1024,384]{2,1,0:T(8,128)(2,1)} custom-call(s32[2]{0:T(128)} %dynamic_slice.3.lens, bf16[1024,384]{1,0:T(8,128)(2,1)} %get-tuple-element.178.q_ref, bf16[1024,384]{1,0:T(8,128)(2,1)} %get-tuple-element.179.k_ref, bf16[1024,384]{1,0:T(8,128)(2,1)} %get-tuple-element.180.v_ref, ...), custom_call_target="tpu_custom_call" | custom-call | flops 1 | bytes 1 | tf_op jit(solution)/shard_map/pallas_call | solution.py:692
  256.0 8.1 %shard_map.323 = (bf16[4,208,384]{2,1,0:T(8,128)(2,1)}, bf16[4,208,384]{2,1,0:T(8,128)(2,1)}, bf16[2,208,384]{2,1,0:T(8,128)(2,1)}, bf16[2,208,384]{2,1,0:T(8,128)(2,1)}, bf16[4,208,384]{2,1,0:T(8,128)(2,1)}) custom-call(s32[2]{0:T(128)} %pad_add_fusion.at_ref, bf16[768,1024]{1,0:T(8,128)(2,1)} %bitcast.69, bf16[3,1024,384]{2,1,0:T(8,128)(2,1)} %shard_map.322.d_ref.d0_ref, ...), custom_call_target="tpu_custom_call" | custom-call | flops 1 | bytes 1 | tf_op jit(solution)/shard_map/pallas_call | solution.py:296
  265.9 6.3 %shard_map.324.f_ref = f32[1024,768]{1,0:T(8,128)} custom-call(f32[1024,768]{1,0:T(8,128)} %get-tuple-element.274.f_ref, bf16[3,1024,384]{2,1,0:T(8,128)(2,1)} %shard_map.322.d_ref.d0_ref, bf16[3,1024,384]{2,1,0:T(8,128)(2,1)} %shard_map.319.d_ref.d1_ref, bf16[3,768,384]{2,1,0:T(8,128)(2,1)} %get-tuple-element.165.w_ref.w0_ref, ...), custom_call_target="tpu_custom_call", output_to_operand_aliasing={{}: (0, {})} | custom-call | flops 1811939328 | bytes 3145728 | tf_op jit(solution)/shard_map/pallas_call | solution.py:449
  272.3 8.0 %collective-permute-done.37.r1_ref.f1_ref = bf16[4,208,384]{2,1,0:T(8,128)(2,1)S(1)} collective-permute-done((bf16[4,208,384]{2,1,0:T(8,128)(2,1)}, bf16[4,208,384]{2,1,0:T(8,128)(2,1)S(1)}, u32[]{:S(2)}, u32[]{:S(2)}) %collective-permute-start.37) | collective-permute-done | bytes 639008 | tf_op jit(solution)/shard_map/ppermute | solution.py:31
  281.8 2.1 shard_map.325
  286.7 5.5 %collective-permute-done.42.r1_ref = bf16[2,208,384]{2,1,0:T(8,128)(2,1)S(1)} collective-permute-done((bf16[2,208,384]{2,1,0:T(8,128)(2,1)}, bf16[2,208,384]{2,1,0:T(8,128)(2,1)S(1)}, u32[]{:S(2)}, u32[]{:S(2)}) %collective-permute-start.42) | collective-permute-done | bytes 319520 | tf_op jit(solution)/shard_map/ppermute | solution.py:31
  293.6 2.6 shard_map.326
  296.3 4.1 %collective-permute-start.44 = (bf16[208,384]{1,0:T(8,128)(2,1)}, bf16[208,384]{1,0:T(8,128)(2,1)S(1)}, u32[]{:S(2)}, u32[]{:S(2)}) collective-permute-start(bf16[208,384]{1,0:T(8,128)(2,1)} %get-tuple-element.287), channel_id=1, source_target_pairs={{0,8},{2,10},{4,12},{6,14},{8,0},{10,2},{12,4},{14,6},{16,24},{18,... | collective-permute-start | bytes 479240 | tf_op jit(solution)/shard_map/ppermute | solution.py:31
  300.4 2.4 collective-permute-start.46
  302.8 6.3 %shard_map.327 = f32[1024,768]{1,0:T(8,128)} custom-call(f32[1024,768]{1,0:T(8,128)} %shard_map.324.f_ref, bf16[3,1024,384]{2,1,0:T(8,128)(2,1)} %shard_map.322.d_ref.d0_ref, bf16[3,1024,384]{2,1,0:T(8,128)(2,1)} %shard_map.319.d_ref.d1_ref, bf16[3,768,384]{2,1,0:T(8,128)(2,1)} %get-tuple-element.165.w_ref.w0_ref, ...), custom_call_target="tpu_custom_call", output_to_operand_aliasing={{}: (0, {})} | custom-call | flops 1811939328 | bytes 3145728 | tf_op jit(solution)/shard_map/pallas_call | solution.py:449
  309.1 3.6 %collective-permute-done.45 = bf16[208,384]{1,0:T(8,128)(2,1)S(1)} collective-permute-done((bf16[208,384]{1,0:T(8,128)(2,1)}, bf16[208,384]{1,0:T(8,128)(2,1)S(1)}, u32[]{:S(2)}, u32[]{:S(2)}) %collective-permute-start.45) | collective-permute-done | bytes 159776 | tf_op jit(solution)/shard_map/ppermute | solution.py:31
  (204 shorter events, 43.8 us)
Async XLA Ops:
  3.4 6.6 %collective-permute-start.1 = (bf16[160,384]{1,0:T(8,128)(2,1)}, bf16[160,384]{1,0:T(8,128)(2,1)S(1)}, u32[]{:S(2)}, u32[]{:S(2)}) collective-permute-start(bf16[160,384]{1,0:T(8,128)(2,1)} %shard_map.305), channel_id=1, source_target_pairs={{0,8},{2,10},{4,12},{6,14},{8,0},{10,2},{12,4},{14,6},{16,24},{18,... | collective-permute-start | bytes 368648 | tf_op jit(solution)/shard_map/ppermute | solution.py:31
  6.5 9.6 %collective-permute-start.2 = (bf16[160,384]{1,0:T(8,128)(2,1)}, bf16[160,384]{1,0:T(8,128)(2,1)S(1)}, u32[]{:S(2)}, u32[]{:S(2)}) collective-permute-start(bf16[160,384]{1,0:T(8,128)(2,1)} %shard_map.305), channel_id=1, source_target_pairs={{0,24},{2,26},{4,28},{6,30},{8,16},{10,18},{12,20},{14,22},{16,8},... | collective-permute-start | bytes 368648 | tf_op jit(solution)/shard_map/ppermute | solution.py:31
  9.0 11.3 %collective-permute-start = (bf16[160,384]{1,0:T(8,128)(2,1)}, bf16[160,384]{1,0:T(8,128)(2,1)S(1)}, u32[]{:S(2)}, u32[]{:S(2)}) collective-permute-start(bf16[160,384]{1,0:T(8,128)(2,1)} %shard_map.305), channel_id=1, source_target_pairs={{0,16},{2,18},{4,20},{6,22},{8,24},{10,26},{12,28},{14,30},{16,0},... | collective-permute-start | bytes 368648 | tf_op jit(solution)/shard_map/ppermute | solution.py:31
  16.1 24.7 %copy-start.21 = (bf16[2,160,384]{2,1,0:T(8,128)(2,1)}, bf16[2,160,384]{2,1,0:T(8,128)(2,1)S(1)}, u32[]{:S(2)}) copy-start(bf16[2,160,384]{2,1,0:T(8,128)(2,1)S(1)} %pad_maximum_fusion.3.refs_1_) | copy-start | bytes 737284
  16.1 8.7 %collective-permute-start.5 = (bf16[2,160,384]{2,1,0:T(8,128)(2,1)S(1)}, bf16[2,160,384]{2,1,0:T(8,128)(2,1)S(1)}, u32[]{:S(2)}, u32[]{:S(2)}) collective-permute-start(bf16[2,160,384]{2,1,0:T(8,128)(2,1)S(1)} %pad_maximum_fusion.3.refs_1_), channel_id=1, source_target_pairs={{0,2},{2,0},{4,6},{6,4},{8,10},{10,8},{12,14},{14,12},{16,18},{18,... | collective-permute-start | bytes 737288 | tf_op jit(solution)/shard_map/ppermute | solution.py:31
  21.2 19.6 %copy-start.22 = (bf16[2,160,384]{2,1,0:T(8,128)(2,1)}, bf16[2,160,384]{2,1,0:T(8,128)(2,1)S(1)}, u32[]{:S(2)}) copy-start(bf16[2,160,384]{2,1,0:T(8,128)(2,1)S(1)} %pad_maximum_fusion.2.refs_0_) | copy-start | bytes 737284
  21.2 8.9 %collective-permute-start.6 = (bf16[2,160,384]{2,1,0:T(8,128)(2,1)S(1)}, bf16[2,160,384]{2,1,0:T(8,128)(2,1)S(1)}, u32[]{:S(2)}, u32[]{:S(2)}) collective-permute-start(bf16[2,160,384]{2,1,0:T(8,128)(2,1)S(1)} %pad_maximum_fusion.2.refs_0_), channel_id=1, source_target_pairs={{0,4},{2,6},{4,0},{6,2},{8,12},{10,14},{12,8},{14,10},{16,20},{18,... | collective-permute-start | bytes 737288 | tf_op jit(solution)/shard_map/ppermute | solution.py:31
  22.8 17.9 %collective-permute-start.7 = (bf16[2,160,384]{2,1,0:T(8,128)(2,1)S(1)}, bf16[2,160,384]{2,1,0:T(8,128)(2,1)S(1)}, u32[]{:S(2)}, u32[]{:S(2)}) collective-permute-start(bf16[2,160,384]{2,1,0:T(8,128)(2,1)S(1)} %pad_maximum_fusion.3.refs_1_), channel_id=1, source_target_pairs={{0,4},{2,6},{4,0},{6,2},{8,12},{10,14},{12,8},{14,10},{16,20},{18,... | collective-permute-start | bytes 737288 | tf_op jit(solution)/shard_map/ppermute | solution.py:31
  23.3 17.4 %collective-permute-start.4 = (bf16[2,160,384]{2,1,0:T(8,128)(2,1)S(1)}, bf16[2,160,384]{2,1,0:T(8,128)(2,1)S(1)}, u32[]{:S(2)}, u32[]{:S(2)}) collective-permute-start(bf16[2,160,384]{2,1,0:T(8,128)(2,1)S(1)} %pad_maximum_fusion.2.refs_0_), channel_id=1, source_target_pairs={{0,2},{2,0},{4,6},{6,4},{8,10},{10,8},{12,14},{14,12},{16,18},{18,... | collective-permute-start | bytes 737288 | tf_op jit(solution)/shard_map/ppermute | solution.py:31
  24.8 16.0 %copy-start.45 = (bf16[2,160,384]{2,1,0:T(8,128)(2,1)}, bf16[2,160,384]{2,1,0:T(8,128)(2,1)S(1)}, u32[]{:S(2)}) copy-start(bf16[2,160,384]{2,1,0:T(8,128)(2,1)S(1)} %collective-permute-done.5.refs_3_) | copy-start | bytes 737284
  24.8 15.9 %collective-permute-start.9 = (bf16[2,160,384]{2,1,0:T(8,128)(2,1)S(1)}, bf16[2,160,384]{2,1,0:T(8,128)(2,1)S(1)}, u32[]{:S(2)}, u32[]{:S(2)}) collective-permute-start(bf16[2,160,384]{2,1,0:T(8,128)(2,1)S(1)} %collective-permute-done.5.refs_3_), channel_id=1, source_target_pairs={{0,4},{2,6},{4,0},{6,2},{8,12},{10,14},{12,8},{14,10},{16,20},{18,... | collective-permute-start | bytes 737288 | tf_op jit(solution)/shard_map/ppermute | solution.py:31
  30.1 10.7 %copy-start.46 = (bf16[2,160,384]{2,1,0:T(8,128)(2,1)}, bf16[2,160,384]{2,1,0:T(8,128)(2,1)S(1)}, u32[]{:S(2)}) copy-start(bf16[2,160,384]{2,1,0:T(8,128)(2,1)S(1)} %collective-permute-done.6.refs_4_) | copy-start | bytes 737284
  30.1 10.6 %collective-permute-start.8 = (bf16[2,160,384]{2,1,0:T(8,128)(2,1)S(1)}, bf16[2,160,384]{2,1,0:T(8,128)(2,1)S(1)}, u32[]{:S(2)}, u32[]{:S(2)}) collective-permute-start(bf16[2,160,384]{2,1,0:T(8,128)(2,1)S(1)} %collective-permute-done.6.refs_4_), channel_id=1, source_target_pairs={{0,2},{2,0},{4,6},{6,4},{8,10},{10,8},{12,14},{14,12},{16,18},{18,... | collective-permute-start | bytes 737288 | tf_op jit(solution)/shard_map/ppermute | solution.py:31
  32.5 8.2 %collective-permute-start.3 = (bf16[48,1920]{1,0:T(8,128)(2,1)S(1)}, bf16[48,1920]{1,0:T(8,128)(2,1)S(1)}, u32[]{:S(2)}, u32[]{:S(2)}) collective-permute-start(bf16[48,1920]{1,0:T(8,128)(2,1)S(1)} %get-tuple-element.155), channel_id=1, source_target_pairs={{0,16},{2,18},{4,20},{6,22},{8,24},{10,26},{12,28},{14,30},{16,0},... | collective-permute-start | bytes 552968 | tf_op jit(solution)/shard_map/ppermute | solution.py:31
  44.7 11.1 %collective-permute-start.11 = (bf16[3,768,384]{2,1,0:T(8,128)(2,1)}, bf16[3,768,384]{2,1,0:T(8,128)(2,1)S(1)}, u32[]{:S(2)}, u32[]{:S(2)}) collective-permute-start(bf16[3,768,384]{2,1,0:T(8,128)(2,1)} %get-tuple-element.165.w_ref.w0_ref), channel_id=1, source_target_pairs={{0,1},{1,0},{2,3},{3,2},{4,5},{5,4},{6,7},{7,6},{8,9},{9,8},{10,11... | collective-permute-start | bytes 5308424 | tf_op jit(solution)/shard_map/ppermute | solution.py:35
  44.7 18.0 %copy-start.19 = (bf16[2,48,1920]{2,1,0:T(8,128)(2,1)}, bf16[2,48,1920]{2,1,0:T(8,128)(2,1)S(1)}, u32[]{:S(2)}) copy-start(bf16[2,48,1920]{2,1,0:T(8,128)(2,1)S(1)} %pad_maximum_fusion.refs_0_) | copy-start | bytes 1105924
  44.7 11.1 %collective-permute-start.10 = (bf16[2,48,1920]{2,1,0:T(8,128)(2,1)S(1)}, bf16[2,48,1920]{2,1,0:T(8,128)(2,1)S(1)}, u32[]{:S(2)}, u32[]{:S(2)}) collective-permute-start(bf16[2,48,1920]{2,1,0:T(8,128)(2,1)S(1)} %pad_maximum_fusion.refs_0_), channel_id=1, source_target_pairs={{0,8},{2,10},{4,12},{6,14},{8,0},{10,2},{12,4},{14,6},{16,24},{18,... | collective-permute-start | bytes 1105928 | tf_op jit(solution)/shard_map/ppermute | solution.py:31
  44.8 20.6 %collective-permute-start.13 = (bf16[2,48,1920]{2,1,0:T(8,128)(2,1)S(1)}, bf16[2,48,1920]{2,1,0:T(8,128)(2,1)S(1)}, u32[]{:S(2)}, u32[]{:S(2)}) collective-permute-start(bf16[2,48,1920]{2,1,0:T(8,128)(2,1)S(1)} %pad_maximum_fusion.refs_0_), channel_id=1, source_target_pairs={{0,2},{2,0},{4,6},{6,4},{8,10},{10,8},{12,14},{14,12},{16,18},{18,... | collective-permute-start | bytes 1105928 | tf_op jit(solution)/shard_map/ppermute | solution.py:31
  45.5 19.9 %collective-permute-start.14 = (bf16[2,48,1920]{2,1,0:T(8,128)(2,1)S(1)}, bf16[2,48,1920]{2,1,0:T(8,128)(2,1)S(1)}, u32[]{:S(2)}, u32[]{:S(2)}) collective-permute-start(bf16[2,48,1920]{2,1,0:T(8,128)(2,1)S(1)} %pad_maximum_fusion.refs_0_), channel_id=1, source_target_pairs={{0,4},{2,6},{4,0},{6,2},{8,12},{10,14},{12,8},{14,10},{16,20},{18,... | collective-permute-start | bytes 1105928 | tf_op jit(solution)/shard_map/ppermute | solution.py:31
  47.1 22.6 %copy-start.55 = (s32[4]{0:T(128)S(1)}, s32[4]{0:T(128)}, u32[]{:S(2)}) copy-start(s32[4]{0:T(128)} %param.20) | copy-start | bytes 52
  55.8 37.2 %copy-start.29 = (bf16[2,48,1920]{2,1,0:T(8,128)(2,1)}, bf16[2,48,1920]{2,1,0:T(8,128)(2,1)S(1)}, u32[]{:S(2)}) copy-start(bf16[2,48,1920]{2,1,0:T(8,128)(2,1)S(1)} %collective-permute-done.10.refs_1_) | copy-start | bytes 1105924
  55.8 9.8 %collective-permute-start.12 = (bf16[48,1536]{1,0:T(8,128)(2,1)}, bf16[48,1536]{1,0:T(8,128)(2,1)}, u32[]{:S(2)}, u32[]{:S(2)}) collective-permute-start(bf16[48,1536]{1,0:T(8,128)(2,1)} %bitcast.72), channel_id=1, source_target_pairs={{0,16},{2,18},{4,20},{6,22},{8,24},{10,26},{12,28},{14,30},{16,0},... | collective-permute-start | bytes 442376 | tf_op jit(solution)/shard_map/ppermute | solution.py:31
  62.8 16.5 %collective-permute-start.15 = (bf16[2,48,1920]{2,1,0:T(8,128)(2,1)S(1)}, bf16[2,48,1920]{2,1,0:T(8,128)(2,1)S(1)}, u32[]{:S(2)}, u32[]{:S(2)}) collective-permute-start(bf16[2,48,1920]{2,1,0:T(8,128)(2,1)S(1)} %collective-permute-done.10.refs_1_), channel_id=1, source_target_pairs={{0,2},{2,0},{4,6},{6,4},{8,10},{10,8},{12,14},{14,12},{16,18},{18,... | collective-permute-start | bytes 1105928 | tf_op jit(solution)/shard_map/ppermute | solution.py:31
  63.9 15.4 %collective-permute-start.16 = (bf16[2,48,1920]{2,1,0:T(8,128)(2,1)S(1)}, bf16[2,48,1920]{2,1,0:T(8,128)(2,1)S(1)}, u32[]{:S(2)}, u32[]{:S(2)}) collective-permute-start(bf16[2,48,1920]{2,1,0:T(8,128)(2,1)S(1)} %collective-permute-done.10.refs_1_), channel_id=1, source_target_pairs={{0,4},{2,6},{4,0},{6,2},{8,12},{10,14},{12,8},{14,10},{16,20},{18,... | collective-permute-start | bytes 1105928 | tf_op jit(solution)/shard_map/ppermute | solution.py:31
  65.4 27.6 %copy-start.30 = (bf16[2,48,1920]{2,1,0:T(8,128)(2,1)}, bf16[2,48,1920]{2,1,0:T(8,128)(2,1)S(1)}, u32[]{:S(2)}) copy-start(bf16[2,48,1920]{2,1,0:T(8,128)(2,1)S(1)} %collective-permute-done.13.refs_2_) | copy-start | bytes 1105924
  65.4 27.6 %copy-start.31 = (bf16[2,48,1920]{2,1,0:T(8,128)(2,1)}, bf16[2,48,1920]{2,1,0:T(8,128)(2,1)S(1)}, u32[]{:S(2)}) copy-start(bf16[2,48,1920]{2,1,0:T(8,128)(2,1)S(1)} %collective-permute-done.14.refs_4_) | copy-start | bytes 1105924
  66.7 30.8 %copy-start.20 = (bf16[2,48,1536]{2,1,0:T(8,128)(2,1)}, bf16[2,48,1536]{2,1,0:T(8,128)(2,1)S(1)}, u32[]{:S(2)}) copy-start(bf16[2,48,1536]{2,1,0:T(8,128)(2,1)S(1)} %pad_maximum_fusion.1.refs_0_) | copy-start | bytes 884740
  66.7 12.6 %collective-permute-start.17 = (bf16[2,48,1536]{2,1,0:T(8,128)(2,1)S(1)}, bf16[2,48,1536]{2,1,0:T(8,128)(2,1)S(1)}, u32[]{:S(2)}, u32[]{:S(2)}) collective-permute-start(bf16[2,48,1536]{2,1,0:T(8,128)(2,1)S(1)} %pad_maximum_fusion.1.refs_0_), channel_id=1, source_target_pairs={{0,8},{2,10},{4,12},{6,14},{8,0},{10,2},{12,4},{14,6},{16,24},{18,... | collective-permute-start | bytes 884744 | tf_op jit(solution)/shard_map/ppermute | solution.py:31
  68.5 11.5 %collective-permute-start.18 = (bf16[2,48,1536]{2,1,0:T(8,128)(2,1)S(1)}, bf16[2,48,1536]{2,1,0:T(8,128)(2,1)S(1)}, u32[]{:S(2)}, u32[]{:S(2)}) collective-permute-start(bf16[2,48,1536]{2,1,0:T(8,128)(2,1)S(1)} %pad_maximum_fusion.1.refs_0_), channel_id=1, source_target_pairs={{0,4},{2,6},{4,0},{6,2},{8,12},{10,14},{12,8},{14,10},{16,20},{18,... | collective-permute-start | bytes 884744 | tf_op jit(solution)/shard_map/ppermute | solution.py:31
  69.0 11.0 %collective-permute-start.19 = (bf16[2,48,1536]{2,1,0:T(8,128)(2,1)S(1)}, bf16[2,48,1536]{2,1,0:T(8,128)(2,1)S(1)}, u32[]{:S(2)}, u32[]{:S(2)}) collective-permute-start(bf16[2,48,1536]{2,1,0:T(8,128)(2,1)S(1)} %pad_maximum_fusion.1.refs_0_), channel_id=1, source_target_pairs={{0,2},{2,0},{4,6},{6,4},{8,10},{10,8},{12,14},{14,12},{16,18},{18,... | collective-permute-start | bytes 884744 | tf_op jit(solution)/shard_map/ppermute | solution.py:31
  79.2 13.8 %copy-start.32 = (bf16[2,48,1920]{2,1,0:T(8,128)(2,1)}, bf16[2,48,1920]{2,1,0:T(8,128)(2,1)S(1)}, u32[]{:S(2)}) copy-start(bf16[2,48,1920]{2,1,0:T(8,128)(2,1)S(1)} %collective-permute-done.15.refs_3_) | copy-start | bytes 1105924
  79.3 13.8 %copy-start.33 = (bf16[2,48,1920]{2,1,0:T(8,128)(2,1)}, bf16[2,48,1920]{2,1,0:T(8,128)(2,1)S(1)}, u32[]{:S(2)}) copy-start(bf16[2,48,1920]{2,1,0:T(8,128)(2,1)S(1)} %collective-permute-done.16.refs_5_) | copy-start | bytes 1105924
  81.5 11.5 %collective-permute-start.21 = (bf16[2,48,1920]{2,1,0:T(8,128)(2,1)S(1)}, bf16[2,48,1920]{2,1,0:T(8,128)(2,1)S(1)}, u32[]{:S(2)}, u32[]{:S(2)}) collective-permute-start(bf16[2,48,1920]{2,1,0:T(8,128)(2,1)S(1)} %collective-permute-done.14.refs_4_), channel_id=1, source_target_pairs={{0,2},{2,0},{4,6},{6,4},{8,10},{10,8},{12,14},{14,12},{16,18},{18,... | collective-permute-start | bytes 1105928 | tf_op jit(solution)/shard_map/ppermute | solution.py:31
  82.4 10.5 %collective-permute-start.22 = (bf16[2,48,1920]{2,1,0:T(8,128)(2,1)S(1)}, bf16[2,48,1920]{2,1,0:T(8,128)(2,1)S(1)}, u32[]{:S(2)}, u32[]{:S(2)}) collective-permute-start(bf16[2,48,1920]{2,1,0:T(8,128)(2,1)S(1)} %collective-permute-done.15.refs_3_), channel_id=1, source_target_pairs={{0,4},{2,6},{4,0},{6,2},{8,12},{10,14},{12,8},{14,10},{16,20},{18,... | collective-permute-start | bytes 1105928 | tf_op jit(solution)/shard_map/ppermute | solution.py:31
  97.5 12.2 %copy-start.11 = (bf16[768,1536]{1,0:T(8,128)(2,1)S(1)}, bf16[768,1536]{1,0:T(8,128)(2,1)}, u32[]{:S(2)}) copy-start(bf16[768,1536]{1,0:T(8,128)(2,1)} %get-tuple-element.211.w0_ref) | copy-start | bytes 7077892
  97.5 2.6 collective-permute-start.23
  97.6 9.7 %collective-permute-start.20 = (bf16[2,48,1536]{2,1,0:T(8,128)(2,1)}, bf16[2,48,1536]{2,1,0:T(8,128)(2,1)}, u32[]{:S(2)}, u32[]{:S(2)}) collective-permute-start(bf16[2,48,1536]{2,1,0:T(8,128)(2,1)} %copy-done.39), channel_id=1, source_target_pairs={{0,2},{2,0},{4,6},{6,4},{8,10},{10,8},{12,14},{14,12},{16,18},{18,... | collective-permute-start | bytes 884744 | tf_op jit(solution)/shard_map/ppermute | solution.py:31
  99.5 17.0 %collective-permute-start.24 = (bf16[2,48,1536]{2,1,0:T(8,128)(2,1)}, bf16[2,48,1536]{2,1,0:T(8,128)(2,1)}, u32[]{:S(2)}, u32[]{:S(2)}) collective-permute-start(bf16[2,48,1536]{2,1,0:T(8,128)(2,1)} %copy-done.39), channel_id=1, source_target_pairs={{0,4},{2,6},{4,0},{6,2},{8,12},{10,14},{12,8},{14,10},{16,20},{18,... | collective-permute-start | bytes 884744 | tf_op jit(solution)/shard_map/ppermute | solution.py:31
  100.1 21.4 %collective-permute-start.27 = (bf16[768,1536]{1,0:T(8,128)(2,1)}, bf16[768,1536]{1,0:T(8,128)(2,1)}, u32[]{:S(2)}, u32[]{:S(2)}) collective-permute-start(bf16[768,1536]{1,0:T(8,128)(2,1)} %get-tuple-element.211.w0_ref), channel_id=1, source_target_pairs={{0,1},{1,0},{2,3},{3,2},{4,5},{5,4},{6,7},{7,6},{8,9},{9,8},{10,11... | collective-permute-start | bytes 7077896 | tf_op jit(solution)/shard_map/ppermute | solution.py:35
  107.3 9.3 %collective-permute-start.25 = (bf16[2,48,1536]{2,1,0:T(8,128)(2,1)S(1)}, bf16[2,48,1536]{2,1,0:T(8,128)(2,1)S(1)}, u32[]{:S(2)}, u32[]{:S(2)}) collective-permute-start(bf16[2,48,1536]{2,1,0:T(8,128)(2,1)S(1)} %copy-done.41), channel_id=1, source_target_pairs={{0,2},{2,0},{4,6},{6,4},{8,10},{10,8},{12,14},{14,12},{16,18},{18,... | collective-permute-start | bytes 884744 | tf_op jit(solution)/shard_map/ppermute | solution.py:31
  108.4 9.1 %collective-permute-start.26 = (bf16[2,48,1536]{2,1,0:T(8,128)(2,1)}, bf16[2,48,1536]{2,1,0:T(8,128)(2,1)S(1)}, u32[]{:S(2)}, u32[]{:S(2)}) collective-permute-start(bf16[2,48,1536]{2,1,0:T(8,128)(2,1)} %collective-permute-done.20.refs_3_), channel_id=1, source_target_pairs={{0,4},{2,6},{4,0},{6,2},{8,12},{10,14},{12,8},{14,10},{16,20},{18,... | collective-permute-start | bytes 884744 | tf_op jit(solution)/shard_map/ppermute | solution.py:31
  121.4 7.4 %collective-permute-start.28 = (bf16[768,1536]{1,0:T(8,128)(2,1)}, bf16[768,1536]{1,0:T(8,128)(2,1)S(1)}, u32[]{:S(2)}, u32[]{:S(2)}) collective-permute-start(bf16[768,1536]{1,0:T(8,128)(2,1)} %shard_map.313.w0_ref), channel_id=1, source_target_pairs={{0,1},{1,0},{2,3},{3,2},{4,5},{5,4},{6,7},{7,6},{8,9},{9,8},{10,11... | collective-permute-start | bytes 7077896 | tf_op jit(solution)/shard_map/ppermute | solution.py:35
  130.2 12.7 %copy-start.7 = (bf16[1024,1536]{1,0:T(8,128)(2,1)S(1)}, bf16[1024,1536]{1,0:T(8,128)(2,1)}, u32[]{:S(2)}) copy-start(bf16[1024,1536]{1,0:T(8,128)(2,1)} %get-tuple-element.313.a1_ref) | copy-start | bytes 9437188
  147.5 4.7 %collective-permute-start.29 = (bf16[768,1536]{1,0:T(8,128)(2,1)S(1)}, bf16[768,1536]{1,0:T(8,128)(2,1)S(1)}, u32[]{:S(2)}, u32[]{:S(2)}) collective-permute-start(bf16[768,1536]{1,0:T(8,128)(2,1)S(1)} %convolution_convert_fusion.2), channel_id=1, source_target_pairs={{0,1},{1,0},{2,3},{3,2},{4,5},{5,4},{6,7},{7,6},{8,9},{9,8},{10,11... | collective-permute-start | bytes 7077896 | tf_op jit(solution)/shard_map/ppermute | solution.py:35
  148.0 13.0 %slice-start = ((s8[6291456]{0:T(1024)(128)(4,1)}), s8[4194304]{0:T(1024)(128)(4,1)S(1)}, s32[]{:S(2)}) async-start(s8[6291456]{0:T(1024)(128)(4,1)} %bitcast.87), calls=%async_computation | async-start | bytes 8388608
  160.6 9.8 %collective-permute-start.30 = (bf16[768,1536]{1,0:T(8,128)(2,1)S(1)}, bf16[768,1536]{1,0:T(8,128)(2,1)S(1)}, u32[]{:S(2)}, u32[]{:S(2)}) collective-permute-start(bf16[768,1536]{1,0:T(8,128)(2,1)S(1)} %convolution_convert_fusion), channel_id=1, source_target_pairs={{0,1},{1,0},{2,3},{3,2},{4,5},{5,4},{6,7},{7,6},{8,9},{9,8},{10,11... | collective-permute-start | bytes 7077896 | tf_op jit(solution)/shard_map/ppermute | solution.py:35
  178.7 28.2 %collective-permute-start.31 = (bf16[4,48,3072]{2,1,0:T(8,128)(2,1)}, bf16[4,48,3072]{2,1,0:T(8,128)(2,1)S(1)}, u32[]{:S(2)}, u32[]{:S(2)}) collective-permute-start(bf16[4,48,3072]{2,1,0:T(8,128)(2,1)} %get-tuple-element.231), channel_id=1, source_target_pairs={{0,2},{2,0},{4,6},{6,4},{8,10},{10,8},{12,14},{14,12},{16,18},{18,... | collective-permute-start | bytes 3538952 | tf_op jit(solution)/shard_map/ppermute | solution.py:31
  179.8 27.9 %collective-permute-start.32 = (bf16[4,48,3072]{2,1,0:T(8,128)(2,1)}, bf16[4,48,3072]{2,1,0:T(8,128)(2,1)S(1)}, u32[]{:S(2)}, u32[]{:S(2)}) collective-permute-start(bf16[4,48,3072]{2,1,0:T(8,128)(2,1)} %get-tuple-element.232), channel_id=1, source_target_pairs={{0,4},{2,6},{4,0},{6,2},{8,12},{10,14},{12,8},{14,10},{16,20},{18,... | collective-permute-start | bytes 3538952 | tf_op jit(solution)/shard_map/ppermute | solution.py:31
  197.6 9.0 %collective-permute-start.33 = (bf16[768,384]{1,0:T(8,128)(2,1)}, bf16[768,384]{1,0:T(8,128)(2,1)}, u32[]{:S(2)}, u32[]{:S(2)}) collective-permute-start(bf16[768,384]{1,0:T(8,128)(2,1)} %convolution_convert_fusion.6), channel_id=1, source_target_pairs={{0,1},{1,0},{2,3},{3,2},{4,5},{5,4},{6,7},{7,6},{8,9},{9,8},{10,11... | collective-permute-start | bytes 1769480 | tf_op jit(solution)/shard_map/ppermute | solution.py:35
  211.5 15.2 %collective-permute-start.34 = (bf16[2,48,3072]{2,1,0:T(8,128)(2,1)}, bf16[2,48,3072]{2,1,0:T(8,128)(2,1)S(1)}, u32[]{:S(2)}, u32[]{:S(2)}) collective-permute-start(bf16[2,48,3072]{2,1,0:T(8,128)(2,1)} %get-tuple-element.249), channel_id=1, source_target_pairs={{0,2},{2,0},{4,6},{6,4},{8,10},{10,8},{12,14},{14,12},{16,18},{18,... | collective-permute-start | bytes 1769480 | tf_op jit(solution)/shard_map/ppermute | solution.py:31
  212.4 14.9 %collective-permute-start.35 = (bf16[2,48,3072]{2,1,0:T(8,128)(2,1)}, bf16[2,48,3072]{2,1,0:T(8,128)(2,1)S(1)}, u32[]{:S(2)}, u32[]{:S(2)}) collective-permute-start(bf16[2,48,3072]{2,1,0:T(8,128)(2,1)} %get-tuple-element.250), channel_id=1, source_target_pairs={{0,4},{2,6},{4,0},{6,2},{8,12},{10,14},{12,8},{14,10},{16,20},{18,... | collective-permute-start | bytes 1769480 | tf_op jit(solution)/shard_map/ppermute | solution.py:31
  237.8 17.0 %collective-permute-start.36 = (bf16[3,768,384]{2,1,0:T(8,128)(2,1)}, bf16[3,768,384]{2,1,0:T(8,128)(2,1)S(1)}, u32[]{:S(2)}, u32[]{:S(2)}) collective-permute-start(bf16[3,768,384]{2,1,0:T(8,128)(2,1)} %get-tuple-element.260), channel_id=1, source_target_pairs={{0,1},{1,0},{2,3},{3,2},{4,5},{5,4},{6,7},{7,6},{8,9},{9,8},{10,11... | collective-permute-start | bytes 5308424 | tf_op jit(solution)/shard_map/ppermute | solution.py:35
  237.8 26.3 %collective-permute-start.39 = (bf16[48,3072]{1,0:T(8,128)(2,1)}, bf16[48,3072]{1,0:T(8,128)(2,1)S(1)}, u32[]{:S(2)}, u32[]{:S(2)}) collective-permute-start(bf16[48,3072]{1,0:T(8,128)(2,1)} %get-tuple-element.269), channel_id=1, source_target_pairs={{0,8},{2,10},{4,12},{6,14},{8,0},{10,2},{12,4},{14,6},{16,24},{18,... | collective-permute-start | bytes 884744 | tf_op jit(solution)/shard_map/ppermute | solution.py:31
  239.2 24.8 %collective-permute-start.40 = (bf16[48,3072]{1,0:T(8,128)(2,1)S(1)}, bf16[48,3072]{1,0:T(8,128)(2,1)S(1)}, u32[]{:S(2)}, u32[]{:S(2)}) collective-permute-start(bf16[48,3072]{1,0:T(8,128)(2,1)S(1)} %copy-done.54), channel_id=1, source_target_pairs={{0,16},{2,18},{4,20},{6,22},{8,24},{10,26},{12,28},{14,30},{16,0},... | collective-permute-start | bytes 884744 | tf_op jit(solution)/shard_map/ppermute | solution.py:31
  240.7 23.4 %collective-permute-start.41 = (bf16[48,3072]{1,0:T(8,128)(2,1)S(1)}, bf16[48,3072]{1,0:T(8,128)(2,1)S(1)}, u32[]{:S(2)}, u32[]{:S(2)}) collective-permute-start(bf16[48,3072]{1,0:T(8,128)(2,1)S(1)} %copy-done.53), channel_id=1, source_target_pairs={{0,24},{2,26},{4,28},{6,30},{8,16},{10,18},{12,20},{14,22},{16,8},... | collective-permute-start | bytes 884744 | tf_op jit(solution)/shard_map/ppermute | solution.py:31
  264.1 16.2 %collective-permute-start.37 = (bf16[4,208,384]{2,1,0:T(8,128)(2,1)}, bf16[4,208,384]{2,1,0:T(8,128)(2,1)S(1)}, u32[]{:S(2)}, u32[]{:S(2)}) collective-permute-start(bf16[4,208,384]{2,1,0:T(8,128)(2,1)} %get-tuple-element.266), channel_id=1, source_target_pairs={{0,2},{2,0},{4,6},{6,4},{8,10},{10,8},{12,14},{14,12},{16,18},{18,... | collective-permute-start | bytes 1916936 | tf_op jit(solution)/shard_map/ppermute | solution.py:31
  265.1 15.9 %collective-permute-start.38 = (bf16[4,208,384]{2,1,0:T(8,128)(2,1)}, bf16[4,208,384]{2,1,0:T(8,128)(2,1)S(1)}, u32[]{:S(2)}, u32[]{:S(2)}) collective-permute-start(bf16[4,208,384]{2,1,0:T(8,128)(2,1)} %get-tuple-element.267), channel_id=1, source_target_pairs={{0,4},{2,6},{4,0},{6,2},{8,12},{10,14},{12,8},{14,10},{16,20},{18,... | collective-permute-start | bytes 1916936 | tf_op jit(solution)/shard_map/ppermute | solution.py:31
  283.9 8.2 %collective-permute-start.42 = (bf16[2,208,384]{2,1,0:T(8,128)(2,1)}, bf16[2,208,384]{2,1,0:T(8,128)(2,1)S(1)}, u32[]{:S(2)}, u32[]{:S(2)}) collective-permute-start(bf16[2,208,384]{2,1,0:T(8,128)(2,1)} %get-tuple-element.282), channel_id=1, source_target_pairs={{0,2},{2,0},{4,6},{6,4},{8,10},{10,8},{12,14},{14,12},{16,18},{18,... | collective-permute-start | bytes 958472 | tf_op jit(solution)/shard_map/ppermute | solution.py:31
  285.0 7.9 %collective-permute-start.43 = (bf16[2,208,384]{2,1,0:T(8,128)(2,1)}, bf16[2,208,384]{2,1,0:T(8,128)(2,1)S(1)}, u32[]{:S(2)}, u32[]{:S(2)}) collective-permute-start(bf16[2,208,384]{2,1,0:T(8,128)(2,1)} %get-tuple-element.283), channel_id=1, source_target_pairs={{0,4},{2,6},{4,0},{6,2},{8,12},{10,14},{12,8},{14,10},{16,20},{18,... | collective-permute-start | bytes 958472 | tf_op jit(solution)/shard_map/ppermute | solution.py:31
  296.3 12.8 %collective-permute-start.44 = (bf16[208,384]{1,0:T(8,128)(2,1)}, bf16[208,384]{1,0:T(8,128)(2,1)S(1)}, u32[]{:S(2)}, u32[]{:S(2)}) collective-permute-start(bf16[208,384]{1,0:T(8,128)(2,1)} %get-tuple-element.287), channel_id=1, source_target_pairs={{0,8},{2,10},{4,12},{6,14},{8,0},{10,2},{12,4},{14,6},{16,24},{18,... | collective-permute-start | bytes 479240 | tf_op jit(solution)/shard_map/ppermute | solution.py:31
  300.4 12.3 %collective-permute-start.45 = (bf16[208,384]{1,0:T(8,128)(2,1)}, bf16[208,384]{1,0:T(8,128)(2,1)S(1)}, u32[]{:S(2)}, u32[]{:S(2)}) collective-permute-start(bf16[208,384]{1,0:T(8,128)(2,1)} %get-tuple-element.288), channel_id=1, source_target_pairs={{0,16},{2,18},{4,20},{6,22},{8,24},{10,26},{12,28},{14,30},{16,0},... | collective-permute-start | bytes 479240 | tf_op jit(solution)/shard_map/ppermute | solution.py:31
  300.4 12.3 %copy-start.38 = (f32[208,384]{1,0:T(8,128)S(1)}, f32[208,384]{1,0:T(8,128)}, u32[]{:S(2)}) copy-start(f32[208,384]{1,0:T(8,128)} %get-tuple-element.284) | copy-start | bytes 958468
  300.4 12.3 %collective-permute-start.46 = (bf16[208,384]{1,0:T(8,128)(2,1)}, bf16[208,384]{1,0:T(8,128)(2,1)S(1)}, u32[]{:S(2)}, u32[]{:S(2)}) collective-permute-start(bf16[208,384]{1,0:T(8,128)(2,1)} %get-tuple-element.289), channel_id=1, source_target_pairs={{0,24},{2,26},{4,28},{6,30},{8,16},{10,18},{12,20},{14,22},{16,8},... | collective-permute-start | bytes 479240 | tf_op jit(solution)/shard_map/ppermute | solution.py:31
  312.8 1.3 collective-permute-start.47
  (43 other events, 123.6 us)

commit v4 on v3

--- a/solution.py
+++ b/solution.py
@@ -93,7 +93,7 @@
             out_ref[g * rows : (g + 1) * rows, :] = ins[g][...]
         table[...] = jnp.zeros(table.shape, f32)
         for i, ref in enumerate(ins[count:]):
-            table[i : i + 1, : ref.shape[1]] = ref[...].astype(f32)
+            table[i : i + 1, : ref.shape[0]] = ref[...].astype(f32)[None, :]
         out_ref[count * rows :, :] = table[...].astype(bf16)
 
     return pl.pallas_call(
@@ -101,7 +101,7 @@
         out_shape=jax.ShapeDtypeStruct((count * rows + 16, cols), bf16),
         scratch_shapes=[pltpu.VMEM((16, cols), f32)],
         cost_estimate=HINT,
-    )(*weights, *[item.reshape(1, -1) for item in vectors])
+    )(*weights, *vectors)
 
 
 def place_first(pieces, index, count, size, lengths):
@@ -791,18 +791,15 @@
     q, k, v, ctx, lse = [], [], [], [], []
     for t in range(2):
         found = project(tokens, wqkv[t], vecs, core, t)
-        if fast and t == 0:
-            high_a, other, *found = lax.optimization_barrier((high_a, wqkv[1], *found))
-            wqkv = (wqkv[0], other)
-            one_high_a, two_high_a = swap_dp(high_a, 1, size), swap_dp(high_a, 2, size)
-            far_b = swap_dp(after(outer_t, other), 8, size)
         q.append(found[0])
         k.append(found[1])
         v.append(found[2])
     if fast:
-        far_b, one_low_a, two_low_a, *q = lax.optimization_barrier(
-            (far_b, one_low_a, two_low_a, *q)
+        far_b = swap_dp(after(outer_t, wqkv[0]), 8, size)
+        high_a, far_b, one_low_a, two_low_a, *q = lax.optimization_barrier(
+            (high_a, far_b, one_low_a, two_low_a, *q)
         )
+        one_high_a, two_high_a = swap_dp(high_a, 1, size), swap_dp(high_a, 2, size)
         low_b = jnp.stack([outer_t, far_b])
         two_low_b, one_low_b = swap_dp(low_b, 2, size), swap_dp(low_b, 1, size)
         high_b = swap_dp(low_b, 4, size)

time: 317 us -> 314 us (level)
    unnamed x119 -> x121, local copies, waits for them, and re-layouts: 15.4 us -> 16.2 us
  transfers between devices with their start and end apart: 48 -> 48, of which waited for: 21 -> 18; matrix products, arithmetic and copies ran while one was open for 15% -> 15% of each run, Pallas kernels for 31% -> 31%
where the time goes in v4:
time: 314 us; the launch traced here: 312 us
  Pallas kernels  143 us (46%)
  matrix products  51.2 us (16%)
  starting transfers between devices  49.2 us (16%)
  waiting for transfers between devices  43.7 us (14%)
  local copies, waits for them, and re-layouts  19.4 us (6%)
  other arithmetic  4.53 us (1%)
    dot_general x12, matrix products, dot(): return lax.dot_general(left, right, dims, preferred_element_type=f32)  51.2 us
    ppermute x39, starting transfers between devices, swap_dp(): return lax.ppermute(value, 'dp', [(i, i ^ mask) for i in range(size)])  48 us
    ppermute x39, waiting for transfers between devices, swap_dp(): return lax.ppermute(value, 'dp', [(i, i ^ mask) for i in range(size)])  43.1 us
    pallas_call x4, Pallas kernels, attend_call(): pl.pallas_call(kernel, out_shape=out_shape, grid_spec=pltpu.PrefetchScala...  42.2 us
    pallas_call x3, Pallas kernels, row_call(): pl.pallas_call(kernel, out_shape=[jax.ShapeDtypeStruct((rows, n), d) for...  31.7 us
    unnamed x121, local copies, waits for them, and re-layouts  16.2 us
    pallas_call x2, Pallas kernels, token_gradient(): pl.pallas_call(kernel, out_shape=jax.ShapeDtypeStruct((rows, width), f32)...  12.6 us
    pallas_call x2, Pallas kernels, project(): pl.pallas_call(kernel, out_shape=[jax.ShapeDtypeStruct((rows, cols), bf16...  11.5 us
  transfers between devices with their start and end apart: 48, of which 18 were waited for; matrix products, arithmetic and copies ran while one was open for 15% of the time, Pallas kernels for 31%

profile of v4, /device:TPU:0, one launch (start us, length us, event | category | flops | bytes accessed | tf_op | source)
XLA Modules:
  0.0 312.3 jit_solution(16044798183314198663)
XLA Ops:
  0.7 1.6 shard_map.305
  2.2 3.1 collective-permute-start.1
  5.3 2.5 collective-permute-start.2
  8.8 6.1 %collective-permute-done.2 = bf16[160,384]{1,0:T(8,128)(2,1)S(1)} collective-permute-done((bf16[160,384]{1,0:T(8,128)(2,1)}, bf16[160,384]{1,0:T(8,128)(2,1)S(1)}, u32[]{:S(2)}, u32[]{:S(2)}) %collective-permute-start.2) | collective-permute-done | bytes 122912 | tf_op jit(solution)/shard_map/ppermute | solution.py:31
  14.9 1.6 collective-permute-start.5
  16.5 2.6 collective-permute-done
  20.0 1.6 collective-permute-start.6
  22.1 1.5 collective-permute-start.4
  23.6 1.5 collective-permute-start.9
  25.1 3.8 %collective-permute-done.6.refs_4_ = bf16[2,160,384]{2,1,0:T(8,128)(2,1)S(1)} collective-permute-done((bf16[2,160,384]{2,1,0:T(8,128)(2,1)S(1)}, bf16[2,160,384]{2,1,0:T(8,128)(2,1)S(1)}, u32[]{:S(2)}, u32[]{:S(2)}) %collective-permute-start.6) | collective-permute-done | bytes 245792 | tf_op jit(solution)/shard_map/ppermute | solution.py:31
  28.9 1.5 collective-permute-start.8
  32.2 2.6 copy.37
  34.8 4.7 %collective-permute-done.3 = bf16[48,1920]{1,0:T(8,128)(2,1)S(1)} collective-permute-done((bf16[48,1920]{1,0:T(8,128)(2,1)S(1)}, bf16[48,1920]{1,0:T(8,128)(2,1)S(1)}, u32[]{:S(2)}, u32[]{:S(2)}) %collective-permute-start.3) | collective-permute-done | bytes 184352 | tf_op jit(solution)/shard_map/ppermute | solution.py:31
  40.4 3.0 shard_map.306
  44.3 1.5 collective-permute-start.13
  45.9 3.3 %collective-permute-start.11 = (bf16[48,1536]{1,0:T(8,128)(2,1)}, bf16[48,1536]{1,0:T(8,128)(2,1)S(1)}, u32[]{:S(2)}, u32[]{:S(2)}) collective-permute-start(bf16[48,1536]{1,0:T(8,128)(2,1)} %bitcast.64), channel_id=1, source_target_pairs={{0,16},{2,18},{4,20},{6,22},{8,24},{10,26},{12,28},{14,30},{16,0},... | collective-permute-start | bytes 442376 | tf_op jit(solution)/shard_map/ppermute | solution.py:31
  49.1 5.8 %shard_map.307 = (bf16[1024,384]{1,0:T(8,128)(2,1)}, bf16[1024,384]{1,0:T(8,128)(2,1)}, bf16[1024,384]{1,0:T(8,128)(2,1)}) custom-call(s32[1]{0:T(128)} %bitcast.10.core_ref, bf16[1024,768]{1,0:T(8,128)(2,1)} %x_ref.5, bf16[3,768,384]{2,1,0:T(8,128)(2,1)} %get-tuple-element.161.w_ref.w0_ref, f32[16,768]{1,0:T(8,128)} %get-tuple-element.163.v_ref), custom_call_target="tpu_custom_call" | custom-call | flops 1 | bytes 1 | tf_op jit(solution)/shard_map/pallas_call | solution.py:417
  56.1 5.8 %shard_map.308 = (bf16[1024,384]{1,0:T(8,128)(2,1)}, bf16[1024,384]{1,0:T(8,128)(2,1)}, bf16[1024,384]{1,0:T(8,128)(2,1)}) custom-call(s32[1]{0:T(128)} %bitcast.10.core_ref, bf16[1024,768]{1,0:T(8,128)(2,1)} %x_ref.5, bf16[3,768,384]{2,1,0:T(8,128)(2,1)} %copy-done, f32[16,768]{1,0:T(8,128)} %get-tuple-element.163.v_ref), custom_call_target="tpu_custom_call" | custom-call | flops 1 | bytes 1 | tf_op jit(solution)/shard_map/pallas_call | solution.py:417
  64.8 1.5 collective-permute-start.18
  66.3 1.4 collective-permute-start.19
  68.3 9.0 %shard_map.309 = (bf16[1024,384]{1,0:T(8,128)(2,1)}, f32[2,3,2,512]{3,2,1,0:T(2,128)}) custom-call(s32[2]{0:T(128)} %dynamic_slice.3.lens, bf16[1024,384]{1,0:T(8,128)(2,1)} %get-tuple-element.170.q_ref, bf16[1024,384]{1,0:T(8,128)(2,1)} %get-tuple-element.171.k_ref, bf16[1024,384]{1,0:T(8,128)(2,1)} %get-tuple-element.172.v_ref), custom_call_target="tpu_custom_call" | custom-call | flops 1 | bytes 1 | tf_op jit(solution)/shard_map/pallas_call | solution.py:692
  77.4 1.7 collective-permute-done.18.refs_4_
  79.9 1.4 collective-permute-start.21
  81.8 9.0 %shard_map.310 = (bf16[1024,384]{1,0:T(8,128)(2,1)}, f32[2,3,2,512]{3,2,1,0:T(2,128)}) custom-call(s32[2]{0:T(128)} %dynamic_slice.3.lens, bf16[1024,384]{1,0:T(8,128)(2,1)} %get-tuple-element.184.q_ref, bf16[1024,384]{1,0:T(8,128)(2,1)} %get-tuple-element.185.k_ref, bf16[1024,384]{1,0:T(8,128)(2,1)} %get-tuple-element.186.v_ref), custom_call_target="tpu_custom_call" | custom-call | flops 1 | bytes 1 | tf_op jit(solution)/shard_map/pallas_call | solution.py:692
  91.7 3.6 %shard_map.311 = (bf16[768,384]{1,0:T(8,128)(2,1)}, bf16[768,1536]{1,0:T(8,128)(2,1)}) custom-call(s32[1]{0:T(128)} %bitcast.9.index_ref, bf16[2,48,1920]{2,1,0:T(8,128)(2,1)} %copy-done.19, bf16[2,48,1920]{2,1,0:T(8,128)(2,1)} %copy-done.29, bf16[2,48,1920]{2,1,0:T(8,128)(2,1)} %copy-done.30, bf16[2,48,1920]{2,1,0:T(8,128)(2,1)} %copy-done.32, ...), custom_call_target="tpu_custom_call" | custom-call | flops 1 | bytes 1 | tf_op jit(solution)/shard_map/pallas_call | solution.py:156
  96.9 1.6 collective-permute-start.24
  99.3 6.2 %shard_map.312 = (f32[1024,768]{1,0:T(8,128)}, bf16[1024,768]{1,0:T(8,128)(2,1)}) custom-call(bf16[1024,768]{1,0:T(8,128)(2,1)} %x_ref.5, bf16[1024,384]{1,0:T(8,128)(2,1)} %get-tuple-element.176.c0_ref.c_ref, bf16[1024,384]{1,0:T(8,128)(2,1)} %get-tuple-element.188.c1_ref.c_ref, bf16[768,384]{1,0:T(8,128)(2,1)} %get-tuple-element.197.w0_ref, ...), custom_call_target="tpu_custom_call" | custom-call | flops 1 | bytes 1 | tf_op jit(solution)/shard_map/pallas_call | solution.py:499
  105.6 1.4 collective-permute-start.25
  107.5 6.8 %multiply_convert_fusion.3 = (bf16[1024,1536]{1,0:T(8,128)(2,1)}, f32[1024,1536]{1,0:T(8,128)}) fusion(f32[1536]{0:T(1024)S(1)} %get-tuple-element.286, bf16[1024,768]{1,0:T(8,128)(2,1)} %get-tuple-element.213.h_ref, bf16[768,1536]{1,0:T(8,128)(2,1)S(1)} %copy-done.11), kind=kOutput, calls=%fused_computation.16 | convolution fusion | flops 2425356288 | bytes 13375488 | tf_op jit(solution)/shard_map/dot_general | solution.py:21
  117.1 3.2 %shard_map.313.w0_ref = bf16[768,1536]{1,0:T(8,128)(2,1)} custom-call(s32[1]{0:T(128)} %bitcast.9.index_ref, bf16[2,48,1536]{2,1,0:T(8,128)(2,1)} %copy-done.20, bf16[2,48,1536]{2,1,0:T(8,128)(2,1)} %copy-done.39, bf16[2,48,1536]{2,1,0:T(8,128)(2,1)} %copy-done.42, bf16[2,48,1536]{2,1,0:T(8,128)(2,1)} %collective-permute-done.20.refs_3_, ...), custom_call_target="tpu_custom_call" | custom-call | flops 1 | bytes 1 | tf_op jit(solution)/shard_map/pallas_call | solution.py:156
  120.3 7.3 %multiply_convert_fusion.2 = (bf16[1024,1536]{1,0:T(8,128)(2,1)}, f32[1024,1536]{1,0:T(8,128)}) fusion(f32[1536]{0:T(1024)S(1)} %get-tuple-element.285, bf16[1024,768]{1,0:T(8,128)(2,1)S(1)} %copy-done.17, bf16[768,1536]{1,0:T(8,128)(2,1)} %collective-permute-done.27.w1_ref), kind=kOutput, calls=%fused_computation.14 | convolution fusion | flops 2425356288 | bytes 13375488 | tf_op jit(solution)/shard_map/dot_general | solution.py:21
  129.0 12.7 %shard_map.314 = (f32[1024,768]{1,0:T(8,128)}, f32[1024,768]{1,0:T(8,128)}, bf16[1024,768]{1,0:T(8,128)(2,1)}, f32[8,768]{1,0:T(8,128)}) custom-call(bf16[1024,768]{1,0:T(8,128)(2,1)} %get-tuple-element.213.h_ref, bf16[1024,768]{1,0:T(8,128)(2,1)} %c_ref.1, bf16[1024,1536]{1,0:T(8,128)(2,1)} %get-tuple-element.214.a0_ref, ...), custom_call_target="tpu_custom_call" | custom-call | flops 1 | bytes 1 | tf_op jit(solution)/shard_map/pallas_call | solution.py:499
  141.8 4.5 %convolution_convert_fusion.2 = bf16[768,1536]{1,0:T(8,128)(2,1)S(1)} fusion(bf16[1024,768]{1,0:T(8,128)(2,1)} %get-tuple-element.220, bf16[1024,1536]{1,0:T(8,128)(2,1)S(1)} %copy-done.7), kind=kOutput, calls=%fused_computation.20 | convolution fusion | flops 2417098752 | bytes 7077888 | tf_op jit(solution)/shard_map/dot_general | solution.py:21
  146.9 4.1 %convolution_convert_fusion.3.refs_0_ = bf16[768,1536]{1,0:T(8,128)(2,1)} fusion(bf16[1024,768]{1,0:T(8,128)(2,1)S(1)} %copy-done.52, bf16[1024,1536]{1,0:T(8,128)(2,1)S(1)} %copy-done.6), kind=kOutput, calls=%fused_computation.21 | convolution fusion | flops 2417098752 | bytes 7077888 | tf_op jit(solution)/shard_map/dot_general | solution.py:21
  151.0 5.4 %multiply_convert_fusion.d1_ref = bf16[1024,1536]{1,0:T(8,128)(2,1)S(1)} fusion(bf16[1024,768]{1,0:T(8,128)(2,1)S(1)} %copy-done.52, bf16[768,1536]{1,0:T(8,128)(2,1)S(1)} %copy-done.14, f32[1024,1536]{1,0:T(8,128)S(1)} %copy-done.57, f32[1536]{0:T(1024)S(1)} %get-tuple-element.285), kind=kOutput, calls=%fused_computation.12 | convolution fusion | flops 2436366336 | bytes 13375488 | tf_op jit(solution)/shard_map/dot_general | solution.py:21
  156.5 2.9 convolution_convert_fusion
  159.9 5.4 %multiply_convert_fusion.1.d0_ref = bf16[1024,1536]{1,0:T(8,128)(2,1)S(1)} fusion(bf16[1024,768]{1,0:T(8,128)(2,1)S(1)} %copy-done.52, bf16[768,1536]{1,0:T(8,128)(2,1)S(1)} %copy-done.1, f32[1024,1536]{1,0:T(8,128)S(1)} %bitcast.73, f32[1536]{0:T(1024)S(1)} %get-tuple-element.286), kind=kOutput, calls=%fused_computation.13 | convolution fusion | flops 2436366336 | bytes 13375488 | tf_op jit(solution)/shard_map/dot_general | solution.py:21
  165.3 4.0 %convolution_convert_fusion.1.refs_2_ = bf16[768,1536]{1,0:T(8,128)(2,1)} fusion(bf16[1024,768]{1,0:T(8,128)(2,1)S(1)} %copy-done.18, bf16[1024,1536]{1,0:T(8,128)(2,1)S(1)} %multiply_convert_fusion.1.d0_ref), kind=kOutput, calls=%fused_computation.19 | convolution fusion | flops 2417098752 | bytes 7077888 | tf_op jit(solution)/shard_map/dot_general | solution.py:21
  169.3 1.4 copy-done.15
  170.8 6.8 %shard_map.315 = (bf16[4,48,3072]{2,1,0:T(8,128)(2,1)}, bf16[4,48,3072]{2,1,0:T(8,128)(2,1)}, bf16[2,48,3072]{2,1,0:T(8,128)(2,1)}, bf16[2,48,3072]{2,1,0:T(8,128)(2,1)}, bf16[4,48,3072]{2,1,0:T(8,128)(2,1)}) custom-call(s32[1]{0:T(128)} %bitcast.9.index_ref, bf16[768,1536]{1,0:T(8,128)(2,1)} %convolution_convert_fusion.3.refs_0_, ...), custom_call_target="tpu_custom_call" | custom-call | flops 1 | bytes 1 | tf_op jit(solution)/shard_map/pallas_call | solution.py:219
  178.8 12.7 %shard_map.316 = (f32[1024,768]{1,0:T(8,128)}, bf16[1024,768]{1,0:T(8,128)(2,1)}, f32[8,768]{1,0:T(8,128)}, f32[8,3072]{1,0:T(8,128)}) custom-call(f32[1024,768]{1,0:T(8,128)} %get-tuple-element.225.s_ref, bf16[1024,1536]{1,0:T(8,128)(2,1)} %copy-done.5, bf16[1024,1536]{1,0:T(8,128)(2,1)} %copy-done.4, f32[1024,768]{1,0:T(8,128)} %get-tuple-element.231.f_ref, ...), custom_call_target="tpu_custom_call" | custom-call | flops 1 | bytes 1 | tf_op jit(solution)/shard_map/pallas_call | solution.py:499
  191.5 3.5 %convolution_convert_fusion.6 = bf16[768,384]{1,0:T(8,128)(2,1)} fusion(bf16[1024,768]{1,0:T(8,128)(2,1)} %get-tuple-element.235, bf16[1024,384]{1,0:T(8,128)(2,1)} %get-tuple-element.188.c1_ref.c_ref), kind=kOutput, calls=%fused_computation.24 | convolution fusion | flops 604274688 | bytes 2949120 | tf_op jit(solution)/shard_map/dot_general | solution.py:21
  195.0 1.8 shard_map.317.table_ref
  196.9 3.4 %convolution_convert_fusion.7.r0_ref = bf16[768,384]{1,0:T(8,128)(2,1)} fusion(bf16[1024,768]{1,0:T(8,128)(2,1)} %get-tuple-element.235, bf16[1024,384]{1,0:T(8,128)(2,1)S(1)} %copy-done.8), kind=kOutput, calls=%fused_computation.25 | convolution fusion | flops 604274688 | bytes 2949120 | tf_op jit(solution)/shard_map/dot_general | solution.py:21
  200.3 1.9 convolution_convert_fusion.5.d_ref
  202.2 1.9 convolution_convert_fusion.4.d_ref
  204.0 1.8 collective-permute-done.31.r1_ref.f1_ref
  207.3 2.7 shard_map.318
  211.9 12.2 %shard_map.319.d_ref.d1_ref = bf16[3,1024,384]{2,1,0:T(8,128)(2,1)} custom-call(s32[2]{0:T(128)} %dynamic_slice.3.lens, bf16[1024,384]{1,0:T(8,128)(2,1)} %get-tuple-element.184.q_ref, bf16[1024,384]{1,0:T(8,128)(2,1)} %get-tuple-element.185.k_ref, bf16[1024,384]{1,0:T(8,128)(2,1)} %get-tuple-element.186.v_ref, ...), custom_call_target="tpu_custom_call" | custom-call | flops 1 | bytes 1 | tf_op jit(solution)/shard_map/pallas_call | solution.py:692
  226.4 3.5 %shard_map.320 = (f32[48,3072]{1,0:T(8,128)}, bf16[48,3072]{1,0:T(8,128)(2,1)}, bf16[48,3072]{1,0:T(8,128)(2,1)}, bf16[48,3072]{1,0:T(8,128)(2,1)}) custom-call(bf16[4,48,3072]{2,1,0:T(8,128)(2,1)} %get-tuple-element.227.own_ref, bf16[4,48,3072]{2,1,0:T(8,128)(2,1)} %copy-done.2, bf16[4,48,3072]{2,1,0:T(8,128)(2,1)} %copy-done.3, ...), custom_call_target="tpu_custom_call" | custom-call | flops 1 | bytes 1 | tf_op jit(solution)/shard_map/pallas_call | solution.py:353
  229.9 5.9 %shard_map.321 = (bf16[3,768,384]{2,1,0:T(8,128)(2,1)}, f32[3,8,384]{2,1,0:T(8,128)}) custom-call(bf16[768,1024]{1,0:T(8,128)(2,1)} %bitcast.60, bf16[3,1024,384]{2,1,0:T(8,128)(2,1)} %shard_map.319.d_ref.d1_ref), custom_call_target="tpu_custom_call" | custom-call | flops 1 | bytes 1 | tf_op jit(solution)/shard_map/pallas_call | solution.py:240
  236.2 1.6 collective-permute-start.40
  237.8 2.4 collective-permute-start.41
  240.8 12.0 %shard_map.322.d_ref.d0_ref = bf16[3,1024,384]{2,1,0:T(8,128)(2,1)} custom-call(s32[2]{0:T(128)} %dynamic_slice.3.lens, bf16[1024,384]{1,0:T(8,128)(2,1)} %get-tuple-element.170.q_ref, bf16[1024,384]{1,0:T(8,128)(2,1)} %get-tuple-element.171.k_ref, bf16[1024,384]{1,0:T(8,128)(2,1)} %get-tuple-element.172.v_ref, ...), custom_call_target="tpu_custom_call" | custom-call | flops 1 | bytes 1 | tf_op jit(solution)/shard_map/pallas_call | solution.py:692
  254.0 8.0 %shard_map.323 = (bf16[4,208,384]{2,1,0:T(8,128)(2,1)}, bf16[4,208,384]{2,1,0:T(8,128)(2,1)}, bf16[2,208,384]{2,1,0:T(8,128)(2,1)}, bf16[2,208,384]{2,1,0:T(8,128)(2,1)}, bf16[4,208,384]{2,1,0:T(8,128)(2,1)}) custom-call(s32[2]{0:T(128)} %pad_add_fusion.at_ref, bf16[768,1024]{1,0:T(8,128)(2,1)} %bitcast.61, bf16[3,1024,384]{2,1,0:T(8,128)(2,1)} %shard_map.322.d_ref.d0_ref, ...), custom_call_target="tpu_custom_call" | custom-call | flops 1 | bytes 1 | tf_op jit(solution)/shard_map/pallas_call | solution.py:296
  264.4 6.3 %shard_map.324.f_ref = f32[1024,768]{1,0:T(8,128)} custom-call(f32[1024,768]{1,0:T(8,128)} %get-tuple-element.266.f_ref, bf16[3,1024,384]{2,1,0:T(8,128)(2,1)} %shard_map.322.d_ref.d0_ref, bf16[3,1024,384]{2,1,0:T(8,128)(2,1)} %shard_map.319.d_ref.d1_ref, bf16[3,768,384]{2,1,0:T(8,128)(2,1)} %get-tuple-element.161.w_ref.w0_ref, ...), custom_call_target="tpu_custom_call", output_to_operand_aliasing={{}: (0, {})} | custom-call | flops 1811939328 | bytes 3145728 | tf_op jit(solution)/shard_map/pallas_call | solution.py:449
  270.9 7.4 %collective-permute-done.37.r1_ref.f1_ref = bf16[4,208,384]{2,1,0:T(8,128)(2,1)S(1)} collective-permute-done((bf16[4,208,384]{2,1,0:T(8,128)(2,1)}, bf16[4,208,384]{2,1,0:T(8,128)(2,1)S(1)}, u32[]{:S(2)}, u32[]{:S(2)}) %collective-permute-start.37) | collective-permute-done | bytes 639008 | tf_op jit(solution)/shard_map/ppermute | solution.py:31
  279.9 2.2 shard_map.325
  285.1 5.1 %collective-permute-done.42.r1_ref = bf16[2,208,384]{2,1,0:T(8,128)(2,1)S(1)} collective-permute-done((bf16[2,208,384]{2,1,0:T(8,128)(2,1)}, bf16[2,208,384]{2,1,0:T(8,128)(2,1)S(1)}, u32[]{:S(2)}, u32[]{:S(2)}) %collective-permute-start.42) | collective-permute-done | bytes 319520 | tf_op jit(solution)/shard_map/ppermute | solution.py:31
  291.7 2.7 shard_map.326
  294.4 3.1 collective-permute-start.44
  297.5 2.4 collective-permute-start.46
  299.8 6.3 %shard_map.327 = f32[1024,768]{1,0:T(8,128)} custom-call(f32[1024,768]{1,0:T(8,128)} %shard_map.324.f_ref, bf16[3,1024,384]{2,1,0:T(8,128)(2,1)} %shard_map.322.d_ref.d0_ref, bf16[3,1024,384]{2,1,0:T(8,128)(2,1)} %shard_map.319.d_ref.d1_ref, bf16[3,768,384]{2,1,0:T(8,128)(2,1)} %get-tuple-element.161.w_ref.w0_ref, ...), custom_call_target="tpu_custom_call", output_to_operand_aliasing={{}: (0, {})} | custom-call | flops 1811939328 | bytes 3145728 | tf_op jit(solution)/shard_map/pallas_call | solution.py:449
  306.1 3.7 %collective-permute-done.45 = bf16[208,384]{1,0:T(8,128)(2,1)S(1)} collective-permute-done((bf16[208,384]{1,0:T(8,128)(2,1)}, bf16[208,384]{1,0:T(8,128)(2,1)S(1)}, u32[]{:S(2)}, u32[]{:S(2)}) %collective-permute-start.45) | collective-permute-done | bytes 159776 | tf_op jit(solution)/shard_map/ppermute | solution.py:31
  (205 shorter events, 41.1 us)
Async XLA Ops:
  2.2 6.6 %collective-permute-start.1 = (bf16[160,384]{1,0:T(8,128)(2,1)}, bf16[160,384]{1,0:T(8,128)(2,1)S(1)}, u32[]{:S(2)}, u32[]{:S(2)}) collective-permute-start(bf16[160,384]{1,0:T(8,128)(2,1)} %shard_map.305), channel_id=1, source_target_pairs={{0,8},{2,10},{4,12},{6,14},{8,0},{10,2},{12,4},{14,6},{16,24},{18,... | collective-permute-start | bytes 368648 | tf_op jit(solution)/shard_map/ppermute | solution.py:31
  5.3 9.6 %collective-permute-start.2 = (bf16[160,384]{1,0:T(8,128)(2,1)}, bf16[160,384]{1,0:T(8,128)(2,1)S(1)}, u32[]{:S(2)}, u32[]{:S(2)}) collective-permute-start(bf16[160,384]{1,0:T(8,128)(2,1)} %shard_map.305), channel_id=1, source_target_pairs={{0,24},{2,26},{4,28},{6,30},{8,16},{10,18},{12,20},{14,22},{16,8},... | collective-permute-start | bytes 368648 | tf_op jit(solution)/shard_map/ppermute | solution.py:31
  7.8 11.3 %collective-permute-start = (bf16[160,384]{1,0:T(8,128)(2,1)}, bf16[160,384]{1,0:T(8,128)(2,1)S(1)}, u32[]{:S(2)}, u32[]{:S(2)}) collective-permute-start(bf16[160,384]{1,0:T(8,128)(2,1)} %shard_map.305), channel_id=1, source_target_pairs={{0,16},{2,18},{4,20},{6,22},{8,24},{10,26},{12,28},{14,30},{16,0},... | collective-permute-start | bytes 368648 | tf_op jit(solution)/shard_map/ppermute | solution.py:31
  14.9 24.7 %copy-start.21 = (bf16[2,160,384]{2,1,0:T(8,128)(2,1)}, bf16[2,160,384]{2,1,0:T(8,128)(2,1)S(1)}, u32[]{:S(2)}) copy-start(bf16[2,160,384]{2,1,0:T(8,128)(2,1)S(1)} %pad_maximum_fusion.3.refs_1_) | copy-start | bytes 737284
  14.9 8.7 %collective-permute-start.5 = (bf16[2,160,384]{2,1,0:T(8,128)(2,1)S(1)}, bf16[2,160,384]{2,1,0:T(8,128)(2,1)S(1)}, u32[]{:S(2)}, u32[]{:S(2)}) collective-permute-start(bf16[2,160,384]{2,1,0:T(8,128)(2,1)S(1)} %pad_maximum_fusion.3.refs_1_), channel_id=1, source_target_pairs={{0,2},{2,0},{4,6},{6,4},{8,10},{10,8},{12,14},{14,12},{16,18},{18,... | collective-permute-start | bytes 737288 | tf_op jit(solution)/shard_map/ppermute | solution.py:31
  20.0 19.6 %copy-start.22 = (bf16[2,160,384]{2,1,0:T(8,128)(2,1)}, bf16[2,160,384]{2,1,0:T(8,128)(2,1)S(1)}, u32[]{:S(2)}) copy-start(bf16[2,160,384]{2,1,0:T(8,128)(2,1)S(1)} %pad_maximum_fusion.2.refs_0_) | copy-start | bytes 737284
  20.0 8.9 %collective-permute-start.6 = (bf16[2,160,384]{2,1,0:T(8,128)(2,1)S(1)}, bf16[2,160,384]{2,1,0:T(8,128)(2,1)S(1)}, u32[]{:S(2)}, u32[]{:S(2)}) collective-permute-start(bf16[2,160,384]{2,1,0:T(8,128)(2,1)S(1)} %pad_maximum_fusion.2.refs_0_), channel_id=1, source_target_pairs={{0,4},{2,6},{4,0},{6,2},{8,12},{10,14},{12,8},{14,10},{16,20},{18,... | collective-permute-start | bytes 737288 | tf_op jit(solution)/shard_map/ppermute | solution.py:31
  21.6 17.9 %collective-permute-start.7 = (bf16[2,160,384]{2,1,0:T(8,128)(2,1)S(1)}, bf16[2,160,384]{2,1,0:T(8,128)(2,1)S(1)}, u32[]{:S(2)}, u32[]{:S(2)}) collective-permute-start(bf16[2,160,384]{2,1,0:T(8,128)(2,1)S(1)} %pad_maximum_fusion.3.refs_1_), channel_id=1, source_target_pairs={{0,4},{2,6},{4,0},{6,2},{8,12},{10,14},{12,8},{14,10},{16,20},{18,... | collective-permute-start | bytes 737288 | tf_op jit(solution)/shard_map/ppermute | solution.py:31
  22.1 17.4 %collective-permute-start.4 = (bf16[2,160,384]{2,1,0:T(8,128)(2,1)S(1)}, bf16[2,160,384]{2,1,0:T(8,128)(2,1)S(1)}, u32[]{:S(2)}, u32[]{:S(2)}) collective-permute-start(bf16[2,160,384]{2,1,0:T(8,128)(2,1)S(1)} %pad_maximum_fusion.2.refs_0_), channel_id=1, source_target_pairs={{0,2},{2,0},{4,6},{6,4},{8,10},{10,8},{12,14},{14,12},{16,18},{18,... | collective-permute-start | bytes 737288 | tf_op jit(solution)/shard_map/ppermute | solution.py:31
  23.6 16.0 %copy-start.45 = (bf16[2,160,384]{2,1,0:T(8,128)(2,1)}, bf16[2,160,384]{2,1,0:T(8,128)(2,1)S(1)}, u32[]{:S(2)}) copy-start(bf16[2,160,384]{2,1,0:T(8,128)(2,1)S(1)} %collective-permute-done.5.refs_3_) | copy-start | bytes 737284
  23.6 15.9 %collective-permute-start.9 = (bf16[2,160,384]{2,1,0:T(8,128)(2,1)S(1)}, bf16[2,160,384]{2,1,0:T(8,128)(2,1)S(1)}, u32[]{:S(2)}, u32[]{:S(2)}) collective-permute-start(bf16[2,160,384]{2,1,0:T(8,128)(2,1)S(1)} %collective-permute-done.5.refs_3_), channel_id=1, source_target_pairs={{0,4},{2,6},{4,0},{6,2},{8,12},{10,14},{12,8},{14,10},{16,20},{18,... | collective-permute-start | bytes 737288 | tf_op jit(solution)/shard_map/ppermute | solution.py:31
  28.9 10.7 %copy-start.46 = (bf16[2,160,384]{2,1,0:T(8,128)(2,1)}, bf16[2,160,384]{2,1,0:T(8,128)(2,1)S(1)}, u32[]{:S(2)}) copy-start(bf16[2,160,384]{2,1,0:T(8,128)(2,1)S(1)} %collective-permute-done.6.refs_4_) | copy-start | bytes 737284
  28.9 10.6 %collective-permute-start.8 = (bf16[2,160,384]{2,1,0:T(8,128)(2,1)S(1)}, bf16[2,160,384]{2,1,0:T(8,128)(2,1)S(1)}, u32[]{:S(2)}, u32[]{:S(2)}) collective-permute-start(bf16[2,160,384]{2,1,0:T(8,128)(2,1)S(1)} %collective-permute-done.6.refs_4_), channel_id=1, source_target_pairs={{0,2},{2,0},{4,6},{6,4},{8,10},{10,8},{12,14},{14,12},{16,18},{18,... | collective-permute-start | bytes 737288 | tf_op jit(solution)/shard_map/ppermute | solution.py:31
  31.3 8.2 %collective-permute-start.3 = (bf16[48,1920]{1,0:T(8,128)(2,1)S(1)}, bf16[48,1920]{1,0:T(8,128)(2,1)S(1)}, u32[]{:S(2)}, u32[]{:S(2)}) collective-permute-start(bf16[48,1920]{1,0:T(8,128)(2,1)S(1)} %get-tuple-element.151), channel_id=1, source_target_pairs={{0,16},{2,18},{4,20},{6,22},{8,24},{10,26},{12,28},{14,30},{16,0},... | collective-permute-start | bytes 552968 | tf_op jit(solution)/shard_map/ppermute | solution.py:31
  43.5 11.4 %collective-permute-start.14 = (bf16[3,768,384]{2,1,0:T(8,128)(2,1)}, bf16[3,768,384]{2,1,0:T(8,128)(2,1)S(1)}, u32[]{:S(2)}, u32[]{:S(2)}) collective-permute-start(bf16[3,768,384]{2,1,0:T(8,128)(2,1)} %get-tuple-element.161.w_ref.w0_ref), channel_id=1, source_target_pairs={{0,1},{1,0},{2,3},{3,2},{4,5},{5,4},{6,7},{7,6},{8,9},{9,8},{10,11... | collective-permute-start | bytes 5308424 | tf_op jit(solution)/shard_map/ppermute | solution.py:35
  43.5 18.3 %copy-start.19 = (bf16[2,48,1920]{2,1,0:T(8,128)(2,1)}, bf16[2,48,1920]{2,1,0:T(8,128)(2,1)S(1)}, u32[]{:S(2)}) copy-start(bf16[2,48,1920]{2,1,0:T(8,128)(2,1)S(1)} %pad_maximum_fusion.refs_0_) | copy-start | bytes 1105924
  43.5 18.4 %collective-permute-start.10 = (bf16[2,48,1920]{2,1,0:T(8,128)(2,1)S(1)}, bf16[2,48,1920]{2,1,0:T(8,128)(2,1)S(1)}, u32[]{:S(2)}, u32[]{:S(2)}) collective-permute-start(bf16[2,48,1920]{2,1,0:T(8,128)(2,1)S(1)} %pad_maximum_fusion.refs_0_), channel_id=1, source_target_pairs={{0,8},{2,10},{4,12},{6,14},{8,0},{10,2},{12,4},{14,6},{16,24},{18,... | collective-permute-start | bytes 1105928 | tf_op jit(solution)/shard_map/ppermute | solution.py:31
  43.6 18.3 %collective-permute-start.12 = (bf16[2,48,1920]{2,1,0:T(8,128)(2,1)S(1)}, bf16[2,48,1920]{2,1,0:T(8,128)(2,1)S(1)}, u32[]{:S(2)}, u32[]{:S(2)}) collective-permute-start(bf16[2,48,1920]{2,1,0:T(8,128)(2,1)S(1)} %pad_maximum_fusion.refs_0_), channel_id=1, source_target_pairs={{0,2},{2,0},{4,6},{6,4},{8,10},{10,8},{12,14},{14,12},{16,18},{18,... | collective-permute-start | bytes 1105928 | tf_op jit(solution)/shard_map/ppermute | solution.py:31
  44.3 17.6 %collective-permute-start.13 = (bf16[2,48,1920]{2,1,0:T(8,128)(2,1)S(1)}, bf16[2,48,1920]{2,1,0:T(8,128)(2,1)S(1)}, u32[]{:S(2)}, u32[]{:S(2)}) collective-permute-start(bf16[2,48,1920]{2,1,0:T(8,128)(2,1)S(1)} %pad_maximum_fusion.refs_0_), channel_id=1, source_target_pairs={{0,4},{2,6},{4,0},{6,2},{8,12},{10,14},{12,8},{14,10},{16,20},{18,... | collective-permute-start | bytes 1105928 | tf_op jit(solution)/shard_map/ppermute | solution.py:31
  45.9 16.0 %collective-permute-start.11 = (bf16[48,1536]{1,0:T(8,128)(2,1)}, bf16[48,1536]{1,0:T(8,128)(2,1)S(1)}, u32[]{:S(2)}, u32[]{:S(2)}) collective-permute-start(bf16[48,1536]{1,0:T(8,128)(2,1)} %bitcast.64), channel_id=1, source_target_pairs={{0,16},{2,18},{4,20},{6,22},{8,24},{10,26},{12,28},{14,30},{16,0},... | collective-permute-start | bytes 442376 | tf_op jit(solution)/shard_map/ppermute | solution.py:31
  49.1 18.6 %copy-start.56 = (s32[4]{0:T(128)S(1)}, s32[4]{0:T(128)}, u32[]{:S(2)}) copy-start(s32[4]{0:T(128)} %param.20) | copy-start | bytes 52
  61.9 29.0 %copy-start.29 = (bf16[2,48,1920]{2,1,0:T(8,128)(2,1)}, bf16[2,48,1920]{2,1,0:T(8,128)(2,1)S(1)}, u32[]{:S(2)}) copy-start(bf16[2,48,1920]{2,1,0:T(8,128)(2,1)S(1)} %collective-permute-done.10.refs_1_) | copy-start | bytes 1105924
  61.9 29.0 %copy-start.30 = (bf16[2,48,1920]{2,1,0:T(8,128)(2,1)}, bf16[2,48,1920]{2,1,0:T(8,128)(2,1)S(1)}, u32[]{:S(2)}) copy-start(bf16[2,48,1920]{2,1,0:T(8,128)(2,1)S(1)} %collective-permute-done.12.refs_2_) | copy-start | bytes 1105924
  61.9 29.0 %copy-start.31 = (bf16[2,48,1920]{2,1,0:T(8,128)(2,1)}, bf16[2,48,1920]{2,1,0:T(8,128)(2,1)S(1)}, u32[]{:S(2)}) copy-start(bf16[2,48,1920]{2,1,0:T(8,128)(2,1)S(1)} %collective-permute-done.13.refs_4_) | copy-start | bytes 1105924
  62.5 16.5 %collective-permute-start.15 = (bf16[2,48,1920]{2,1,0:T(8,128)(2,1)S(1)}, bf16[2,48,1920]{2,1,0:T(8,128)(2,1)S(1)}, u32[]{:S(2)}, u32[]{:S(2)}) collective-permute-start(bf16[2,48,1920]{2,1,0:T(8,128)(2,1)S(1)} %collective-permute-done.10.refs_1_), channel_id=1, source_target_pairs={{0,2},{2,0},{4,6},{6,4},{8,10},{10,8},{12,14},{14,12},{16,18},{18,... | collective-permute-start | bytes 1105928 | tf_op jit(solution)/shard_map/ppermute | solution.py:31
  63.1 15.9 %collective-permute-start.16 = (bf16[2,48,1920]{2,1,0:T(8,128)(2,1)S(1)}, bf16[2,48,1920]{2,1,0:T(8,128)(2,1)S(1)}, u32[]{:S(2)}, u32[]{:S(2)}) collective-permute-start(bf16[2,48,1920]{2,1,0:T(8,128)(2,1)S(1)} %collective-permute-done.10.refs_1_), channel_id=1, source_target_pairs={{0,4},{2,6},{4,0},{6,2},{8,12},{10,14},{12,8},{14,10},{16,20},{18,... | collective-permute-start | bytes 1105928 | tf_op jit(solution)/shard_map/ppermute | solution.py:31
  64.7 30.7 %copy-start.20 = (bf16[2,48,1536]{2,1,0:T(8,128)(2,1)}, bf16[2,48,1536]{2,1,0:T(8,128)(2,1)S(1)}, u32[]{:S(2)}) copy-start(bf16[2,48,1536]{2,1,0:T(8,128)(2,1)S(1)} %pad_maximum_fusion.1.refs_0_) | copy-start | bytes 884740
  64.7 12.7 %collective-permute-start.17 = (bf16[2,48,1536]{2,1,0:T(8,128)(2,1)S(1)}, bf16[2,48,1536]{2,1,0:T(8,128)(2,1)S(1)}, u32[]{:S(2)}, u32[]{:S(2)}) collective-permute-start(bf16[2,48,1536]{2,1,0:T(8,128)(2,1)S(1)} %pad_maximum_fusion.1.refs_0_), channel_id=1, source_target_pairs={{0,8},{2,10},{4,12},{6,14},{8,0},{10,2},{12,4},{14,6},{16,24},{18,... | collective-permute-start | bytes 884744 | tf_op jit(solution)/shard_map/ppermute | solution.py:31
  64.8 14.2 %collective-permute-start.18 = (bf16[2,48,1536]{2,1,0:T(8,128)(2,1)S(1)}, bf16[2,48,1536]{2,1,0:T(8,128)(2,1)S(1)}, u32[]{:S(2)}, u32[]{:S(2)}) collective-permute-start(bf16[2,48,1536]{2,1,0:T(8,128)(2,1)S(1)} %pad_maximum_fusion.1.refs_0_), channel_id=1, source_target_pairs={{0,4},{2,6},{4,0},{6,2},{8,12},{10,14},{12,8},{14,10},{16,20},{18,... | collective-permute-start | bytes 884744 | tf_op jit(solution)/shard_map/ppermute | solution.py:31
  66.3 12.7 %collective-permute-start.19 = (bf16[2,48,1536]{2,1,0:T(8,128)(2,1)S(1)}, bf16[2,48,1536]{2,1,0:T(8,128)(2,1)S(1)}, u32[]{:S(2)}, u32[]{:S(2)}) collective-permute-start(bf16[2,48,1536]{2,1,0:T(8,128)(2,1)S(1)} %pad_maximum_fusion.1.refs_0_), channel_id=1, source_target_pairs={{0,2},{2,0},{4,6},{6,4},{8,10},{10,8},{12,14},{14,12},{16,18},{18,... | collective-permute-start | bytes 884744 | tf_op jit(solution)/shard_map/ppermute | solution.py:31
  79.1 11.8 %copy-start.32 = (bf16[2,48,1920]{2,1,0:T(8,128)(2,1)}, bf16[2,48,1920]{2,1,0:T(8,128)(2,1)S(1)}, u32[]{:S(2)}) copy-start(bf16[2,48,1920]{2,1,0:T(8,128)(2,1)S(1)} %collective-permute-done.15.refs_3_) | copy-start | bytes 1105924
  79.8 11.1 %copy-start.33 = (bf16[2,48,1920]{2,1,0:T(8,128)(2,1)}, bf16[2,48,1920]{2,1,0:T(8,128)(2,1)S(1)}, u32[]{:S(2)}) copy-start(bf16[2,48,1920]{2,1,0:T(8,128)(2,1)S(1)} %collective-permute-done.16.refs_5_) | copy-start | bytes 1105924
  79.9 11.0 %collective-permute-start.21 = (bf16[2,48,1920]{2,1,0:T(8,128)(2,1)S(1)}, bf16[2,48,1920]{2,1,0:T(8,128)(2,1)S(1)}, u32[]{:S(2)}, u32[]{:S(2)}) collective-permute-start(bf16[2,48,1920]{2,1,0:T(8,128)(2,1)S(1)} %collective-permute-done.13.refs_4_), channel_id=1, source_target_pairs={{0,2},{2,0},{4,6},{6,4},{8,10},{10,8},{12,14},{14,12},{16,18},{18,... | collective-permute-start | bytes 1105928 | tf_op jit(solution)/shard_map/ppermute | solution.py:31
  81.3 9.6 %collective-permute-start.22 = (bf16[2,48,1920]{2,1,0:T(8,128)(2,1)S(1)}, bf16[2,48,1920]{2,1,0:T(8,128)(2,1)S(1)}, u32[]{:S(2)}, u32[]{:S(2)}) collective-permute-start(bf16[2,48,1920]{2,1,0:T(8,128)(2,1)S(1)} %collective-permute-done.15.refs_3_), channel_id=1, source_target_pairs={{0,4},{2,6},{4,0},{6,2},{8,12},{10,14},{12,8},{14,10},{16,20},{18,... | collective-permute-start | bytes 1105928 | tf_op jit(solution)/shard_map/ppermute | solution.py:31
  95.4 12.2 %copy-start.11 = (bf16[768,1536]{1,0:T(8,128)(2,1)S(1)}, bf16[768,1536]{1,0:T(8,128)(2,1)}, u32[]{:S(2)}) copy-start(bf16[768,1536]{1,0:T(8,128)(2,1)} %get-tuple-element.203.w0_ref) | copy-start | bytes 7077892
  95.4 3.1 %collective-permute-start.23 = (bf16[768,384]{1,0:T(8,128)(2,1)}, bf16[768,384]{1,0:T(8,128)(2,1)S(1)}, u32[]{:S(2)}, u32[]{:S(2)}) collective-permute-start(bf16[768,384]{1,0:T(8,128)(2,1)} %get-tuple-element.197.w0_ref), channel_id=1, source_target_pairs={{0,1},{1,0},{2,3},{3,2},{4,5},{5,4},{6,7},{7,6},{8,9},{9,8},{10,11... | collective-permute-start | bytes 1769480 | tf_op jit(solution)/shard_map/ppermute | solution.py:35
  95.4 10.1 %collective-permute-start.20 = (bf16[2,48,1536]{2,1,0:T(8,128)(2,1)}, bf16[2,48,1536]{2,1,0:T(8,128)(2,1)}, u32[]{:S(2)}, u32[]{:S(2)}) collective-permute-start(bf16[2,48,1536]{2,1,0:T(8,128)(2,1)} %copy-done.39), channel_id=1, source_target_pairs={{0,2},{2,0},{4,6},{6,4},{8,10},{10,8},{12,14},{14,12},{16,18},{18,... | collective-permute-start | bytes 884744 | tf_op jit(solution)/shard_map/ppermute | solution.py:31
  96.9 17.4 %collective-permute-start.24 = (bf16[2,48,1536]{2,1,0:T(8,128)(2,1)}, bf16[2,48,1536]{2,1,0:T(8,128)(2,1)}, u32[]{:S(2)}, u32[]{:S(2)}) collective-permute-start(bf16[2,48,1536]{2,1,0:T(8,128)(2,1)} %copy-done.39), channel_id=1, source_target_pairs={{0,4},{2,6},{4,0},{6,2},{8,12},{10,14},{12,8},{14,10},{16,20},{18,... | collective-permute-start | bytes 884744 | tf_op jit(solution)/shard_map/ppermute | solution.py:31
  98.5 21.8 %collective-permute-start.27 = (bf16[768,1536]{1,0:T(8,128)(2,1)}, bf16[768,1536]{1,0:T(8,128)(2,1)}, u32[]{:S(2)}, u32[]{:S(2)}) collective-permute-start(bf16[768,1536]{1,0:T(8,128)(2,1)} %get-tuple-element.203.w0_ref), channel_id=1, source_target_pairs={{0,1},{1,0},{2,3},{3,2},{4,5},{5,4},{6,7},{7,6},{8,9},{9,8},{10,11... | collective-permute-start | bytes 7077896 | tf_op jit(solution)/shard_map/ppermute | solution.py:35
  105.6 9.5 %collective-permute-start.25 = (bf16[2,48,1536]{2,1,0:T(8,128)(2,1)S(1)}, bf16[2,48,1536]{2,1,0:T(8,128)(2,1)S(1)}, u32[]{:S(2)}, u32[]{:S(2)}) collective-permute-start(bf16[2,48,1536]{2,1,0:T(8,128)(2,1)S(1)} %copy-done.41), channel_id=1, source_target_pairs={{0,2},{2,0},{4,6},{6,4},{8,10},{10,8},{12,14},{14,12},{16,18},{18,... | collective-permute-start | bytes 884744 | tf_op jit(solution)/shard_map/ppermute | solution.py:31
  107.0 9.4 %collective-permute-start.26 = (bf16[2,48,1536]{2,1,0:T(8,128)(2,1)}, bf16[2,48,1536]{2,1,0:T(8,128)(2,1)S(1)}, u32[]{:S(2)}, u32[]{:S(2)}) collective-permute-start(bf16[2,48,1536]{2,1,0:T(8,128)(2,1)} %collective-permute-done.20.refs_3_), channel_id=1, source_target_pairs={{0,4},{2,6},{4,0},{6,2},{8,12},{10,14},{12,8},{14,10},{16,20},{18,... | collective-permute-start | bytes 884744 | tf_op jit(solution)/shard_map/ppermute | solution.py:31
  120.3 7.4 %collective-permute-start.28 = (bf16[768,1536]{1,0:T(8,128)(2,1)}, bf16[768,1536]{1,0:T(8,128)(2,1)S(1)}, u32[]{:S(2)}, u32[]{:S(2)}) collective-permute-start(bf16[768,1536]{1,0:T(8,128)(2,1)} %shard_map.313.w0_ref), channel_id=1, source_target_pairs={{0,1},{1,0},{2,3},{3,2},{4,5},{5,4},{6,7},{7,6},{8,9},{9,8},{10,11... | collective-permute-start | bytes 7077896 | tf_op jit(solution)/shard_map/ppermute | solution.py:35
  129.0 12.7 %copy-start.7 = (bf16[1024,1536]{1,0:T(8,128)(2,1)S(1)}, bf16[1024,1536]{1,0:T(8,128)(2,1)}, u32[]{:S(2)}) copy-start(bf16[1024,1536]{1,0:T(8,128)(2,1)} %get-tuple-element.305.a1_ref) | copy-start | bytes 9437188
  146.3 4.7 %collective-permute-start.29 = (bf16[768,1536]{1,0:T(8,128)(2,1)S(1)}, bf16[768,1536]{1,0:T(8,128)(2,1)S(1)}, u32[]{:S(2)}, u32[]{:S(2)}) collective-permute-start(bf16[768,1536]{1,0:T(8,128)(2,1)S(1)} %convolution_convert_fusion.2), channel_id=1, source_target_pairs={{0,1},{1,0},{2,3},{3,2},{4,5},{5,4},{6,7},{7,6},{8,9},{9,8},{10,11... | collective-permute-start | bytes 7077896 | tf_op jit(solution)/shard_map/ppermute | solution.py:35
  146.9 13.0 %slice-start = ((s8[6291456]{0:T(1024)(128)(4,1)}), s8[4194304]{0:T(1024)(128)(4,1)S(1)}, s32[]{:S(2)}) async-start(s8[6291456]{0:T(1024)(128)(4,1)} %bitcast.72), calls=%async_computation | async-start | bytes 8388608
  159.4 9.9 %collective-permute-start.30 = (bf16[768,1536]{1,0:T(8,128)(2,1)S(1)}, bf16[768,1536]{1,0:T(8,128)(2,1)S(1)}, u32[]{:S(2)}, u32[]{:S(2)}) collective-permute-start(bf16[768,1536]{1,0:T(8,128)(2,1)S(1)} %convolution_convert_fusion), channel_id=1, source_target_pairs={{0,1},{1,0},{2,3},{3,2},{4,5},{5,4},{6,7},{7,6},{8,9},{9,8},{10,11... | collective-permute-start | bytes 7077896 | tf_op jit(solution)/shard_map/ppermute | solution.py:35
  177.6 28.2 %collective-permute-start.31 = (bf16[4,48,3072]{2,1,0:T(8,128)(2,1)}, bf16[4,48,3072]{2,1,0:T(8,128)(2,1)S(1)}, u32[]{:S(2)}, u32[]{:S(2)}) collective-permute-start(bf16[4,48,3072]{2,1,0:T(8,128)(2,1)} %get-tuple-element.223), channel_id=1, source_target_pairs={{0,2},{2,0},{4,6},{6,4},{8,10},{10,8},{12,14},{14,12},{16,18},{18,... | collective-permute-start | bytes 3538952 | tf_op jit(solution)/shard_map/ppermute | solution.py:31
  178.3 27.9 %collective-permute-start.32 = (bf16[4,48,3072]{2,1,0:T(8,128)(2,1)}, bf16[4,48,3072]{2,1,0:T(8,128)(2,1)S(1)}, u32[]{:S(2)}, u32[]{:S(2)}) collective-permute-start(bf16[4,48,3072]{2,1,0:T(8,128)(2,1)} %get-tuple-element.224), channel_id=1, source_target_pairs={{0,4},{2,6},{4,0},{6,2},{8,12},{10,14},{12,8},{14,10},{16,20},{18,... | collective-permute-start | bytes 3538952 | tf_op jit(solution)/shard_map/ppermute | solution.py:31
  195.0 9.0 %collective-permute-start.33 = (bf16[768,384]{1,0:T(8,128)(2,1)}, bf16[768,384]{1,0:T(8,128)(2,1)}, u32[]{:S(2)}, u32[]{:S(2)}) collective-permute-start(bf16[768,384]{1,0:T(8,128)(2,1)} %convolution_convert_fusion.6), channel_id=1, source_target_pairs={{0,1},{1,0},{2,3},{3,2},{4,5},{5,4},{6,7},{7,6},{8,9},{9,8},{10,11... | collective-permute-start | bytes 1769480 | tf_op jit(solution)/shard_map/ppermute | solution.py:35
  210.0 14.7 %collective-permute-start.34 = (bf16[2,48,3072]{2,1,0:T(8,128)(2,1)}, bf16[2,48,3072]{2,1,0:T(8,128)(2,1)S(1)}, u32[]{:S(2)}, u32[]{:S(2)}) collective-permute-start(bf16[2,48,3072]{2,1,0:T(8,128)(2,1)} %get-tuple-element.241), channel_id=1, source_target_pairs={{0,2},{2,0},{4,6},{6,4},{8,10},{10,8},{12,14},{14,12},{16,18},{18,... | collective-permute-start | bytes 1769480 | tf_op jit(solution)/shard_map/ppermute | solution.py:31
  211.4 14.2 %collective-permute-start.35 = (bf16[2,48,3072]{2,1,0:T(8,128)(2,1)}, bf16[2,48,3072]{2,1,0:T(8,128)(2,1)S(1)}, u32[]{:S(2)}, u32[]{:S(2)}) collective-permute-start(bf16[2,48,3072]{2,1,0:T(8,128)(2,1)} %get-tuple-element.242), channel_id=1, source_target_pairs={{0,4},{2,6},{4,0},{6,2},{8,12},{10,14},{12,8},{14,10},{16,20},{18,... | collective-permute-start | bytes 1769480 | tf_op jit(solution)/shard_map/ppermute | solution.py:31
  235.8 17.0 %collective-permute-start.36 = (bf16[3,768,384]{2,1,0:T(8,128)(2,1)}, bf16[3,768,384]{2,1,0:T(8,128)(2,1)S(1)}, u32[]{:S(2)}, u32[]{:S(2)}) collective-permute-start(bf16[3,768,384]{2,1,0:T(8,128)(2,1)} %get-tuple-element.252), channel_id=1, source_target_pairs={{0,1},{1,0},{2,3},{3,2},{4,5},{5,4},{6,7},{7,6},{8,9},{9,8},{10,11... | collective-permute-start | bytes 5308424 | tf_op jit(solution)/shard_map/ppermute | solution.py:35
  235.8 26.2 %collective-permute-start.39 = (bf16[48,3072]{1,0:T(8,128)(2,1)}, bf16[48,3072]{1,0:T(8,128)(2,1)S(1)}, u32[]{:S(2)}, u32[]{:S(2)}) collective-permute-start(bf16[48,3072]{1,0:T(8,128)(2,1)} %get-tuple-element.261), channel_id=1, source_target_pairs={{0,8},{2,10},{4,12},{6,14},{8,0},{10,2},{12,4},{14,6},{16,24},{18,... | collective-permute-start | bytes 884744 | tf_op jit(solution)/shard_map/ppermute | solution.py:31
  236.2 25.9 %collective-permute-start.40 = (bf16[48,3072]{1,0:T(8,128)(2,1)S(1)}, bf16[48,3072]{1,0:T(8,128)(2,1)S(1)}, u32[]{:S(2)}, u32[]{:S(2)}) collective-permute-start(bf16[48,3072]{1,0:T(8,128)(2,1)S(1)} %copy-done.55), channel_id=1, source_target_pairs={{0,16},{2,18},{4,20},{6,22},{8,24},{10,26},{12,28},{14,30},{16,0},... | collective-permute-start | bytes 884744 | tf_op jit(solution)/shard_map/ppermute | solution.py:31
  237.8 24.2 %collective-permute-start.41 = (bf16[48,3072]{1,0:T(8,128)(2,1)S(1)}, bf16[48,3072]{1,0:T(8,128)(2,1)S(1)}, u32[]{:S(2)}, u32[]{:S(2)}) collective-permute-start(bf16[48,3072]{1,0:T(8,128)(2,1)S(1)} %copy-done.54), channel_id=1, source_target_pairs={{0,24},{2,26},{4,28},{6,30},{8,16},{10,18},{12,20},{14,22},{16,8},... | collective-permute-start | bytes 884744 | tf_op jit(solution)/shard_map/ppermute | solution.py:31
  262.1 16.2 %collective-permute-start.37 = (bf16[4,208,384]{2,1,0:T(8,128)(2,1)}, bf16[4,208,384]{2,1,0:T(8,128)(2,1)S(1)}, u32[]{:S(2)}, u32[]{:S(2)}) collective-permute-start(bf16[4,208,384]{2,1,0:T(8,128)(2,1)} %get-tuple-element.258), channel_id=1, source_target_pairs={{0,2},{2,0},{4,6},{6,4},{8,10},{10,8},{12,14},{14,12},{16,18},{18,... | collective-permute-start | bytes 1916936 | tf_op jit(solution)/shard_map/ppermute | solution.py:31
  263.2 15.9 %collective-permute-start.38 = (bf16[4,208,384]{2,1,0:T(8,128)(2,1)}, bf16[4,208,384]{2,1,0:T(8,128)(2,1)S(1)}, u32[]{:S(2)}, u32[]{:S(2)}) collective-permute-start(bf16[4,208,384]{2,1,0:T(8,128)(2,1)} %get-tuple-element.259), channel_id=1, source_target_pairs={{0,4},{2,6},{4,0},{6,2},{8,12},{10,14},{12,8},{14,10},{16,20},{18,... | collective-permute-start | bytes 1916936 | tf_op jit(solution)/shard_map/ppermute | solution.py:31
  282.0 8.2 %collective-permute-start.42 = (bf16[2,208,384]{2,1,0:T(8,128)(2,1)}, bf16[2,208,384]{2,1,0:T(8,128)(2,1)S(1)}, u32[]{:S(2)}, u32[]{:S(2)}) collective-permute-start(bf16[2,208,384]{2,1,0:T(8,128)(2,1)} %get-tuple-element.274), channel_id=1, source_target_pairs={{0,2},{2,0},{4,6},{6,4},{8,10},{10,8},{12,14},{14,12},{16,18},{18,... | collective-permute-start | bytes 958472 | tf_op jit(solution)/shard_map/ppermute | solution.py:31
  283.0 7.9 %collective-permute-start.43 = (bf16[2,208,384]{2,1,0:T(8,128)(2,1)}, bf16[2,208,384]{2,1,0:T(8,128)(2,1)S(1)}, u32[]{:S(2)}, u32[]{:S(2)}) collective-permute-start(bf16[2,208,384]{2,1,0:T(8,128)(2,1)} %get-tuple-element.275), channel_id=1, source_target_pairs={{0,4},{2,6},{4,0},{6,2},{8,12},{10,14},{12,8},{14,10},{16,20},{18,... | collective-permute-start | bytes 958472 | tf_op jit(solution)/shard_map/ppermute | solution.py:31
  294.4 11.8 %collective-permute-start.44 = (bf16[208,384]{1,0:T(8,128)(2,1)}, bf16[208,384]{1,0:T(8,128)(2,1)S(1)}, u32[]{:S(2)}, u32[]{:S(2)}) collective-permute-start(bf16[208,384]{1,0:T(8,128)(2,1)} %get-tuple-element.279), channel_id=1, source_target_pairs={{0,8},{2,10},{4,12},{6,14},{8,0},{10,2},{12,4},{14,6},{16,24},{18,... | collective-permute-start | bytes 479240 | tf_op jit(solution)/shard_map/ppermute | solution.py:31
  297.5 12.3 %collective-permute-start.45 = (bf16[208,384]{1,0:T(8,128)(2,1)}, bf16[208,384]{1,0:T(8,128)(2,1)S(1)}, u32[]{:S(2)}, u32[]{:S(2)}) collective-permute-start(bf16[208,384]{1,0:T(8,128)(2,1)} %get-tuple-element.280), channel_id=1, source_target_pairs={{0,16},{2,18},{4,20},{6,22},{8,24},{10,26},{12,28},{14,30},{16,0},... | collective-permute-start | bytes 479240 | tf_op jit(solution)/shard_map/ppermute | solution.py:31
  297.5 12.4 %copy-start.38 = (f32[208,384]{1,0:T(8,128)S(1)}, f32[208,384]{1,0:T(8,128)}, u32[]{:S(2)}) copy-start(f32[208,384]{1,0:T(8,128)} %get-tuple-element.276) | copy-start | bytes 958468
  297.5 12.3 %collective-permute-start.46 = (bf16[208,384]{1,0:T(8,128)(2,1)}, bf16[208,384]{1,0:T(8,128)(2,1)S(1)}, u32[]{:S(2)}, u32[]{:S(2)}) collective-permute-start(bf16[208,384]{1,0:T(8,128)(2,1)} %get-tuple-element.281), channel_id=1, source_target_pairs={{0,24},{2,26},{4,28},{6,30},{8,16},{10,18},{12,20},{14,22},{16,8},... | collective-permute-start | bytes 479240 | tf_op jit(solution)/shard_map/ppermute | solution.py:31
  309.9 1.3 collective-permute-start.47
  (44 other events, 125.5 us)

commit v5 on v4

--- a/solution.py
+++ b/solution.py
@@ -350,11 +350,15 @@
 
 
 def whole_call(kernel, outs, ins, blocks):
+    def some(array, n):
+        rest = (0,) * (array.ndim - 1)
+        return pl.BlockSpec((abs(n), *array.shape[1:]), lambda *_: (int(n < 0), *rest))
+
     return pl.pallas_call(
         kernel,
         out_shape=[jax.ShapeDtypeStruct(o, d) for o, d in outs],
         grid=(1,),
-        in_specs=[vmem((n, *a.shape[1:])) for a, n in zip(ins, blocks)],
+        in_specs=[some(a, n) for a, n in zip(ins, blocks)],
         out_specs=[vmem(o) for o, _ in outs],
         cost_estimate=HINT,
     )(*ins)
@@ -383,7 +387,7 @@
 def near_add(own, first, got):
     def kernel(own_ref, f1_ref, f2_ref, r1_ref, r2_ref, keep_ref, *outs):
         def total(k):
-            early = f1_ref[2 + k] if k < 2 else f2_ref[k]
+            early = f1_ref[k] if k < 2 else f2_ref[k - 2]
             late = r2_ref[k] if k < 2 else r1_ref[k - 2]
             return own_ref[k].astype(f32) + early.astype(f32) + late.astype(f32)
 
@@ -393,7 +397,7 @@
 
     shape = own.shape[1:]
     return whole_call(
-        kernel, [(shape, f32)] + [(shape, bf16)] * 3, [own, *first, *got], (4, 4, 4, 2, 2)
+        kernel, [(shape, f32)] + [(shape, bf16)] * 3, [own, *first, *got], (4, -2, -2, 2, 2)
     )
 
 

time: 314 us -> 313 us (level)
  transfers between devices with their start and end apart: 48 -> 48, of which waited for: 18 -> 18; matrix products, arithmetic and copies ran while one was open for 15% -> 15% of each run, Pallas kernels for 31% -> 32%
where the time goes in v5:
time: 313 us; the launch traced here: 312 us
  Pallas kernels  143 us (46%)
  matrix products  51.2 us (16%)
  starting transfers between devices  49.2 us (16%)
  waiting for transfers between devices  43.7 us (14%)
  local copies, waits for them, and re-layouts  19.4 us (6%)
  other arithmetic  4.53 us (1%)
    dot_general x12, matrix products, dot(): return lax.dot_general(left, right, dims, preferred_element_type=f32)  51.2 us
    ppermute x39, starting transfers between devices, swap_dp(): return lax.ppermute(value, 'dp', [(i, i ^ mask) for i in range(size)])  48 us
    ppermute x39, waiting for transfers between devices, swap_dp(): return lax.ppermute(value, 'dp', [(i, i ^ mask) for i in range(size)])  43.1 us
    pallas_call x4, Pallas kernels, attend_call(): pl.pallas_call(kernel, out_shape=out_shape, grid_spec=pltpu.PrefetchScala...  42.2 us
    pallas_call x3, Pallas kernels, row_call(): pl.pallas_call(kernel, out_shape=[jax.ShapeDtypeStruct((rows, n), d) for...  31.7 us
    unnamed x121, local copies, waits for them, and re-layouts  16.2 us
    pallas_call x2, Pallas kernels, token_gradient(): pl.pallas_call(kernel, out_shape=jax.ShapeDtypeStruct((rows, width), f32)...  12.6 us
    pallas_call x2, Pallas kernels, project(): pl.pallas_call(kernel, out_shape=[jax.ShapeDtypeStruct((rows, cols), bf16...  11.5 us
  transfers between devices with their start and end apart: 48, of which 18 were waited for; matrix products, arithmetic and copies ran while one was open for 15% of the time, Pallas kernels for 32%

profile of v5, /device:TPU:0, one launch (start us, length us, event | category | flops | bytes accessed | tf_op | source)
XLA Modules:
  0.0 311.7 jit_solution(1086053984481269655)
XLA Ops:
  0.7 1.6 shard_map.305
  2.2 3.1 collective-permute-start.1
  5.3 2.5 collective-permute-start.2
  8.8 6.1 %collective-permute-done.2 = bf16[160,384]{1,0:T(8,128)(2,1)S(1)} collective-permute-done((bf16[160,384]{1,0:T(8,128)(2,1)}, bf16[160,384]{1,0:T(8,128)(2,1)S(1)}, u32[]{:S(2)}, u32[]{:S(2)}) %collective-permute-start.2) | collective-permute-done | bytes 122912 | tf_op jit(solution)/shard_map/ppermute | solution.py:31
  14.9 1.6 collective-permute-start.5
  16.5 2.6 collective-permute-done
  20.0 1.6 collective-permute-start.6
  22.1 1.5 collective-permute-start.4
  23.6 1.5 collective-permute-start.9
  25.1 3.8 %collective-permute-done.6.refs_4_ = bf16[2,160,384]{2,1,0:T(8,128)(2,1)S(1)} collective-permute-done((bf16[2,160,384]{2,1,0:T(8,128)(2,1)S(1)}, bf16[2,160,384]{2,1,0:T(8,128)(2,1)S(1)}, u32[]{:S(2)}, u32[]{:S(2)}) %collective-permute-start.6) | collective-permute-done | bytes 245792 | tf_op jit(solution)/shard_map/ppermute | solution.py:31
  28.9 1.5 collective-permute-start.8
  32.2 2.6 copy.37
  34.8 4.7 %collective-permute-done.3 = bf16[48,1920]{1,0:T(8,128)(2,1)S(1)} collective-permute-done((bf16[48,1920]{1,0:T(8,128)(2,1)S(1)}, bf16[48,1920]{1,0:T(8,128)(2,1)S(1)}, u32[]{:S(2)}, u32[]{:S(2)}) %collective-permute-start.3) | collective-permute-done | bytes 184352 | tf_op jit(solution)/shard_map/ppermute | solution.py:31
  40.4 3.0 shard_map.306
  44.3 1.5 collective-permute-start.13
  45.9 3.3 %collective-permute-start.11 = (bf16[48,1536]{1,0:T(8,128)(2,1)}, bf16[48,1536]{1,0:T(8,128)(2,1)S(1)}, u32[]{:S(2)}, u32[]{:S(2)}) collective-permute-start(bf16[48,1536]{1,0:T(8,128)(2,1)} %bitcast.64), channel_id=1, source_target_pairs={{0,16},{2,18},{4,20},{6,22},{8,24},{10,26},{12,28},{14,30},{16,0},... | collective-permute-start | bytes 442376 | tf_op jit(solution)/shard_map/ppermute | solution.py:31
  49.1 5.8 %shard_map.307 = (bf16[1024,384]{1,0:T(8,128)(2,1)}, bf16[1024,384]{1,0:T(8,128)(2,1)}, bf16[1024,384]{1,0:T(8,128)(2,1)}) custom-call(s32[1]{0:T(128)} %bitcast.10.core_ref, bf16[1024,768]{1,0:T(8,128)(2,1)} %x_ref.5, bf16[3,768,384]{2,1,0:T(8,128)(2,1)} %get-tuple-element.161.w_ref.w0_ref, f32[16,768]{1,0:T(8,128)} %get-tuple-element.163.v_ref), custom_call_target="tpu_custom_call" | custom-call | flops 1 | bytes 1 | tf_op jit(solution)/shard_map/pallas_call | solution.py:421
  56.1 5.8 %shard_map.308 = (bf16[1024,384]{1,0:T(8,128)(2,1)}, bf16[1024,384]{1,0:T(8,128)(2,1)}, bf16[1024,384]{1,0:T(8,128)(2,1)}) custom-call(s32[1]{0:T(128)} %bitcast.10.core_ref, bf16[1024,768]{1,0:T(8,128)(2,1)} %x_ref.5, bf16[3,768,384]{2,1,0:T(8,128)(2,1)} %copy-done, f32[16,768]{1,0:T(8,128)} %get-tuple-element.163.v_ref), custom_call_target="tpu_custom_call" | custom-call | flops 1 | bytes 1 | tf_op jit(solution)/shard_map/pallas_call | solution.py:421
  64.8 1.5 collective-permute-start.18
  66.3 1.4 collective-permute-start.19
  68.3 9.0 %shard_map.309 = (bf16[1024,384]{1,0:T(8,128)(2,1)}, f32[2,3,2,512]{3,2,1,0:T(2,128)}) custom-call(s32[2]{0:T(128)} %dynamic_slice.3.lens, bf16[1024,384]{1,0:T(8,128)(2,1)} %get-tuple-element.170.q_ref, bf16[1024,384]{1,0:T(8,128)(2,1)} %get-tuple-element.171.k_ref, bf16[1024,384]{1,0:T(8,128)(2,1)} %get-tuple-element.172.v_ref), custom_call_target="tpu_custom_call" | custom-call | flops 1 | bytes 1 | tf_op jit(solution)/shard_map/pallas_call | solution.py:696
  77.4 1.7 collective-permute-done.18.refs_4_
  79.9 1.4 collective-permute-start.21
  81.8 9.0 %shard_map.310 = (bf16[1024,384]{1,0:T(8,128)(2,1)}, f32[2,3,2,512]{3,2,1,0:T(2,128)}) custom-call(s32[2]{0:T(128)} %dynamic_slice.3.lens, bf16[1024,384]{1,0:T(8,128)(2,1)} %get-tuple-element.184.q_ref, bf16[1024,384]{1,0:T(8,128)(2,1)} %get-tuple-element.185.k_ref, bf16[1024,384]{1,0:T(8,128)(2,1)} %get-tuple-element.186.v_ref), custom_call_target="tpu_custom_call" | custom-call | flops 1 | bytes 1 | tf_op jit(solution)/shard_map/pallas_call | solution.py:696
  91.7 3.6 %shard_map.311 = (bf16[768,384]{1,0:T(8,128)(2,1)}, bf16[768,1536]{1,0:T(8,128)(2,1)}) custom-call(s32[1]{0:T(128)} %bitcast.9.index_ref, bf16[2,48,1920]{2,1,0:T(8,128)(2,1)} %copy-done.19, bf16[2,48,1920]{2,1,0:T(8,128)(2,1)} %copy-done.29, bf16[2,48,1920]{2,1,0:T(8,128)(2,1)} %copy-done.30, bf16[2,48,1920]{2,1,0:T(8,128)(2,1)} %copy-done.32, ...), custom_call_target="tpu_custom_call" | custom-call | flops 1 | bytes 1 | tf_op jit(solution)/shard_map/pallas_call | solution.py:156
  96.9 1.6 collective-permute-start.24
  99.3 6.2 %shard_map.312 = (f32[1024,768]{1,0:T(8,128)}, bf16[1024,768]{1,0:T(8,128)(2,1)}) custom-call(bf16[1024,768]{1,0:T(8,128)(2,1)} %x_ref.5, bf16[1024,384]{1,0:T(8,128)(2,1)} %get-tuple-element.176.c0_ref.c_ref, bf16[1024,384]{1,0:T(8,128)(2,1)} %get-tuple-element.188.c1_ref.c_ref, bf16[768,384]{1,0:T(8,128)(2,1)} %get-tuple-element.197.w0_ref, ...), custom_call_target="tpu_custom_call" | custom-call | flops 1 | bytes 1 | tf_op jit(solution)/shard_map/pallas_call | solution.py:503
  105.6 1.4 collective-permute-start.25
  107.5 6.8 %multiply_convert_fusion.3 = (bf16[1024,1536]{1,0:T(8,128)(2,1)}, f32[1024,1536]{1,0:T(8,128)}) fusion(f32[1536]{0:T(1024)S(1)} %get-tuple-element.286, bf16[1024,768]{1,0:T(8,128)(2,1)} %get-tuple-element.213.h_ref, bf16[768,1536]{1,0:T(8,128)(2,1)S(1)} %copy-done.11), kind=kOutput, calls=%fused_computation.16 | convolution fusion | flops 2425356288 | bytes 13375488 | tf_op jit(solution)/shard_map/dot_general | solution.py:21
  117.1 3.2 %shard_map.313.w0_ref = bf16[768,1536]{1,0:T(8,128)(2,1)} custom-call(s32[1]{0:T(128)} %bitcast.9.index_ref, bf16[2,48,1536]{2,1,0:T(8,128)(2,1)} %copy-done.20, bf16[2,48,1536]{2,1,0:T(8,128)(2,1)} %copy-done.39, bf16[2,48,1536]{2,1,0:T(8,128)(2,1)} %copy-done.42, bf16[2,48,1536]{2,1,0:T(8,128)(2,1)} %collective-permute-done.20.refs_3_, ...), custom_call_target="tpu_custom_call" | custom-call | flops 1 | bytes 1 | tf_op jit(solution)/shard_map/pallas_call | solution.py:156
  120.3 7.3 %multiply_convert_fusion.2 = (bf16[1024,1536]{1,0:T(8,128)(2,1)}, f32[1024,1536]{1,0:T(8,128)}) fusion(f32[1536]{0:T(1024)S(1)} %get-tuple-element.285, bf16[1024,768]{1,0:T(8,128)(2,1)S(1)} %copy-done.17, bf16[768,1536]{1,0:T(8,128)(2,1)} %collective-permute-done.27.w1_ref), kind=kOutput, calls=%fused_computation.14 | convolution fusion | flops 2425356288 | bytes 13375488 | tf_op jit(solution)/shard_map/dot_general | solution.py:21
  129.0 12.7 %shard_map.314 = (f32[1024,768]{1,0:T(8,128)}, f32[1024,768]{1,0:T(8,128)}, bf16[1024,768]{1,0:T(8,128)(2,1)}, f32[8,768]{1,0:T(8,128)}) custom-call(bf16[1024,768]{1,0:T(8,128)(2,1)} %get-tuple-element.213.h_ref, bf16[1024,768]{1,0:T(8,128)(2,1)} %c_ref.1, bf16[1024,1536]{1,0:T(8,128)(2,1)} %get-tuple-element.214.a0_ref, ...), custom_call_target="tpu_custom_call" | custom-call | flops 1 | bytes 1 | tf_op jit(solution)/shard_map/pallas_call | solution.py:503
  141.8 4.5 %convolution_convert_fusion.2 = bf16[768,1536]{1,0:T(8,128)(2,1)S(1)} fusion(bf16[1024,768]{1,0:T(8,128)(2,1)} %get-tuple-element.220, bf16[1024,1536]{1,0:T(8,128)(2,1)S(1)} %copy-done.7), kind=kOutput, calls=%fused_computation.20 | convolution fusion | flops 2417098752 | bytes 7077888 | tf_op jit(solution)/shard_map/dot_general | solution.py:21
  146.9 4.1 %convolution_convert_fusion.3.refs_0_ = bf16[768,1536]{1,0:T(8,128)(2,1)} fusion(bf16[1024,768]{1,0:T(8,128)(2,1)S(1)} %copy-done.52, bf16[1024,1536]{1,0:T(8,128)(2,1)S(1)} %copy-done.6), kind=kOutput, calls=%fused_computation.21 | convolution fusion | flops 2417098752 | bytes 7077888 | tf_op jit(solution)/shard_map/dot_general | solution.py:21
  151.0 5.4 %multiply_convert_fusion.d1_ref = bf16[1024,1536]{1,0:T(8,128)(2,1)S(1)} fusion(bf16[1024,768]{1,0:T(8,128)(2,1)S(1)} %copy-done.52, bf16[768,1536]{1,0:T(8,128)(2,1)S(1)} %copy-done.14, f32[1024,1536]{1,0:T(8,128)S(1)} %copy-done.57, f32[1536]{0:T(1024)S(1)} %get-tuple-element.285), kind=kOutput, calls=%fused_computation.12 | convolution fusion | flops 2436366336 | bytes 13375488 | tf_op jit(solution)/shard_map/dot_general | solution.py:21
  156.5 2.9 convolution_convert_fusion
  159.9 5.4 %multiply_convert_fusion.1.d0_ref = bf16[1024,1536]{1,0:T(8,128)(2,1)S(1)} fusion(bf16[1024,768]{1,0:T(8,128)(2,1)S(1)} %copy-done.52, bf16[768,1536]{1,0:T(8,128)(2,1)S(1)} %copy-done.1, f32[1024,1536]{1,0:T(8,128)S(1)} %bitcast.73, f32[1536]{0:T(1024)S(1)} %get-tuple-element.286), kind=kOutput, calls=%fused_computation.13 | convolution fusion | flops 2436366336 | bytes 13375488 | tf_op jit(solution)/shard_map/dot_general | solution.py:21
  165.3 4.0 %convolution_convert_fusion.1.refs_2_ = bf16[768,1536]{1,0:T(8,128)(2,1)} fusion(bf16[1024,768]{1,0:T(8,128)(2,1)S(1)} %copy-done.18, bf16[1024,1536]{1,0:T(8,128)(2,1)S(1)} %multiply_convert_fusion.1.d0_ref), kind=kOutput, calls=%fused_computation.19 | convolution fusion | flops 2417098752 | bytes 7077888 | tf_op jit(solution)/shard_map/dot_general | solution.py:21
  169.3 1.4 copy-done.15
  170.8 6.8 %shard_map.315 = (bf16[4,48,3072]{2,1,0:T(8,128)(2,1)}, bf16[4,48,3072]{2,1,0:T(8,128)(2,1)}, bf16[2,48,3072]{2,1,0:T(8,128)(2,1)}, bf16[2,48,3072]{2,1,0:T(8,128)(2,1)}, bf16[4,48,3072]{2,1,0:T(8,128)(2,1)}) custom-call(s32[1]{0:T(128)} %bitcast.9.index_ref, bf16[768,1536]{1,0:T(8,128)(2,1)} %convolution_convert_fusion.3.refs_0_, ...), custom_call_target="tpu_custom_call" | custom-call | flops 1 | bytes 1 | tf_op jit(solution)/shard_map/pallas_call | solution.py:219
  178.8 12.7 %shard_map.316 = (f32[1024,768]{1,0:T(8,128)}, bf16[1024,768]{1,0:T(8,128)(2,1)}, f32[8,768]{1,0:T(8,128)}, f32[8,3072]{1,0:T(8,128)}) custom-call(f32[1024,768]{1,0:T(8,128)} %get-tuple-element.225.s_ref, bf16[1024,1536]{1,0:T(8,128)(2,1)} %copy-done.5, bf16[1024,1536]{1,0:T(8,128)(2,1)} %copy-done.4, f32[1024,768]{1,0:T(8,128)} %get-tuple-element.231.f_ref, ...), custom_call_target="tpu_custom_call" | custom-call | flops 1 | bytes 1 | tf_op jit(solution)/shard_map/pallas_call | solution.py:503
  191.5 3.5 %convolution_convert_fusion.6 = bf16[768,384]{1,0:T(8,128)(2,1)} fusion(bf16[1024,768]{1,0:T(8,128)(2,1)} %get-tuple-element.235, bf16[1024,384]{1,0:T(8,128)(2,1)} %get-tuple-element.188.c1_ref.c_ref), kind=kOutput, calls=%fused_computation.24 | convolution fusion | flops 604274688 | bytes 2949120 | tf_op jit(solution)/shard_map/dot_general | solution.py:21
  195.0 1.8 shard_map.317.table_ref
  196.9 3.4 %convolution_convert_fusion.7.r0_ref = bf16[768,384]{1,0:T(8,128)(2,1)} fusion(bf16[1024,768]{1,0:T(8,128)(2,1)} %get-tuple-element.235, bf16[1024,384]{1,0:T(8,128)(2,1)S(1)} %copy-done.8), kind=kOutput, calls=%fused_computation.25 | convolution fusion | flops 604274688 | bytes 2949120 | tf_op jit(solution)/shard_map/dot_general | solution.py:21
  200.3 1.9 convolution_convert_fusion.5.d_ref
  202.2 1.9 convolution_convert_fusion.4.d_ref
  204.0 1.8 collective-permute-done.31.r1_ref.f1_ref
  207.3 2.7 shard_map.318
  211.9 12.2 %shard_map.319.d_ref.d1_ref = bf16[3,1024,384]{2,1,0:T(8,128)(2,1)} custom-call(s32[2]{0:T(128)} %dynamic_slice.3.lens, bf16[1024,384]{1,0:T(8,128)(2,1)} %get-tuple-element.184.q_ref, bf16[1024,384]{1,0:T(8,128)(2,1)} %get-tuple-element.185.k_ref, bf16[1024,384]{1,0:T(8,128)(2,1)} %get-tuple-element.186.v_ref, ...), custom_call_target="tpu_custom_call" | custom-call | flops 1 | bytes 1 | tf_op jit(solution)/shard_map/pallas_call | solution.py:696
  226.4 3.2 %shard_map.320 = (f32[48,3072]{1,0:T(8,128)}, bf16[48,3072]{1,0:T(8,128)(2,1)}, bf16[48,3072]{1,0:T(8,128)(2,1)}, bf16[48,3072]{1,0:T(8,128)(2,1)}) custom-call(bf16[4,48,3072]{2,1,0:T(8,128)(2,1)} %get-tuple-element.227.own_ref, bf16[4,48,3072]{2,1,0:T(8,128)(2,1)} %copy-done.2, bf16[4,48,3072]{2,1,0:T(8,128)(2,1)} %copy-done.3, ...), custom_call_target="tpu_custom_call" | custom-call | flops 1 | bytes 1 | tf_op jit(solution)/shard_map/pallas_call | solution.py:357
  229.6 5.9 %shard_map.321 = (bf16[3,768,384]{2,1,0:T(8,128)(2,1)}, f32[3,8,384]{2,1,0:T(8,128)}) custom-call(bf16[768,1024]{1,0:T(8,128)(2,1)} %bitcast.60, bf16[3,1024,384]{2,1,0:T(8,128)(2,1)} %shard_map.319.d_ref.d1_ref), custom_call_target="tpu_custom_call" | custom-call | flops 1 | bytes 1 | tf_op jit(solution)/shard_map/pallas_call | solution.py:240
  235.8 1.6 collective-permute-start.40
  237.5 2.4 collective-permute-start.41
  240.5 12.0 %shard_map.322.d_ref.d0_ref = bf16[3,1024,384]{2,1,0:T(8,128)(2,1)} custom-call(s32[2]{0:T(128)} %dynamic_slice.3.lens, bf16[1024,384]{1,0:T(8,128)(2,1)} %get-tuple-element.170.q_ref, bf16[1024,384]{1,0:T(8,128)(2,1)} %get-tuple-element.171.k_ref, bf16[1024,384]{1,0:T(8,128)(2,1)} %get-tuple-element.172.v_ref, ...), custom_call_target="tpu_custom_call" | custom-call | flops 1 | bytes 1 | tf_op jit(solution)/shard_map/pallas_call | solution.py:696
  253.7 8.0 %shard_map.323 = (bf16[4,208,384]{2,1,0:T(8,128)(2,1)}, bf16[4,208,384]{2,1,0:T(8,128)(2,1)}, bf16[2,208,384]{2,1,0:T(8,128)(2,1)}, bf16[2,208,384]{2,1,0:T(8,128)(2,1)}, bf16[4,208,384]{2,1,0:T(8,128)(2,1)}) custom-call(s32[2]{0:T(128)} %pad_add_fusion.at_ref, bf16[768,1024]{1,0:T(8,128)(2,1)} %bitcast.61, bf16[3,1024,384]{2,1,0:T(8,128)(2,1)} %shard_map.322.d_ref.d0_ref, ...), custom_call_target="tpu_custom_call" | custom-call | flops 1 | bytes 1 | tf_op jit(solution)/shard_map/pallas_call | solution.py:296
  264.1 6.3 %shard_map.324.f_ref = f32[1024,768]{1,0:T(8,128)} custom-call(f32[1024,768]{1,0:T(8,128)} %get-tuple-element.266.f_ref, bf16[3,1024,384]{2,1,0:T(8,128)(2,1)} %shard_map.322.d_ref.d0_ref, bf16[3,1024,384]{2,1,0:T(8,128)(2,1)} %shard_map.319.d_ref.d1_ref, bf16[3,768,384]{2,1,0:T(8,128)(2,1)} %get-tuple-element.161.w_ref.w0_ref, ...), custom_call_target="tpu_custom_call", output_to_operand_aliasing={{}: (0, {})} | custom-call | flops 1811939328 | bytes 3145728 | tf_op jit(solution)/shard_map/pallas_call | solution.py:453
  270.5 7.4 %collective-permute-done.37.r1_ref.f1_ref = bf16[4,208,384]{2,1,0:T(8,128)(2,1)S(1)} collective-permute-done((bf16[4,208,384]{2,1,0:T(8,128)(2,1)}, bf16[4,208,384]{2,1,0:T(8,128)(2,1)S(1)}, u32[]{:S(2)}, u32[]{:S(2)}) %collective-permute-start.37) | collective-permute-done | bytes 639008 | tf_op jit(solution)/shard_map/ppermute | solution.py:31
  279.5 2.2 shard_map.325
  284.7 5.1 %collective-permute-done.42.r1_ref = bf16[2,208,384]{2,1,0:T(8,128)(2,1)S(1)} collective-permute-done((bf16[2,208,384]{2,1,0:T(8,128)(2,1)}, bf16[2,208,384]{2,1,0:T(8,128)(2,1)S(1)}, u32[]{:S(2)}, u32[]{:S(2)}) %collective-permute-start.42) | collective-permute-done | bytes 319520 | tf_op jit(solution)/shard_map/ppermute | solution.py:31
  291.4 2.5 shard_map.326
  293.8 3.1 collective-permute-start.44
  296.9 2.4 collective-permute-start.46
  299.3 6.3 %shard_map.327 = f32[1024,768]{1,0:T(8,128)} custom-call(f32[1024,768]{1,0:T(8,128)} %shard_map.324.f_ref, bf16[3,1024,384]{2,1,0:T(8,128)(2,1)} %shard_map.322.d_ref.d0_ref, bf16[3,1024,384]{2,1,0:T(8,128)(2,1)} %shard_map.319.d_ref.d1_ref, bf16[3,768,384]{2,1,0:T(8,128)(2,1)} %get-tuple-element.161.w_ref.w0_ref, ...), custom_call_target="tpu_custom_call", output_to_operand_aliasing={{}: (0, {})} | custom-call | flops 1811939328 | bytes 3145728 | tf_op jit(solution)/shard_map/pallas_call | solution.py:453
  305.6 3.7 %collective-permute-done.45 = bf16[208,384]{1,0:T(8,128)(2,1)S(1)} collective-permute-done((bf16[208,384]{1,0:T(8,128)(2,1)}, bf16[208,384]{1,0:T(8,128)(2,1)S(1)}, u32[]{:S(2)}, u32[]{:S(2)}) %collective-permute-start.45) | collective-permute-done | bytes 159776 | tf_op jit(solution)/shard_map/ppermute | solution.py:31
  (205 shorter events, 41.1 us)
Async XLA Ops:
  2.2 6.6 %collective-permute-start.1 = (bf16[160,384]{1,0:T(8,128)(2,1)}, bf16[160,384]{1,0:T(8,128)(2,1)S(1)}, u32[]{:S(2)}, u32[]{:S(2)}) collective-permute-start(bf16[160,384]{1,0:T(8,128)(2,1)} %shard_map.305), channel_id=1, source_target_pairs={{0,8},{2,10},{4,12},{6,14},{8,0},{10,2},{12,4},{14,6},{16,24},{18,... | collective-permute-start | bytes 368648 | tf_op jit(solution)/shard_map/ppermute | solution.py:31
  5.3 9.6 %collective-permute-start.2 = (bf16[160,384]{1,0:T(8,128)(2,1)}, bf16[160,384]{1,0:T(8,128)(2,1)S(1)}, u32[]{:S(2)}, u32[]{:S(2)}) collective-permute-start(bf16[160,384]{1,0:T(8,128)(2,1)} %shard_map.305), channel_id=1, source_target_pairs={{0,24},{2,26},{4,28},{6,30},{8,16},{10,18},{12,20},{14,22},{16,8},... | collective-permute-start | bytes 368648 | tf_op jit(solution)/shard_map/ppermute | solution.py:31
  7.8 11.3 %collective-permute-start = (bf16[160,384]{1,0:T(8,128)(2,1)}, bf16[160,384]{1,0:T(8,128)(2,1)S(1)}, u32[]{:S(2)}, u32[]{:S(2)}) collective-permute-start(bf16[160,384]{1,0:T(8,128)(2,1)} %shard_map.305), channel_id=1, source_target_pairs={{0,16},{2,18},{4,20},{6,22},{8,24},{10,26},{12,28},{14,30},{16,0},... | collective-permute-start | bytes 368648 | tf_op jit(solution)/shard_map/ppermute | solution.py:31
  14.9 24.7 %copy-start.21 = (bf16[2,160,384]{2,1,0:T(8,128)(2,1)}, bf16[2,160,384]{2,1,0:T(8,128)(2,1)S(1)}, u32[]{:S(2)}) copy-start(bf16[2,160,384]{2,1,0:T(8,128)(2,1)S(1)} %pad_maximum_fusion.3.refs_1_) | copy-start | bytes 737284
  14.9 8.7 %collective-permute-start.5 = (bf16[2,160,384]{2,1,0:T(8,128)(2,1)S(1)}, bf16[2,160,384]{2,1,0:T(8,128)(2,1)S(1)}, u32[]{:S(2)}, u32[]{:S(2)}) collective-permute-start(bf16[2,160,384]{2,1,0:T(8,128)(2,1)S(1)} %pad_maximum_fusion.3.refs_1_), channel_id=1, source_target_pairs={{0,2},{2,0},{4,6},{6,4},{8,10},{10,8},{12,14},{14,12},{16,18},{18,... | collective-permute-start | bytes 737288 | tf_op jit(solution)/shard_map/ppermute | solution.py:31
  20.0 19.6 %copy-start.22 = (bf16[2,160,384]{2,1,0:T(8,128)(2,1)}, bf16[2,160,384]{2,1,0:T(8,128)(2,1)S(1)}, u32[]{:S(2)}) copy-start(bf16[2,160,384]{2,1,0:T(8,128)(2,1)S(1)} %pad_maximum_fusion.2.refs_0_) | copy-start | bytes 737284
  20.0 8.9 %collective-permute-start.6 = (bf16[2,160,384]{2,1,0:T(8,128)(2,1)S(1)}, bf16[2,160,384]{2,1,0:T(8,128)(2,1)S(1)}, u32[]{:S(2)}, u32[]{:S(2)}) collective-permute-start(bf16[2,160,384]{2,1,0:T(8,128)(2,1)S(1)} %pad_maximum_fusion.2.refs_0_), channel_id=1, source_target_pairs={{0,4},{2,6},{4,0},{6,2},{8,12},{10,14},{12,8},{14,10},{16,20},{18,... | collective-permute-start | bytes 737288 | tf_op jit(solution)/shard_map/ppermute | solution.py:31
  21.6 17.9 %collective-permute-start.7 = (bf16[2,160,384]{2,1,0:T(8,128)(2,1)S(1)}, bf16[2,160,384]{2,1,0:T(8,128)(2,1)S(1)}, u32[]{:S(2)}, u32[]{:S(2)}) collective-permute-start(bf16[2,160,384]{2,1,0:T(8,128)(2,1)S(1)} %pad_maximum_fusion.3.refs_1_), channel_id=1, source_target_pairs={{0,4},{2,6},{4,0},{6,2},{8,12},{10,14},{12,8},{14,10},{16,20},{18,... | collective-permute-start | bytes 737288 | tf_op jit(solution)/shard_map/ppermute | solution.py:31
  22.1 17.4 %collective-permute-start.4 = (bf16[2,160,384]{2,1,0:T(8,128)(2,1)S(1)}, bf16[2,160,384]{2,1,0:T(8,128)(2,1)S(1)}, u32[]{:S(2)}, u32[]{:S(2)}) collective-permute-start(bf16[2,160,384]{2,1,0:T(8,128)(2,1)S(1)} %pad_maximum_fusion.2.refs_0_), channel_id=1, source_target_pairs={{0,2},{2,0},{4,6},{6,4},{8,10},{10,8},{12,14},{14,12},{16,18},{18,... | collective-permute-start | bytes 737288 | tf_op jit(solution)/shard_map/ppermute | solution.py:31
  23.6 16.0 %copy-start.45 = (bf16[2,160,384]{2,1,0:T(8,128)(2,1)}, bf16[2,160,384]{2,1,0:T(8,128)(2,1)S(1)}, u32[]{:S(2)}) copy-start(bf16[2,160,384]{2,1,0:T(8,128)(2,1)S(1)} %collective-permute-done.5.refs_3_) | copy-start | bytes 737284
  23.6 15.9 %collective-permute-start.9 = (bf16[2,160,384]{2,1,0:T(8,128)(2,1)S(1)}, bf16[2,160,384]{2,1,0:T(8,128)(2,1)S(1)}, u32[]{:S(2)}, u32[]{:S(2)}) collective-permute-start(bf16[2,160,384]{2,1,0:T(8,128)(2,1)S(1)} %collective-permute-done.5.refs_3_), channel_id=1, source_target_pairs={{0,4},{2,6},{4,0},{6,2},{8,12},{10,14},{12,8},{14,10},{16,20},{18,... | collective-permute-start | bytes 737288 | tf_op jit(solution)/shard_map/ppermute | solution.py:31
  28.9 10.7 %copy-start.46 = (bf16[2,160,384]{2,1,0:T(8,128)(2,1)}, bf16[2,160,384]{2,1,0:T(8,128)(2,1)S(1)}, u32[]{:S(2)}) copy-start(bf16[2,160,384]{2,1,0:T(8,128)(2,1)S(1)} %collective-permute-done.6.refs_4_) | copy-start | bytes 737284
  28.9 10.6 %collective-permute-start.8 = (bf16[2,160,384]{2,1,0:T(8,128)(2,1)S(1)}, bf16[2,160,384]{2,1,0:T(8,128)(2,1)S(1)}, u32[]{:S(2)}, u32[]{:S(2)}) collective-permute-start(bf16[2,160,384]{2,1,0:T(8,128)(2,1)S(1)} %collective-permute-done.6.refs_4_), channel_id=1, source_target_pairs={{0,2},{2,0},{4,6},{6,4},{8,10},{10,8},{12,14},{14,12},{16,18},{18,... | collective-permute-start | bytes 737288 | tf_op jit(solution)/shard_map/ppermute | solution.py:31
  31.3 8.2 %collective-permute-start.3 = (bf16[48,1920]{1,0:T(8,128)(2,1)S(1)}, bf16[48,1920]{1,0:T(8,128)(2,1)S(1)}, u32[]{:S(2)}, u32[]{:S(2)}) collective-permute-start(bf16[48,1920]{1,0:T(8,128)(2,1)S(1)} %get-tuple-element.151), channel_id=1, source_target_pairs={{0,16},{2,18},{4,20},{6,22},{8,24},{10,26},{12,28},{14,30},{16,0},... | collective-permute-start | bytes 552968 | tf_op jit(solution)/shard_map/ppermute | solution.py:31
  43.5 11.4 %collective-permute-start.14 = (bf16[3,768,384]{2,1,0:T(8,128)(2,1)}, bf16[3,768,384]{2,1,0:T(8,128)(2,1)S(1)}, u32[]{:S(2)}, u32[]{:S(2)}) collective-permute-start(bf16[3,768,384]{2,1,0:T(8,128)(2,1)} %get-tuple-element.161.w_ref.w0_ref), channel_id=1, source_target_pairs={{0,1},{1,0},{2,3},{3,2},{4,5},{5,4},{6,7},{7,6},{8,9},{9,8},{10,11... | collective-permute-start | bytes 5308424 | tf_op jit(solution)/shard_map/ppermute | solution.py:35
  43.5 18.3 %copy-start.19 = (bf16[2,48,1920]{2,1,0:T(8,128)(2,1)}, bf16[2,48,1920]{2,1,0:T(8,128)(2,1)S(1)}, u32[]{:S(2)}) copy-start(bf16[2,48,1920]{2,1,0:T(8,128)(2,1)S(1)} %pad_maximum_fusion.refs_0_) | copy-start | bytes 1105924
  43.5 18.4 %collective-permute-start.10 = (bf16[2,48,1920]{2,1,0:T(8,128)(2,1)S(1)}, bf16[2,48,1920]{2,1,0:T(8,128)(2,1)S(1)}, u32[]{:S(2)}, u32[]{:S(2)}) collective-permute-start(bf16[2,48,1920]{2,1,0:T(8,128)(2,1)S(1)} %pad_maximum_fusion.refs_0_), channel_id=1, source_target_pairs={{0,8},{2,10},{4,12},{6,14},{8,0},{10,2},{12,4},{14,6},{16,24},{18,... | collective-permute-start | bytes 1105928 | tf_op jit(solution)/shard_map/ppermute | solution.py:31
  43.6 18.3 %collective-permute-start.12 = (bf16[2,48,1920]{2,1,0:T(8,128)(2,1)S(1)}, bf16[2,48,1920]{2,1,0:T(8,128)(2,1)S(1)}, u32[]{:S(2)}, u32[]{:S(2)}) collective-permute-start(bf16[2,48,1920]{2,1,0:T(8,128)(2,1)S(1)} %pad_maximum_fusion.refs_0_), channel_id=1, source_target_pairs={{0,2},{2,0},{4,6},{6,4},{8,10},{10,8},{12,14},{14,12},{16,18},{18,... | collective-permute-start | bytes 1105928 | tf_op jit(solution)/shard_map/ppermute | solution.py:31
  44.3 17.6 %collective-permute-start.13 = (bf16[2,48,1920]{2,1,0:T(8,128)(2,1)S(1)}, bf16[2,48,1920]{2,1,0:T(8,128)(2,1)S(1)}, u32[]{:S(2)}, u32[]{:S(2)}) collective-permute-start(bf16[2,48,1920]{2,1,0:T(8,128)(2,1)S(1)} %pad_maximum_fusion.refs_0_), channel_id=1, source_target_pairs={{0,4},{2,6},{4,0},{6,2},{8,12},{10,14},{12,8},{14,10},{16,20},{18,... | collective-permute-start | bytes 1105928 | tf_op jit(solution)/shard_map/ppermute | solution.py:31
  45.9 16.0 %collective-permute-start.11 = (bf16[48,1536]{1,0:T(8,128)(2,1)}, bf16[48,1536]{1,0:T(8,128)(2,1)S(1)}, u32[]{:S(2)}, u32[]{:S(2)}) collective-permute-start(bf16[48,1536]{1,0:T(8,128)(2,1)} %bitcast.64), channel_id=1, source_target_pairs={{0,16},{2,18},{4,20},{6,22},{8,24},{10,26},{12,28},{14,30},{16,0},... | collective-permute-start | bytes 442376 | tf_op jit(solution)/shard_map/ppermute | solution.py:31
  49.1 18.6 %copy-start.56 = (s32[4]{0:T(128)S(1)}, s32[4]{0:T(128)}, u32[]{:S(2)}) copy-start(s32[4]{0:T(128)} %param.20) | copy-start | bytes 52
  61.9 29.0 %copy-start.29 = (bf16[2,48,1920]{2,1,0:T(8,128)(2,1)}, bf16[2,48,1920]{2,1,0:T(8,128)(2,1)S(1)}, u32[]{:S(2)}) copy-start(bf16[2,48,1920]{2,1,0:T(8,128)(2,1)S(1)} %collective-permute-done.10.refs_1_) | copy-start | bytes 1105924
  61.9 29.0 %copy-start.30 = (bf16[2,48,1920]{2,1,0:T(8,128)(2,1)}, bf16[2,48,1920]{2,1,0:T(8,128)(2,1)S(1)}, u32[]{:S(2)}) copy-start(bf16[2,48,1920]{2,1,0:T(8,128)(2,1)S(1)} %collective-permute-done.12.refs_2_) | copy-start | bytes 1105924
  61.9 29.0 %copy-start.31 = (bf16[2,48,1920]{2,1,0:T(8,128)(2,1)}, bf16[2,48,1920]{2,1,0:T(8,128)(2,1)S(1)}, u32[]{:S(2)}) copy-start(bf16[2,48,1920]{2,1,0:T(8,128)(2,1)S(1)} %collective-permute-done.13.refs_4_) | copy-start | bytes 1105924
  62.5 16.5 %collective-permute-start.15 = (bf16[2,48,1920]{2,1,0:T(8,128)(2,1)S(1)}, bf16[2,48,1920]{2,1,0:T(8,128)(2,1)S(1)}, u32[]{:S(2)}, u32[]{:S(2)}) collective-permute-start(bf16[2,48,1920]{2,1,0:T(8,128)(2,1)S(1)} %collective-permute-done.10.refs_1_), channel_id=1, source_target_pairs={{0,2},{2,0},{4,6},{6,4},{8,10},{10,8},{12,14},{14,12},{16,18},{18,... | collective-permute-start | bytes 1105928 | tf_op jit(solution)/shard_map/ppermute | solution.py:31
  63.1 15.9 %collective-permute-start.16 = (bf16[2,48,1920]{2,1,0:T(8,128)(2,1)S(1)}, bf16[2,48,1920]{2,1,0:T(8,128)(2,1)S(1)}, u32[]{:S(2)}, u32[]{:S(2)}) collective-permute-start(bf16[2,48,1920]{2,1,0:T(8,128)(2,1)S(1)} %collective-permute-done.10.refs_1_), channel_id=1, source_target_pairs={{0,4},{2,6},{4,0},{6,2},{8,12},{10,14},{12,8},{14,10},{16,20},{18,... | collective-permute-start | bytes 1105928 | tf_op jit(solution)/shard_map/ppermute | solution.py:31
  64.7 30.7 %copy-start.20 = (bf16[2,48,1536]{2,1,0:T(8,128)(2,1)}, bf16[2,48,1536]{2,1,0:T(8,128)(2,1)S(1)}, u32[]{:S(2)}) copy-start(bf16[2,48,1536]{2,1,0:T(8,128)(2,1)S(1)} %pad_maximum_fusion.1.refs_0_) | copy-start | bytes 884740
  64.7 12.7 %collective-permute-start.17 = (bf16[2,48,1536]{2,1,0:T(8,128)(2,1)S(1)}, bf16[2,48,1536]{2,1,0:T(8,128)(2,1)S(1)}, u32[]{:S(2)}, u32[]{:S(2)}) collective-permute-start(bf16[2,48,1536]{2,1,0:T(8,128)(2,1)S(1)} %pad_maximum_fusion.1.refs_0_), channel_id=1, source_target_pairs={{0,8},{2,10},{4,12},{6,14},{8,0},{10,2},{12,4},{14,6},{16,24},{18,... | collective-permute-start | bytes 884744 | tf_op jit(solution)/shard_map/ppermute | solution.py:31
  64.8 14.2 %collective-permute-start.18 = (bf16[2,48,1536]{2,1,0:T(8,128)(2,1)S(1)}, bf16[2,48,1536]{2,1,0:T(8,128)(2,1)S(1)}, u32[]{:S(2)}, u32[]{:S(2)}) collective-permute-start(bf16[2,48,1536]{2,1,0:T(8,128)(2,1)S(1)} %pad_maximum_fusion.1.refs_0_), channel_id=1, source_target_pairs={{0,4},{2,6},{4,0},{6,2},{8,12},{10,14},{12,8},{14,10},{16,20},{18,... | collective-permute-start | bytes 884744 | tf_op jit(solution)/shard_map/ppermute | solution.py:31
  66.3 12.7 %collective-permute-start.19 = (bf16[2,48,1536]{2,1,0:T(8,128)(2,1)S(1)}, bf16[2,48,1536]{2,1,0:T(8,128)(2,1)S(1)}, u32[]{:S(2)}, u32[]{:S(2)}) collective-permute-start(bf16[2,48,1536]{2,1,0:T(8,128)(2,1)S(1)} %pad_maximum_fusion.1.refs_0_), channel_id=1, source_target_pairs={{0,2},{2,0},{4,6},{6,4},{8,10},{10,8},{12,14},{14,12},{16,18},{18,... | collective-permute-start | bytes 884744 | tf_op jit(solution)/shard_map/ppermute | solution.py:31
  79.1 11.8 %copy-start.32 = (bf16[2,48,1920]{2,1,0:T(8,128)(2,1)}, bf16[2,48,1920]{2,1,0:T(8,128)(2,1)S(1)}, u32[]{:S(2)}) copy-start(bf16[2,48,1920]{2,1,0:T(8,128)(2,1)S(1)} %collective-permute-done.15.refs_3_) | copy-start | bytes 1105924
  79.8 11.1 %copy-start.33 = (bf16[2,48,1920]{2,1,0:T(8,128)(2,1)}, bf16[2,48,1920]{2,1,0:T(8,128)(2,1)S(1)}, u32[]{:S(2)}) copy-start(bf16[2,48,1920]{2,1,0:T(8,128)(2,1)S(1)} %collective-permute-done.16.refs_5_) | copy-start | bytes 1105924
  79.9 11.0 %collective-permute-start.21 = (bf16[2,48,1920]{2,1,0:T(8,128)(2,1)S(1)}, bf16[2,48,1920]{2,1,0:T(8,128)(2,1)S(1)}, u32[]{:S(2)}, u32[]{:S(2)}) collective-permute-start(bf16[2,48,1920]{2,1,0:T(8,128)(2,1)S(1)} %collective-permute-done.13.refs_4_), channel_id=1, source_target_pairs={{0,2},{2,0},{4,6},{6,4},{8,10},{10,8},{12,14},{14,12},{16,18},{18,... | collective-permute-start | bytes 1105928 | tf_op jit(solution)/shard_map/ppermute | solution.py:31
  81.3 9.6 %collective-permute-start.22 = (bf16[2,48,1920]{2,1,0:T(8,128)(2,1)S(1)}, bf16[2,48,1920]{2,1,0:T(8,128)(2,1)S(1)}, u32[]{:S(2)}, u32[]{:S(2)}) collective-permute-start(bf16[2,48,1920]{2,1,0:T(8,128)(2,1)S(1)} %collective-permute-done.15.refs_3_), channel_id=1, source_target_pairs={{0,4},{2,6},{4,0},{6,2},{8,12},{10,14},{12,8},{14,10},{16,20},{18,... | collective-permute-start | bytes 1105928 | tf_op jit(solution)/shard_map/ppermute | solution.py:31
  95.4 12.2 %copy-start.11 = (bf16[768,1536]{1,0:T(8,128)(2,1)S(1)}, bf16[768,1536]{1,0:T(8,128)(2,1)}, u32[]{:S(2)}) copy-start(bf16[768,1536]{1,0:T(8,128)(2,1)} %get-tuple-element.203.w0_ref) | copy-start | bytes 7077892
  95.4 3.1 %collective-permute-start.23 = (bf16[768,384]{1,0:T(8,128)(2,1)}, bf16[768,384]{1,0:T(8,128)(2,1)S(1)}, u32[]{:S(2)}, u32[]{:S(2)}) collective-permute-start(bf16[768,384]{1,0:T(8,128)(2,1)} %get-tuple-element.197.w0_ref), channel_id=1, source_target_pairs={{0,1},{1,0},{2,3},{3,2},{4,5},{5,4},{6,7},{7,6},{8,9},{9,8},{10,11... | collective-permute-start | bytes 1769480 | tf_op jit(solution)/shard_map/ppermute | solution.py:35
  95.4 10.1 %collective-permute-start.20 = (bf16[2,48,1536]{2,1,0:T(8,128)(2,1)}, bf16[2,48,1536]{2,1,0:T(8,128)(2,1)}, u32[]{:S(2)}, u32[]{:S(2)}) collective-permute-start(bf16[2,48,1536]{2,1,0:T(8,128)(2,1)} %copy-done.39), channel_id=1, source_target_pairs={{0,2},{2,0},{4,6},{6,4},{8,10},{10,8},{12,14},{14,12},{16,18},{18,... | collective-permute-start | bytes 884744 | tf_op jit(solution)/shard_map/ppermute | solution.py:31
  96.9 17.4 %collective-permute-start.24 = (bf16[2,48,1536]{2,1,0:T(8,128)(2,1)}, bf16[2,48,1536]{2,1,0:T(8,128)(2,1)}, u32[]{:S(2)}, u32[]{:S(2)}) collective-permute-start(bf16[2,48,1536]{2,1,0:T(8,128)(2,1)} %copy-done.39), channel_id=1, source_target_pairs={{0,4},{2,6},{4,0},{6,2},{8,12},{10,14},{12,8},{14,10},{16,20},{18,... | collective-permute-start | bytes 884744 | tf_op jit(solution)/shard_map/ppermute | solution.py:31
  98.5 21.8 %collective-permute-start.27 = (bf16[768,1536]{1,0:T(8,128)(2,1)}, bf16[768,1536]{1,0:T(8,128)(2,1)}, u32[]{:S(2)}, u32[]{:S(2)}) collective-permute-start(bf16[768,1536]{1,0:T(8,128)(2,1)} %get-tuple-element.203.w0_ref), channel_id=1, source_target_pairs={{0,1},{1,0},{2,3},{3,2},{4,5},{5,4},{6,7},{7,6},{8,9},{9,8},{10,11... | collective-permute-start | bytes 7077896 | tf_op jit(solution)/shard_map/ppermute | solution.py:35
  105.6 9.5 %collective-permute-start.25 = (bf16[2,48,1536]{2,1,0:T(8,128)(2,1)S(1)}, bf16[2,48,1536]{2,1,0:T(8,128)(2,1)S(1)}, u32[]{:S(2)}, u32[]{:S(2)}) collective-permute-start(bf16[2,48,1536]{2,1,0:T(8,128)(2,1)S(1)} %copy-done.41), channel_id=1, source_target_pairs={{0,2},{2,0},{4,6},{6,4},{8,10},{10,8},{12,14},{14,12},{16,18},{18,... | collective-permute-start | bytes 884744 | tf_op jit(solution)/shard_map/ppermute | solution.py:31
  107.0 9.4 %collective-permute-start.26 = (bf16[2,48,1536]{2,1,0:T(8,128)(2,1)}, bf16[2,48,1536]{2,1,0:T(8,128)(2,1)S(1)}, u32[]{:S(2)}, u32[]{:S(2)}) collective-permute-start(bf16[2,48,1536]{2,1,0:T(8,128)(2,1)} %collective-permute-done.20.refs_3_), channel_id=1, source_target_pairs={{0,4},{2,6},{4,0},{6,2},{8,12},{10,14},{12,8},{14,10},{16,20},{18,... | collective-permute-start | bytes 884744 | tf_op jit(solution)/shard_map/ppermute | solution.py:31
  120.3 7.4 %collective-permute-start.28 = (bf16[768,1536]{1,0:T(8,128)(2,1)}, bf16[768,1536]{1,0:T(8,128)(2,1)S(1)}, u32[]{:S(2)}, u32[]{:S(2)}) collective-permute-start(bf16[768,1536]{1,0:T(8,128)(2,1)} %shard_map.313.w0_ref), channel_id=1, source_target_pairs={{0,1},{1,0},{2,3},{3,2},{4,5},{5,4},{6,7},{7,6},{8,9},{9,8},{10,11... | collective-permute-start | bytes 7077896 | tf_op jit(solution)/shard_map/ppermute | solution.py:35
  129.0 12.7 %copy-start.7 = (bf16[1024,1536]{1,0:T(8,128)(2,1)S(1)}, bf16[1024,1536]{1,0:T(8,128)(2,1)}, u32[]{:S(2)}) copy-start(bf16[1024,1536]{1,0:T(8,128)(2,1)} %get-tuple-element.305.a1_ref) | copy-start | bytes 9437188
  146.3 4.7 %collective-permute-start.29 = (bf16[768,1536]{1,0:T(8,128)(2,1)S(1)}, bf16[768,1536]{1,0:T(8,128)(2,1)S(1)}, u32[]{:S(2)}, u32[]{:S(2)}) collective-permute-start(bf16[768,1536]{1,0:T(8,128)(2,1)S(1)} %convolution_convert_fusion.2), channel_id=1, source_target_pairs={{0,1},{1,0},{2,3},{3,2},{4,5},{5,4},{6,7},{7,6},{8,9},{9,8},{10,11... | collective-permute-start | bytes 7077896 | tf_op jit(solution)/shard_map/ppermute | solution.py:35
  146.9 13.0 %slice-start = ((s8[6291456]{0:T(1024)(128)(4,1)}), s8[4194304]{0:T(1024)(128)(4,1)S(1)}, s32[]{:S(2)}) async-start(s8[6291456]{0:T(1024)(128)(4,1)} %bitcast.72), calls=%async_computation | async-start | bytes 8388608
  159.4 9.9 %collective-permute-start.30 = (bf16[768,1536]{1,0:T(8,128)(2,1)S(1)}, bf16[768,1536]{1,0:T(8,128)(2,1)S(1)}, u32[]{:S(2)}, u32[]{:S(2)}) collective-permute-start(bf16[768,1536]{1,0:T(8,128)(2,1)S(1)} %convolution_convert_fusion), channel_id=1, source_target_pairs={{0,1},{1,0},{2,3},{3,2},{4,5},{5,4},{6,7},{7,6},{8,9},{9,8},{10,11... | collective-permute-start | bytes 7077896 | tf_op jit(solution)/shard_map/ppermute | solution.py:35
  177.6 28.2 %collective-permute-start.31 = (bf16[4,48,3072]{2,1,0:T(8,128)(2,1)}, bf16[4,48,3072]{2,1,0:T(8,128)(2,1)S(1)}, u32[]{:S(2)}, u32[]{:S(2)}) collective-permute-start(bf16[4,48,3072]{2,1,0:T(8,128)(2,1)} %get-tuple-element.223), channel_id=1, source_target_pairs={{0,2},{2,0},{4,6},{6,4},{8,10},{10,8},{12,14},{14,12},{16,18},{18,... | collective-permute-start | bytes 3538952 | tf_op jit(solution)/shard_map/ppermute | solution.py:31
  178.3 27.9 %collective-permute-start.32 = (bf16[4,48,3072]{2,1,0:T(8,128)(2,1)}, bf16[4,48,3072]{2,1,0:T(8,128)(2,1)S(1)}, u32[]{:S(2)}, u32[]{:S(2)}) collective-permute-start(bf16[4,48,3072]{2,1,0:T(8,128)(2,1)} %get-tuple-element.224), channel_id=1, source_target_pairs={{0,4},{2,6},{4,0},{6,2},{8,12},{10,14},{12,8},{14,10},{16,20},{18,... | collective-permute-start | bytes 3538952 | tf_op jit(solution)/shard_map/ppermute | solution.py:31
  195.0 9.0 %collective-permute-start.33 = (bf16[768,384]{1,0:T(8,128)(2,1)}, bf16[768,384]{1,0:T(8,128)(2,1)}, u32[]{:S(2)}, u32[]{:S(2)}) collective-permute-start(bf16[768,384]{1,0:T(8,128)(2,1)} %convolution_convert_fusion.6), channel_id=1, source_target_pairs={{0,1},{1,0},{2,3},{3,2},{4,5},{5,4},{6,7},{7,6},{8,9},{9,8},{10,11... | collective-permute-start | bytes 1769480 | tf_op jit(solution)/shard_map/ppermute | solution.py:35
  210.0 14.7 %collective-permute-start.34 = (bf16[2,48,3072]{2,1,0:T(8,128)(2,1)}, bf16[2,48,3072]{2,1,0:T(8,128)(2,1)S(1)}, u32[]{:S(2)}, u32[]{:S(2)}) collective-permute-start(bf16[2,48,3072]{2,1,0:T(8,128)(2,1)} %get-tuple-element.241), channel_id=1, source_target_pairs={{0,2},{2,0},{4,6},{6,4},{8,10},{10,8},{12,14},{14,12},{16,18},{18,... | collective-permute-start | bytes 1769480 | tf_op jit(solution)/shard_map/ppermute | solution.py:31
  211.4 14.2 %collective-permute-start.35 = (bf16[2,48,3072]{2,1,0:T(8,128)(2,1)}, bf16[2,48,3072]{2,1,0:T(8,128)(2,1)S(1)}, u32[]{:S(2)}, u32[]{:S(2)}) collective-permute-start(bf16[2,48,3072]{2,1,0:T(8,128)(2,1)} %get-tuple-element.242), channel_id=1, source_target_pairs={{0,4},{2,6},{4,0},{6,2},{8,12},{10,14},{12,8},{14,10},{16,20},{18,... | collective-permute-start | bytes 1769480 | tf_op jit(solution)/shard_map/ppermute | solution.py:31
  235.5 17.0 %collective-permute-start.36 = (bf16[3,768,384]{2,1,0:T(8,128)(2,1)}, bf16[3,768,384]{2,1,0:T(8,128)(2,1)S(1)}, u32[]{:S(2)}, u32[]{:S(2)}) collective-permute-start(bf16[3,768,384]{2,1,0:T(8,128)(2,1)} %get-tuple-element.252), channel_id=1, source_target_pairs={{0,1},{1,0},{2,3},{3,2},{4,5},{5,4},{6,7},{7,6},{8,9},{9,8},{10,11... | collective-permute-start | bytes 5308424 | tf_op jit(solution)/shard_map/ppermute | solution.py:35
  235.5 26.2 %collective-permute-start.39 = (bf16[48,3072]{1,0:T(8,128)(2,1)}, bf16[48,3072]{1,0:T(8,128)(2,1)S(1)}, u32[]{:S(2)}, u32[]{:S(2)}) collective-permute-start(bf16[48,3072]{1,0:T(8,128)(2,1)} %get-tuple-element.261), channel_id=1, source_target_pairs={{0,8},{2,10},{4,12},{6,14},{8,0},{10,2},{12,4},{14,6},{16,24},{18,... | collective-permute-start | bytes 884744 | tf_op jit(solution)/shard_map/ppermute | solution.py:31
  235.8 25.9 %collective-permute-start.40 = (bf16[48,3072]{1,0:T(8,128)(2,1)S(1)}, bf16[48,3072]{1,0:T(8,128)(2,1)S(1)}, u32[]{:S(2)}, u32[]{:S(2)}) collective-permute-start(bf16[48,3072]{1,0:T(8,128)(2,1)S(1)} %copy-done.55), channel_id=1, source_target_pairs={{0,16},{2,18},{4,20},{6,22},{8,24},{10,26},{12,28},{14,30},{16,0},... | collective-permute-start | bytes 884744 | tf_op jit(solution)/shard_map/ppermute | solution.py:31
  237.5 24.2 %collective-permute-start.41 = (bf16[48,3072]{1,0:T(8,128)(2,1)S(1)}, bf16[48,3072]{1,0:T(8,128)(2,1)S(1)}, u32[]{:S(2)}, u32[]{:S(2)}) collective-permute-start(bf16[48,3072]{1,0:T(8,128)(2,1)S(1)} %copy-done.54), channel_id=1, source_target_pairs={{0,24},{2,26},{4,28},{6,30},{8,16},{10,18},{12,20},{14,22},{16,8},... | collective-permute-start | bytes 884744 | tf_op jit(solution)/shard_map/ppermute | solution.py:31
  261.7 16.2 %collective-permute-start.37 = (bf16[4,208,384]{2,1,0:T(8,128)(2,1)}, bf16[4,208,384]{2,1,0:T(8,128)(2,1)S(1)}, u32[]{:S(2)}, u32[]{:S(2)}) collective-permute-start(bf16[4,208,384]{2,1,0:T(8,128)(2,1)} %get-tuple-element.258), channel_id=1, source_target_pairs={{0,2},{2,0},{4,6},{6,4},{8,10},{10,8},{12,14},{14,12},{16,18},{18,... | collective-permute-start | bytes 1916936 | tf_op jit(solution)/shard_map/ppermute | solution.py:31
  262.8 15.9 %collective-permute-start.38 = (bf16[4,208,384]{2,1,0:T(8,128)(2,1)}, bf16[4,208,384]{2,1,0:T(8,128)(2,1)S(1)}, u32[]{:S(2)}, u32[]{:S(2)}) collective-permute-start(bf16[4,208,384]{2,1,0:T(8,128)(2,1)} %get-tuple-element.259), channel_id=1, source_target_pairs={{0,4},{2,6},{4,0},{6,2},{8,12},{10,14},{12,8},{14,10},{16,20},{18,... | collective-permute-start | bytes 1916936 | tf_op jit(solution)/shard_map/ppermute | solution.py:31
  281.7 8.2 %collective-permute-start.42 = (bf16[2,208,384]{2,1,0:T(8,128)(2,1)}, bf16[2,208,384]{2,1,0:T(8,128)(2,1)S(1)}, u32[]{:S(2)}, u32[]{:S(2)}) collective-permute-start(bf16[2,208,384]{2,1,0:T(8,128)(2,1)} %get-tuple-element.274), channel_id=1, source_target_pairs={{0,2},{2,0},{4,6},{6,4},{8,10},{10,8},{12,14},{14,12},{16,18},{18,... | collective-permute-start | bytes 958472 | tf_op jit(solution)/shard_map/ppermute | solution.py:31
  282.7 7.9 %collective-permute-start.43 = (bf16[2,208,384]{2,1,0:T(8,128)(2,1)}, bf16[2,208,384]{2,1,0:T(8,128)(2,1)S(1)}, u32[]{:S(2)}, u32[]{:S(2)}) collective-permute-start(bf16[2,208,384]{2,1,0:T(8,128)(2,1)} %get-tuple-element.275), channel_id=1, source_target_pairs={{0,4},{2,6},{4,0},{6,2},{8,12},{10,14},{12,8},{14,10},{16,20},{18,... | collective-permute-start | bytes 958472 | tf_op jit(solution)/shard_map/ppermute | solution.py:31
  293.8 11.7 %collective-permute-start.44 = (bf16[208,384]{1,0:T(8,128)(2,1)}, bf16[208,384]{1,0:T(8,128)(2,1)S(1)}, u32[]{:S(2)}, u32[]{:S(2)}) collective-permute-start(bf16[208,384]{1,0:T(8,128)(2,1)} %get-tuple-element.279), channel_id=1, source_target_pairs={{0,8},{2,10},{4,12},{6,14},{8,0},{10,2},{12,4},{14,6},{16,24},{18,... | collective-permute-start | bytes 479240 | tf_op jit(solution)/shard_map/ppermute | solution.py:31
  296.9 12.3 %collective-permute-start.45 = (bf16[208,384]{1,0:T(8,128)(2,1)}, bf16[208,384]{1,0:T(8,128)(2,1)S(1)}, u32[]{:S(2)}, u32[]{:S(2)}) collective-permute-start(bf16[208,384]{1,0:T(8,128)(2,1)} %get-tuple-element.280), channel_id=1, source_target_pairs={{0,16},{2,18},{4,20},{6,22},{8,24},{10,26},{12,28},{14,30},{16,0},... | collective-permute-start | bytes 479240 | tf_op jit(solution)/shard_map/ppermute | solution.py:31
  296.9 12.4 %copy-start.38 = (f32[208,384]{1,0:T(8,128)S(1)}, f32[208,384]{1,0:T(8,128)}, u32[]{:S(2)}) copy-start(f32[208,384]{1,0:T(8,128)} %get-tuple-element.276) | copy-start | bytes 958468
  296.9 12.3 %collective-permute-start.46 = (bf16[208,384]{1,0:T(8,128)(2,1)}, bf16[208,384]{1,0:T(8,128)(2,1)S(1)}, u32[]{:S(2)}, u32[]{:S(2)}) collective-permute-start(bf16[208,384]{1,0:T(8,128)(2,1)} %get-tuple-element.281), channel_id=1, source_target_pairs={{0,24},{2,26},{4,28},{6,30},{8,16},{10,18},{12,20},{14,22},{16,8},... | collective-permute-start | bytes 479240 | tf_op jit(solution)/shard_map/ppermute | solution.py:31
  309.4 1.3 collective-permute-start.47
  (44 other events, 125.5 us)
